TPU v7x, 32 devices: a whole 2x2x4 slice. The times are simulated.
32 devices in a mesh: batch: 4 (over z), seq: 8 (over y, x, core).
Axes of the slice: x: 2, y: 2, z: 4, core: 2. Of those that a mesh axis runs over, the one named last changes fastest.
Arguments:
- inputs: bfloat16 [4, 2048, 2048], P('batch', 'seq'), may hold values from -6 to 6
- segment_ids: int32 [4, 2048], P('batch'), may hold values from 0 to 3, never falling along the last dimension, each value on 1 to 1024 neighbouring positions
- w_qkv: bfloat16 [6144, 2048], P('seq'), may hold values from -0.125 to 0.125
- w_out: bfloat16 [2048, 2048], P('seq'), may hold values from -0.125 to 0.125
- w_up: bfloat16 [8192, 2048], P('seq'), may hold values from -0.125 to 0.125
- w_down: bfloat16 [2048, 8192], P('seq'), may hold values from -0.0625 to 0.0625
- gain_attn: float32 [2048], replicated, may hold values from 0.5 to 1.5
- gain_mix: float32 [2048], replicated, may hold values from 0.5 to 1.5
- gain_ffn: float32 [2048], replicated, may hold values from 0.5 to 1.5
- gain_hidden: float32 [8192], replicated, may hold values from 0.5 to 1.5
- cotangent: bfloat16 [4, 2048, 2048], P('batch', 'seq'), may hold values from -6 to 6
Outputs:
- outputs: bfloat16 [4, 2048, 2048], P('batch', 'seq')
- grad_inputs: float32 [4, 2048, 2048], P('batch', 'seq')
- grad_w_qkv: float32 [6144, 2048], P('seq')
- grad_w_out: float32 [2048, 2048], P('seq')
- grad_w_up: float32 [8192, 2048], P('seq')
- grad_w_down: float32 [2048, 8192], P('seq')
- grad_gain_attn: float32 [2048], replicated
- grad_gain_mix: float32 [2048], replicated
- grad_gain_ffn: float32 [2048], replicated
- grad_gain_hidden: float32 [8192], replicated
Inputs may be any that keep to these rules, and one draw needn't show every extreme that they name: `segment_ids`: along a row the ids never fall and each id from 0 to 3 marks one document of 1 to 1024 tokens.
All inputs are finite; a program needn't handle non-finite values.
Results may differ from a plain program's by a relative error of at most 0.02.
Values may be sent and summed in bfloat16 or wider, within the bound.
A program may use at most 448 MiB of HBM per device.

v0:
```python
import math

import jax
import jax.numpy as jnp
from jax import lax
from jax.sharding import PartitionSpec as P

HEADS = 32
HEAD_DIM = 64
LENGTH = 2048
QBLOCK = 512
XBASE = 512


EPSILON = 1e-05
MASKED = -1e30


def norm_rows(values, gain):
    average = jnp.mean(values, axis=-1, keepdims=True)
    centered = values - average
    spread = jnp.mean(centered * centered, axis=-1, keepdims=True)
    return centered * lax.rsqrt(spread + EPSILON) * gain


def gelu_norm(upper, gain):
    return norm_rows(jax.nn.gelu(upper, approximate=False), gain)


def doc_positions(seg_row):
    index = jnp.arange(seg_row.shape[0], dtype=jnp.int32)
    change = jnp.concatenate([jnp.ones((1,), dtype=bool), seg_row[1:] != seg_row[:-1]])
    starts = jnp.where(change, index, jnp.zeros_like(index))
    return index - lax.cummax(starts, axis=0)


def xpos_tables(positions):
    half_dim = HEAD_DIM // 2
    channel = jnp.arange(half_dim, dtype=jnp.float32)
    inverse = jnp.exp(channel * (-math.log(10000.0) / half_dim))
    zeta = (channel * (2.0 / HEAD_DIM) + 0.4) / 1.4
    place = positions.astype(jnp.float32)[..., None]
    angle = place * inverse
    growth = jnp.exp((place - 0.5 * LENGTH) * (1.0 / XBASE) * jnp.log(zeta))
    return (jnp.cos(angle), jnp.sin(angle), growth)


def rotate(values, cosine, sine, growth):
    half_dim = values.shape[-1] // 2
    first = values[..., :half_dim]
    second = values[..., half_dim:]
    cosine = cosine[..., None, :]
    sine = sine[..., None, :]
    growth = growth[..., None, :]
    return jnp.concatenate(
        [(first * cosine - second * sine) * growth, (second * cosine + first * sine) * growth],
        axis=-1,
    )


def allowed_pairs(seg_row, start, count):
    seg_block = lax.dynamic_slice_in_dim(seg_row, start, count, 0)
    query_place = start + jnp.arange(count, dtype=jnp.int32)
    key_place = jnp.arange(seg_row.shape[0], dtype=jnp.int32)
    return (seg_block[:, None] == seg_row[None, :]) & (key_place[None, :] <= query_place[:, None])


def block_scores(query_block, keys, allowed):
    scores = jnp.einsum(
        "qhd,khd->hqk", query_block, keys, preferred_element_type=jnp.float32
    ) * HEAD_DIM ** (-0.5)
    return jnp.where(allowed[None], scores, MASKED)


def attend_row(pieces):
    packed, seg_row = pieces
    query = packed[:, 0]
    keys = packed[:, 1]
    values = packed[:, 2]

    def one_block(start):
        allowed = allowed_pairs(seg_row, start, QBLOCK)
        query_block = lax.dynamic_slice_in_dim(query, start, QBLOCK, 0)
        scores = block_scores(query_block, keys, allowed)
        peak = jnp.max(scores, axis=-1, keepdims=True)
        expo = jnp.exp(scores - peak)
        total = jnp.sum(expo, axis=-1, keepdims=True)
        weights = (expo / total).astype(jnp.bfloat16)
        mixed = jnp.einsum("hqk,khd->qhd", weights, values, preferred_element_type=jnp.float32)
        return (mixed, (peak + jnp.log(total))[..., 0])

    starts = jnp.arange(packed.shape[0] // QBLOCK, dtype=jnp.int32) * QBLOCK
    mixed, logsum = lax.map(one_block, starts)
    return (mixed.reshape(keys.shape), logsum)


def attend_row_back(pieces):
    packed, logsum, grad_row, seg_row = pieces
    query = packed[:, 0]
    keys = packed[:, 1]
    values = packed[:, 2]
    factor = HEAD_DIM ** (-0.5)

    def one_block(carry, block_inputs):
        grad_keys, grad_values = carry
        start, lse_block = block_inputs
        allowed = allowed_pairs(seg_row, start, QBLOCK)
        query_block = lax.dynamic_slice_in_dim(query, start, QBLOCK, 0)
        grad_block = lax.dynamic_slice_in_dim(grad_row, start, QBLOCK, 0)
        scores = block_scores(query_block, keys, allowed)
        weights = jnp.exp(scores - lse_block[..., None])
        grad_weights = jnp.einsum(
            "qhd,khd->hqk", grad_block, values, preferred_element_type=jnp.float32
        )
        inner = jnp.sum(weights * grad_weights, axis=-1, keepdims=True)
        grad_scores = (weights * (grad_weights - inner)).astype(jnp.bfloat16)
        grad_query = (
            jnp.einsum("hqk,khd->qhd", grad_scores, keys, preferred_element_type=jnp.float32)
            * factor
        )
        grad_keys = (
            grad_keys
            + jnp.einsum(
                "hqk,qhd->khd", grad_scores, query_block, preferred_element_type=jnp.float32
            )
            * factor
        )
        grad_values = grad_values + jnp.einsum(
            "hqk,qhd->khd",
            weights.astype(jnp.bfloat16),
            grad_block,
            preferred_element_type=jnp.float32,
        )
        return ((grad_keys, grad_values), grad_query)

    starts = jnp.arange(packed.shape[0] // QBLOCK, dtype=jnp.int32) * QBLOCK
    zeros = jnp.zeros(keys.shape, jnp.float32)
    (grad_keys, grad_values), grad_query = lax.scan(one_block, (zeros, zeros), (starts, logsum))
    grad_query = grad_query.reshape(keys.shape)
    return jnp.stack([grad_query, grad_keys, grad_values], axis=1).astype(jnp.bfloat16)


def times_rows(activations, matrix):
    return lax.dot_general(
        activations,
        matrix,
        (((activations.ndim - 1,), (1,)), ((), ())),
        preferred_element_type=jnp.float32,
    )


def times_matrix(activations, matrix):
    return lax.dot_general(
        activations,
        matrix,
        (((activations.ndim - 1,), (0,)), ((), ())),
        preferred_element_type=jnp.float32,
    )


def weight_term(grads, activations):
    return jnp.einsum("rpe,rpd->ed", grads, activations, preferred_element_type=jnp.float32)


def body(
    inputs,
    segment_ids,
    w_qkv,
    w_out,
    w_up,
    w_down,
    gain_attn,
    gain_mix,
    gain_ffn,
    gain_hidden,
    cotangent,
):
    rows, local, width = inputs.shape
    groups = lax.axis_size("seq")
    length = local * groups
    heads_here = HEADS // groups
    group_width = heads_here * HEAD_DIM
    all_full = (
        lax.all_gather(w_qkv, "seq", axis=0, tiled=True),
        lax.all_gather(w_out, "seq", axis=0, tiled=True),
        lax.all_gather(w_up, "seq", axis=0, tiled=True),
        lax.all_gather(w_down, "seq", axis=0, tiled=True),
    )
    full_positions = jax.vmap(doc_positions)(segment_ids)
    positions = lax.dynamic_slice_in_dim(full_positions, lax.axis_index("seq") * local, local, 1)
    cosine, sine, growth = xpos_tables(positions)
    inputs_f32 = inputs.astype(jnp.float32)
    normed_f32, attn_pull = jax.vjp(norm_rows, inputs_f32, gain_attn)
    normed = normed_f32.astype(jnp.bfloat16)
    qkv = times_rows(normed, all_full[0]).reshape(rows, local, 3, HEADS, HEAD_DIM)
    query, query_pull = jax.vjp(lambda part: rotate(part, cosine, sine, growth), qkv[:, :, 0])
    keys, keys_pull = jax.vjp(lambda part: rotate(part, cosine, sine, 1.0 / growth), qkv[:, :, 1])
    stacked = jnp.stack([query, keys, qkv[:, :, 2]], axis=2).astype(jnp.bfloat16)
    stacked = stacked.reshape(rows, local, 3, groups, group_width)
    gathered = lax.all_to_all(stacked, "seq", split_axis=3, concat_axis=1, tiled=True)
    head_view = gathered.reshape(rows, length, 3, heads_here, HEAD_DIM)
    attended_heads, logsum = lax.map(attend_row, (head_view, segment_ids))
    attended_low = attended_heads.astype(jnp.bfloat16).reshape(rows, length, 1, group_width)
    returned = lax.all_to_all(attended_low, "seq", split_axis=1, concat_axis=2, tiled=True)
    attended = returned.reshape(rows, local, width).astype(jnp.float32)
    mix_f32, mix_pull = jax.vjp(norm_rows, attended, gain_mix)
    mix_in = mix_f32.astype(jnp.bfloat16)
    middle = inputs_f32 + times_rows(mix_in, all_full[1])
    ffn_f32, ffn_pull = jax.vjp(norm_rows, middle, gain_ffn)
    ffn_in = ffn_f32.astype(jnp.bfloat16)
    upper = times_rows(ffn_in, all_full[2])
    hidden_f32, hidden_pull = jax.vjp(gelu_norm, upper, gain_hidden)
    hidden = hidden_f32.astype(jnp.bfloat16)
    outputs = (middle + times_rows(hidden, all_full[3])).astype(jnp.bfloat16)
    back_full = (
        lax.all_gather(w_qkv, "seq", axis=0, tiled=True),
        lax.all_gather(w_out, "seq", axis=0, tiled=True),
        lax.all_gather(w_up, "seq", axis=0, tiled=True),
        lax.all_gather(w_down, "seq", axis=0, tiled=True),
    )
    grad_hidden_in = times_matrix(cotangent, back_full[3])
    grad_upper_f32, grad_gain_hidden = hidden_pull(grad_hidden_in)
    grad_upper = grad_upper_f32.astype(jnp.bfloat16)
    grad_ffn_in = times_matrix(grad_upper, back_full[2])
    grad_middle_part, grad_gain_ffn = ffn_pull(grad_ffn_in)
    grad_middle = cotangent.astype(jnp.float32) + grad_middle_part
    grad_branch = grad_middle.astype(jnp.bfloat16)
    grad_mix_in = times_matrix(grad_branch, back_full[1])
    grad_attended_f32, grad_gain_mix = mix_pull(grad_mix_in)
    grad_attended = grad_attended_f32.astype(jnp.bfloat16).reshape(rows, local, groups, group_width)
    grad_heads_view = lax.all_to_all(grad_attended, "seq", split_axis=2, concat_axis=1, tiled=True)
    grad_heads_view = grad_heads_view.reshape(rows, length, heads_here, HEAD_DIM)
    grad_packed = lax.map(attend_row_back, (head_view, logsum, grad_heads_view, segment_ids))
    grad_packed = grad_packed.reshape(rows, length, 3, 1, group_width)
    grad_local = lax.all_to_all(grad_packed, "seq", split_axis=1, concat_axis=3, tiled=True)
    grad_local = grad_local.reshape(rows, local, 3, HEADS, HEAD_DIM).astype(jnp.float32)
    grad_query_pre = query_pull(grad_local[:, :, 0])[0]
    grad_keys_pre = keys_pull(grad_local[:, :, 1])[0]
    grad_qkv = jnp.stack([grad_query_pre, grad_keys_pre, grad_local[:, :, 2]], axis=2)
    grad_qkv = grad_qkv.reshape(rows, local, 3 * width).astype(jnp.bfloat16)
    grad_normed = times_matrix(grad_qkv, back_full[0])
    grad_input_part, grad_gain_attn = attn_pull(grad_normed)
    grad_inputs = grad_middle + grad_input_part
    grad_w_down = lax.psum_scatter(
        weight_term(cotangent, hidden).astype(jnp.bfloat16), "seq", scatter_dimension=0, tiled=True
    ).astype(jnp.float32)
    grad_w_up = lax.psum_scatter(
        weight_term(grad_upper, ffn_in).astype(jnp.bfloat16), "seq", scatter_dimension=0, tiled=True
    ).astype(jnp.float32)
    grad_w_out = lax.psum_scatter(
        weight_term(grad_branch, mix_in).astype(jnp.bfloat16),
        "seq",
        scatter_dimension=0,
        tiled=True,
    ).astype(jnp.float32)
    grad_w_qkv = lax.psum_scatter(
        weight_term(grad_qkv, normed).astype(jnp.bfloat16), "seq", scatter_dimension=0, tiled=True
    ).astype(jnp.float32)
    grad_w_qkv, grad_w_out, grad_w_up, grad_w_down = (
        lax.psum(grad_w_qkv.astype(jnp.bfloat16), "batch").astype(jnp.float32),
        lax.psum(grad_w_out.astype(jnp.bfloat16), "batch").astype(jnp.float32),
        lax.psum(grad_w_up.astype(jnp.bfloat16), "batch").astype(jnp.float32),
        lax.psum(grad_w_down.astype(jnp.bfloat16), "batch").astype(jnp.float32),
    )
    grad_gain_attn, grad_gain_mix, grad_gain_ffn, grad_gain_hidden = lax.psum(
        (grad_gain_attn, grad_gain_mix, grad_gain_ffn, grad_gain_hidden), ("batch", "seq")
    )
    return (
        outputs,
        grad_inputs,
        grad_w_qkv,
        grad_w_out,
        grad_w_up,
        grad_w_down,
        grad_gain_attn,
        grad_gain_mix,
        grad_gain_ffn,
        grad_gain_hidden,
    )


def solution(mesh):
    in_specs = (
        P("batch", "seq", None),
        P("batch", None),
        P("seq", None),
        P("seq", None),
        P("seq", None),
        P("seq", None),
        P(),
        P(),
        P(),
        P(),
        P("batch", "seq", None),
    )
    out_specs = (
        P("batch", "seq", None),
        P("batch", "seq", None),
        P("seq", None),
        P("seq", None),
        P("seq", None),
        P("seq", None),
        P(),
        P(),
        P(),
        P(),
    )
    return jax.shard_map(body, mesh=mesh, in_specs=in_specs, out_specs=out_specs, check_vma=False)
```

profile of v0, /device:TPU:0, one launch (start us, length us, event | category | flops | bytes accessed | tf_op | source)
XLA Modules:
  0.0 2033.4 jit_solution(4240888310886022481)
XLA Ops:
  12.6 125.4 %all-gather.5.cloned.1.call-done = bf16[6144,2048]{1,0:T(8,128)(2,1)} async-done(((bf16[768,2048]{1,0:T(8,128)(2,1)}), bf16[6144,2048]{1,0:T(8,128)(2,1)}) %all-gather.5.cloned.1.call-update) | async-done | bytes 25165840 | tf_op jit(solution)/shard_map/all_gather | solution.py:184
  138.0 14.7 convolution_bitcast_fusion.2
  159.9 60.2 %all-to-all-done = bf16[1,256,3,8,256]{1,4,2,0,3:T(8,128)(2,1)S(1)} async-done(((bf16[1,256,3,8,256]{1,4,2,0,3:T(8,128)(2,1)}), bf16[1,256,3,8,256]{1,4,2,0,3:T(8,128)(2,1)S(1)}, u32[]{:S(2)}, u32[]{:S(2)}) %all-to-all-start) | async-done | bytes 3145760 | tf_op jit(solution)/shard_map/all_to_all | solution.py:200
  233.3 72.1 %while.45 = (s32[]{:T(128)}, bf16[4,512,4,64]{1,3,2,0:T(8,128)(2,1)}, f32[4,4,512]{2,1,0:T(4,128)}, s32[4]{0:T(128)S(1)}, s32[2048]{0:T(1024)S(1)}, /*index=5*/b...) while((s32[]{:T(128)}, ...), condition=%wide.region_7.8_spmd, body=%wide.region_4.7_spmd.sunk | while | flops 1127217664 | bytes 65882348 | solution.py:93
  309.6 8.3 reshape.1109
  318.4 12.8 reduce.36
  333.4 30.4 %all_to_all.49 = bf16[8,2,32768]{2,1,0:T(2,128)(2,1)S(1)} all-to-all(bf16[8,2,32768]{2,1,0:T(2,128)(2,1)} %reshape.1112), channel_id=1, replica_groups=mesh['batch'=4,'seq'=8] {'seq'}, dimensions={0} | all-to-all | bytes 2097152 | tf_op jit(solution)/shard_map/all_to_all | solution.py:204
  384.5 10.7 all-gather.9.cloned.1.call-done
  395.1 34.0 %fusion.87 = (f32[256]{0:T(256)S(1)}, f32[256,8192]{1,0:T(8,128)}, f32[256,8192]{1,0:T(8,128)}, f32[256,8192]{1,0:T(8,128)}) fusion(bf16[8192,2048]{1,0:T(8,128)(2,1)} %all-gather.9.cloned.1.call-done, f32[1,256,2048]{2,1,0:T(8,128)} %copy-done.9, f32[2048]{0:T(1024)S(1)} %copy-done.48, f32[256]{0:T(256)S(1)} %fusion.76, f32[256]{0:T(256)S(1)} %broadcast_multiply_fusion.1), kind=kOutput, calls=%fused_computation.193 | convolution fusion | flops 8728346624 | bytes 60828672 | tf_op jit(solution)/shard_map/dot_general | solution.py:144
  429.2 128.6 %all-gather.11.cloned.1.call-done = bf16[2048,8192]{1,0:T(8,128)(2,1)} async-done(((bf16[256,8192]{1,0:T(8,128)(2,1)}), bf16[2048,8192]{1,0:T(8,128)(2,1)}) %all-gather.11.cloned.1.call-update) | async-done | bytes 33554448 | tf_op jit(solution)/shard_map/all_gather | solution.py:187
  557.7 20.5 %multiply_reduce_fusion.2 = (f32[256]{0:T(256)S(1)}, f32[256]{0:T(256)S(1)}, f32[256,8192]{1,0:T(8,128)}) fusion(f32[256,8192]{1,0:T(8,128)} %get-tuple-element.328, f32[8192]{0:T(1024)S(1)} %copy-done.29, f32[256]{0:T(256)S(1)} %broadcast_multiply_fusion, bf16[2048,8192]{1,0:T(8,128)(2,1)} %all-gather.11.cloned.1.call-done, ...), kind=kOutput, calls=%fused_computation.55 | convolution fusion | flops 8602517504 | bytes 51416064 | tf_op jit(solution)/shard_map/dot_general | solution.py:153
  578.3 10.0 multiply_reduce_fusion.1
  588.3 12.6 add_convert_fusion
  600.9 18.2 fusion.57
  623.3 7.0 multiply_reduce_fusion.4
  656.8 246.3 %while.46 = (s32[]{:T(128)}, f32[2048,4,64]{0,2,1:T(8,128)}, f32[2048,4,64]{0,2,1:T(8,128)}, bf16[4,512,4,64]{1,3,2,0:T(8,128)(2,1)}, s32[4]{0:T(128)S(1)}, /*in...) while((s32[]{:T(128)}, f32[2048,4,64]{0,2,1:T(8,128)}, ...), condition=%wide.region_23.24_spmd.clone, body=%wide.region_21.23_spmd.clone.sunk | while | flops 2753165824 | bytes 193538464 | solution.py:138
  659.8 9.3 fusion.147
  671.7 13.1 multiply_reduce_fusion.8
  684.8 15.7 multiply_convert_fusion.13
  700.5 6.8 fusion.149
  707.3 8.6 fusion.150
  722.1 9.2 fusion.147
  733.9 12.5 multiply_reduce_fusion.8
  746.4 14.9 multiply_convert_fusion.13
  761.3 7.2 fusion.149
  768.5 8.6 fusion.150
  783.3 9.2 fusion.147
  795.1 12.5 multiply_reduce_fusion.8
  807.6 14.9 multiply_convert_fusion.13
  822.5 7.2 fusion.149
  829.7 8.6 fusion.150
  844.4 9.2 fusion.147
  856.2 12.5 multiply_reduce_fusion.8
  868.7 14.9 multiply_convert_fusion.13
  883.6 7.2 fusion.149
  890.7 8.6 fusion.150
  916.6 52.7 %all_to_all.48 = bf16[1,2048,3,1,256]{4,2,3,0,1:T(4,128)(2,1)S(1)} all-to-all(bf16[1,2048,3,1,256]{4,2,3,0,1:T(4,128)(2,1)} %copy.106), channel_id=1, replica_groups=mesh['batch'=4,'seq'=8] {'seq'}, dimensions={1} | all-to-all | bytes 6291456 | tf_op jit(solution)/shard_map/all_to_all | solution.py:235
  987.5 13.8 convolution_convert_fusion.1
  1002.5 26.2 %convert_bitcast_fusion = bf16[2048,8192]{0,1:T(8,128)(2,1)} fusion(bf16[1,256,2048]{2,1,0:T(8,128)(2,1)S(1)} %copy-done.14, f32[256,8192]{1,0:T(8,128)} %get-tuple-element.328, f32[8192]{0:T(1024)S(1)} %copy-done.30, f32[256]{0:T(256)S(1)} %copy-done.45, f32[256]{0:T(256)S(1)} %copy-done.43), kind=kOutput, calls=%fused_computation.47 | convolution fusion | flops 8615100416 | bytes 43026432 | tf_op jit(solution)/shard_map/rpe,rpd->ed/dot_general | solution.py:162
  1030.7 17.3 convolution_convert_fusion
  1048.1 109.3 %reduce-scatter.5.cloned.1.call-done = bf16[768,2048]{1,0:T(8,128)(2,1)} async-done(((bf16[6144,2048]{1,0:T(8,128)(2,1)}), bf16[768,2048]{1,0:T(8,128)(2,1)}) %reduce-scatter.5.cloned.1.call-update) | async-done | bytes 3145744 | tf_op jit(solution)/shard_map/reduce_scatter | solution.py:256
  1157.5 209.3 %reduce-scatter.11.cloned.1.call-done = bf16[256,8192]{0,1:T(8,128)(2,1)} async-done(((bf16[2048,8192]{0,1:T(8,128)(2,1)}), bf16[256,8192]{0,1:T(8,128)(2,1)}) %reduce-scatter.11.cloned.1.call-update) | async-done | bytes 4194320 | tf_op jit(solution)/shard_map/reduce_scatter | solution.py:244
  1366.8 208.8 %reduce-scatter.9.cloned.1.call-done = bf16[1024,2048]{1,0:T(8,128)(2,1)} async-done(((bf16[8192,2048]{1,0:T(8,128)(2,1)}), bf16[1024,2048]{1,0:T(8,128)(2,1)}) %reduce-scatter.9.cloned.1.call-update) | async-done | bytes 4194320 | tf_op jit(solution)/shard_map/reduce_scatter | solution.py:247
  1575.6 18.8 fusion.50
  1594.5 12.7 fusion.56
  1608.3 50.4 %all-reduce.4 = (f32[2048]{0:T(1024)}, f32[2048]{0:T(1024)}, f32[2048]{0:T(1024)}, f32[8192]{0:T(1024)}) all-reduce(f32[2048]{0:T(1024)S(1)} %get-tuple-element.275, f32[2048]{0:T(1024)S(1)} %copy-done.62, f32[2048]{0:T(1024)S(1)} %copy-done.61, f32[8192]{0:T(1024)S(1)} %copy-done.41), channel_id=1, replica_groups=mesh['batch'=4,'seq'=8] {'batch','seq'}, use_global_device_ids=true, to_apply=%region_35.36 | all-reduce | flops 14336 | bytes 114688 | tf_op jit(solution)/shard_map/psum | solution.py:265
  1662.8 345.2 %all-reduce.8.cloned.1.call-done = (bf16[256,8192]{0,1:T(8,128)(2,1)}, bf16[768,2048]{1,0:T(8,128)(2,1)}, bf16[256,2048]{1,0:T(8,128)(2,1)}, bf16[1024,2048]{1,0:T(8,128)(2,1)}) async-done(((bf16[256,8192]{0,1:T(8,128)(2,1)}, bf16[768,2048]{1,0:T(8,128)(2,1)}, bf16[256,2048]{1,0:T(8,128)(2,1)}, bf16[1024,2048]{1,0:T(8,128)(2,1)}), (bf16[256,8192]{0,1:T(8,128)(2,1)}, bf16[768,2048]{1,0:T(8,128)(2,1)}, ...) | async-done | bytes 12582928 | tf_op jit(solution)/shard_map/psum | solution.py:263
  2019.5 7.0 copy.110
  (360 shorter events, 226.7 us)
Async XLA Ops:
  7.2 130.8 %all-gather.5.cloned.1.call-start = ((), (), s32[]{:S(2)}) async-start(), calls=%async_computation.8 | async-start | bytes 28311552 | tf_op jit(solution)/shard_map/all_gather | solution.py:184
  7.9 368.3 %all-gather.7.cloned.1.call-start = ((), (), s32[]{:S(2)}) async-start(), calls=%async_computation.9 | async-start | bytes 9437184 | tf_op jit(solution)/shard_map/all_gather | solution.py:185
  8.7 386.4 %all-gather.9.cloned.1.call-start = ((), (), s32[]{:S(2)}) async-start(), calls=%async_computation.10 | async-start | bytes 37748736 | tf_op jit(solution)/shard_map/all_gather | solution.py:186
  9.4 128.5 %copy-start.39 = (f32[2048]{0:T(1024)S(1)}, f32[2048]{0:T(1024)}, u32[]{:S(2)}) copy-start(f32[2048]{0:T(1024)} %param.21) | copy-start | bytes 24580
  9.4 548.3 %all-gather.11.cloned.1.call-start = ((), (), s32[]{:S(2)}) async-start(), calls=%async_computation.11 | async-start | bytes 37748736 | tf_op jit(solution)/shard_map/all_gather | solution.py:187
  11.2 141.4 %copy-start.46 = (f32[256]{0:T(256)}, f32[256]{0:T(256)S(1)}, u32[]{:S(2)}) copy-start(f32[256]{0:T(256)S(1)} %broadcast_multiply_fusion.3) | copy-start | bytes 3076
  11.7 140.9 %copy-start.51 = (f32[256]{0:T(256)}, f32[256]{0:T(256)S(1)}, u32[]{:S(2)}) copy-start(f32[256]{0:T(256)S(1)} %fusion.74) | copy-start | bytes 3076
  12.5 140.6 %copy-start.31 = (f32[256,32]{0,1:T(8,128)}, f32[256,32]{0,1:T(8,128)S(1)}, u32[]{:S(2)}) copy-start(f32[256,32]{0,1:T(8,128)S(1)} %get-tuple-element.355) | copy-start | bytes 98308
  12.5 140.6 %copy-start.33 = (f32[256,32]{0,1:T(8,128)}, f32[256,32]{0,1:T(8,128)S(1)}, u32[]{:S(2)}) copy-start(f32[256,32]{0,1:T(8,128)S(1)} %get-tuple-element.356) | copy-start | bytes 98308
  12.6 140.5 %copy-start.35 = (f32[256,32]{0,1:T(8,128)}, f32[256,32]{0,1:T(8,128)S(1)}, u32[]{:S(2)}) copy-start(f32[256,32]{0,1:T(8,128)S(1)} %get-tuple-element.353) | copy-start | bytes 98308
  12.6 140.5 %copy-start.37 = (f32[256,32]{0,1:T(8,128)}, f32[256,32]{0,1:T(8,128)S(1)}, u32[]{:S(2)}) copy-start(f32[256,32]{0,1:T(8,128)S(1)} %get-tuple-element.354) | copy-start | bytes 98308
  156.0 64.1 %all-to-all-start = ((bf16[1,256,3,8,256]{1,4,2,0,3:T(8,128)(2,1)}), bf16[1,256,3,8,256]{1,4,2,0,3:T(8,128)(2,1)S(1)}, u32[]{:S(2)}, u32[]{:S(2)}) async-start(bf16[1,256,3,8,256]{1,4,2,0,3:T(8,128)(2,1)} %pad_maximum_fusion), calls=%async_computation | async-start | bytes 6291456 | tf_op jit(solution)/shard_map/all_to_all | solution.py:200
  305.4 25.9 %copy-start = (bf16[2048,4,64]{0,2,1:T(8,128)(2,1)}, bf16[2048,4,64]{0,2,1:T(8,128)(2,1)S(1)}, u32[]{:S(2)}) copy-start(bf16[2048,4,64]{0,2,1:T(8,128)(2,1)S(1)} %get-tuple-element.584) | copy-start | bytes 3145732
  305.4 25.9 %copy-start.6 = (bf16[2048,4,64]{0,2,1:T(8,128)(2,1)}, bf16[2048,4,64]{0,2,1:T(8,128)(2,1)S(1)}, u32[]{:S(2)}) copy-start(bf16[2048,4,64]{0,2,1:T(8,128)(2,1)S(1)} %get-tuple-element.593) | copy-start | bytes 3145732
  305.4 25.9 %copy-start.8 = (bf16[2048,4,64]{0,2,1:T(8,128)(2,1)}, bf16[2048,4,64]{0,2,1:T(8,128)(2,1)S(1)}, u32[]{:S(2)}) copy-start(bf16[2048,4,64]{0,2,1:T(8,128)(2,1)S(1)} %get-tuple-element.595) | copy-start | bytes 3145732
  305.4 25.9 %copy-start.63 = (s32[4]{0:T(128)}, s32[4]{0:T(128)S(1)}, u32[]{:S(2)}) copy-start(s32[4]{0:T(128)S(1)} %get-tuple-element.627) | copy-start | bytes 52
  376.2 18.9 copy-start.48
  382.8 236.3 %copy-start.53 = (f32[256]{0:T(256)}, f32[256]{0:T(256)S(1)}, u32[]{:S(2)}) copy-start(f32[256]{0:T(256)S(1)} %broadcast_multiply_fusion.1) | copy-start | bytes 3076
  384.4 234.7 %copy-start.55 = (f32[256]{0:T(256)}, f32[256]{0:T(256)S(1)}, u32[]{:S(2)}) copy-start(f32[256]{0:T(256)S(1)} %fusion.76) | copy-start | bytes 3076
  384.4 173.3 %copy-start.13 = (bf16[1,256,2048]{2,1,0:T(8,128)(2,1)S(1)}, bf16[1,256,2048]{2,1,0:T(8,128)(2,1)}, u32[]{:S(2)}) copy-start(bf16[1,256,2048]{2,1,0:T(8,128)(2,1)} %param.25) | copy-start | bytes 3145732
  384.5 173.3 %copy-start.29 = (f32[8192]{0:T(1024)S(1)}, f32[8192]{0:T(1024)}, u32[]{:S(2)}) copy-start(f32[8192]{0:T(1024)} %param.24) | copy-start | bytes 98308
  429.2 159.1 %copy-start.42 = (f32[256]{0:T(256)}, f32[256]{0:T(256)S(1)}, u32[]{:S(2)}) copy-start(f32[256]{0:T(256)S(1)} %broadcast_multiply_fusion) | copy-start | bytes 3076
  578.2 10.0 copy-start.44
  578.2 10.0 slice-start.2
  578.3 10.0 slice-start.3
  588.3 12.6 copy-start.10
  621.5 8.8 copy-start.57
  632.7 19.8 all-to-all-start.2
  637.0 411.1 %reduce-scatter.7.cloned.1.call-start = ((), (), s32[]{:S(2)}) async-start(), calls=%async_computation.13 | async-start | bytes 9437184 | tf_op jit(solution)/shard_map/reduce_scatter | solution.py:250
  645.9 10.9 copy-start.1
  645.9 10.9 copy-start.7
  645.9 10.9 copy-start.27
  645.9 10.9 copy-start.64
  645.9 511.5 %reduce-scatter.5.cloned.1.call-start = ((), (), s32[]{:S(2)}) async-start(), calls=%async_computation.12 | async-start | bytes 28311552 | tf_op jit(solution)/shard_map/reduce_scatter | solution.py:256
  700.5 15.5 slice-start
  707.3 8.7 slice-start.1
  707.3 8.7 copy-start.21
  761.3 15.8 slice-start
  822.5 15.8 slice-start
  883.6 15.8 slice-start
  1001.3 365.5 %reduce-scatter.11.cloned.1.call-start = ((), (), s32[]{:S(2)}) async-start(), calls=%async_computation.15 | async-start | bytes 37748736 | tf_op jit(solution)/shard_map/reduce_scatter | solution.py:244
  1028.7 546.9 %reduce-scatter.9.cloned.1.call-start = ((), (), s32[]{:S(2)}) async-start(), calls=%async_computation.14 | async-start | bytes 37748736 | tf_op jit(solution)/shard_map/reduce_scatter | solution.py:247
  1048.1 959.9 %all-reduce.8.cloned.1.call-start = ((), (), s32[]{:S(2)}) async-start(), calls=%async_computation.16 | async-start | bytes 25165824 | tf_op jit(solution)/shard_map/psum | solution.py:263
  1594.4 12.8 copy-start.60
  1594.4 13.8 copy-start.41
  1594.5 13.9 copy-start.61
  1594.5 13.9 copy-start.62
  1594.5 64.2 %copy-start.58 = (f32[256]{0:T(256)S(1)}, f32[256]{0:T(256)}, u32[]{:S(2)}) copy-start(f32[256]{0:T(256)} %copy-done.57) | copy-start | bytes 3076
  (56 other events, 205.2 us)
Sparse Core Ops, SparseCore 0:
  9.9 128.0 all-gather.4
  139.8 76.6 all-gather.6
  218.4 176.6 all-gather.8
  396.9 160.8 all-gather.10
  646.0 72.5 reduce-scatter.6
  1001.4 156.0 reduce-scatter.4
  1161.5 205.2 reduce-scatter.10
  1370.3 205.2 reduce-scatter.8
  1578.8 429.1 all-reduce.7
where the time goes:
time: 2040 us; the launch traced here: 2030 us
  waiting for transfers between devices  1210 us (59%)
  matrix products  389 us (19%)
  other arithmetic  176 us (9%)
  blocking collectives  133 us (7%)
  local copies, waits for them, and re-layouts  88.6 us (4%)
    psum x1, waiting for transfers between devices, body(): lax.psum(grad_w_down.astype(jnp.bfloat16), 'batch').astype(jnp.float32)  345 us
    reduce_scatter x1, waiting for transfers between devices, body(): lax.psum_scatter(weight_term(cotangent, hidden).astype(jnp.bfloat16), 'se...  209 us
    reduce_scatter x1, waiting for transfers between devices, body(): lax.psum_scatter(weight_term(grad_upper, ffn_in).astype(jnp.bfloat16), 's...  209 us
    all_gather x1, waiting for transfers between devices, body(): lax.all_gather(w_down, 'seq', axis=0, tiled=True)  129 us
    all_gather x1, waiting for transfers between devices, body(): lax.all_gather(w_qkv, 'seq', axis=0, tiled=True)  125 us
    reduce_scatter x1, waiting for transfers between devices, body(): lax.psum_scatter(weight_term(grad_qkv, normed).astype(jnp.bfloat16), 'seq...  109 us
    dot_general x4, matrix products, times_rows(): lax.dot_general(activations, matrix, (((activations.ndim - 1,), (1,)), ((...  74 us
    dot_general x4, matrix products, weight_term(): jnp.einsum('rpe,rpd->ed', grads, activations, preferred_element_type=jnp....  63.1 us
  transfers between devices with their start and end apart: 11, of which 9 were waited for; matrix products, arithmetic and copies ran while one was open for 27% of the time, Pallas kernels for 0%

commit v1 on v0

v1 whole, which is shorter than its diff:
```python
import functools
import math

import jax
import jax.numpy as jnp
from jax import lax
from jax.experimental import pallas as pl
from jax.experimental.pallas import tpu as pltpu
from jax.sharding import PartitionSpec as P

HEADS = 32
HEAD_DIM = 64
LENGTH = 2048
XBASE = 512
DOCS = 4
EPSILON = 1e-05
MASKED = -1e30
TILE = 256

MESH = pl.DeviceIdType.MESH
F32 = jnp.float32
BF16 = jnp.bfloat16
ANY = pl.BlockSpec(memory_space=pl.ANY)


def nn(a, b):
    return lax.dot_general(a, b, (((1,), (0,)), ((), ())), preferred_element_type=F32)


def nt(a, b):
    return lax.dot_general(a, b, (((1,), (1,)), ((), ())), preferred_element_type=F32)


def tn(a, b):
    return lax.dot_general(a, b, (((0,), (0,)), ((), ())), preferred_element_type=F32)


def norm_parts(values):
    average = jnp.mean(values, axis=-1, keepdims=True)
    centered = values - average
    spread = jnp.mean(centered * centered, axis=-1, keepdims=True)
    scale = lax.rsqrt(spread + EPSILON)
    return centered * scale, scale


def norm_back(grad, normal, scale, gain):
    part = grad * gain
    inner = (
        part
        - jnp.mean(part, axis=-1, keepdims=True)
        - normal * jnp.mean(part * normal, axis=-1, keepdims=True)
    )
    return scale * inner, jnp.sum(grad * normal, axis=0)


def places():
    me = lax.axis_index("seq")
    core = lax.rem(me, 2)
    along_x = lax.rem(me // 2, 2)
    along_y = me // 4
    twin = 1 - 2 * core
    near_x = me + 2 - 4 * along_x
    near_y = me + 4 - 8 * along_y
    across = near_x + 4 - 8 * along_y
    return me, twin, near_x, near_y, across


def remote(src, dst, send_sem, recv_sem, partner):
    return pltpu.make_async_remote_copy(
        src_ref=src,
        dst_ref=dst,
        send_sem=send_sem,
        recv_sem=recv_sem,
        device_id={"seq": partner},
        device_id_type=MESH,
    )


def meet(partners):
    barrier = pltpu.get_barrier_semaphore()
    for partner in partners:
        pl.semaphore_signal(
            barrier, inc=1, device_id={"seq": partner}, device_id_type=MESH
        )
    pl.semaphore_wait(barrier, len(partners))


def gather_copies(x_ref, o_ref, send_sem, recv_sem):
    me, twin, near_x, near_y, across = places()
    half = x_ref.shape[0] // 2
    low, high = pl.ds(0, half), pl.ds(half, half)

    def copy(k, src, dst, partner):
        return remote(src, dst, send_sem.at[k], recv_sem.at[k], partner)

    def relay(k, owner, rows, partner):
        place = o_ref.at[owner, rows]
        return copy(k, place, place, partner)

    return [
        copy(0, x_ref.at[low], o_ref.at[me, low], near_x),
        copy(1, x_ref.at[high], o_ref.at[me, high], near_y),
        copy(2, x_ref.at[high], o_ref.at[me, high], near_x),
        copy(3, x_ref.at[low], o_ref.at[me, low], near_y),
        copy(4, x_ref, o_ref.at[me], me + twin),
        relay(5, near_x, low, near_y),
        relay(6, near_y, high, near_x),
        relay(7, near_x, low, me + twin),
        relay(8, near_y, high, me + twin),
        relay(9, near_x, high, me + twin),
        relay(10, near_y, low, me + twin),
        relay(11, across, low, me + twin),
        relay(12, across, high, me + twin),
    ]


def gather_run(sends, between=None):
    sends[0].wait_recv()
    sends[5].start()
    sends[7].start()
    sends[1].wait_recv()
    sends[6].start()
    sends[8].start()
    sends[2].wait_recv()
    sends[9].start()
    sends[3].wait_recv()
    sends[10].start()
    if between is not None:
        between()
    sends[5].wait_recv()
    sends[11].start()
    sends[6].wait_recv()
    sends[12].start()
    for k in (4, 7, 8, 9, 10, 11, 12):
        sends[k].wait_recv()
    for send in sends:
        send.wait_send()


def meet_all(n, depth):
    me = lax.axis_index("seq")
    z = lax.axis_index("batch")
    barrier = pltpu.get_barrier_semaphore()
    for k in range(1, n):
        pl.semaphore_signal(
            barrier, inc=1, device_id={"seq": lax.rem(me + k, n)}, device_id_type=MESH
        )
    for sign in (-1, 1):

        @pl.when((z + sign >= 0) & (z + sign < depth))
        def _():
            pl.semaphore_signal(
                barrier, inc=1, device_id={"batch": z + sign}, device_id_type=MESH
            )

    ends = (z == 0).astype(jnp.int32) + (z == depth - 1).astype(jnp.int32)
    pl.semaphore_wait(barrier, n + 1 - ends)


def line_remote(src, dst, send_sem, recv_sem, partner):
    return pltpu.make_async_remote_copy(
        src_ref=src,
        dst_ref=dst,
        send_sem=send_sem,
        recv_sem=recv_sem,
        device_id={"batch": partner},
        device_id_type=MESH,
    )


class Line:
    def __init__(self, depth, source, target, send_sem, recv_sem):
        self.depth, self.source, self.target = depth, source, target
        self.send_sem, self.recv_sem = send_sem, recv_sem
        self.z = lax.axis_index("batch")

    def message(self, side, k):
        sign = 2 * side - 1
        owner = self.z - sign * k
        return line_remote(
            self.source(owner, k),
            self.target(owner),
            self.send_sem.at[side, k],
            self.recv_sem.at[side, k],
            self.z + sign,
        )

    def sends(self, side, k):
        sign = 2 * side - 1
        owner, target = self.z - sign * k, self.z + sign
        inside = (owner >= 0) & (owner < self.depth)
        return inside & (target >= 0) & (target < self.depth)

    def land(self, k):
        for side in (0, 1):
            sign = 2 * side - 1
            owner = self.z - sign * (k + 1)

            @pl.when((owner >= 0) & (owner < self.depth))
            def _():
                place = self.target(owner)
                line_remote(
                    place,
                    place,
                    self.send_sem.at[side, k],
                    self.recv_sem.at[side, k],
                    self.z - sign,
                ).wait_recv()

    def start(self, k):
        for side in (0, 1):

            @pl.when(self.sends(side, k))
            def _():
                self.message(side, k).start()

    def sent(self, k):
        for side in (0, 1):

            @pl.when(self.sends(side, k))
            def _():
                self.message(side, k).wait_send()


def gather_kernel(
    n, depth, x_ref, near_ref, o_ref, all_ref, local_sem, send_sem, recv_sem, line_send, line_recv
):
    me, twin, near_x, near_y, _ = places()
    z = lax.axis_index("batch")
    own = pltpu.make_async_copy(x_ref, o_ref.at[me], local_sem.at[0])
    own.start()

    def keep(shift):
        return pltpu.make_async_copy(
            near_ref.at[:, z + shift], all_ref.at[:, z + shift], local_sem.at[2 + shift]
        )

    def kept(shift):
        return (z + shift >= 0) & (z + shift < depth)

    for shift in (-1, 0, 1):

        @pl.when(kept(shift))
        def _():
            keep(shift).start()

    meet_all(n, depth)
    sends = gather_copies(x_ref, o_ref, send_sem, recv_sem)
    for k in range(5):
        sends[k].start()
    line = Line(
        depth,
        lambda owner, k: (near_ref if k == 1 else all_ref).at[:, owner],
        lambda owner: all_ref.at[:, owner],
        line_send,
        line_recv,
    )
    line.start(1)

    def between():
        for k in range(2, depth - 1):
            line.land(k - 1)
            line.start(k)

    gather_run(sends, between)
    line.land(depth - 2)
    for k in range(1, depth - 1):
        line.sent(k)
    for shift in (-1, 0, 1):

        @pl.when(kept(shift))
        def _():
            keep(shift).wait()

    own.wait()


def gather_seq(block, near, collective_id):
    n, depth = lax.axis_size("seq"), lax.axis_size("batch")
    rows, width = block.shape
    if n != 8:
        return lax.all_gather(block, "seq", axis=0, tiled=True), near
    gathered, every = pl.pallas_call(
        functools.partial(gather_kernel, n, depth),
        out_shape=(
            jax.ShapeDtypeStruct((n, rows, width), block.dtype),
            jax.ShapeDtypeStruct(near.shape, near.dtype),
        ),
        in_specs=[ANY, ANY],
        out_specs=(ANY, ANY),
        scratch_shapes=[
            pltpu.SemaphoreType.DMA((4,)),
            pltpu.SemaphoreType.DMA((13,)),
            pltpu.SemaphoreType.DMA((13,)),
            pltpu.SemaphoreType.DMA((2, depth)),
            pltpu.SemaphoreType.DMA((2, depth)),
        ],
        compiler_params=pltpu.CompilerParams(
            collective_id=collective_id, has_side_effects=True
        ),
        name="gather_seq",
    )(block, near)
    return gathered.reshape(n * rows, width), every.reshape(-1, near.shape[-1])


def lane_tables(place):
    half = HEAD_DIM // 2
    lane = lax.broadcasted_iota(jnp.int32, (1, 128), 1)
    channel = lax.rem(lane, half).astype(F32)
    inverse = jnp.exp(channel * (-math.log(10000.0) / half))
    zeta = (channel * (2.0 / HEAD_DIM) + 0.4) / 1.4
    sign = jnp.where(lax.rem(lane, HEAD_DIM) < half, -1.0, 1.0)
    angle = place * inverse
    growth = jnp.exp((place - 0.5 * LENGTH) * (1.0 / XBASE) * jnp.log(zeta))
    shrink = 1.0 / growth
    cosine = jnp.cos(angle)
    sine = jnp.sin(angle) * sign
    return cosine * growth, sine * growth, cosine * shrink, sine * shrink


def start_kernel(
    n, depth, x_ref, w_ref, wd_ref, pos_ref,
    o_ref, wq_ref, wk_ref, wv_ref, wc_ref, cq_ref, sq_ref, ck_ref, sk_ref,
    local_sem, send_sem, recv_sem, hop_send, hop_recv, col_send, col_recv, line_send, line_recv,
):
    z = lax.axis_index("batch")
    rows_z = wc_ref.shape[2]
    cols = wc_ref.shape[3]
    me, twin, near_x, near_y, _ = places()
    parts = (wq_ref, wk_ref, wv_ref)
    own = pltpu.make_async_copy(x_ref, o_ref.at[me], local_sem.at[0])
    own.start()
    wd_rows = pl.ds(pl.multiple_of(z * rows_z, rows_z), rows_z)

    def column(k):
        return wd_ref.at[wd_rows, pl.ds(pl.multiple_of(k * cols, cols), cols)]

    own_column = pltpu.make_async_copy(column(me), wc_ref.at[me, z], local_sem.at[4])
    own_column.start()
    meet_all(n, depth)
    turns = [
        remote(
            column(lax.rem(me + k, n)),
            wc_ref.at[me, z],
            col_send.at[k],
            col_recv.at[k],
            lax.rem(me + k, n),
        )
        for k in range(1, n)
    ]
    for turn in turns:
        turn.start()
    sends = gather_copies(x_ref, o_ref, send_sem, recv_sem)
    for k in range(5):
        sends[k].start()

    line = Line(
        depth,
        lambda owner, k: wc_ref.at[:, owner],
        lambda owner: wc_ref.at[:, owner],
        line_send,
        line_recv,
    )

    def hop(j, part, target):
        return remote(
            w_ref.at[j], parts[part], hop_send.at[j], hop_recv.at[part], target
        )

    def here(j, part):
        return pltpu.make_async_copy(w_ref.at[j], parts[part], local_sem.at[1 + j])

    for j in range(3):
        block = 3 * me + j
        target = lax.rem(block, n)
        for part in range(3):
            inside = block // n == part

            @pl.when(inside & (target != me))
            def _():
                hop(j, part, target).start()

            @pl.when(inside & (target == me))
            def _():
                here(j, part).start()

    @pl.loop(0, pos_ref.shape[0])
    def _(r):
        at = pl.ds(pl.multiple_of(r * 128, 128), 128)
        places_here = jnp.broadcast_to(pos_ref[pl.ds(r, 1), :], (128, 128)).T
        tables = lane_tables(places_here)
        for ref, table in zip((cq_ref, sq_ref, ck_ref, sk_ref), tables, strict=True):
            ref[at] = table

    own_column.wait()
    for turn in turns:
        turn.wait_recv()
    line.start(0)
    gather_run(sends)
    line.land(0)
    line.sent(0)
    for turn in turns:
        turn.wait_send()
    for j in range(3):
        block = 3 * me + j
        target = lax.rem(block, n)

        for part in range(3):
            inside = block // n == part

            @pl.when(inside & (target != me))
            def _():
                hop(j, part, target).wait_send()

            @pl.when(inside & (target == me))
            def _():
                here(j, part).wait()

    for part in range(3):
        source = (part * n + me) // 3

        @pl.when(source != me)
        def _():
            hop(0, part, source).wait_recv()

    own.wait()


def start_exchange(block, w_qkv, w_down, positions, collective_id):
    n, depth = lax.axis_size("seq"), lax.axis_size("batch")
    rows, width = block.shape
    piece = w_qkv.shape[0] // 3
    w = w_qkv.reshape(3, piece, width)
    if n != 8:
        me = lax.axis_index("seq")
        turned = [
            lax.ppermute(w[j], "seq", [(d, (3 * d + j) % n) for d in range(n)])
            for j in range(3)
        ]
        parts = [pick_part(turned, me, n, part) for part in range(3)]
        place = jnp.broadcast_to(positions[:, None], (positions.shape[0], 128))
        return (
            lax.all_gather(block, "seq", axis=0, tiled=True),
            parts,
            lax.all_to_all(w_down, "seq", split_axis=1, concat_axis=0, tiled=True),
            lane_tables(place),
        )
    rows_z, cols = w_down.shape[0] // depth, w_down.shape[1] // n
    inside = pl.BlockSpec(memory_space=pltpu.VMEM)
    table = jax.ShapeDtypeStruct((n * rows, 128), F32)
    part = jax.ShapeDtypeStruct((piece, width), w.dtype)
    gathered, wq, wk, wv, columns, *tables = pl.pallas_call(
        functools.partial(start_kernel, n, depth),
        out_shape=(
            jax.ShapeDtypeStruct((n, rows, width), block.dtype),
            part,
            part,
            part,
            jax.ShapeDtypeStruct((n, depth, rows_z, cols), w_down.dtype),
            *([table] * 4),
        ),
        in_specs=[ANY, ANY, ANY, inside],
        out_specs=(ANY, ANY, ANY, ANY, ANY, *([inside] * 4)),
        scratch_shapes=[
            pltpu.SemaphoreType.DMA((5,)),
            pltpu.SemaphoreType.DMA((13,)),
            pltpu.SemaphoreType.DMA((13,)),
            pltpu.SemaphoreType.DMA((3,)),
            pltpu.SemaphoreType.DMA((3,)),
            pltpu.SemaphoreType.DMA((n,)),
            pltpu.SemaphoreType.DMA((n,)),
            pltpu.SemaphoreType.DMA((2, depth)),
            pltpu.SemaphoreType.DMA((2, depth)),
        ],
        compiler_params=pltpu.CompilerParams(
            collective_id=collective_id, has_side_effects=True
        ),
        name="start_exchange",
    )(block, w, w_down, positions.reshape(-1, 128))
    return gathered.reshape(n * rows, width), (wq, wk, wv), columns, tables


def scatter_kernel(
    p_ref, o_ref, own, twin_in, held, local_sem, send_sem, recv_sem
):
    me, twin, near_x, near_y, across = places()
    rows = p_ref.shape[1]
    half = rows // 2
    low, high = pl.ds(0, half), pl.ds(half, half)
    mine = (across, near_x, near_y, me)

    loads = [
        pltpu.make_async_copy(p_ref.at[block], own.at[i], local_sem.at[i])
        for i, block in enumerate(mine)
    ]
    for load in loads:
        load.start()
    meet((me + twin, near_x, near_y))

    def copy(k, src, dst, partner):
        return remote(src, dst, send_sem.at[k], recv_sem.at[k], partner)

    twins = [
        copy(i, p_ref.at[block + twin], twin_in.at[i], me + twin)
        for i, block in enumerate(mine)
    ]
    for send in twins:
        send.start()
    sends = [
        copy(4, own.at[0, low], held.at[0], near_x),
        copy(5, own.at[0, high], held.at[1], near_y),
        copy(6, own.at[1, low], held.at[2], near_x),
        copy(7, own.at[2, high], held.at[3], near_y),
        copy(8, own.at[1, high], held.at[4], near_x),
        copy(9, own.at[2, low], held.at[5], near_y),
    ]
    step = 32

    def add_twin(i):
        loads[i].wait()
        twins[i].wait_recv()

        @pl.loop(0, rows // step)
        def _(r):
            at = pl.ds(pl.multiple_of(r * step, step), step)
            own[i, at] = (
                own[i, at].astype(F32) + twin_in[i, at].astype(F32)
            ).astype(own.dtype)

    def add_held(i, base, slot):
        @pl.loop(0, half // step)
        def _(r):
            at = pl.ds(pl.multiple_of(r * step, step), step)
            to = pl.ds(pl.multiple_of(base + r * step, step), step)
            own[i, to] = (
                own[i, to].astype(F32) + held[slot, at].astype(F32)
            ).astype(own.dtype)

    add_twin(0)
    sends[0].start()
    sends[1].start()
    add_twin(1)
    sends[2].start()
    add_twin(2)
    sends[3].start()
    sends[1].wait_recv()
    add_held(1, half, 1)
    sends[4].start()
    sends[0].wait_recv()
    add_held(2, 0, 0)
    sends[5].start()
    loads[3].wait()
    twins[3].wait_recv()
    for k in (2, 3, 4, 5):
        sends[k].wait_recv()

    def final(base, first, second):
        @pl.loop(0, half // step)
        def _(r):
            at = pl.ds(pl.multiple_of(r * step, step), step)
            to = pl.ds(pl.multiple_of(base + r * step, step), step)
            o_ref[to] = (
                own[3, to].astype(F32)
                + twin_in[3, to].astype(F32)
                + held[first, at].astype(F32)
                + held[second, at].astype(F32)
            )

    final(0, 2, 5)
    final(half, 3, 4)
    for send in twins + sends:
        send.wait_send()


def scatter_seq(partial, collective_id):
    n = lax.axis_size("seq")
    rows, width = partial.shape[0] // n, partial.shape[1]
    if n != 8:
        return lax.psum_scatter(
            partial, "seq", scatter_dimension=0, tiled=True
        ).astype(F32)
    return pl.pallas_call(
        scatter_kernel,
        out_shape=jax.ShapeDtypeStruct((rows, width), F32),
        in_specs=[ANY],
        out_specs=pl.BlockSpec(memory_space=pltpu.VMEM),
        scratch_shapes=[
            pltpu.VMEM((4, rows, width), BF16),
            pltpu.VMEM((4, rows, width), BF16),
            pltpu.VMEM((6, rows // 2, width), BF16),
            pltpu.SemaphoreType.DMA((4,)),
            pltpu.SemaphoreType.DMA((10,)),
            pltpu.SemaphoreType.DMA((10,)),
        ],
        compiler_params=pltpu.CompilerParams(
            collective_id=collective_id,
            has_side_effects=True,
            vmem_limit_bytes=32 * 1024 * 1024,
        ),
        name="scatter_seq",
    )(partial.reshape(n, rows, width))


def heads_to_tokens_kernel(n, x_ref, o_ref, local_sem, send_sem, recv_sem):
    me = lax.axis_index("seq")
    rows = o_ref.shape[0]
    cols = x_ref.shape[1]
    exchange(
        n,
        me,
        lambda k: x_ref.at[pl.ds(pl.multiple_of(k * rows, rows), rows)],
        o_ref.at[:, pl.ds(pl.multiple_of(me * cols, cols), cols)],
        local_sem,
        send_sem,
        recv_sem,
    )


def exchange(n, me, source, target, local_sem, send_sem, recv_sem):
    own = pltpu.make_async_copy(source(me), target, local_sem)
    own.start()
    barrier = pltpu.get_barrier_semaphore()
    for k in range(1, n):
        pl.semaphore_signal(
            barrier,
            inc=1,
            device_id={"seq": lax.rem(me + k, n)},
            device_id_type=MESH,
        )
    pl.semaphore_wait(barrier, n - 1)
    copies = []
    for k in range(1, n):
        partner = lax.rem(me + k, n)
        copies.append(
            pltpu.make_async_remote_copy(
                src_ref=source(partner),
                dst_ref=target,
                send_sem=send_sem.at[k],
                recv_sem=recv_sem.at[k],
                device_id={"seq": partner},
                device_id_type=MESH,
            )
        )
        copies[-1].start()
    for copy in copies:
        copy.wait()
    own.wait()


def heads_to_tokens(heads, collective_id):
    n = lax.axis_size("seq")
    total, cols = heads.shape
    rows = total // n
    return pl.pallas_call(
        functools.partial(heads_to_tokens_kernel, n),
        out_shape=jax.ShapeDtypeStruct((rows, n * cols), heads.dtype),
        in_specs=[ANY],
        out_specs=ANY,
        scratch_shapes=[
            pltpu.SemaphoreType.DMA,
            pltpu.SemaphoreType.DMA((n,)),
            pltpu.SemaphoreType.DMA((n,)),
        ],
        compiler_params=pltpu.CompilerParams(
            collective_id=collective_id, has_side_effects=True
        ),
        name="heads_to_tokens",
    )(heads)


def tokens_to_heads_kernel(n, x_ref, o_ref, local_sem, send_sem, recv_sem):
    me = lax.axis_index("seq")
    rows = x_ref.shape[0]
    cols = o_ref.shape[1]
    exchange(
        n,
        me,
        lambda k: x_ref.at[:, pl.ds(pl.multiple_of(k * cols, cols), cols)],
        o_ref.at[pl.ds(pl.multiple_of(me * rows, rows), rows)],
        local_sem,
        send_sem,
        recv_sem,
    )


def tokens_to_heads(tokens, collective_id):
    n = lax.axis_size("seq")
    rows, total = tokens.shape
    return pl.pallas_call(
        functools.partial(tokens_to_heads_kernel, n),
        out_shape=jax.ShapeDtypeStruct((rows * n, total // n), tokens.dtype),
        in_specs=[ANY],
        out_specs=ANY,
        scratch_shapes=[
            pltpu.SemaphoreType.DMA,
            pltpu.SemaphoreType.DMA((n,)),
            pltpu.SemaphoreType.DMA((n,)),
        ],
        compiler_params=pltpu.CompilerParams(
            collective_id=collective_id, has_side_effects=True
        ),
        name="tokens_to_heads",
    )(tokens)


def swap_halves(values):
    width = values.shape[-1]
    half = HEAD_DIM // 2
    lane = lax.broadcasted_iota(jnp.int32, values.shape, 1)
    ahead = pltpu.roll(values, width - half, 1)
    behind = pltpu.roll(values, half, 1)
    return jnp.where(lane % HEAD_DIM < half, ahead, behind)


def spread_lanes(table, width):
    return jnp.concatenate([table] * (width // table.shape[-1]), axis=-1)


def qkv_kernel(
    x_ref, wq_ref, wk_ref, wv_ref, cq_ref, sq_ref, ck_ref, sk_ref,
    q_ref, k_ref, v_ref, kt_ref, vt_ref,
):
    x = x_ref[...]
    width = q_ref.shape[1]
    query = nt(x, wq_ref[...])
    query = query * spread_lanes(cq_ref[...], width) + swap_halves(
        query
    ) * spread_lanes(sq_ref[...], width)
    q_ref[...] = query.astype(BF16) * (HEAD_DIM**-0.5)
    keys = nt(x, wk_ref[...])
    keys = keys * spread_lanes(ck_ref[...], width) + swap_halves(
        keys
    ) * spread_lanes(sk_ref[...], width)
    k_ref[...] = keys.astype(BF16)
    kt_ref[...] = keys.T.astype(BF16)
    values = nt(x, wv_ref[...])
    v_ref[...] = values.astype(BF16)
    vt_ref[...] = values.T.astype(BF16)


def project_qkv(x, wq, wk, wv, tables):
    length, width = x.shape
    cols = wq.shape[0]
    steps = length // TILE
    weight = pl.BlockSpec((cols, width), lambda i: (0, 0))
    table = pl.BlockSpec((TILE, tables[0].shape[1]), lambda i: (i, 0))
    row_out = pl.BlockSpec((TILE, cols), lambda i: (i, 0))
    col_out = pl.BlockSpec((cols, TILE), lambda i: (0, i))
    rows = jax.ShapeDtypeStruct((length, cols), BF16)
    columns = jax.ShapeDtypeStruct((cols, length), BF16)
    return pl.pallas_call(
        qkv_kernel,
        grid=(steps,),
        out_shape=(rows, rows, rows, columns, columns),
        in_specs=[pl.BlockSpec((TILE, width), lambda i: (i, 0))]
        + [weight] * 3
        + [table] * 4,
        out_specs=(row_out, row_out, row_out, col_out, col_out),
        compiler_params=pltpu.CompilerParams(vmem_limit_bytes=40 * 1024 * 1024),
        cost_estimate=pl.CostEstimate(
            flops=6 * length * width * cols,
            bytes_accessed=2 * length * width + 6 * width * cols + 10 * length * cols,
            transcendentals=0,
        ),
        name="project_qkv",
    )(x, wq, wk, wv, *tables)


def pair_mask(start_row, i, j):
    key_place = j * TILE + lax.broadcasted_iota(jnp.int32, (TILE, TILE), 0)
    query_place = i * TILE + lax.broadcasted_iota(jnp.int32, (TILE, TILE), 1)
    return (key_place <= query_place) & (key_place >= start_row)


def head_rows(query, heads):
    lane = lax.broadcasted_iota(jnp.int32, query.shape, 1) // HEAD_DIM
    zero = jnp.zeros_like(query)
    return [jnp.where(lane == h, query, zero) for h in range(heads)]


def attend_kernel(
    heads, first_ref, start_ref, q_ref, k_ref, vt_ref, o_ref, lse_ref, peak, total, mixed
):
    i = pl.program_id(0)
    queries = head_rows(q_ref[...], heads)
    start_row = start_ref[...]

    def block(j, first):
        at = pl.ds(pl.multiple_of(j * TILE, TILE), TILE)
        keys = k_ref[at, :]
        mask = pair_mask(start_row, i, j)
        for h in range(heads):
            here = slice(h * HEAD_DIM, (h + 1) * HEAD_DIM)
            scores = jnp.where(mask, nt(keys, queries[h]), MASKED)
            if first:
                new_peak = jnp.max(scores, axis=0, keepdims=True)
                expo = jnp.exp(scores - new_peak)
                total[h : h + 1] = jnp.sum(expo, axis=0, keepdims=True)
                mixed[here] = nn(vt_ref[here, at], expo.astype(BF16))
            else:
                old_peak = peak[h : h + 1]
                new_peak = jnp.maximum(old_peak, jnp.max(scores, axis=0, keepdims=True))
                expo = jnp.exp(scores - new_peak)
                shrink = jnp.exp(old_peak - new_peak)
                total[h : h + 1] = total[h : h + 1] * shrink + jnp.sum(
                    expo, axis=0, keepdims=True
                )
                mixed[here] = mixed[here] * shrink + nn(
                    vt_ref[here, at], expo.astype(BF16)
                )
            peak[h : h + 1] = new_peak

    block(i, True)

    @pl.loop(0, i - first_ref[i])
    def _(t):
        block(i - 1 - t, False)

    for h in range(heads):
        here = slice(h * HEAD_DIM, (h + 1) * HEAD_DIM)
        mixed[here] = mixed[here] / total[h : h + 1]
    o_ref[...] = mixed[...].T.astype(BF16)
    lse_ref[0] = peak[...] + jnp.log(total[...])


def attend(first, start, q, k, vt):
    length, cols = q.shape
    heads = cols // HEAD_DIM
    steps = length // TILE
    row = pl.BlockSpec((TILE, cols), lambda i, *_: (i, 0))
    return pl.pallas_call(
        functools.partial(attend_kernel, heads),
        out_shape=(
            jax.ShapeDtypeStruct((length, cols), BF16),
            jax.ShapeDtypeStruct((steps, heads, TILE), F32),
        ),
        grid_spec=pltpu.PrefetchScalarGridSpec(
            num_scalar_prefetch=1,
            grid=(steps,),
            in_specs=[
                pl.BlockSpec((1, TILE), lambda i, *_: (0, i)),
                row,
                pl.BlockSpec((length, cols), lambda i, *_: (0, 0)),
                pl.BlockSpec((cols, length), lambda i, *_: (0, 0)),
            ],
            out_specs=(
                row,
                pl.BlockSpec((1, heads, TILE), lambda i, *_: (i, 0, 0)),
            ),
            scratch_shapes=[
                pltpu.VMEM((heads, TILE), F32),
                pltpu.VMEM((heads, TILE), F32),
                pltpu.VMEM((cols, TILE), F32),
            ],
        ),
        compiler_params=pltpu.CompilerParams(vmem_limit_bytes=32 * 1024 * 1024),
        cost_estimate=pl.CostEstimate(
            flops=4 * length * 1024 * cols,
            bytes_accessed=8 * length * cols,
            transcendentals=length * 1024 * heads,
        ),
        name="attend",
    )(first, start, q, k, vt)


def attend_back_kernel(
    heads, first_ref, start_ref, q_ref, k_ref, kt_ref, v_ref, o_ref, lse_ref, do_ref,
    cq_ref, sq_ref, ck_ref, sk_ref, dq_ref, dk_ref, dv_ref, dqt, dk_sum, dv_sum,
):
    i = pl.program_id(0)
    steps = pl.num_programs(0)
    width = q_ref.shape[1]
    queries = head_rows(q_ref[...], heads)
    grads = head_rows(do_ref[...], heads)
    start_row = start_ref[...]
    product = (do_ref[...].astype(F32) * o_ref[...].astype(F32)).T
    inner = [
        jnp.sum(product[h * HEAD_DIM : (h + 1) * HEAD_DIM], axis=0, keepdims=True)
        for h in range(heads)
    ]

    def block(j, first):
        at = pl.ds(pl.multiple_of(j * TILE, TILE), TILE)
        keys = k_ref[at, :]
        values = v_ref[at, :]
        mask = pair_mask(start_row, i, j)
        key_term = None
        value_term = None
        for h in range(heads):
            here = slice(h * HEAD_DIM, (h + 1) * HEAD_DIM)
            scores = nt(keys, queries[h])
            weights = jnp.where(mask, jnp.exp(scores - lse_ref[0, h : h + 1]), 0.0)
            grad_weights = nt(values, grads[h])
            grad_scores = (weights * (grad_weights - inner[h])).astype(BF16)
            term = nn(weights.astype(BF16), grads[h])
            value_term = term if value_term is None else value_term + term
            term = nn(grad_scores, queries[h])
            key_term = term if key_term is None else key_term + term
            term = nn(kt_ref[here, at], grad_scores)
            if first:
                dqt[here] = term
            else:
                dqt[here] = dqt[here] + term
        if first:
            dk_sum[at] = key_term
            dv_sum[at] = value_term
        else:
            dk_sum[at] = dk_sum[at] + key_term
            dv_sum[at] = dv_sum[at] + value_term

    block(i, True)

    @pl.loop(0, i - first_ref[i])
    def _(t):
        block(i - 1 - t, False)

    def unturn(grad, cosine, sine):
        grad = grad.astype(BF16).astype(F32)
        cosine = spread_lanes(cosine, width)
        sine = spread_lanes(sine, width)
        return (grad * cosine - swap_halves(grad) * sine).astype(BF16)

    rows = pl.ds(pl.multiple_of(i * TILE, TILE), TILE)
    dq_ref[...] = unturn(
        dqt[...].T * (HEAD_DIM**-0.5), cq_ref[rows, :], sq_ref[rows, :]
    )

    @pl.when(i == steps - 1)
    def _():
        @pl.loop(0, steps)
        def _(j):
            at = pl.ds(pl.multiple_of(j * TILE, TILE), TILE)
            dk_ref[at] = unturn(dk_sum[at], ck_ref[at, :], sk_ref[at, :])
            dv_ref[at] = dv_sum[at].astype(BF16)


def attend_back(first, start, q, k, kt, v, o, lse, do, tables):
    length, cols = q.shape
    heads = cols // HEAD_DIM
    steps = length // TILE
    row = pl.BlockSpec((TILE, cols), lambda i, *_: (i, 0))
    whole = pl.BlockSpec((length, cols), lambda i, *_: (0, 0))
    table = pl.BlockSpec((length, tables[0].shape[1]), lambda i, *_: (0, 0))
    shape = jax.ShapeDtypeStruct((length, cols), BF16)
    return pl.pallas_call(
        functools.partial(attend_back_kernel, heads),
        out_shape=(shape, shape, shape),
        grid_spec=pltpu.PrefetchScalarGridSpec(
            num_scalar_prefetch=1,
            grid=(steps,),
            in_specs=[
                pl.BlockSpec((1, TILE), lambda i, *_: (0, i)),
                row,
                whole,
                pl.BlockSpec((cols, length), lambda i, *_: (0, 0)),
                whole,
                row,
                pl.BlockSpec((1, heads, TILE), lambda i, *_: (i, 0, 0)),
                row,
            ]
            + [table] * 4,
            out_specs=(row, whole, whole),
            scratch_shapes=[
                pltpu.VMEM((cols, TILE), F32),
                pltpu.VMEM((length, cols), F32),
                pltpu.VMEM((length, cols), F32),
            ],
        ),
        compiler_params=pltpu.CompilerParams(vmem_limit_bytes=48 * 1024 * 1024),
        cost_estimate=pl.CostEstimate(
            flops=10 * length * 1024 * cols,
            bytes_accessed=16 * length * cols,
            transcendentals=length * 1024 * heads,
        ),
        name="attend_back",
    )(first, start, q, k, kt, v, o, lse, do, *tables)


def upper_kernel(
    x_ref, wu_ref, c_ref, wd_ref, gain_ref, act_ref, slope_ref, grad_ref, stat_ref
):
    upper = nt(x_ref[...], wu_ref[...])
    grad = nn(c_ref[...], wd_ref[...])
    below = 0.5 * (1.0 + lax.erf(upper * (0.5**0.5)))
    act = upper * below
    slope = below + upper * (jnp.exp(-0.5 * upper * upper) * ((2.0 * math.pi) ** -0.5))
    act_ref[...] = act
    slope_ref[...] = slope.astype(BF16)
    grad_ref[...] = grad
    part = grad * gain_ref[...]
    average = jnp.mean(act, axis=-1, keepdims=True)
    centered = act - average
    spread = jnp.sum(centered * centered, axis=-1, keepdims=True)
    part_sum = jnp.sum(part, axis=-1, keepdims=True)
    cross = jnp.sum(part * centered, axis=-1, keepdims=True)
    lane = lax.broadcasted_iota(jnp.int32, (x_ref.shape[0], 128), 1)
    columns = jnp.where(
        lane == 0,
        average,
        jnp.where(lane == 1, spread, jnp.where(lane == 2, part_sum, cross)),
    )
    stat_ref[...] = columns.T[:8]


def upper_pass(x, w_up, cot, w_down, gain):
    length, width = x.shape
    feats = w_up.shape[0]
    rows = TILE
    row = pl.BlockSpec((rows, width), lambda i: (i, 0))
    out = pl.BlockSpec((rows, feats), lambda i: (i, 0))
    return pl.pallas_call(
        upper_kernel,
        grid=(length // rows,),
        out_shape=(
            jax.ShapeDtypeStruct((length, feats), F32),
            jax.ShapeDtypeStruct((length, feats), BF16),
            jax.ShapeDtypeStruct((length, feats), F32),
            jax.ShapeDtypeStruct((8, length), F32),
        ),
        in_specs=[
            row,
            pl.BlockSpec((feats, width), lambda i: (0, 0)),
            row,
            pl.BlockSpec((width, feats), lambda i: (0, 0)),
            pl.BlockSpec((1, feats), lambda i: (0, 0)),
        ],
        out_specs=(out, out, out, pl.BlockSpec((8, rows), lambda i: (0, i))),
        compiler_params=pltpu.CompilerParams(vmem_limit_bytes=48 * 1024 * 1024),
        cost_estimate=pl.CostEstimate(
            flops=4 * length * width * feats,
            bytes_accessed=8 * length * width + 8 * length * feats,
            transcendentals=2 * length * feats,
        ),
        name="upper_pass",
    )(x, w_up, cot, w_down, gain)


def hidden_kernel(act_ref, slope_ref, grad_ref, stat_ref, gain_ref, hid_ref, gu_ref, gg_ref):
    i = pl.program_id(0)
    stats = stat_ref[...].T
    average = stats[:, 0:1]
    scale = stats[:, 1:2]
    part_mean = stats[:, 2:3]
    cross_mean = stats[:, 3:4]
    gain = gain_ref[...]
    normal = (act_ref[...] - average) * scale
    grad = grad_ref[...]
    hid_ref[...] = (normal * gain).astype(BF16)
    back = scale * (grad * gain - part_mean - normal * cross_mean)
    gu_ref[...] = (slope_ref[...].astype(F32) * back).astype(BF16)
    term = jnp.sum(grad * normal, axis=0, keepdims=True)

    @pl.when(i == 0)
    def _():
        gg_ref[...] = term

    @pl.when(i > 0)
    def _():
        gg_ref[...] = gg_ref[...] + term


def hidden_pass(act, slope, grad, stats, gain):
    length, feats = act.shape
    out = pl.BlockSpec((TILE, feats), lambda i: (i, 0))
    one = pl.BlockSpec((1, feats), lambda i: (0, 0))
    return pl.pallas_call(
        hidden_kernel,
        grid=(length // TILE,),
        out_shape=(
            jax.ShapeDtypeStruct((length, feats), BF16),
            jax.ShapeDtypeStruct((length, feats), BF16),
            jax.ShapeDtypeStruct((1, feats), F32),
        ),
        in_specs=[out, out, out, pl.BlockSpec((8, TILE), lambda i: (0, i)), one],
        out_specs=(out, out, one),
        compiler_params=pltpu.CompilerParams(vmem_limit_bytes=40 * 1024 * 1024),
        cost_estimate=pl.CostEstimate(
            flops=12 * length * feats,
            bytes_accessed=14 * length * feats,
            transcendentals=0,
        ),
        name="hidden_pass",
    )(act, slope, grad, stats, gain)


def stat_kernel(n, feats, x_ref, o_ref, held, send_sem, recv_sem):
    me = lax.axis_index("seq")
    held[me] = x_ref[...]
    meet([lax.rem(me + k, n) for k in range(1, n)])
    copies = [
        remote(x_ref, held.at[me], send_sem.at[k], recv_sem.at[k], lax.rem(me + k, n))
        for k in range(1, n)
    ]
    for copy in copies:
        copy.start()
    for copy in copies:
        copy.wait()
    average = held[0, 0:1]
    for d in range(1, n):
        average = average + held[d, 0:1]
    average = average * (1.0 / n)
    spread = jnp.zeros_like(average)
    part = jnp.zeros_like(average)
    cross = jnp.zeros_like(average)
    for d in range(n):
        shift = held[d, 0:1] - average
        spread = spread + held[d, 1:2] + feats * (shift * shift)
        part = part + held[d, 2:3]
        cross = cross + held[d, 3:4] + shift * held[d, 2:3]
    whole = 1.0 / (n * feats)
    scale = lax.rsqrt(spread * whole + EPSILON)
    o_ref[0:1] = average
    o_ref[1:2] = scale
    o_ref[2:3] = part * whole
    o_ref[3:4] = cross * scale * whole
    o_ref[4:8] = jnp.zeros((4, average.shape[1]), F32)


def join_stats(stat, feats, collective_id):
    n = lax.axis_size("seq")
    inside = pl.BlockSpec(memory_space=pltpu.VMEM)
    return pl.pallas_call(
        functools.partial(stat_kernel, n, feats),
        out_shape=jax.ShapeDtypeStruct(stat.shape, F32),
        in_specs=[inside],
        out_specs=inside,
        scratch_shapes=[
            pltpu.VMEM((n, *stat.shape), F32),
            pltpu.SemaphoreType.DMA((n,)),
            pltpu.SemaphoreType.DMA((n,)),
        ],
        compiler_params=pltpu.CompilerParams(
            collective_id=collective_id, has_side_effects=True
        ),
        name="join_stats",
    )(stat)


STEP = 32


def mix_kernel(att_ref, x_ref, w_ref, gm_ref, gf_ref, mix_ref, mid_ref, ffn_ref):
    j = pl.program_id(0)
    rows = att_ref.shape[0]
    cols = w_ref.shape[0]

    @pl.when(j == 0)
    def _():
        @pl.loop(0, rows // STEP)
        def _(r):
            at = pl.ds(pl.multiple_of(r * STEP, STEP), STEP)
            normal, _ = norm_parts(att_ref[at].astype(F32))
            mix_ref[at] = (normal * gm_ref[...]).astype(BF16)

    here = pl.ds(pl.multiple_of(j * cols, cols), cols)
    mid_ref[:, here] = x_ref[:, here].astype(F32) + nt(mix_ref[...], w_ref[...])

    @pl.when(j == pl.num_programs(0) - 1)
    def _():
        @pl.loop(0, rows // STEP)
        def _(r):
            at = pl.ds(pl.multiple_of(r * STEP, STEP), STEP)
            normal, _ = norm_parts(mid_ref[at])
            ffn_ref[at] = (normal * gf_ref[...]).astype(BF16)


def mix_pass(attended, x, w_out, gain_mix, gain_ffn):
    rows, width = x.shape
    cols = TILE
    n = width // cols
    whole = pl.BlockSpec((rows, width), lambda j: (0, 0))
    gain = pl.BlockSpec((1, width), lambda j: (0, 0))
    low = jax.ShapeDtypeStruct((rows, width), BF16)
    return pl.pallas_call(
        mix_kernel,
        grid=(n,),
        out_shape=(low, jax.ShapeDtypeStruct((rows, width), F32), low),
        in_specs=[
            whole,
            whole,
            pl.BlockSpec((cols, width), lambda j: (j, 0)),
            gain,
            gain,
        ],
        out_specs=(whole, whole, whole),
        compiler_params=pltpu.CompilerParams(vmem_limit_bytes=32 * 1024 * 1024),
        cost_estimate=pl.CostEstimate(
            flops=2 * rows * width * width,
            bytes_accessed=2 * width * width + 12 * rows * width,
            transcendentals=0,
        ),
        name="mix_pass",
    )(attended, x, w_out, gain_mix[None], gain_ffn[None])


def branch_kernel(
    g_ref, mid_ref, cot_ref, att_ref, w_ref, gm_ref, gf_ref,
    gmid_ref, gbr_ref, gatt_ref, ggf_ref, ggm_ref, total,
):
    j = pl.program_id(0)
    rows = att_ref.shape[0]
    cols = w_ref.shape[0]

    @pl.when(j == 0)
    def _():
        ggf_ref[...] = jnp.zeros_like(ggf_ref)
        total[...] = jnp.zeros_like(total)

        @pl.loop(0, rows // STEP)
        def _(r):
            at = pl.ds(pl.multiple_of(r * STEP, STEP), STEP)
            normal, scale = norm_parts(mid_ref[at])
            part, gain_part = norm_back(g_ref[at], normal, scale, gf_ref[...])
            ggf_ref[...] += gain_part[None]
            grad = cot_ref[at].astype(F32) + part
            gmid_ref[at] = grad
            gbr_ref[at] = grad.astype(BF16)

    here = pl.ds(pl.multiple_of(j * cols, cols), cols)
    total[...] += nn(gbr_ref[:, here], w_ref[...])

    @pl.when(j == pl.num_programs(0) - 1)
    def _():
        ggm_ref[...] = jnp.zeros_like(ggm_ref)

        @pl.loop(0, rows // STEP)
        def _(r):
            at = pl.ds(pl.multiple_of(r * STEP, STEP), STEP)
            normal, scale = norm_parts(att_ref[at].astype(F32))
            part, gain_part = norm_back(total[at], normal, scale, gm_ref[...])
            ggm_ref[...] += gain_part[None]
            gatt_ref[at] = part.astype(BF16)


def branch_pass(grad_ffn_in, middle, cot, attended, w_out, gain_mix, gain_ffn):
    rows, width = cot.shape
    cols = TILE
    n = width // cols
    whole = pl.BlockSpec((rows, width), lambda j: (0, 0))
    gain = pl.BlockSpec((1, width), lambda j: (0, 0))
    low = jax.ShapeDtypeStruct((rows, width), BF16)
    sums = jax.ShapeDtypeStruct((1, width), F32)
    return pl.pallas_call(
        branch_kernel,
        grid=(n,),
        out_shape=(jax.ShapeDtypeStruct((rows, width), F32), low, low, sums, sums),
        in_specs=[
            whole,
            whole,
            whole,
            whole,
            pl.BlockSpec((cols, width), lambda j: (j, 0)),
            gain,
            gain,
        ],
        out_specs=(whole, whole, whole, gain, gain),
        scratch_shapes=[pltpu.VMEM((rows, width), F32)],
        compiler_params=pltpu.CompilerParams(vmem_limit_bytes=40 * 1024 * 1024),
        cost_estimate=pl.CostEstimate(
            flops=2 * rows * width * width,
            bytes_accessed=2 * width * width + 20 * rows * width,
            transcendentals=0,
        ),
        name="branch_pass",
    )(grad_ffn_in, middle, cot, attended, w_out, gain_mix[None], gain_ffn[None])


def finish_kernel(
    n, depth, gq_ref, pw_ref, pn_ref, po_ref, gu_ref, oq_ref, ow_ref, sn_ref, so_ref, ou_ref,
    own, twin_in, held, zown, zin, zfin,
    local_sem, send_sem, recv_sem, keep_sem,
    up_send, up_recv, down_send, down_recv, home_send, home_recv, half_keep, half_send, half_recv,
):
    me, twin, near_x, near_y, across = places()
    z = lax.axis_index("batch")
    rows = pn_ref.shape[1]
    half = rows // 2
    low, high = pl.ds(0, half), pl.ds(half, half)
    mine = (across, near_x, near_y, me)
    chunk = zown.shape[1]
    turned = gq_ref.shape[0]
    chunks = zown.shape[0]
    per_part = turned // 3
    per_side = chunks // 2

    load_q = pltpu.make_async_copy(
        gq_ref, zown.at[pl.ds(0, turned)], local_sem.at[12]
    )
    load_q.start()
    partials = (pw_ref, pn_ref, po_ref)
    loads = [
        [
            pltpu.make_async_copy(p.at[block], own.at[m, i], local_sem.at[4 * m + i])
            for i, block in enumerate(mine)
        ]
        for m, p in enumerate(partials)
    ]
    for part in loads:
        for load in part:
            load.start()
    meet_all(n, depth)

    def copy(m, k, src, dst, partner):
        return remote(src, dst, send_sem.at[m, k], recv_sem.at[m, k], partner)

    twins = [
        [
            copy(m, i, p.at[block + twin], twin_in.at[m, i], me + twin)
            for i, block in enumerate(mine)
        ]
        for m, p in enumerate(partials)
    ]
    sends = [
        [
            copy(m, 4, own.at[m, 0, low], held.at[m, 0], near_x),
            copy(m, 5, own.at[m, 0, high], held.at[m, 1], near_y),
            copy(m, 6, own.at[m, 1, low], held.at[m, 2], near_x),
            copy(m, 7, own.at[m, 2, high], held.at[m, 3], near_y),
            copy(m, 8, own.at[m, 1, high], held.at[m, 4], near_x),
            copy(m, 9, own.at[m, 2, low], held.at[m, 5], near_y),
        ]
        for m in range(3)
    ]
    for part in twins:
        for send in part:
            send.start()

    def add_twin(m, i):
        loads[m][i].wait()
        twins[m][i].wait_recv()

        @pl.loop(0, rows // STEP)
        def _(r):
            at = pl.ds(pl.multiple_of(r * STEP, STEP), STEP)
            own[m, i, at] = (
                own[m, i, at].astype(F32) + twin_in[m, i, at].astype(F32)
            ).astype(BF16)

    def add_held(m, i, base, slot):
        @pl.loop(0, half // STEP)
        def _(r):
            at = pl.ds(pl.multiple_of(r * STEP, STEP), STEP)
            to = pl.ds(pl.multiple_of(base + r * STEP, STEP), STEP)
            own[m, i, to] = (
                own[m, i, to].astype(F32) + held[m, slot, at].astype(F32)
            ).astype(BF16)

    def first(m):
        add_twin(m, 0)
        sends[m][0].start()
        sends[m][1].start()
        add_twin(m, 1)
        sends[m][2].start()
        add_twin(m, 2)
        sends[m][3].start()

    def second(m):
        sends[m][1].wait_recv()
        add_held(m, 1, half, 1)
        sends[m][4].start()
        sends[m][0].wait_recv()
        add_held(m, 2, 0, 0)
        sends[m][5].start()

    def last(m, store):
        loads[m][3].wait()
        twins[m][3].wait_recv()
        for k in (2, 3, 4, 5):
            sends[m][k].wait_recv()
        for base, one, two in ((0, 2, 5), (half, 3, 4)):

            @pl.loop(0, half // STEP)
            def _(r):
                at = pl.ds(pl.multiple_of(r * STEP, STEP), STEP)
                place = base + r * STEP
                to = pl.ds(pl.multiple_of(place, STEP), STEP)
                store(
                    place,
                    own[m, 3, to].astype(F32)
                    + twin_in[m, 3, to].astype(F32)
                    + held[m, one, at].astype(F32)
                    + held[m, two, at].astype(F32),
                )

    def store_line(place, value):
        zown[
            turned + place // chunk,
            pl.ds(pl.multiple_of(lax.rem(place, chunk), STEP), STEP),
        ] = value.astype(BF16)

    def store_into(ref):
        def store(place, value):
            ref[pl.ds(pl.multiple_of(place, STEP), STEP)] = value

        return store

    def home(part):
        block = part * n + me
        return block // 3, lax.rem(block, 3)

    def deliver_far(g):
        target, slot = home(g // per_part)
        piece = lax.rem(g, per_part)
        return remote(
            zfin.at[g],
            oq_ref.at[slot, piece],
            home_send.at[g],
            home_recv.at[slot, piece],
            target,
        )

    def deliver_near(g):
        _, slot = home(g // per_part)
        return pltpu.make_async_copy(
            zfin.at[g], oq_ref.at[slot, lax.rem(g, per_part)], keep_sem.at[g]
        )

    def deliver_out(g):
        return pltpu.make_async_copy(zfin.at[g], ow_ref.at[g - turned], keep_sem.at[g])

    def deliver(g, wait):
        target, _ = home(g // per_part)

        @pl.when((g < turned) & (target != me))
        def _():
            deliver_far(g).wait_send() if wait else deliver_far(g).start()

        @pl.when((g < turned) & (target == me))
        def _():
            deliver_near(g).wait() if wait else deliver_near(g).start()

        @pl.when(g >= turned)
        def _():
            deliver_out(g).wait() if wait else deliver_out(g).start()

    def go_up(g, ahead):
        return line_remote(zown.at[g], zin.at[g], up_send.at[g], up_recv.at[g], ahead)

    def go_down(g, behind):
        return line_remote(
            zfin.at[g], zfin.at[g], down_send.at[g], down_recv.at[g], behind
        )

    def ranks(side):
        if side == 0:
            return z, z + 1, z - 1
        return depth - 1 - z, z - 1, z + 1

    def add_line(g, target):
        @pl.loop(0, chunk // STEP)
        def _(r):
            at = pl.ds(pl.multiple_of(r * STEP, STEP), STEP)
            target[g, at] = (zown[g, at].astype(F32) + zin[g, at].astype(F32)).astype(
                BF16
            )

    def line_step(t):
        half_step(t)
        for side in (0, 1):
            rank, ahead, behind = ranks(side)
            c = t - rank
            g = 2 * c + side
            there = (c >= 0) & (c < per_side)

            @pl.when(there & (rank == 0))
            def _():
                go_up(g, ahead).start()

            @pl.when(there & (rank > 0) & (rank < depth - 1))
            def _():
                go_up(g, behind).wait_recv()
                add_line(g, zown)
                go_up(g, ahead).start()

            @pl.when(there & (rank == depth - 1))
            def _():
                go_up(g, behind).wait_recv()
                add_line(g, zfin)
                go_down(g, behind).start()
                deliver(g, False)

            c_back = t - 2 * (depth - 1) + rank
            g_back = 2 * c_back + side
            there = (c_back >= 0) & (c_back < per_side) & (rank < depth - 1)

            @pl.when(there)
            def _():
                go_down(g_back, ahead).wait_recv()

            @pl.when(there & (rank > 0))
            def _():
                go_down(g_back, behind).start()

            @pl.when(there)
            def _():
                deliver(g_back, False)

    pieces = gu_ref.shape[0]

    def half_rank(side):
        return depth - 1 - z if side == 0 else z

    def half_keeps(side, c):
        return pltpu.make_async_copy(gu_ref.at[c], ou_ref.at[side, c], half_keep.at[c])

    def half_copy(side, c, source):
        return line_remote(
            source,
            ou_ref.at[side, c],
            half_send.at[side, c],
            half_recv.at[side, c],
            z - 1 if side == 0 else z + 1,
        )

    def half_land(side, c):
        place = ou_ref.at[side, c]
        return line_remote(
            place,
            place,
            half_send.at[side, c],
            half_recv.at[side, c],
            z + 1 if side == 0 else z - 1,
        )

    def half_step(t):
        for side in (0, 1):
            rank = half_rank(side)
            c = t - rank
            there = (c >= 0) & (c < pieces)

            @pl.when(there & (rank == 0))
            def _():
                half_keeps(side, c).start()
                half_copy(side, c, gu_ref.at[c]).start()

            @pl.when(there & (rank > 0))
            def _():
                half_land(side, c).wait_recv()

            @pl.when(there & (rank > 0) & (rank < depth - 1))
            def _():
                half_copy(side, c, ou_ref.at[side, c]).start()

    first(0)
    load_q.wait()
    line_step(0)
    line_step(1)
    first(1)
    line_step(2)
    second(0)
    line_step(3)
    last(0, store_line)
    for t in (4, 5, 6):
        line_step(t)
    first(2)
    line_step(7)
    second(1)
    line_step(8)
    last(1, store_into(sn_ref))
    for t in (9, 10):
        line_step(t)
    second(2)
    for t in range(11, per_side + 2 * (depth - 1) - 1):
        line_step(t)
    last(2, store_into(so_ref))
    line_step(per_side + 2 * (depth - 1) - 1)

    for m in range(3):
        for send in twins[m] + sends[m]:
            send.wait_send()
    for side in (0, 1):
        rank = half_rank(side)
        for c in range(pieces):

            @pl.when(rank == 0)
            def _():
                half_keeps(side, c).wait()
                half_copy(side, c, gu_ref.at[c]).wait_send()

            @pl.when((rank > 0) & (rank < depth - 1))
            def _():
                half_copy(side, c, ou_ref.at[side, c]).wait_send()

    for g in range(chunks):
        rank, ahead, behind = ranks(g % 2)

        @pl.when(rank < depth - 1)
        def _():
            go_up(g, ahead).wait_send()

        @pl.when(rank > 0)
        def _():
            go_down(g, behind).wait_send()

        deliver(g, True)
    for slot in range(3):
        block = 3 * me + slot
        source = lax.rem(block, n)

        @pl.when(source != me)
        def _():
            for piece in range(per_part):
                remote(
                    zfin.at[0],
                    oq_ref.at[slot, piece],
                    home_send.at[0],
                    home_recv.at[slot, piece],
                    source,
                ).wait_recv()


CHUNK = 64


def finish(grad_qkv, part_out, part_normed, part_outputs, grad_up, collective_id):
    n, depth = lax.axis_size("seq"), lax.axis_size("batch")
    rows, width = part_out.shape[0] // n, part_out.shape[1]
    cols = grad_qkv.shape[0] // 3
    if n != 8 or depth != 4:
        me = lax.axis_index("seq")
        blocks = lax.psum(grad_qkv, "batch").reshape(3, cols, width)
        back = [
            lax.ppermute(
                give_part(blocks, me, n, j),
                "seq",
                [((3 * d + j) % n, d) for d in range(n)],
            )
            for j in range(3)
        ]
        w_out = lax.psum(scatter_seq(part_out, None).astype(BF16), "batch")
        return (
            jnp.concatenate(back, axis=0),
            w_out,
            scatter_seq(part_normed, None),
            scatter_seq(part_outputs, None),
            grad_up,
        )
    pieces = grad_up.shape[0] // CHUNK
    turned, chunks = 3 * cols // CHUNK, (3 * cols + rows) // CHUNK
    inside = pl.BlockSpec(memory_space=pltpu.VMEM)
    dma = pltpu.SemaphoreType.DMA
    line = pltpu.VMEM((chunks, CHUNK, width), BF16)
    w_qkv, w_out, normed, outputs, w_up = pl.pallas_call(
        functools.partial(finish_kernel, n, depth),
        out_shape=(
            jax.ShapeDtypeStruct((3, cols // CHUNK, CHUNK, width), BF16),
            jax.ShapeDtypeStruct((rows // CHUNK, CHUNK, width), BF16),
            jax.ShapeDtypeStruct((rows, width), F32),
            jax.ShapeDtypeStruct((rows, width), F32),
            jax.ShapeDtypeStruct((2, pieces, CHUNK, width), BF16),
        ),
        in_specs=[ANY] * 5,
        out_specs=(ANY, ANY, inside, inside, ANY),
        scratch_shapes=[
            pltpu.VMEM((3, 4, rows, width), BF16),
            pltpu.VMEM((3, 4, rows, width), BF16),
            pltpu.VMEM((3, 6, rows // 2, width), BF16),
            line,
            line,
            line,
            dma((13,)),
            dma((3, 10)),
            dma((3, 10)),
            dma((chunks,)),
            dma((chunks,)),
            dma((chunks,)),
            dma((chunks,)),
            dma((chunks,)),
            dma((chunks,)),
            dma((3, cols // CHUNK)),
            dma((pieces,)),
            dma((2, pieces)),
            dma((2, pieces)),
        ],
        compiler_params=pltpu.CompilerParams(
            collective_id=collective_id,
            has_side_effects=True,
            vmem_limit_bytes=58 * 1024 * 1024,
        ),
        name="finish",
    )(
        grad_qkv.reshape(turned, CHUNK, width),
        *[p.reshape(n, rows, width) for p in (part_out, part_normed, part_outputs)],
        grad_up.reshape(pieces, CHUNK, width),
    )
    return (
        w_qkv.reshape(3 * cols, width),
        w_out.reshape(rows, width),
        normed,
        outputs,
        w_up.reshape(-1, width),
    )


def half_hop(grad, came, hop):
    n, depth = lax.axis_size("seq"), lax.axis_size("batch")
    if n != 8 or depth != 4:
        return lax.psum(grad, "batch") if hop == 1 else came
    z = lax.axis_index("batch")
    rows = grad.shape[0] // 2
    low, high = grad[:rows], grad[rows:]
    part = jnp.where(z == hop - 1, low, high)
    if hop > 1:
        part = (part.astype(F32) + came.astype(F32)).astype(BF16)
    if hop == depth:
        return part
    pairs = [(hop - 1, hop), (depth - hop, depth - 1 - hop)]
    return lax.ppermute(part, "batch", pairs)


def gains_kernel(
    n, depth, a_ref, b_ref, oa_ref, ob_ref, held_a, held_b, pack, held_c, send_sem, recv_sem, last_send, last_recv
):
    me = lax.axis_index("seq")
    z = lax.axis_index("batch")
    p, q = a_ref.shape[0], b_ref.shape[0]
    barrier = pltpu.get_barrier_semaphore()
    for k in range(1, n):
        pl.semaphore_signal(
            barrier, inc=1, device_id={"seq": lax.rem(me + k, n)}, device_id_type=MESH
        )
    for k in range(1, depth):
        pl.semaphore_signal(
            barrier,
            inc=1,
            device_id={"batch": lax.rem(z + k, depth)},
            device_id_type=MESH,
        )
    pl.semaphore_wait(barrier, n + depth - 2)
    held_a[me] = a_ref[...]
    held_b[me] = b_ref[...]
    copies = []
    for k in range(1, n):
        partner = lax.rem(me + k, n)
        copies.append(
            remote(a_ref, held_a.at[me], send_sem.at[0, k], recv_sem.at[0, k], partner)
        )
        copies.append(
            remote(b_ref, held_b.at[me], send_sem.at[1, k], recv_sem.at[1, k], partner)
        )
    for copy in copies:
        copy.start()
    for copy in copies:
        copy.wait()
    total = held_a[0]
    for d in range(1, n):
        total = total + held_a[d]
    pack[0:p] = total
    for d in range(n):
        pack[p + d * q : p + (d + 1) * q] = held_b[d]
    held_c[z] = pack[...]
    copies = [
        pltpu.make_async_remote_copy(
            src_ref=pack,
            dst_ref=held_c.at[z],
            send_sem=last_send.at[k],
            recv_sem=last_recv.at[k],
            device_id={"batch": lax.rem(z + k, depth)},
            device_id_type=MESH,
        )
        for k in range(1, depth)
    ]
    for copy in copies:
        copy.start()
    for copy in copies:
        copy.wait()
    total = held_c[0]
    for d in range(1, depth):
        total = total + held_c[d]
    oa_ref[...] = total[0:p]
    ob_ref[...] = total[p:]


def sum_gains(shared, mine, collective_id):
    n, depth = lax.axis_size("seq"), lax.axis_size("batch")
    p, q = shared.shape[0], mine.shape[0]
    inside = pl.BlockSpec(memory_space=pltpu.VMEM)
    return pl.pallas_call(
        functools.partial(gains_kernel, n, depth),
        out_shape=(
            jax.ShapeDtypeStruct((p, 128), F32),
            jax.ShapeDtypeStruct((n * q, 128), F32),
        ),
        in_specs=[inside, inside],
        out_specs=(inside, inside),
        scratch_shapes=[
            pltpu.VMEM((n, p, 128), F32),
            pltpu.VMEM((n, q, 128), F32),
            pltpu.VMEM((p + n * q, 128), F32),
            pltpu.VMEM((depth, p + n * q, 128), F32),
            pltpu.SemaphoreType.DMA((2, n)),
            pltpu.SemaphoreType.DMA((2, n)),
            pltpu.SemaphoreType.DMA((depth,)),
            pltpu.SemaphoreType.DMA((depth,)),
        ],
        compiler_params=pltpu.CompilerParams(
            collective_id=collective_id, has_side_effects=True
        ),
        name="sum_gains",
    )(shared, mine)


def body(
    inputs,
    segment_ids,
    w_qkv,
    w_out,
    w_up,
    w_down,
    gain_attn,
    gain_mix,
    gain_ffn,
    gain_hidden,
    cotangent,
):
    _, local, width = inputs.shape
    n, depth = lax.axis_size("seq"), lax.axis_size("batch")
    me = lax.axis_index("seq")
    length = local * n
    feats = w_up.shape[0]
    x_low = inputs[0]
    x = x_low.astype(F32)
    cot = cotangent[0]
    segment = segment_ids[0]

    w_out_full = lax.all_gather(w_out, "seq", axis=0, tiled=True)
    normal_attn, scale_attn = norm_parts(x)
    normed = (normal_attn * gain_attn).astype(BF16)
    before = [jnp.sum((segment < d).astype(jnp.int32)) for d in range(1, DOCS)]
    start = jnp.zeros_like(segment)
    for d in range(1, DOCS):
        start = jnp.where(segment == d, before[d - 1], start)
    positions = jnp.arange(length, dtype=jnp.int32) - start
    first = start[::TILE] // TILE
    start_row = start[None, :]

    normed_full, (wq, wk, wv), w_down_near, tables = start_exchange(
        normed, w_qkv, w_down, positions.astype(F32), 1
    )
    cot_late, _ = lax.optimization_barrier((cot, wq))
    cot_full = lax.all_gather(cot_late, "seq", axis=0, tiled=True)

    q, k, v, kt, vt = project_qkv(normed_full, wq, wk, wv, tables)
    attended_heads, lse = attend(first, start_row, q, k, vt)
    attended = heads_to_tokens(attended_heads, 2)
    mix_in, middle, ffn_in = mix_pass(attended, x_low, w_out_full, gain_mix, gain_ffn)
    ffn_full, w_down_cols = gather_seq(ffn_in, w_down_near, 3)

    gain_here = lax.dynamic_slice_in_dim(gain_hidden, me * feats, feats, 0)[None, :]
    act, slope, grad_hidden, stat = upper_pass(
        ffn_full, w_up, cot_full, w_down_cols, gain_here
    )
    stats = join_stats(stat, feats, 8)
    hidden, grad_upper, grad_gain_here = hidden_pass(act, slope, grad_hidden, stats, gain_here)

    grad_w_down = tn(cot_full, hidden).astype(BF16)
    grad_upper, grad_w_down = lax.optimization_barrier((grad_upper, grad_w_down))
    grad_w_up = tn(grad_upper, ffn_full).astype(BF16)
    grad_upper, grad_w_up = lax.optimization_barrier((grad_upper, grad_w_up))
    down_part = lax.psum_scatter(
        grad_w_down.reshape(n, local, feats), "batch", scatter_dimension=1, tiled=True
    )
    hop_one = half_hop(grad_w_up, None, 1)
    grad_ffn_in = scatter_seq(nn(grad_upper, w_up).astype(BF16), 4)
    hop_one, grad_ffn_in = lax.optimization_barrier((hop_one, grad_ffn_in))
    hop_two = half_hop(grad_w_up, hop_one, 2)
    grad_middle, grad_branch, grad_att, grad_gain_ffn, grad_gain_mix = branch_pass(
        grad_ffn_in, middle, cot, attended, w_out_full, gain_mix, gain_ffn
    )
    grad_heads = tokens_to_heads(grad_att, 5)
    down_part, grad_heads = lax.optimization_barrier((down_part, grad_heads))
    down_part = lax.all_to_all(down_part, "seq", split_axis=0, concat_axis=0, tiled=True)
    down_part = jnp.swapaxes(down_part, 0, 1).reshape(local // depth, n * feats)
    grad_w_down = lax.all_gather(down_part, "batch", axis=0, tiled=True)

    dq, dk, dv = attend_back(
        first, start_row, q, k, kt, v, attended_heads, lse, grad_heads, tables
    )
    hop_two, dq = lax.optimization_barrier((hop_two, dq))
    hop_three = half_hop(grad_w_up, hop_two, 3)
    grads = jnp.concatenate([dq, dk, dv], axis=1)
    weights = jnp.concatenate([wq, wk, wv], axis=0)
    grad_w_qkv, grad_w_out, grad_normed, down_sum, grad_w_up = finish(
        tn(grads, normed_full).astype(BF16),
        tn(grad_branch, mix_in).astype(BF16),
        nn(grads, weights).astype(BF16),
        nt(hidden, w_down_cols).astype(BF16),
        half_hop(grad_w_up, hop_three, depth),
        6,
    )
    grad_part, grad_gain_attn = norm_back(grad_normed, normal_attn, scale_attn, gain_attn)
    grad_inputs = grad_middle + grad_part
    outputs = (middle + down_sum).astype(BF16)
    shared, hidden_gains = sum_gains(
        jnp.concatenate([grad_gain_attn, grad_gain_mix[0], grad_gain_ffn[0]]).reshape(-1, 128),
        grad_gain_here.reshape(-1, 128),
        9,
    )
    shared = shared.reshape(-1)
    return (
        outputs[None],
        grad_inputs[None],
        grad_w_qkv.astype(F32),
        grad_w_out.astype(F32),
        grad_w_up.astype(F32),
        grad_w_down.astype(F32),
        shared[:width],
        shared[width : 2 * width],
        shared[2 * width :],
        hidden_gains.reshape(-1),
    )


def pick_part(turned, me, n, part):
    chosen = turned[0]
    home = part * n + me
    for j in (1, 2):
        chosen = jnp.where(lax.rem(home, 3) == j, turned[j], chosen)
    return chosen


def give_part(blocks, me, n, j):
    chosen = blocks[0]
    for part in (1, 2):
        chosen = jnp.where(lax.rem(part * n + me, 3) == j, blocks[part], chosen)
    return chosen


def solution(mesh):
    in_specs = (
        P("batch", "seq", None),
        P("batch", None),
        P("seq", None),
        P("seq", None),
        P("seq", None),
        P("seq", None),
        P(),
        P(),
        P(),
        P(),
        P("batch", "seq", None),
    )
    out_specs = (
        P("batch", "seq", None),
        P("batch", "seq", None),
        P("seq", None),
        P("seq", None),
        P("seq", None),
        P("seq", None),
        P(),
        P(),
        P(),
        P(),
    )
    return jax.shard_map(body, mesh=mesh, in_specs=in_specs, out_specs=out_specs, check_vma=False)
```

time: 2040 us -> 983 us (0.48)
  waiting for transfers between devices: 1210 us -> 119 us
  Pallas kernels: 0 us -> 633 us
  matrix products: 389 us -> 77.7 us
  blocking collectives: 133 us -> 0 us
  other arithmetic: 176 us -> 48.1 us
  local copies, waits for them, and re-layouts: 88.6 us -> 40.1 us
  starting transfers between devices: 8.55 us -> 44.3 us
    pallas_call x0 -> x15, Pallas kernels: none -> 633 us  [the longest x1 189 us: finish(): pl.pallas_call(functools.partial(finish_kernel, n, depth), out_shape=(jax...]
    reduce_scatter x4 -> x1, waiting for transfers between devices: 527 us -> 0.01 us  [body(): lax.psum_scatter(grad_w_down.reshape(n, local, feats), 'batch', scatter_d...]
    psum x1 -> x0, waiting for transfers between devices: 345 us -> none  [body(): lax.psum(grad_w_down.astype(jnp.bfloat16), 'batch').astype(jnp.float32)]
    dot_general x40 -> x7, matrix products: 389 us -> 77.7 us  [the longest x4 43.5 us: tn(): lax.dot_general(a, b, (((0,), (0,)), ((), ())), preferred_element_type=F32)]
    all_gather x4 -> x3, waiting for transfers between devices: 265 us -> 0.02 us  [the longest x1 0.02 us: body(): cot_full = lax.all_gather(cot_late, 'seq', axis=0, tiled=True)]
    ppermute x0 -> x3, waiting for transfers between devices: none -> 113 us  [half_hop(): return lax.ppermute(part, 'batch', pairs)]
    all_to_all x2 -> x0, blocking collectives: 83 us -> none  [the longest x1 52.7 us: body(): lax.all_to_all(grad_packed, 'seq', split_axis=1, concat_axis=3, tiled=True)]
    all_to_all x2 -> x1, waiting for transfers between devices: 66.7 us -> 5.16 us  [body(): lax.all_to_all(down_part, 'seq', split_axis=0, concat_axis=0, tiled=True)]
  transfers between devices with their start and end apart: 11 -> 8, of which waited for: 9 -> 3; matrix products, arithmetic and copies ran while one was open for 27% -> 12% of each run, Pallas kernels for 0% -> 60%
where the time goes in v1:
time: 983 us; the launch traced here: 977 us
  Pallas kernels  633 us (64%)
  waiting for transfers between devices  119 us (12%)
  matrix products  77.7 us (8%)
  other arithmetic  48.1 us (5%)
  starting transfers between devices  44.3 us (5%)
  local copies, waits for them, and re-layouts  40.1 us (4%)
  between operations  14.6 us (1%)
    pallas_call x1, Pallas kernels, finish(): pl.pallas_call(functools.partial(finish_kernel, n, depth), out_shape=(jax...  189 us
    ppermute x3, waiting for transfers between devices, half_hop(): return lax.ppermute(part, 'batch', pairs)  113 us
    pallas_call x1, Pallas kernels, start_exchange(): pl.pallas_call(functools.partial(start_kernel, n, depth), out_shape=(jax....  113 us
    pallas_call x1, Pallas kernels, gather_seq(): pl.pallas_call(functools.partial(gather_kernel, n, depth), out_shape=(jax...  96.8 us
    dot_general x4, matrix products, tn(): lax.dot_general(a, b, (((0,), (0,)), ((), ())), preferred_element_type=F32)  43.5 us
    pallas_call x1, Pallas kernels, scatter_seq(): pl.pallas_call(scatter_kernel, out_shape=jax.ShapeDtypeStruct((rows, widt...  40.7 us
    ppermute x3, starting transfers between devices, half_hop(): return lax.ppermute(part, 'batch', pairs)  39.9 us
    pallas_call x1, Pallas kernels, attend_back(): pl.pallas_call(functools.partial(attend_back_kernel, heads), out_shape=(s...  35.2 us
  transfers between devices with their start and end apart: 8, of which 3 were waited for; matrix products, arithmetic and copies ran while one was open for 12% of the time, Pallas kernels for 60%

profile of v1, /device:TPU:0, one launch (start us, length us, event | category | flops | bytes accessed | tf_op | source)
XLA Modules:
  0.0 976.8 jit_solution(5631490734901508823)
XLA Ops:
  8.0 1.4 fusion.20
  9.4 1.4 convert_reduce_fusion
  10.9 1.6 fusion.18
  12.5 2.0 compare_select_fusion.2.start_ref
  16.5 112.8 %start_exchange.1 = (bf16[8,256,2048]{2,1,0:T(8,128)(2,1)}, bf16[256,2048]{1,0:T(8,128)(2,1)}, bf16[256,2048]{1,0:T(8,128)(2,1)}, bf16[256,2048]{1,0:T(8,128)(2,...) custom-call(bf16[256,2048]{1,0:T(8,128)(2,1)} %fusion.11.x_ref, ...), custom_call_target="tpu_custom_call" | custom-call | tf_op jit(solution)/shard_map/start_exchange/pallas_call | solution.py:452
  138.3 11.7 %project_qkv.1 = (bf16[2048,256]{1,0:T(8,128)(2,1)S(1)}, bf16[2048,256]{1,0:T(8,128)(2,1)S(1)}, bf16[2048,256]{1,0:T(8,128)(2,1)S(1)}, bf16[256,2048]{1,0:T(8,128)(2,1)S(1)}, bf16[256,2048]{1,0:T(8,128)(2,1)S(1)}) custom-call(bf16[2048,2048]{1,0:T(8,128)(2,1)} %bitcast.89, bf16[256,2048]{1,0:T(8,128)(2,1)S(1)} %copy-done.28, ...), custom_call_target="tpu_custom_call" | custom-call | flops 6442450944 | bytes 16777216 | tf_op jit(solution)/shard_map/project_qkv/pallas_call | solution.py:751
  150.1 25.8 %attend.1 = (bf16[2048,256]{1,0:T(8,128)(2,1)S(1)}, f32[8,4,256]{2,1,0:T(4,128)S(1)}) custom-call(s32[8]{0:T(128)S(1)} %and_select_fusion.first_ref, s32[1,2048]{1,0:T(1,128)S(1)} %compare_select_fusion.2.start_ref, bf16[2048,256]{1,0:T(8,128)(2,1)S(1)} %get-tuple-element.72.q_ref, bf16[2048,256]{1,0:T(8,128)(2,1)S(1)} %get-tuple-element.73.k_ref, ...), custom_call_target="tpu_custom_call" | custom-call | flops 2147483648 | bytes 4194304 | tf_op jit(solution)/shard_map/attend/pallas_call | solution.py:831
  177.0 14.6 %heads_to_tokens.1.att_ref = bf16[256,2048]{1,0:T(8,128)(2,1)} custom-call(bf16[2048,256]{1,0:T(8,128)(2,1)} %copy-done.12), custom_call_target="tpu_custom_call" | custom-call | tf_op jit(solution)/shard_map/heads_to_tokens/pallas_call | solution.py:654
  192.3 3.4 copy-done.1
  196.9 7.4 mix_pass.1
  206.3 96.8 %gather_seq.1 = (bf16[8,256,2048]{2,1,0:T(8,128)(2,1)}, bf16[8,4,64,1024]{3,2,1,0:T(8,128)(2,1)}) custom-call(bf16[256,2048]{1,0:T(8,128)(2,1)} %copy-done.11, bf16[8,4,64,1024]{3,2,1,0:T(8,128)(2,1)} %get-tuple-element.78.near_ref), custom_call_target="tpu_custom_call" | custom-call | tf_op jit(solution)/shard_map/gather_seq/pallas_call | solution.py:283
  303.1 28.6 %upper_pass.1 = (f32[2048,1024]{1,0:T(8,128)}, bf16[2048,1024]{1,0:T(8,128)(2,1)S(1)}, f32[2048,1024]{1,0:T(8,128)}, f32[8,2048]{1,0:T(8,128)S(1)}) custom-call(bf16[2048,2048]{1,0:T(8,128)(2,1)} %bitcast.91, bf16[1024,2048]{1,0:T(8,128)(2,1)} %wu_ref.1, bf16[2048,2048]{1,0:T(8,128)(2,1)} %all-gather.6.cloned.1.call-done.c_ref, bf16[2048,1024]{1,0:T(8,128)(2,1)} %bitcast.93, ...), custom_call_target="tpu_custom_call" | custom-call | flops 17179869184 | bytes 50331648 | tf_op jit(solution)/shard_map/upper_pass/pallas_call | solution.py:1011
  331.8 2.0 copy-done.5
  334.4 11.9 %join_stats.1.stat_ref = f32[8,2048]{1,0:T(8,128)} custom-call(f32[8,2048]{1,0:T(8,128)} %copy-done.21), custom_call_target="tpu_custom_call" | custom-call | tf_op jit(solution)/shard_map/join_stats/pallas_call | solution.py:1122
  346.3 2.2 copy-done.6
  349.3 10.7 %hidden_pass.1 = (bf16[2048,1024]{1,0:T(8,128)(2,1)S(1)}, bf16[2048,1024]{1,0:T(8,128)(2,1)S(1)}, f32[1,1024]{1,0:T(1,128)S(1)}) custom-call(f32[2048,1024]{1,0:T(8,128)} %get-tuple-element.82.act_ref, bf16[2048,1024]{1,0:T(8,128)(2,1)S(1)} %copy-done.6, f32[2048,1024]{1,0:T(8,128)} %get-tuple-element.84.grad_ref, f32[8,2048]{1,0:T(8,128)S(1)} %copy-done.20, ...), custom_call_target="tpu_custom_call" | custom-call | flops 25165824 | bytes 29360128 | tf_op jit(solution)/shard_map/hidden_pass/pallas_call | solution.py:1066
  360.1 10.9 %convolution_convert_fusion.5 = bf16[2048,1024]{1,0:T(8,128)(2,1)} fusion(bf16[2048,2048]{1,0:T(8,128)(2,1)S(1)} %copy-done.56, bf16[2048,1024]{1,0:T(8,128)(2,1)S(1)} %get-tuple-element.87), kind=kOutput, calls=%fused_computation.9 | convolution fusion | flops 8592031744 | bytes 16777216 | tf_op jit(solution)/shard_map/dot_general | solution.py:35
  371.0 13.2 %convolution_convert_fusion.4 = bf16[1024,2048]{1,0:T(8,128)(2,1)S(1)} fusion(bf16[2048,1024]{1,0:T(8,128)(2,1)} %copy-done.27, bf16[2048,2048]{1,0:T(8,128)(2,1)} %bitcast.92), kind=kOutput, calls=%fused_computation.8 | convolution fusion | flops 8592031744 | bytes 16777216 | tf_op jit(solution)/shard_map/dot_general | solution.py:35
  384.2 1.7 broadcast_select_fusion
  386.9 36.5 %collective-permute-start = (bf16[512,2048]{1,0:T(8,128)(2,1)}, bf16[512,2048]{1,0:T(8,128)(2,1)}, u32[]{:S(2)}, u32[]{:S(2)}) collective-permute-start(bf16[512,2048]{1,0:T(8,128)(2,1)} %broadcast_select_fusion), channel_id=1, source_target_pairs={{0,8},{24,16},{1,9},{25,17},{2,10},{26,18},{3,11},{27,19},{4,12},{... | collective-permute-start | bytes 6291464 | tf_op jit(solution)/shard_map/ppermute | solution.py:1708
  423.3 11.9 %convolution_convert_fusion.3 = bf16[2048,2048]{1,0:T(8,128)(2,1)S(1)} fusion(bf16[2048,1024]{1,0:T(8,128)(2,1)} %copy-done.27, bf16[1024,2048]{1,0:T(8,128)(2,1)} %wu_ref.1), kind=kOutput, calls=%fused_computation.3 | convolution fusion | flops 8594128896 | bytes 16777216 | tf_op jit(solution)/shard_map/dot_general | solution.py:27
  435.3 40.7 %scatter_seq.1.g_ref = f32[256,2048]{1,0:T(8,128)S(1)} custom-call(bf16[8,256,2048]{2,1,0:T(8,128)(2,1)S(1)} %bitcast.65), custom_call_target="tpu_custom_call" | custom-call | tf_op jit(solution)/shard_map/scatter_seq/pallas_call | solution.py:582
  475.9 37.2 %collective-permute-done = bf16[512,2048]{1,0:T(8,128)(2,1)} collective-permute-done((bf16[512,2048]{1,0:T(8,128)(2,1)}, bf16[512,2048]{1,0:T(8,128)(2,1)}, u32[]{:S(2)}, u32[]{:S(2)}) %collective-permute-start) | collective-permute-done | bytes 2097184 | tf_op jit(solution)/shard_map/ppermute | solution.py:1708
  513.2 4.3 add_convert_fusion.2
  517.5 2.1 collective-permute-start.1
  519.6 10.9 %convolution_convert_fusion = bf16[2048,2048]{1,0:T(8,128)(2,1)} fusion(bf16[2048,1024]{1,0:T(8,128)(2,1)S(1)} %copy-done.26, bf16[2048,1024]{1,0:T(8,128)(2,1)S(1)} %bitcast.94), kind=kOutput, calls=%fused_computation | convolution fusion | flops 8594128896 | bytes 16777216 | tf_op jit(solution)/shard_map/dot_general | solution.py:31
  530.4 13.6 %branch_pass.1 = (f32[256,2048]{1,0:T(8,128)S(1)}, bf16[256,2048]{1,0:T(8,128)(2,1)S(1)}, bf16[256,2048]{1,0:T(8,128)(2,1)S(1)}, f32[1,2048]{1,0:T(1,128)S(1)}, f32[1,2048]{1,0:T(1,128)S(1)}) custom-call(f32[256,2048]{1,0:T(8,128)S(1)} %scatter_seq.1.g_ref, f32[256,2048]{1,0:T(8,128)S(1)} %get-tuple-element.76.mid_ref, bf16[256,2048]{1,0:T(8,128)(2,1)S(1)} %bitcast.67, ...), custom_call_target="tpu_custom_call" | custom-call | flops 2147483648 | bytes 18874368 | tf_op jit(solution)/shard_map/branch_pass/pallas_call | solution.py:1243
  547.3 13.7 %tokens_to_heads.1.do_ref = bf16[2048,256]{1,0:T(8,128)(2,1)} custom-call(bf16[256,2048]{1,0:T(8,128)(2,1)} %copy-done.19), custom_call_target="tpu_custom_call" | custom-call | tf_op jit(solution)/shard_map/tokens_to_heads/pallas_call | solution.py:689
  561.0 7.3 convolution_convert_fusion.2
  570.8 35.2 %attend_back.1 = (bf16[2048,256]{1,0:T(8,128)(2,1)S(1)}, bf16[2048,256]{1,0:T(8,128)(2,1)S(1)}, bf16[2048,256]{1,0:T(8,128)(2,1)S(1)}) custom-call(s32[8]{0:T(128)S(1)} %and_select_fusion.first_ref, s32[1,2048]{1,0:T(1,128)S(1)} %compare_select_fusion.2.start_ref, bf16[2048,256]{1,0:T(8,128)(2,1)S(1)} %copy-done.36, bf16[2048,256]{1,0:T(8,128)(2,1)S(1)} %copy-done.38, ...), custom_call_target="tpu_custom_call" | custom-call | flops 5368709120 | bytes 8388608 | tf_op jit(solution)/shard_map/attend_back/pallas_call | solution.py:945
  608.9 4.2 all-to-all-start
  613.2 5.7 add_convert_fusion.1
  618.9 1.4 collective-permute-start.2
  623.5 5.2 all-to-all-done
  628.6 2.3 copy.22
  631.0 11.5 %convolution_convert_fusion.1 = bf16[2048,2048]{1,0:T(8,128)(2,1)} fusion(bf16[2048,768]{1,0:T(8,128)(2,1)} %constant_dynamic-update-slice_fusion, bf16[256,2048]{1,0:T(8,128)(2,1)} %get-tuple-element.67.wv_ref, bf16[256,2048]{1,0:T(8,128)(2,1)} %get-tuple-element.66.wk_ref, bf16[256,2048]{1,0:T(8,128)(2,1)} %get-tuple-element.65.wq_ref), kind=kOutput, calls=%fused_computation.1 | convolution fusion | flops 6456082432 | bytes 14680064 | tf_op jit(solution)/shard_map/dot_general | solution.py:27
  642.5 12.1 %convolution_convert_fusion.6 = bf16[768,2048]{1,0:T(8,128)(2,1)} fusion(bf16[2048,768]{1,0:T(8,128)(2,1)} %constant_dynamic-update-slice_fusion, bf16[2048,2048]{1,0:T(8,128)(2,1)} %bitcast.90), kind=kOutput, calls=%fused_computation.10 | convolution fusion | flops 6444023808 | bytes 14680064 | tf_op jit(solution)/shard_map/dot_general | solution.py:35
  654.6 76.1 %collective-permute-done.2 = bf16[512,2048]{1,0:T(8,128)(2,1)} collective-permute-done((bf16[512,2048]{1,0:T(8,128)(2,1)}, bf16[512,2048]{1,0:T(8,128)(2,1)}, u32[]{:S(2)}, u32[]{:S(2)}) %collective-permute-start.2) | collective-permute-done | bytes 2097184 | tf_op jit(solution)/shard_map/ppermute | solution.py:1708
  730.7 4.2 add_convert_fusion
  734.9 189.4 %finish.1 = (bf16[3,4,64,2048]{3,2,1,0:T(8,128)(2,1)}, bf16[4,64,2048]{2,1,0:T(8,128)(2,1)}, f32[256,2048]{1,0:T(8,128)}, f32[256,2048]{1,0:T(8,128)}, bf16[2,8,64,2048]{3,2,1,0:T(8,128)(2,1)}) custom-call(bf16[12,64,2048]{2,1,0:T(8,128)(2,1)} %bitcast.85, bf16[8,256,2048]{2,1,0:T(8,128)(2,1)} %bitcast.79, bf16[8,256,2048]{2,1,0:T(8,128)(2,1)} %bitcast.81, ...), custom_call_target="tpu_custom_call" | custom-call | tf_op jit(solution)/shard_map/finish/pallas_call | solution.py:1643
  924.3 2.5 fusion.17
  927.4 19.8 %sum_gains.1 = (f32[48,128]{1,0:T(8,128)}, f32[64,128]{1,0:T(8,128)}) custom-call(f32[48,128]{1,0:T(8,128)} %pad_maximum_fusion.a_ref, f32[8,128]{1,0:T(8,128)} %bitcast.78), custom_call_target="tpu_custom_call" | custom-call | tf_op jit(solution)/shard_map/sum_gains/pallas_call | solution.py:1778
  947.2 1.5 slice_bitcast_fusion
  948.7 2.8 bitcast_convert_fusion.2
  951.5 3.8 bitcast_convert_fusion.1
  955.3 4.7 bitcast_convert_fusion
  960.0 2.8 fusion.16
  962.8 6.6 convert_element_type.123
  (140 shorter events, 32.3 us)
Async XLA Ops:
  7.2 5.3 copy-start.51
  7.2 7.9 copy-start
  7.2 7.9 copy-start.48
  7.2 185.1 %all-gather.4.cloned.1.call-start = ((), (), s32[]{:S(2)}) async-start(), calls=%async_computation.2 | async-start | bytes 9437184 | tf_op jit(solution)/shard_map/all_gather | solution.py:1826
  7.9 295.2 %all-gather.6.cloned.1.call-start = ((), (), s32[]{:S(2)}) async-start(), calls=%async_computation.3 | async-start | bytes 9437184 | tf_op jit(solution)/shard_map/all_gather | solution.py:1841
  10.8 118.5 %copy-start.52 = (f32[256]{0:T(256)}, f32[256]{0:T(256)S(1)}, u32[]{:S(2)}) copy-start(f32[256]{0:T(256)S(1)} %broadcast_multiply_fusion.2) | copy-start | bytes 3076
  12.5 116.8 %copy-start.54 = (f32[256]{0:T(256)}, f32[256]{0:T(256)S(1)}, u32[]{:S(2)}) copy-start(f32[256]{0:T(256)S(1)} %add_rsqrt_fusion) | copy-start | bytes 3076
  129.4 439.0 %reduce-scatter.2.cloned.1.call-start = ((), (), s32[]{:S(2)}) async-start(), calls=%async_computation.4 | async-start | bytes 5242880 | tf_op jit(solution)/shard_map/reduce_scatter | solution.py:1860
  135.6 1.3 copy-start.33
  137.0 1.4 copy-start.34
  150.1 25.9 %copy-start.35 = (bf16[2048,256]{1,0:T(8,128)(2,1)}, bf16[2048,256]{1,0:T(8,128)(2,1)S(1)}, u32[]{:S(2)}) copy-start(bf16[2048,256]{1,0:T(8,128)(2,1)S(1)} %get-tuple-element.72.q_ref) | copy-start | bytes 3145732
  150.1 25.9 %copy-start.37 = (bf16[2048,256]{1,0:T(8,128)(2,1)}, bf16[2048,256]{1,0:T(8,128)(2,1)S(1)}, u32[]{:S(2)}) copy-start(bf16[2048,256]{1,0:T(8,128)(2,1)S(1)} %get-tuple-element.73.k_ref) | copy-start | bytes 3145732
  150.1 25.9 %copy-start.39 = (bf16[2048,256]{1,0:T(8,128)(2,1)}, bf16[2048,256]{1,0:T(8,128)(2,1)S(1)}, u32[]{:S(2)}) copy-start(bf16[2048,256]{1,0:T(8,128)(2,1)S(1)} %get-tuple-element.93.v_ref) | copy-start | bytes 3145732
  150.1 25.9 %copy-start.40 = (bf16[256,2048]{1,0:T(8,128)(2,1)}, bf16[256,2048]{1,0:T(8,128)(2,1)S(1)}, u32[]{:S(2)}) copy-start(bf16[256,2048]{1,0:T(8,128)(2,1)S(1)} %get-tuple-element.92.kt_ref) | copy-start | bytes 3145732
  150.1 42.2 %copy-start.22 = (f32[2048]{0:T(1024)S(1)}, f32[2048]{0:T(1024)}, u32[]{:S(2)}) copy-start(f32[2048]{0:T(1024)} %param.18) | copy-start | bytes 24580
  150.1 42.2 %copy-start.23 = (f32[2048]{0:T(1024)S(1)}, f32[2048]{0:T(1024)}, u32[]{:S(2)}) copy-start(f32[2048]{0:T(1024)} %param.19) | copy-start | bytes 24580
  192.3 3.4 copy-start.1
  331.8 2.0 copy-start.5
  346.3 2.2 copy-start.6
  349.3 10.7 %copy-start.56 = (bf16[2048,2048]{1,0:T(8,128)(2,1)S(1)}, bf16[2048,2048]{1,0:T(8,128)(2,1)}, u32[]{:S(2)}) copy-start(bf16[2048,2048]{1,0:T(8,128)(2,1)} %all-gather.6.cloned.1.call-done.c_ref) | copy-start | bytes 25165828
  360.0 10.9 %copy-start.24 = (f32[1,1024]{1,0:T(1,128)}, f32[1,1024]{1,0:T(1,128)S(1)}, u32[]{:S(2)}) copy-start(f32[1,1024]{1,0:T(1,128)S(1)} %get-tuple-element.115) | copy-start | bytes 12292
  360.0 10.9 %copy-start.25 = (bf16[2048,1024]{1,0:T(8,128)(2,1)}, bf16[2048,1024]{1,0:T(8,128)(2,1)S(1)}, u32[]{:S(2)}) copy-start(bf16[2048,1024]{1,0:T(8,128)(2,1)S(1)} %get-tuple-element.87) | copy-start | bytes 12582916
  360.0 10.9 %copy-start.27 = (bf16[2048,1024]{1,0:T(8,128)(2,1)}, bf16[2048,1024]{1,0:T(8,128)(2,1)S(1)}, u32[]{:S(2)}) copy-start(bf16[2048,1024]{1,0:T(8,128)(2,1)S(1)} %get-tuple-element.90) | copy-start | bytes 12582916
  384.1 2.7 copy-start.41
  386.9 126.3 %collective-permute-start = (bf16[512,2048]{1,0:T(8,128)(2,1)}, bf16[512,2048]{1,0:T(8,128)(2,1)}, u32[]{:S(2)}, u32[]{:S(2)}) collective-permute-start(bf16[512,2048]{1,0:T(8,128)(2,1)} %broadcast_select_fusion), channel_id=1, source_target_pairs={{0,8},{24,16},{1,9},{25,17},{2,10},{26,18},{3,11},{27,19},{4,12},{... | collective-permute-start | bytes 6291464 | tf_op jit(solution)/shard_map/ppermute | solution.py:1708
  435.2 77.9 %copy-start.42 = (bf16[1024,2048]{1,0:T(8,128)(2,1)S(1)}, bf16[1024,2048]{1,0:T(8,128)(2,1)}, u32[]{:S(2)}) copy-start(bf16[1024,2048]{1,0:T(8,128)(2,1)} %copy-done.41) | copy-start | bytes 12582916
  475.9 43.7 %copy-start.26 = (bf16[2048,1024]{1,0:T(8,128)(2,1)S(1)}, bf16[2048,1024]{1,0:T(8,128)(2,1)}, u32[]{:S(2)}) copy-start(bf16[2048,1024]{1,0:T(8,128)(2,1)} %copy-done.25) | copy-start | bytes 12582916
  475.9 43.6 %copy-start.57 = (bf16[8,4,64,1024]{3,2,1,0:T(8,128)(2,1)S(1)}, bf16[8,4,64,1024]{3,2,1,0:T(8,128)(2,1)}, u32[]{:S(2)}) copy-start(bf16[8,4,64,1024]{3,2,1,0:T(8,128)(2,1)} %get-tuple-element.81) | copy-start | bytes 12582916
  517.5 12.9 %copy-start.3 = (bf16[256,2048]{1,0:T(8,128)(2,1)S(1)}, bf16[256,2048]{1,0:T(8,128)(2,1)}, u32[]{:S(2)}) copy-start(bf16[256,2048]{1,0:T(8,128)(2,1)} %heads_to_tokens.1.att_ref) | copy-start | bytes 3145732
  517.5 12.9 %copy-start.4 = (bf16[1,256,2048]{2,1,0:T(8,128)(2,1)S(1)}, bf16[1,256,2048]{2,1,0:T(8,128)(2,1)}, u32[]{:S(2)}) copy-start(bf16[1,256,2048]{2,1,0:T(8,128)(2,1)} %param.21) | copy-start | bytes 3145732
  517.5 91.4 %collective-permute-start.1 = (bf16[512,2048]{1,0:T(8,128)(2,1)}, bf16[512,2048]{1,0:T(8,128)(2,1)}, u32[]{:S(2)}, u32[]{:S(2)}) collective-permute-start(bf16[512,2048]{1,0:T(8,128)(2,1)} %add_convert_fusion.2), channel_id=1, source_target_pairs={{8,16},{16,8},{9,17},{17,9},{10,18},{18,10},{11,19},{19,11},{12,20... | collective-permute-start | bytes 6291464 | tf_op jit(solution)/shard_map/ppermute | solution.py:1708
  544.0 1.3 copy-start.7
  608.9 19.8 %all-to-all-start = ((bf16[8,64,1024]{2,1,0:T(8,128)(2,1)}), bf16[8,64,1024]{2,1,0:T(8,128)(2,1)}, u32[]{:S(2)}, u32[]{:S(2)}) async-start(bf16[8,64,1024]{2,1,0:T(8,128)(2,1)} %reduce-scatter.2.cloned.1.call-done), calls=%async_computation.1 | async-start | bytes 2097152 | tf_op jit(solution)/shard_map/all_to_all | solution.py:1872
  613.1 349.7 %all-gather.8.cloned.1.call-start = ((), (), s32[]{:S(2)}) async-start(), calls=%async_computation.5 | async-start | bytes 5242880 | tf_op jit(solution)/shard_map/all_gather | solution.py:1874
  613.2 7.2 copy-start.18
  613.2 8.2 copy-start.16
  618.9 3.5 copy-start.14
  618.9 111.8 %collective-permute-start.2 = (bf16[512,2048]{1,0:T(8,128)(2,1)}, bf16[512,2048]{1,0:T(8,128)(2,1)}, u32[]{:S(2)}, u32[]{:S(2)}) collective-permute-start(bf16[512,2048]{1,0:T(8,128)(2,1)} %add_convert_fusion.1), channel_id=1, source_target_pairs={{16,24},{8,0},{17,25},{9,1},{18,26},{10,2},{19,27},{11,3},{20,28},... | collective-permute-start | bytes 6291464 | tf_op jit(solution)/shard_map/ppermute | solution.py:1708
  642.5 88.2 %copy-start.43 = (bf16[1024,2048]{1,0:T(8,128)(2,1)S(1)}, bf16[1024,2048]{1,0:T(8,128)(2,1)}, u32[]{:S(2)}) copy-start(bf16[1024,2048]{1,0:T(8,128)(2,1)} %copy-done.41) | copy-start | bytes 12582916
  734.9 189.4 %copy-start.49 = (f32[2048]{0:T(1024)S(1)}, f32[2048]{0:T(1024)}, u32[]{:S(2)}) copy-start(f32[2048]{0:T(1024)} %param.17) | copy-start | bytes 24580
  734.9 189.4 %copy-start.53 = (f32[256]{0:T(256)S(1)}, f32[256]{0:T(256)}, u32[]{:S(2)}) copy-start(f32[256]{0:T(256)} %copy-done.52) | copy-start | bytes 3076
  734.9 189.4 %copy-start.55 = (f32[256]{0:T(256)S(1)}, f32[256]{0:T(256)}, u32[]{:S(2)}) copy-start(f32[256]{0:T(256)} %copy-done.54) | copy-start | bytes 3076
  947.2 4.3 copy-start.46
  951.5 3.8 copy-start.45
  955.3 4.8 copy-start.8
  955.3 4.8 copy-start.44
  955.3 4.8 copy-start.47
  962.8 6.6 copy-start.50
  (18 other events, 19.1 us)
Sparse Core Ops, SparseCore 0:
  9.9 96.1 all-gather.3
  129.5 62.1 all-gather.5
  371.1 152.2 reduce-scatter.1
  631.1 106.2 all-gather.7

commit v2 on v1

--- a/solution.py
+++ b/solution.py
@@ -21,6 +21,7 @@
 F32 = jnp.float32
 BF16 = jnp.bfloat16
 ANY = pl.BlockSpec(memory_space=pl.ANY)
+INSIDE = pl.BlockSpec(memory_space=pltpu.VMEM)
 
 
 def nn(a, b):
@@ -223,16 +224,21 @@
 
 
 def gather_kernel(
-    n, depth, x_ref, near_ref, o_ref, all_ref, local_sem, send_sem, recv_sem, line_send, line_recv
+    n, depth, x_ref, near_ref, o_ref, all_ref, keep_ref, local_sem, send_sem, recv_sem, line_send, line_recv
 ):
     me, twin, near_x, near_y, _ = places()
     z = lax.axis_index("batch")
     own = pltpu.make_async_copy(x_ref, o_ref.at[me], local_sem.at[0])
     own.start()
 
+    def load(shift):
+        return pltpu.make_async_copy(
+            near_ref.at[:, z + shift], keep_ref.at[1 + shift], local_sem.at[2 + shift]
+        )
+
     def keep(shift):
         return pltpu.make_async_copy(
-            near_ref.at[:, z + shift], all_ref.at[:, z + shift], local_sem.at[2 + shift]
+            keep_ref.at[1 + shift], all_ref.at[:, z + shift], local_sem.at[5 + shift]
         )
 
     def kept(shift):
@@ -242,7 +248,7 @@
 
         @pl.when(kept(shift))
         def _():
-            keep(shift).start()
+            load(shift).start()
 
     meet_all(n, depth)
     sends = gather_copies(x_ref, o_ref, send_sem, recv_sem)
@@ -256,6 +262,12 @@
         line_recv,
     )
     line.start(1)
+    for shift in (-1, 0, 1):
+
+        @pl.when(kept(shift))
+        def _():
+            load(shift).wait()
+            keep(shift).start()
 
     def between():
         for k in range(2, depth - 1):
@@ -286,10 +298,11 @@
             jax.ShapeDtypeStruct((n, rows, width), block.dtype),
             jax.ShapeDtypeStruct(near.shape, near.dtype),
         ),
-        in_specs=[ANY, ANY],
+        in_specs=[INSIDE, ANY],
         out_specs=(ANY, ANY),
         scratch_shapes=[
-            pltpu.SemaphoreType.DMA((4,)),
+            pltpu.VMEM((3, n, *near.shape[2:]), near.dtype),
+            pltpu.SemaphoreType.DMA((7,)),
             pltpu.SemaphoreType.DMA((13,)),
             pltpu.SemaphoreType.DMA((13,)),
             pltpu.SemaphoreType.DMA((2, depth)),
@@ -321,7 +334,7 @@
 def start_kernel(
     n, depth, x_ref, w_ref, wd_ref, pos_ref,
     o_ref, wq_ref, wk_ref, wv_ref, wc_ref, cq_ref, sq_ref, ck_ref, sk_ref,
-    local_sem, send_sem, recv_sem, hop_send, hop_recv, col_send, col_recv, line_send, line_recv,
+    keep_w, keep_c, local_sem, send_sem, recv_sem, hop_send, hop_recv, col_send, col_recv, line_send, line_recv,
 ):
     z = lax.axis_index("batch")
     rows_z = wc_ref.shape[2]
@@ -335,9 +348,12 @@
     def column(k):
         return wd_ref.at[wd_rows, pl.ds(pl.multiple_of(k * cols, cols), cols)]
 
-    own_column = pltpu.make_async_copy(column(me), wc_ref.at[me, z], local_sem.at[4])
+    load_column = pltpu.make_async_copy(column(me), keep_c, local_sem.at[4])
+    own_column = pltpu.make_async_copy(keep_c, wc_ref.at[me, z], local_sem.at[5])
+    load_column.start()
+    meet_all(n, depth)
+    load_column.wait()
     own_column.start()
-    meet_all(n, depth)
     turns = [
         remote(
             column(lax.rem(me + k, n)),
@@ -367,8 +383,11 @@
             w_ref.at[j], parts[part], hop_send.at[j], hop_recv.at[part], target
         )
 
+    def load(j):
+        return pltpu.make_async_copy(w_ref.at[j], keep_w, local_sem.at[6])
+
     def here(j, part):
-        return pltpu.make_async_copy(w_ref.at[j], parts[part], local_sem.at[1 + j])
+        return pltpu.make_async_copy(keep_w, parts[part], local_sem.at[1 + j])
 
     for j in range(3):
         block = 3 * me + j
@@ -382,6 +401,8 @@
 
             @pl.when(inside & (target == me))
             def _():
+                load(j).start()
+                load(j).wait()
                 here(j, part).start()
 
     @pl.loop(0, pos_ref.shape[0])
@@ -459,10 +480,12 @@
             jax.ShapeDtypeStruct((n, depth, rows_z, cols), w_down.dtype),
             *([table] * 4),
         ),
-        in_specs=[ANY, ANY, ANY, inside],
-        out_specs=(ANY, ANY, ANY, ANY, ANY, *([inside] * 4)),
+        in_specs=[INSIDE, ANY, ANY, INSIDE],
+        out_specs=(ANY, ANY, ANY, ANY, ANY, *([INSIDE] * 4)),
         scratch_shapes=[
-            pltpu.SemaphoreType.DMA((5,)),
+            pltpu.VMEM((piece, width), BF16),
+            pltpu.VMEM((rows_z, cols), BF16),
+            pltpu.SemaphoreType.DMA((7,)),
             pltpu.SemaphoreType.DMA((13,)),
             pltpu.SemaphoreType.DMA((13,)),
             pltpu.SemaphoreType.DMA((3,)),
@@ -601,7 +624,7 @@
     )(partial.reshape(n, rows, width))
 
 
-def heads_to_tokens_kernel(n, x_ref, o_ref, local_sem, send_sem, recv_sem):
+def heads_to_tokens_kernel(n, x_ref, o_ref, keep, local_sem, send_sem, recv_sem):
     me = lax.axis_index("seq")
     rows = o_ref.shape[0]
     cols = x_ref.shape[1]
@@ -610,15 +633,17 @@
         me,
         lambda k: x_ref.at[pl.ds(pl.multiple_of(k * rows, rows), rows)],
         o_ref.at[:, pl.ds(pl.multiple_of(me * cols, cols), cols)],
+        keep,
         local_sem,
         send_sem,
         recv_sem,
     )
 
 
-def exchange(n, me, source, target, local_sem, send_sem, recv_sem):
-    own = pltpu.make_async_copy(source(me), target, local_sem)
-    own.start()
+def exchange(n, me, source, target, keep, local_sem, send_sem, recv_sem):
+    load = pltpu.make_async_copy(source(me), keep, local_sem.at[0])
+    own = pltpu.make_async_copy(keep, target, local_sem.at[1])
+    load.start()
     barrier = pltpu.get_barrier_semaphore()
     for k in range(1, n):
         pl.semaphore_signal(
@@ -642,6 +667,8 @@
             )
         )
         copies[-1].start()
+    load.wait()
+    own.start()
     for copy in copies:
         copy.wait()
     own.wait()
@@ -657,7 +684,8 @@
         in_specs=[ANY],
         out_specs=ANY,
         scratch_shapes=[
-            pltpu.SemaphoreType.DMA,
+            pltpu.VMEM((rows, cols), heads.dtype),
+            pltpu.SemaphoreType.DMA((2,)),
             pltpu.SemaphoreType.DMA((n,)),
             pltpu.SemaphoreType.DMA((n,)),
         ],
@@ -668,7 +696,7 @@
     )(heads)
 
 
-def tokens_to_heads_kernel(n, x_ref, o_ref, local_sem, send_sem, recv_sem):
+def tokens_to_heads_kernel(n, x_ref, o_ref, keep, local_sem, send_sem, recv_sem):
     me = lax.axis_index("seq")
     rows = x_ref.shape[0]
     cols = o_ref.shape[1]
@@ -677,6 +705,7 @@
         me,
         lambda k: x_ref.at[:, pl.ds(pl.multiple_of(k * cols, cols), cols)],
         o_ref.at[pl.ds(pl.multiple_of(me * rows, rows), rows)],
+        keep,
         local_sem,
         send_sem,
         recv_sem,
@@ -692,7 +721,8 @@
         in_specs=[ANY],
         out_specs=ANY,
         scratch_shapes=[
-            pltpu.SemaphoreType.DMA,
+            pltpu.VMEM((rows, total // n), tokens.dtype),
+            pltpu.SemaphoreType.DMA((2,)),
             pltpu.SemaphoreType.DMA((n,)),
             pltpu.SemaphoreType.DMA((n,)),
         ],
@@ -1267,9 +1297,9 @@
 
 def finish_kernel(
     n, depth, gq_ref, pw_ref, pn_ref, po_ref, gu_ref, oq_ref, ow_ref, sn_ref, so_ref, ou_ref,
-    own, twin_in, held, zown, zin, zfin,
+    own, twin_in, held, zown, zin,
     local_sem, send_sem, recv_sem, keep_sem,
-    up_send, up_recv, down_send, down_recv, home_send, home_recv, half_keep, half_send, half_recv,
+    up_send, up_recv, down_send, down_recv, home_send, home_recv,
 ):
     me, twin, near_x, near_y, across = places()
     z = lax.axis_index("batch")
@@ -1279,6 +1309,7 @@
     mine = (across, near_x, near_y, me)
     chunk = zown.shape[1]
     turned = gq_ref.shape[0]
+    upper = turned + gu_ref.shape[0]
     chunks = zown.shape[0]
     per_part = turned // 3
     per_side = chunks // 2
@@ -1286,7 +1317,11 @@
     load_q = pltpu.make_async_copy(
         gq_ref, zown.at[pl.ds(0, turned)], local_sem.at[12]
     )
+    load_u = pltpu.make_async_copy(
+        gu_ref, zown.at[pl.ds(turned, upper - turned)], local_sem.at[13]
+    )
     load_q.start()
+    load_u.start()
     partials = (pw_ref, pn_ref, po_ref)
     loads = [
         [
@@ -1384,7 +1419,7 @@
 
     def store_line(place, value):
         zown[
-            turned + place // chunk,
+            upper + place // chunk,
             pl.ds(pl.multiple_of(lax.rem(place, chunk), STEP), STEP),
         ] = value.astype(BF16)
 
@@ -1402,7 +1437,7 @@
         target, slot = home(g // per_part)
         piece = lax.rem(g, per_part)
         return remote(
-            zfin.at[g],
+            zin.at[g],
             oq_ref.at[slot, piece],
             home_send.at[g],
             home_recv.at[slot, piece],
@@ -1412,11 +1447,14 @@
     def deliver_near(g):
         _, slot = home(g // per_part)
         return pltpu.make_async_copy(
-            zfin.at[g], oq_ref.at[slot, lax.rem(g, per_part)], keep_sem.at[g]
+            zin.at[g], oq_ref.at[slot, lax.rem(g, per_part)], keep_sem.at[g]
         )
 
+    def deliver_up(g):
+        return pltpu.make_async_copy(zin.at[g], ou_ref.at[g - turned], keep_sem.at[g])
+
     def deliver_out(g):
-        return pltpu.make_async_copy(zfin.at[g], ow_ref.at[g - turned], keep_sem.at[g])
+        return pltpu.make_async_copy(zin.at[g], ow_ref.at[g - upper], keep_sem.at[g])
 
     def deliver(g, wait):
         target, _ = home(g // per_part)
@@ -1429,7 +1467,11 @@
         def _():
             deliver_near(g).wait() if wait else deliver_near(g).start()
 
-        @pl.when(g >= turned)
+        @pl.when((g >= turned) & (g < upper))
+        def _():
+            deliver_up(g).wait() if wait else deliver_up(g).start()
+
+        @pl.when(g >= upper)
         def _():
             deliver_out(g).wait() if wait else deliver_out(g).start()
 
@@ -1438,7 +1480,7 @@
 
     def go_down(g, behind):
         return line_remote(
-            zfin.at[g], zfin.at[g], down_send.at[g], down_recv.at[g], behind
+            zin.at[g], zin.at[g], down_send.at[g], down_recv.at[g], behind
         )
 
     def ranks(side):
@@ -1455,7 +1497,6 @@
             )
 
     def line_step(t):
-        half_step(t)
         for side in (0, 1):
             rank, ahead, behind = ranks(side)
             c = t - rank
@@ -1475,7 +1516,7 @@
             @pl.when(there & (rank == depth - 1))
             def _():
                 go_up(g, behind).wait_recv()
-                add_line(g, zfin)
+                add_line(g, zin)
                 go_down(g, behind).start()
                 deliver(g, False)
 
@@ -1495,54 +1536,9 @@
             def _():
                 deliver(g_back, False)
 
-    pieces = gu_ref.shape[0]
-
-    def half_rank(side):
-        return depth - 1 - z if side == 0 else z
-
-    def half_keeps(side, c):
-        return pltpu.make_async_copy(gu_ref.at[c], ou_ref.at[side, c], half_keep.at[c])
-
-    def half_copy(side, c, source):
-        return line_remote(
-            source,
-            ou_ref.at[side, c],
-            half_send.at[side, c],
-            half_recv.at[side, c],
-            z - 1 if side == 0 else z + 1,
-        )
-
-    def half_land(side, c):
-        place = ou_ref.at[side, c]
-        return line_remote(
-            place,
-            place,
-            half_send.at[side, c],
-            half_recv.at[side, c],
-            z + 1 if side == 0 else z - 1,
-        )
-
-    def half_step(t):
-        for side in (0, 1):
-            rank = half_rank(side)
-            c = t - rank
-            there = (c >= 0) & (c < pieces)
-
-            @pl.when(there & (rank == 0))
-            def _():
-                half_keeps(side, c).start()
-                half_copy(side, c, gu_ref.at[c]).start()
-
-            @pl.when(there & (rank > 0))
-            def _():
-                half_land(side, c).wait_recv()
-
-            @pl.when(there & (rank > 0) & (rank < depth - 1))
-            def _():
-                half_copy(side, c, ou_ref.at[side, c]).start()
-
     first(0)
     load_q.wait()
+    load_u.wait()
     line_step(0)
     line_step(1)
     first(1)
@@ -1553,34 +1549,24 @@
     for t in (4, 5, 6):
         line_step(t)
     first(2)
-    line_step(7)
+    for t in (7, 8):
+        line_step(t)
     second(1)
-    line_step(8)
-    last(1, store_into(sn_ref))
     for t in (9, 10):
         line_step(t)
+    last(1, store_into(sn_ref))
+    for t in (11, 12, 13):
+        line_step(t)
     second(2)
-    for t in range(11, per_side + 2 * (depth - 1) - 1):
+    steps = per_side + 2 * (depth - 1)
+    for t in range(14, steps - 1):
         line_step(t)
     last(2, store_into(so_ref))
-    line_step(per_side + 2 * (depth - 1) - 1)
+    line_step(steps - 1)
 
     for m in range(3):
         for send in twins[m] + sends[m]:
             send.wait_send()
-    for side in (0, 1):
-        rank = half_rank(side)
-        for c in range(pieces):
-
-            @pl.when(rank == 0)
-            def _():
-                half_keeps(side, c).wait()
-                half_copy(side, c, gu_ref.at[c]).wait_send()
-
-            @pl.when((rank > 0) & (rank < depth - 1))
-            def _():
-                half_copy(side, c, ou_ref.at[side, c]).wait_send()
-
     for g in range(chunks):
         rank, ahead, behind = ranks(g % 2)
 
@@ -1601,7 +1587,7 @@
         def _():
             for piece in range(per_part):
                 remote(
-                    zfin.at[0],
+                    zin.at[0],
                     oq_ref.at[slot, piece],
                     home_send.at[0],
                     home_recv.at[slot, piece],
@@ -1633,10 +1619,11 @@
             w_out,
             scatter_seq(part_normed, None),
             scatter_seq(part_outputs, None),
-            grad_up,
+            lax.psum(grad_up, "batch"),
         )
     pieces = grad_up.shape[0] // CHUNK
-    turned, chunks = 3 * cols // CHUNK, (3 * cols + rows) // CHUNK
+    turned = 3 * cols // CHUNK
+    chunks = turned + pieces + rows // CHUNK
     inside = pl.BlockSpec(memory_space=pltpu.VMEM)
     dma = pltpu.SemaphoreType.DMA
     line = pltpu.VMEM((chunks, CHUNK, width), BF16)
@@ -1647,7 +1634,7 @@
             jax.ShapeDtypeStruct((rows // CHUNK, CHUNK, width), BF16),
             jax.ShapeDtypeStruct((rows, width), F32),
             jax.ShapeDtypeStruct((rows, width), F32),
-            jax.ShapeDtypeStruct((2, pieces, CHUNK, width), BF16),
+            jax.ShapeDtypeStruct((pieces, CHUNK, width), BF16),
         ),
         in_specs=[ANY] * 5,
         out_specs=(ANY, ANY, inside, inside, ANY),
@@ -1657,8 +1644,7 @@
             pltpu.VMEM((3, 6, rows // 2, width), BF16),
             line,
             line,
-            line,
-            dma((13,)),
+            dma((14,)),
             dma((3, 10)),
             dma((3, 10)),
             dma((chunks,)),
@@ -1668,9 +1654,6 @@
             dma((chunks,)),
             dma((chunks,)),
             dma((3, cols // CHUNK)),
-            dma((pieces,)),
-            dma((2, pieces)),
-            dma((2, pieces)),
         ],
         compiler_params=pltpu.CompilerParams(
             collective_id=collective_id,
@@ -1690,22 +1673,6 @@
         outputs,
         w_up.reshape(-1, width),
     )
-
-
-def half_hop(grad, came, hop):
-    n, depth = lax.axis_size("seq"), lax.axis_size("batch")
-    if n != 8 or depth != 4:
-        return lax.psum(grad, "batch") if hop == 1 else came
-    z = lax.axis_index("batch")
-    rows = grad.shape[0] // 2
-    low, high = grad[:rows], grad[rows:]
-    part = jnp.where(z == hop - 1, low, high)
-    if hop > 1:
-        part = (part.astype(F32) + came.astype(F32)).astype(BF16)
-    if hop == depth:
-        return part
-    pairs = [(hop - 1, hop), (depth - hop, depth - 1 - hop)]
-    return lax.ppermute(part, "batch", pairs)
 
 
 def gains_kernel(
@@ -1860,10 +1827,9 @@
     down_part = lax.psum_scatter(
         grad_w_down.reshape(n, local, feats), "batch", scatter_dimension=1, tiled=True
     )
-    hop_one = half_hop(grad_w_up, None, 1)
+    late = feats // 2
+    grad_up_early = lax.psum(grad_w_up[late:], "batch")
     grad_ffn_in = scatter_seq(nn(grad_upper, w_up).astype(BF16), 4)
-    hop_one, grad_ffn_in = lax.optimization_barrier((hop_one, grad_ffn_in))
-    hop_two = half_hop(grad_w_up, hop_one, 2)
     grad_middle, grad_branch, grad_att, grad_gain_ffn, grad_gain_mix = branch_pass(
         grad_ffn_in, middle, cot, attended, w_out_full, gain_mix, gain_ffn
     )
@@ -1876,16 +1842,14 @@
     dq, dk, dv = attend_back(
         first, start_row, q, k, kt, v, attended_heads, lse, grad_heads, tables
     )
-    hop_two, dq = lax.optimization_barrier((hop_two, dq))
-    hop_three = half_hop(grad_w_up, hop_two, 3)
     grads = jnp.concatenate([dq, dk, dv], axis=1)
     weights = jnp.concatenate([wq, wk, wv], axis=0)
-    grad_w_qkv, grad_w_out, grad_normed, down_sum, grad_w_up = finish(
+    grad_w_qkv, grad_w_out, grad_normed, down_sum, grad_up_late = finish(
         tn(grads, normed_full).astype(BF16),
         tn(grad_branch, mix_in).astype(BF16),
         nn(grads, weights).astype(BF16),
         nt(hidden, w_down_cols).astype(BF16),
-        half_hop(grad_w_up, hop_three, depth),
+        grad_w_up[:late],
         6,
     )
     grad_part, grad_gain_attn = norm_back(grad_normed, normal_attn, scale_attn, gain_attn)
@@ -1902,7 +1866,7 @@
         grad_inputs[None],
         grad_w_qkv.astype(F32),
         grad_w_out.astype(F32),
-        grad_w_up.astype(F32),
+        jnp.concatenate([grad_up_late.astype(F32), grad_up_early.astype(F32)], axis=0),
         grad_w_down.astype(F32),
         shared[:width],
         shared[width : 2 * width],

time: 983 us -> 799 us (0.81)
  waiting for transfers between devices: 119 us -> 0.78 us
  starting transfers between devices: 44.3 us -> 5.01 us
  Pallas kernels: 633 us -> 617 us
  other arithmetic: 48.1 us -> 33.2 us
    ppermute x3 -> x0, waiting for transfers between devices: 113 us -> none  [half_hop(): return lax.ppermute(part, 'batch', pairs)]
    pallas_call x1, Pallas kernels: 96.8 us -> 55.7 us  [gather_seq(): pl.pallas_call(functools.partial(gather_kernel, n, depth), out_shape=(jax...]
    ppermute x3 -> x0, starting transfers between devices: 39.9 us -> none  [half_hop(): return lax.ppermute(part, 'batch', pairs)]
    pallas_call x1, Pallas kernels: 189 us -> 213 us  [finish(): pl.pallas_call(functools.partial(finish_kernel, n, depth), out_shape=(jax...]
    convert_element_type x4 -> x0, other arithmetic: 19 us -> none  [the longest x3 14.2 us: half_hop(): part = (part.astype(F32) + came.astype(F32)).astype(BF16)]
    unnamed x119 -> x103, local copies, waits for them, and re-layouts: 34.5 us -> 35.7 us
  transfers between devices with their start and end apart: 8 -> 6, of which waited for: 3 -> 0; matrix products, arithmetic and copies ran while one was open for 12% -> 13% of each run, Pallas kernels for 60% -> 72%
where the time goes in v2:
time: 799 us; the launch traced here: 792 us
  Pallas kernels  617 us (77%)
  matrix products  77.1 us (10%)
  local copies, waits for them, and re-layouts  44.9 us (6%)
  other arithmetic  33.2 us (4%)
  between operations  14.5 us (2%)
    pallas_call x1, Pallas kernels, finish(): pl.pallas_call(functools.partial(finish_kernel, n, depth), out_shape=(jax...  213 us
    pallas_call x1, Pallas kernels, start_exchange(): pl.pallas_call(functools.partial(start_kernel, n, depth), out_shape=(jax....  113 us
    pallas_call x1, Pallas kernels, gather_seq(): pl.pallas_call(functools.partial(gather_kernel, n, depth), out_shape=(jax...  55.7 us
    dot_general x4, matrix products, tn(): lax.dot_general(a, b, (((0,), (0,)), ((), ())), preferred_element_type=F32)  43 us
    pallas_call x1, Pallas kernels, scatter_seq(): pl.pallas_call(scatter_kernel, out_shape=jax.ShapeDtypeStruct((rows, widt...  40.9 us
    pallas_call x1, Pallas kernels, attend_back(): pl.pallas_call(functools.partial(attend_back_kernel, heads), out_shape=(s...  35.9 us
    unnamed x103, local copies, waits for them, and re-layouts  35.7 us
    pallas_call x1, Pallas kernels, upper_pass(): pl.pallas_call(upper_kernel, grid=(length // rows,), out_shape=(jax.Shape...  28.4 us
  transfers between devices with their start and end apart: 6, of which 0 were waited for; matrix products, arithmetic and copies ran while one was open for 13% of the time, Pallas kernels for 72%

profile of v2, /device:TPU:0, one launch (start us, length us, event | category | flops | bytes accessed | tf_op | source)
XLA Modules:
  0.0 792.5 jit_solution(8361414026303465954)
XLA Ops:
  8.0 1.4 fusion.20
  9.4 1.4 convert_reduce_fusion
  10.9 1.6 fusion.18
  12.5 2.0 compare_select_fusion.2.start_ref
  15.1 1.4 fusion.11.x_ref
  16.5 113.3 %start_exchange.1 = (bf16[8,256,2048]{2,1,0:T(8,128)(2,1)}, bf16[256,2048]{1,0:T(8,128)(2,1)}, bf16[256,2048]{1,0:T(8,128)(2,1)}, bf16[256,2048]{1,0:T(8,128)(2,...) custom-call(bf16[256,2048]{1,0:T(8,128)(2,1)} %fusion.11.x_ref, ...), custom_call_target="tpu_custom_call" | custom-call | tf_op jit(solution)/shard_map/start_exchange/pallas_call | solution.py:473
  131.2 1.2 copy-done.24
  132.4 1.2 copy-done.25
  136.1 1.3 copy-done.28
  137.4 1.4 copy-done.29
  138.8 11.7 %project_qkv.1 = (bf16[2048,256]{1,0:T(8,128)(2,1)S(1)}, bf16[2048,256]{1,0:T(8,128)(2,1)S(1)}, bf16[2048,256]{1,0:T(8,128)(2,1)S(1)}, bf16[256,2048]{1,0:T(8,128)(2,1)S(1)}, bf16[256,2048]{1,0:T(8,128)(2,1)S(1)}) custom-call(bf16[2048,2048]{1,0:T(8,128)(2,1)} %bitcast.88, bf16[256,2048]{1,0:T(8,128)(2,1)S(1)} %copy-done.23, ...), custom_call_target="tpu_custom_call" | custom-call | flops 6442450944 | bytes 16777216 | tf_op jit(solution)/shard_map/project_qkv/pallas_call | solution.py:781
  150.6 25.9 %attend.1 = (bf16[2048,256]{1,0:T(8,128)(2,1)S(1)}, f32[8,4,256]{2,1,0:T(4,128)S(1)}) custom-call(s32[8]{0:T(128)S(1)} %and_select_fusion.first_ref, s32[1,2048]{1,0:T(1,128)S(1)} %compare_select_fusion.2.start_ref, bf16[2048,256]{1,0:T(8,128)(2,1)S(1)} %get-tuple-element.68.q_ref, bf16[2048,256]{1,0:T(8,128)(2,1)S(1)} %get-tuple-element.69.k_ref, ...), custom_call_target="tpu_custom_call" | custom-call | flops 2147483648 | bytes 4194304 | tf_op jit(solution)/shard_map/attend/pallas_call | solution.py:861
  177.5 14.9 %heads_to_tokens.1.att_ref = bf16[256,2048]{1,0:T(8,128)(2,1)} custom-call(bf16[2048,256]{1,0:T(8,128)(2,1)} %copy-done.12), custom_call_target="tpu_custom_call" | custom-call | tf_op jit(solution)/shard_map/heads_to_tokens/pallas_call | solution.py:681
  193.1 3.4 copy-done.1
  197.7 7.4 mix_pass.1
  207.0 55.7 %gather_seq.1 = (bf16[8,256,2048]{2,1,0:T(8,128)(2,1)}, bf16[8,4,64,1024]{3,2,1,0:T(8,128)(2,1)}) custom-call(bf16[256,2048]{1,0:T(8,128)(2,1)} %copy-done.11, bf16[8,4,64,1024]{3,2,1,0:T(8,128)(2,1)} %get-tuple-element.77.near_ref), custom_call_target="tpu_custom_call" | custom-call | tf_op jit(solution)/shard_map/gather_seq/pallas_call | solution.py:295
  262.8 28.4 %upper_pass.1 = (f32[2048,1024]{1,0:T(8,128)}, bf16[2048,1024]{1,0:T(8,128)(2,1)S(1)}, f32[2048,1024]{1,0:T(8,128)}, f32[8,2048]{1,0:T(8,128)S(1)}) custom-call(bf16[2048,2048]{1,0:T(8,128)(2,1)} %bitcast.90, bf16[1024,2048]{1,0:T(8,128)(2,1)} %wu_ref.1, bf16[2048,2048]{1,0:T(8,128)(2,1)} %all-gather.6.cloned.1.call-done.c_ref, bf16[2048,1024]{1,0:T(8,128)(2,1)} %bitcast.92, ...), custom_call_target="tpu_custom_call" | custom-call | flops 17179869184 | bytes 50331648 | tf_op jit(solution)/shard_map/upper_pass/pallas_call | solution.py:1041
  291.2 2.0 copy-done.5
  293.8 10.1 %join_stats.1.stat_ref = f32[8,2048]{1,0:T(8,128)} custom-call(f32[8,2048]{1,0:T(8,128)} %copy-done.16), custom_call_target="tpu_custom_call" | custom-call | tf_op jit(solution)/shard_map/join_stats/pallas_call | solution.py:1152
  304.0 2.2 copy-done.6
  307.0 10.7 %hidden_pass.1 = (bf16[2048,1024]{1,0:T(8,128)(2,1)S(1)}, bf16[2048,1024]{1,0:T(8,128)(2,1)S(1)}, f32[1,1024]{1,0:T(1,128)S(1)}) custom-call(f32[2048,1024]{1,0:T(8,128)} %get-tuple-element.81.act_ref, bf16[2048,1024]{1,0:T(8,128)(2,1)S(1)} %copy-done.6, f32[2048,1024]{1,0:T(8,128)} %get-tuple-element.83.grad_ref, f32[8,2048]{1,0:T(8,128)S(1)} %copy-done.15, ...), custom_call_target="tpu_custom_call" | custom-call | flops 25165824 | bytes 29360128 | tf_op jit(solution)/shard_map/hidden_pass/pallas_call | solution.py:1096
  317.8 11.0 %convolution_convert_fusion.5 = bf16[2048,1024]{1,0:T(8,128)(2,1)} fusion(bf16[2048,2048]{1,0:T(8,128)(2,1)S(1)} %copy-done.48, bf16[2048,1024]{1,0:T(8,128)(2,1)S(1)} %get-tuple-element.86), kind=kOutput, calls=%fused_computation.6 | convolution fusion | flops 8592031744 | bytes 16777216 | tf_op jit(solution)/shard_map/dot_general | solution.py:36
  329.2 12.7 %convolution_convert_fusion.4 = bf16[1024,2048]{1,0:T(8,128)(2,1)S(1)} fusion(bf16[2048,1024]{1,0:T(8,128)(2,1)} %copy-done.20, bf16[2048,2048]{1,0:T(8,128)(2,1)} %bitcast.91), kind=kOutput, calls=%fused_computation.5 | convolution fusion | flops 8592031744 | bytes 16777216 | tf_op jit(solution)/shard_map/dot_general | solution.py:36
  341.9 2.5 fusion.24
  344.4 1.2 copy-done.22
  345.6 1.3 copy-done.49
  346.9 10.9 %convolution_convert_fusion = bf16[2048,2048]{1,0:T(8,128)(2,1)} fusion(bf16[2048,1024]{1,0:T(8,128)(2,1)S(1)} %copy-done.22, bf16[2048,1024]{1,0:T(8,128)(2,1)S(1)} %bitcast.93), kind=kOutput, calls=%fused_computation | convolution fusion | flops 8594128896 | bytes 16777216 | tf_op jit(solution)/shard_map/dot_general | solution.py:32
  357.8 11.9 %convolution_convert_fusion.3 = bf16[2048,2048]{1,0:T(8,128)(2,1)S(1)} fusion(bf16[2048,1024]{1,0:T(8,128)(2,1)} %copy-done.20, bf16[1024,2048]{1,0:T(8,128)(2,1)} %wu_ref.1), kind=kOutput, calls=%fused_computation.3 | convolution fusion | flops 8594128896 | bytes 16777216 | tf_op jit(solution)/shard_map/dot_general | solution.py:28
  369.8 40.9 %scatter_seq.1.g_ref = f32[256,2048]{1,0:T(8,128)S(1)} custom-call(bf16[8,256,2048]{2,1,0:T(8,128)(2,1)S(1)} %bitcast.63), custom_call_target="tpu_custom_call" | custom-call | tf_op jit(solution)/shard_map/scatter_seq/pallas_call | solution.py:605
  410.7 13.6 %branch_pass.1 = (f32[256,2048]{1,0:T(8,128)S(1)}, bf16[256,2048]{1,0:T(8,128)(2,1)S(1)}, bf16[256,2048]{1,0:T(8,128)(2,1)S(1)}, f32[1,2048]{1,0:T(1,128)S(1)}, f32[1,2048]{1,0:T(1,128)S(1)}) custom-call(f32[256,2048]{1,0:T(8,128)S(1)} %scatter_seq.1.g_ref, f32[256,2048]{1,0:T(8,128)S(1)} %get-tuple-element.72.mid_ref, bf16[256,2048]{1,0:T(8,128)(2,1)S(1)} %bitcast.65, ...), custom_call_target="tpu_custom_call" | custom-call | flops 2147483648 | bytes 18874368 | tf_op jit(solution)/shard_map/branch_pass/pallas_call | solution.py:1273
  424.3 1.3 copy-done.7
  427.6 13.7 %tokens_to_heads.1.do_ref = bf16[2048,256]{1,0:T(8,128)(2,1)} custom-call(bf16[256,2048]{1,0:T(8,128)(2,1)} %copy-done.14), custom_call_target="tpu_custom_call" | custom-call | tf_op jit(solution)/shard_map/tokens_to_heads/pallas_call | solution.py:718
  441.3 7.3 convolution_convert_fusion.2
  448.6 4.4 all-to-all-start
  455.5 35.9 %attend_back.1 = (bf16[2048,256]{1,0:T(8,128)(2,1)S(1)}, bf16[2048,256]{1,0:T(8,128)(2,1)S(1)}, bf16[2048,256]{1,0:T(8,128)(2,1)S(1)}) custom-call(s32[8]{0:T(128)S(1)} %and_select_fusion.first_ref, s32[1,2048]{1,0:T(1,128)S(1)} %compare_select_fusion.2.start_ref, bf16[2048,256]{1,0:T(8,128)(2,1)S(1)} %copy-done.31, bf16[2048,256]{1,0:T(8,128)(2,1)S(1)} %copy-done.33, ...), custom_call_target="tpu_custom_call" | custom-call | flops 5368709120 | bytes 8388608 | tf_op jit(solution)/shard_map/attend_back/pallas_call | solution.py:975
  494.5 2.3 copy.22
  496.9 2.3 constant_dynamic-update-slice_fusion
  499.2 11.3 %convolution_convert_fusion.1 = bf16[2048,2048]{1,0:T(8,128)(2,1)} fusion(bf16[2048,768]{1,0:T(8,128)(2,1)} %constant_dynamic-update-slice_fusion, bf16[256,2048]{1,0:T(8,128)(2,1)} %get-tuple-element.63.wv_ref, bf16[256,2048]{1,0:T(8,128)(2,1)} %get-tuple-element.62.wk_ref, bf16[256,2048]{1,0:T(8,128)(2,1)} %get-tuple-element.61.wq_ref), kind=kOutput, calls=%fused_computation.1 | convolution fusion | flops 6456082432 | bytes 14680064 | tf_op jit(solution)/shard_map/dot_general | solution.py:28
  510.5 12.0 %convolution_convert_fusion.6 = bf16[768,2048]{1,0:T(8,128)(2,1)} fusion(bf16[2048,768]{1,0:T(8,128)(2,1)} %constant_dynamic-update-slice_fusion, bf16[2048,2048]{1,0:T(8,128)(2,1)} %bitcast.89), kind=kOutput, calls=%fused_computation.7 | convolution fusion | flops 6444023808 | bytes 14680064 | tf_op jit(solution)/shard_map/dot_general | solution.py:36
  522.4 213.5 %finish.1 = (bf16[3,4,64,2048]{3,2,1,0:T(8,128)(2,1)}, bf16[4,64,2048]{2,1,0:T(8,128)(2,1)}, f32[256,2048]{1,0:T(8,128)}, f32[256,2048]{1,0:T(8,128)}, bf16[8,64,2048]{2,1,0:T(8,128)(2,1)}) custom-call(bf16[12,64,2048]{2,1,0:T(8,128)(2,1)} %bitcast.83, bf16[8,256,2048]{2,1,0:T(8,128)(2,1)} %bitcast.77, bf16[8,256,2048]{2,1,0:T(8,128)(2,1)} %bitcast.79, ...), custom_call_target="tpu_custom_call" | custom-call | tf_op jit(solution)/shard_map/finish/pallas_call | solution.py:1630
  735.9 2.5 fusion.17
  739.0 21.2 %sum_gains.1 = (f32[48,128]{1,0:T(8,128)}, f32[64,128]{1,0:T(8,128)}) custom-call(f32[48,128]{1,0:T(8,128)} %pad_maximum_fusion.a_ref, f32[8,128]{1,0:T(8,128)} %bitcast.76), custom_call_target="tpu_custom_call" | custom-call | tf_op jit(solution)/shard_map/sum_gains/pallas_call | solution.py:1745
  760.3 1.3 slice_bitcast_fusion
  761.6 6.6 maximum_convert_fusion
  768.2 1.6 bitcast_convert_fusion.1
  770.9 4.1 bitcast_convert_fusion
  775.7 2.8 fusion.16
  778.5 6.6 convert_element_type.85
  (118 shorter events, 22.6 us)
Async XLA Ops:
  7.2 5.3 copy-start.43
  7.2 7.9 copy-start
  7.2 7.9 copy-start.40
  7.2 185.8 %all-gather.4.cloned.1.call-start = ((), (), s32[]{:S(2)}) async-start(), calls=%async_computation.2 | async-start | bytes 9437184 | tf_op jit(solution)/shard_map/all_gather | solution.py:1793
  7.9 254.8 %all-gather.6.cloned.1.call-start = ((), (), s32[]{:S(2)}) async-start(), calls=%async_computation.3 | async-start | bytes 9437184 | tf_op jit(solution)/shard_map/all_gather | solution.py:1808
  10.8 118.9 %copy-start.44 = (f32[256]{0:T(256)}, f32[256]{0:T(256)S(1)}, u32[]{:S(2)}) copy-start(f32[256]{0:T(256)S(1)} %broadcast_multiply_fusion.2) | copy-start | bytes 3076
  12.5 117.2 %copy-start.46 = (f32[256]{0:T(256)}, f32[256]{0:T(256)S(1)}, u32[]{:S(2)}) copy-start(f32[256]{0:T(256)S(1)} %add_rsqrt_fusion) | copy-start | bytes 3076
  129.8 318.8 %reduce-scatter.2.cloned.1.call-start = ((), (), s32[]{:S(2)}) async-start(), calls=%async_computation.4 | async-start | bytes 5242880 | tf_op jit(solution)/shard_map/reduce_scatter | solution.py:1827
  129.9 1.2 copy-start.23
  131.2 1.2 copy-start.24
  132.4 1.2 copy-start.25
  133.6 1.2 copy-start.26
  134.8 1.2 copy-start.27
  136.1 1.3 copy-start.28
  137.4 1.4 copy-start.29
  150.5 26.0 %copy-start.30 = (bf16[2048,256]{1,0:T(8,128)(2,1)}, bf16[2048,256]{1,0:T(8,128)(2,1)S(1)}, u32[]{:S(2)}) copy-start(bf16[2048,256]{1,0:T(8,128)(2,1)S(1)} %get-tuple-element.68.q_ref) | copy-start | bytes 3145732
  150.5 26.0 %copy-start.32 = (bf16[2048,256]{1,0:T(8,128)(2,1)}, bf16[2048,256]{1,0:T(8,128)(2,1)S(1)}, u32[]{:S(2)}) copy-start(bf16[2048,256]{1,0:T(8,128)(2,1)S(1)} %get-tuple-element.69.k_ref) | copy-start | bytes 3145732
  150.5 26.0 %copy-start.34 = (bf16[2048,256]{1,0:T(8,128)(2,1)}, bf16[2048,256]{1,0:T(8,128)(2,1)S(1)}, u32[]{:S(2)}) copy-start(bf16[2048,256]{1,0:T(8,128)(2,1)S(1)} %get-tuple-element.74.v_ref) | copy-start | bytes 3145732
  150.5 26.0 %copy-start.35 = (bf16[256,2048]{1,0:T(8,128)(2,1)}, bf16[256,2048]{1,0:T(8,128)(2,1)S(1)}, u32[]{:S(2)}) copy-start(bf16[256,2048]{1,0:T(8,128)(2,1)S(1)} %get-tuple-element.73.kt_ref) | copy-start | bytes 3145732
  150.5 42.5 %copy-start.17 = (f32[2048]{0:T(1024)S(1)}, f32[2048]{0:T(1024)}, u32[]{:S(2)}) copy-start(f32[2048]{0:T(1024)} %param.18) | copy-start | bytes 24580
  150.6 42.5 %copy-start.18 = (f32[2048]{0:T(1024)S(1)}, f32[2048]{0:T(1024)}, u32[]{:S(2)}) copy-start(f32[2048]{0:T(1024)} %param.19) | copy-start | bytes 24580
  193.0 3.4 copy-start.1
  196.4 1.2 copy-start.2
  291.2 2.0 copy-start.5
  304.0 2.2 copy-start.6
  307.0 10.7 %copy-start.48 = (bf16[2048,2048]{1,0:T(8,128)(2,1)S(1)}, bf16[2048,2048]{1,0:T(8,128)(2,1)}, u32[]{:S(2)}) copy-start(bf16[2048,2048]{1,0:T(8,128)(2,1)} %all-gather.6.cloned.1.call-done.c_ref) | copy-start | bytes 25165828
  317.7 11.0 %copy-start.19 = (f32[1,1024]{1,0:T(1,128)}, f32[1,1024]{1,0:T(1,128)S(1)}, u32[]{:S(2)}) copy-start(f32[1,1024]{1,0:T(1,128)S(1)} %get-tuple-element.107) | copy-start | bytes 12292
  317.7 11.0 %copy-start.20 = (bf16[2048,1024]{1,0:T(8,128)(2,1)}, bf16[2048,1024]{1,0:T(8,128)(2,1)S(1)}, u32[]{:S(2)}) copy-start(bf16[2048,1024]{1,0:T(8,128)(2,1)S(1)} %get-tuple-element.89) | copy-start | bytes 12582916
  317.7 11.0 %copy-start.21 = (bf16[2048,1024]{1,0:T(8,128)(2,1)}, bf16[2048,1024]{1,0:T(8,128)(2,1)S(1)}, u32[]{:S(2)}) copy-start(bf16[2048,1024]{1,0:T(8,128)(2,1)S(1)} %get-tuple-element.86) | copy-start | bytes 12582916
  328.8 432.9 %all-reduce.2.cloned.1.call-start = ((), (), s32[]{:S(2)}) async-start(), calls=%async_computation.5 | async-start | bytes 4194304 | tf_op jit(solution)/shard_map/psum | solution.py:1831
  341.9 3.7 copy-start.22
  341.9 5.0 copy-start.49
  369.8 40.9 %copy-start.3 = (bf16[256,2048]{1,0:T(8,128)(2,1)S(1)}, bf16[256,2048]{1,0:T(8,128)(2,1)}, u32[]{:S(2)}) copy-start(bf16[256,2048]{1,0:T(8,128)(2,1)} %heads_to_tokens.1.att_ref) | copy-start | bytes 3145732
  369.8 40.9 %copy-start.4 = (bf16[1,256,2048]{2,1,0:T(8,128)(2,1)S(1)}, bf16[1,256,2048]{2,1,0:T(8,128)(2,1)}, u32[]{:S(2)}) copy-start(bf16[1,256,2048]{2,1,0:T(8,128)(2,1)} %param.21) | copy-start | bytes 3145732
  424.3 1.3 copy-start.7
  448.6 45.9 %all-to-all-start = ((bf16[8,64,1024]{2,1,0:T(8,128)(2,1)}), bf16[8,64,1024]{2,1,0:T(8,128)(2,1)}, u32[]{:S(2)}, u32[]{:S(2)}) async-start(bf16[8,64,1024]{2,1,0:T(8,128)(2,1)} %reduce-scatter.2.cloned.1.call-done), calls=%async_computation.1 | async-start | bytes 2097152 | tf_op jit(solution)/shard_map/all_to_all | solution.py:1838
  453.0 325.5 %all-gather.8.cloned.1.call-start = ((), (), s32[]{:S(2)}) async-start(), calls=%async_computation.6 | async-start | bytes 5242880 | tf_op jit(solution)/shard_map/all_gather | solution.py:1840
  453.1 1.2 copy-start.31
  454.3 1.2 copy-start.33
  522.4 213.5 %copy-start.41 = (f32[2048]{0:T(1024)S(1)}, f32[2048]{0:T(1024)}, u32[]{:S(2)}) copy-start(f32[2048]{0:T(1024)} %param.17) | copy-start | bytes 24580
  522.4 213.5 %copy-start.45 = (f32[256]{0:T(256)S(1)}, f32[256]{0:T(256)}, u32[]{:S(2)}) copy-start(f32[256]{0:T(256)} %copy-done.44) | copy-start | bytes 3076
  522.4 213.5 %copy-start.47 = (f32[256]{0:T(256)S(1)}, f32[256]{0:T(256)}, u32[]{:S(2)}) copy-start(f32[256]{0:T(256)} %copy-done.46) | copy-start | bytes 3076
  761.6 6.6 copy-start.39
  768.2 2.6 copy-start.37
  770.9 4.1 copy-start.8
  770.9 4.1 copy-start.36
  770.9 4.8 copy-start.38
  778.5 6.6 copy-start.42
  (8 other events, 7.3 us)
Sparse Core Ops, SparseCore 0:
  9.9 96.1 all-gather.3
  129.9 62.2 all-gather.5
  328.9 76.1 reduce-scatter.1
  408.0 86.8 all-reduce.1
  497.0 118.9 all-gather.7

commit v3 on v2

--- a/solution.py
+++ b/solution.py
@@ -146,16 +146,14 @@
         pl.semaphore_signal(
             barrier, inc=1, device_id={"seq": lax.rem(me + k, n)}, device_id_type=MESH
         )
-    for sign in (-1, 1):
-
-        @pl.when((z + sign >= 0) & (z + sign < depth))
-        def _():
-            pl.semaphore_signal(
-                barrier, inc=1, device_id={"batch": z + sign}, device_id_type=MESH
-            )
-
-    ends = (z == 0).astype(jnp.int32) + (z == depth - 1).astype(jnp.int32)
-    pl.semaphore_wait(barrier, n + 1 - ends)
+    for k in range(1, depth):
+        pl.semaphore_signal(
+            barrier,
+            inc=1,
+            device_id={"batch": lax.rem(z + k, depth)},
+            device_id_type=MESH,
+        )
+    pl.semaphore_wait(barrier, n + depth - 2)
 
 
 def line_remote(src, dst, send_sem, recv_sem, partner):
@@ -333,14 +331,13 @@
 
 def start_kernel(
     n, depth, x_ref, w_ref, wd_ref, pos_ref,
-    o_ref, wq_ref, wk_ref, wv_ref, wc_ref, cq_ref, sq_ref, ck_ref, sk_ref,
+    o_ref, wt_ref, wc_ref, cq_ref, sq_ref, ck_ref, sk_ref,
     keep_w, keep_c, local_sem, send_sem, recv_sem, hop_send, hop_recv, col_send, col_recv, line_send, line_recv,
 ):
     z = lax.axis_index("batch")
     rows_z = wc_ref.shape[2]
     cols = wc_ref.shape[3]
     me, twin, near_x, near_y, _ = places()
-    parts = (wq_ref, wk_ref, wv_ref)
     own = pltpu.make_async_copy(x_ref, o_ref.at[me], local_sem.at[0])
     own.start()
     wd_rows = pl.ds(pl.multiple_of(z * rows_z, rows_z), rows_z)
@@ -380,14 +377,14 @@
 
     def hop(j, part, target):
         return remote(
-            w_ref.at[j], parts[part], hop_send.at[j], hop_recv.at[part], target
+            w_ref.at[j], wt_ref.at[part], hop_send.at[j], hop_recv.at[part], target
         )
 
     def load(j):
         return pltpu.make_async_copy(w_ref.at[j], keep_w, local_sem.at[6])
 
     def here(j, part):
-        return pltpu.make_async_copy(keep_w, parts[part], local_sem.at[1 + j])
+        return pltpu.make_async_copy(keep_w, wt_ref.at[part], local_sem.at[1 + j])
 
     for j in range(3):
         block = 3 * me + j
@@ -462,26 +459,23 @@
         place = jnp.broadcast_to(positions[:, None], (positions.shape[0], 128))
         return (
             lax.all_gather(block, "seq", axis=0, tiled=True),
-            parts,
+            jnp.concatenate(parts, axis=0),
             lax.all_to_all(w_down, "seq", split_axis=1, concat_axis=0, tiled=True),
             lane_tables(place),
         )
     rows_z, cols = w_down.shape[0] // depth, w_down.shape[1] // n
     inside = pl.BlockSpec(memory_space=pltpu.VMEM)
     table = jax.ShapeDtypeStruct((n * rows, 128), F32)
-    part = jax.ShapeDtypeStruct((piece, width), w.dtype)
-    gathered, wq, wk, wv, columns, *tables = pl.pallas_call(
+    gathered, turned, columns, *tables = pl.pallas_call(
         functools.partial(start_kernel, n, depth),
         out_shape=(
             jax.ShapeDtypeStruct((n, rows, width), block.dtype),
-            part,
-            part,
-            part,
+            jax.ShapeDtypeStruct((3, piece, width), w.dtype),
             jax.ShapeDtypeStruct((n, depth, rows_z, cols), w_down.dtype),
             *([table] * 4),
         ),
         in_specs=[INSIDE, ANY, ANY, INSIDE],
-        out_specs=(ANY, ANY, ANY, ANY, ANY, *([INSIDE] * 4)),
+        out_specs=(ANY, ANY, ANY, *([INSIDE] * 4)),
         scratch_shapes=[
             pltpu.VMEM((piece, width), BF16),
             pltpu.VMEM((rows_z, cols), BF16),
@@ -500,7 +494,12 @@
         ),
         name="start_exchange",
     )(block, w, w_down, positions.reshape(-1, 128))
-    return gathered.reshape(n * rows, width), (wq, wk, wv), columns, tables
+    return (
+        gathered.reshape(n * rows, width),
+        turned.reshape(3 * piece, width),
+        columns,
+        tables,
+    )
 
 
 def scatter_kernel(
@@ -747,32 +746,32 @@
 
 
 def qkv_kernel(
-    x_ref, wq_ref, wk_ref, wv_ref, cq_ref, sq_ref, ck_ref, sk_ref,
+    x_ref, w_ref, cq_ref, sq_ref, ck_ref, sk_ref,
     q_ref, k_ref, v_ref, kt_ref, vt_ref,
 ):
     x = x_ref[...]
     width = q_ref.shape[1]
-    query = nt(x, wq_ref[...])
+    query = nt(x, w_ref[0:width])
     query = query * spread_lanes(cq_ref[...], width) + swap_halves(
         query
     ) * spread_lanes(sq_ref[...], width)
     q_ref[...] = query.astype(BF16) * (HEAD_DIM**-0.5)
-    keys = nt(x, wk_ref[...])
+    keys = nt(x, w_ref[width : 2 * width])
     keys = keys * spread_lanes(ck_ref[...], width) + swap_halves(
         keys
     ) * spread_lanes(sk_ref[...], width)
     k_ref[...] = keys.astype(BF16)
     kt_ref[...] = keys.T.astype(BF16)
-    values = nt(x, wv_ref[...])
+    values = nt(x, w_ref[2 * width :])
     v_ref[...] = values.astype(BF16)
     vt_ref[...] = values.T.astype(BF16)
 
 
-def project_qkv(x, wq, wk, wv, tables):
+def project_qkv(x, w, tables):
     length, width = x.shape
-    cols = wq.shape[0]
+    cols = w.shape[0] // 3
     steps = length // TILE
-    weight = pl.BlockSpec((cols, width), lambda i: (0, 0))
+    weight = pl.BlockSpec((3 * cols, width), lambda i: (0, 0))
     table = pl.BlockSpec((TILE, tables[0].shape[1]), lambda i: (i, 0))
     row_out = pl.BlockSpec((TILE, cols), lambda i: (i, 0))
     col_out = pl.BlockSpec((cols, TILE), lambda i: (0, i))
@@ -783,7 +782,7 @@
         grid=(steps,),
         out_shape=(rows, rows, rows, columns, columns),
         in_specs=[pl.BlockSpec((TILE, width), lambda i: (i, 0))]
-        + [weight] * 3
+        + [weight]
         + [table] * 4,
         out_specs=(row_out, row_out, row_out, col_out, col_out),
         compiler_params=pltpu.CompilerParams(vmem_limit_bytes=40 * 1024 * 1024),
@@ -793,7 +792,7 @@
             transcendentals=0,
         ),
         name="project_qkv",
-    )(x, wq, wk, wv, *tables)
+    )(x, w, *tables)
 
 
 def pair_mask(start_row, i, j):
@@ -895,7 +894,7 @@
 
 def attend_back_kernel(
     heads, first_ref, start_ref, q_ref, k_ref, kt_ref, v_ref, o_ref, lse_ref, do_ref,
-    cq_ref, sq_ref, ck_ref, sk_ref, dq_ref, dk_ref, dv_ref, dqt, dk_sum, dv_sum,
+    cq_ref, sq_ref, ck_ref, sk_ref, grad_ref, dqt, dk_sum, dv_sum,
 ):
     i = pl.program_id(0)
     steps = pl.num_programs(0)
@@ -951,7 +950,7 @@
         return (grad * cosine - swap_halves(grad) * sine).astype(BF16)
 
     rows = pl.ds(pl.multiple_of(i * TILE, TILE), TILE)
-    dq_ref[...] = unturn(
+    grad_ref[rows, 0:width] = unturn(
         dqt[...].T * (HEAD_DIM**-0.5), cq_ref[rows, :], sq_ref[rows, :]
     )
 
@@ -960,8 +959,10 @@
         @pl.loop(0, steps)
         def _(j):
             at = pl.ds(pl.multiple_of(j * TILE, TILE), TILE)
-            dk_ref[at] = unturn(dk_sum[at], ck_ref[at, :], sk_ref[at, :])
-            dv_ref[at] = dv_sum[at].astype(BF16)
+            grad_ref[at, width : 2 * width] = unturn(
+                dk_sum[at], ck_ref[at, :], sk_ref[at, :]
+            )
+            grad_ref[at, 2 * width :] = dv_sum[at].astype(BF16)
 
 
 def attend_back(first, start, q, k, kt, v, o, lse, do, tables):
@@ -971,10 +972,9 @@
     row = pl.BlockSpec((TILE, cols), lambda i, *_: (i, 0))
     whole = pl.BlockSpec((length, cols), lambda i, *_: (0, 0))
     table = pl.BlockSpec((length, tables[0].shape[1]), lambda i, *_: (0, 0))
-    shape = jax.ShapeDtypeStruct((length, cols), BF16)
     return pl.pallas_call(
         functools.partial(attend_back_kernel, heads),
-        out_shape=(shape, shape, shape),
+        out_shape=jax.ShapeDtypeStruct((length, 3 * cols), BF16),
         grid_spec=pltpu.PrefetchScalarGridSpec(
             num_scalar_prefetch=1,
             grid=(steps,),
@@ -989,7 +989,7 @@
                 row,
             ]
             + [table] * 4,
-            out_specs=(row, whole, whole),
+            out_specs=pl.BlockSpec((length, 3 * cols), lambda i, *_: (0, 0)),
             scratch_shapes=[
                 pltpu.VMEM((cols, TILE), F32),
                 pltpu.VMEM((length, cols), F32),
@@ -1295,33 +1295,48 @@
     )(grad_ffn_in, middle, cot, attended, w_out, gain_mix[None], gain_ffn[None])
 
 
+CHUNK = 128
+
+
 def finish_kernel(
-    n, depth, gq_ref, pw_ref, pn_ref, po_ref, gu_ref, oq_ref, ow_ref, sn_ref, so_ref, ou_ref,
-    own, twin_in, held, zown, zin,
-    local_sem, send_sem, recv_sem, keep_sem,
-    up_send, up_recv, down_send, down_recv, home_send, home_recv,
+    n, depth, gq_ref, gd_ref, pw_ref, pn_ref, po_ref, x_ref, grad_ref, mid_ref, ga_ref, gm_ref, gf_ref, gh_ref,
+    oq_ref, od_ref, ow_ref, gi_ref, out_ref, sums_ref,
+    own, twin_in, held, zown, zin, gain_here, gain_row, gain_pack, gain_line,
+    local_sem, load_sem, send_sem, recv_sem, keep_sem,
+    up_send, up_recv, down_send, down_recv, home_send, home_recv, gain_send, gain_recv,
 ):
     me, twin, near_x, near_y, across = places()
     z = lax.axis_index("batch")
-    rows = pn_ref.shape[1]
+    rows, width = pn_ref.shape[1:]
     half = rows // 2
     low, high = pl.ds(0, half), pl.ds(half, half)
     mine = (across, near_x, near_y, me)
-    chunk = zown.shape[1]
-    turned = gq_ref.shape[0]
-    upper = turned + gu_ref.shape[0]
+    _, chunk, cols = zown.shape
+    across_width = width // cols
+    per_part = (gq_ref.shape[1] // chunk) * across_width
+    turned = gq_ref.shape[0] * per_part
+    outer = turned + (rows // chunk) * across_width
+    per_source = gd_ref.shape[1] // chunk
     chunks = zown.shape[0]
-    per_part = turned // 3
     per_side = chunks // 2
 
-    load_q = pltpu.make_async_copy(
-        gq_ref, zown.at[pl.ds(0, turned)], local_sem.at[12]
-    )
-    load_u = pltpu.make_async_copy(
-        gu_ref, zown.at[pl.ds(turned, upper - turned)], local_sem.at[13]
-    )
-    load_q.start()
-    load_u.start()
+    def cut(i, size):
+        return pl.ds(pl.multiple_of(i * size, size), size)
+
+    def wide(i):
+        return cut(i // across_width, chunk), cut(lax.rem(i, across_width), cols)
+
+    line_loads = []
+    for g in range(turned):
+        source = gq_ref.at[(g // per_part, *wide(g % per_part))]
+        line_loads.append(pltpu.make_async_copy(source, zown.at[g], load_sem.at[g]))
+    for g in range(outer, chunks):
+        source = gd_ref.at[
+            (g - outer) // per_source, cut((g - outer) % per_source, chunk)
+        ]
+        line_loads.append(pltpu.make_async_copy(source, zown.at[g], load_sem.at[g]))
+    for load in line_loads:
+        load.start()
     partials = (pw_ref, pn_ref, po_ref)
     loads = [
         [
@@ -1366,7 +1381,7 @@
 
         @pl.loop(0, rows // STEP)
         def _(r):
-            at = pl.ds(pl.multiple_of(r * STEP, STEP), STEP)
+            at = cut(r, STEP)
             own[m, i, at] = (
                 own[m, i, at].astype(F32) + twin_in[m, i, at].astype(F32)
             ).astype(BF16)
@@ -1374,7 +1389,7 @@
     def add_held(m, i, base, slot):
         @pl.loop(0, half // STEP)
         def _(r):
-            at = pl.ds(pl.multiple_of(r * STEP, STEP), STEP)
+            at = cut(r, STEP)
             to = pl.ds(pl.multiple_of(base + r * STEP, STEP), STEP)
             own[m, i, to] = (
                 own[m, i, to].astype(F32) + held[m, slot, at].astype(F32)
@@ -1406,28 +1421,34 @@
 
             @pl.loop(0, half // STEP)
             def _(r):
-                at = pl.ds(pl.multiple_of(r * STEP, STEP), STEP)
+                at = cut(r, STEP)
                 place = base + r * STEP
                 to = pl.ds(pl.multiple_of(place, STEP), STEP)
                 store(
                     place,
+                    to,
                     own[m, 3, to].astype(F32)
                     + twin_in[m, 3, to].astype(F32)
                     + held[m, one, at].astype(F32)
                     + held[m, two, at].astype(F32),
                 )
 
-    def store_line(place, value):
-        zown[
-            upper + place // chunk,
-            pl.ds(pl.multiple_of(lax.rem(place, chunk), STEP), STEP),
-        ] = value.astype(BF16)
-
-    def store_into(ref):
-        def store(place, value):
-            ref[pl.ds(pl.multiple_of(place, STEP), STEP)] = value
-
-        return store
+    def store_line(place, to, value):
+        value = value.astype(BF16)
+        for side in range(across_width):
+            zown[
+                turned + (place // chunk) * across_width + side,
+                pl.ds(pl.multiple_of(lax.rem(place, chunk), STEP), STEP),
+            ] = value[:, side * cols : (side + 1) * cols]
+
+    def store_inputs(place, to, value):
+        normal, scale = norm_parts(x_ref[to].astype(F32))
+        part, gain_part = norm_back(value, normal, scale, ga_ref[...])
+        gi_ref[to] = grad_ref[to] + part
+        gain_here[0:1] = gain_here[0:1] + gain_part[None]
+
+    def store_outputs(place, to, value):
+        out_ref[to] = (mid_ref[to] + value).astype(BF16)
 
     def home(part):
         block = part * n + me
@@ -1438,7 +1459,7 @@
         piece = lax.rem(g, per_part)
         return remote(
             zin.at[g],
-            oq_ref.at[slot, piece],
+            oq_ref.at[(slot, *wide(piece))],
             home_send.at[g],
             home_recv.at[slot, piece],
             target,
@@ -1447,14 +1468,18 @@
     def deliver_near(g):
         _, slot = home(g // per_part)
         return pltpu.make_async_copy(
-            zin.at[g], oq_ref.at[slot, lax.rem(g, per_part)], keep_sem.at[g]
+            zin.at[g], oq_ref.at[(slot, *wide(lax.rem(g, per_part)))], keep_sem.at[g]
         )
 
-    def deliver_up(g):
-        return pltpu.make_async_copy(zin.at[g], ou_ref.at[g - turned], keep_sem.at[g])
-
     def deliver_out(g):
-        return pltpu.make_async_copy(zin.at[g], ow_ref.at[g - upper], keep_sem.at[g])
+        return pltpu.make_async_copy(
+            zin.at[g], ow_ref.at[wide(g - turned)], keep_sem.at[g]
+        )
+
+    def deliver_down(g):
+        at = g - outer
+        place = cut(lax.rem(at, per_source), chunk), cut(at // per_source, cols)
+        return pltpu.make_async_copy(zin.at[g], od_ref.at[place], keep_sem.at[g])
 
     def deliver(g, wait):
         target, _ = home(g // per_part)
@@ -1467,13 +1492,13 @@
         def _():
             deliver_near(g).wait() if wait else deliver_near(g).start()
 
-        @pl.when((g >= turned) & (g < upper))
-        def _():
-            deliver_up(g).wait() if wait else deliver_up(g).start()
-
-        @pl.when(g >= upper)
+        @pl.when((g >= turned) & (g < outer))
         def _():
             deliver_out(g).wait() if wait else deliver_out(g).start()
+
+        @pl.when(g >= outer)
+        def _():
+            deliver_down(g).wait() if wait else deliver_down(g).start()
 
     def go_up(g, ahead):
         return line_remote(zown.at[g], zin.at[g], up_send.at[g], up_recv.at[g], ahead)
@@ -1491,7 +1516,7 @@
     def add_line(g, target):
         @pl.loop(0, chunk // STEP)
         def _(r):
-            at = pl.ds(pl.multiple_of(r * STEP, STEP), STEP)
+            at = cut(r, STEP)
             target[g, at] = (zown[g, at].astype(F32) + zin[g, at].astype(F32)).astype(
                 BF16
             )
@@ -1536,9 +1561,10 @@
             def _():
                 deliver(g_back, False)
 
+    gain_here[...] = jnp.zeros_like(gain_here)
     first(0)
-    load_q.wait()
-    load_u.wait()
+    for load in line_loads:
+        load.wait()
     line_step(0)
     line_step(1)
     first(1)
@@ -1554,15 +1580,60 @@
     second(1)
     for t in (9, 10):
         line_step(t)
-    last(1, store_into(sn_ref))
-    for t in (11, 12, 13):
+    last(1, store_inputs)
+
+    gain_here[1:2] = gm_ref[...]
+    gain_here[2:3] = gf_ref[...]
+    gain_here[3:4, 0 : gh_ref.shape[1]] = gh_ref[...]
+    gain_row[me] = gain_here[...]
+    rounds = [
+        remote(
+            gain_here,
+            gain_row.at[me],
+            gain_send.at[0, k],
+            gain_recv.at[0, k],
+            lax.rem(me + k, n),
+        )
+        for k in range(1, n)
+    ]
+    for send in rounds:
+        send.start()
+    for t in (11, 12):
         line_step(t)
     second(2)
-    steps = per_side + 2 * (depth - 1)
-    for t in range(14, steps - 1):
+    for t in (13, 14):
         line_step(t)
-    last(2, store_into(so_ref))
-    line_step(steps - 1)
+    last(2, store_outputs)
+    line_step(15)
+    for send in rounds:
+        send.wait()
+    total = gain_row[0]
+    for d in range(1, n):
+        total = total + gain_row[d]
+    gain_pack[0:8] = total
+    for d in range(n):
+        gain_pack[8 + d : 9 + d] = gain_row[d, 3:4]
+    gain_line[z] = gain_pack[...]
+    rounds = [
+        line_remote(
+            gain_pack,
+            gain_line.at[z],
+            gain_send.at[1, k],
+            gain_recv.at[1, k],
+            lax.rem(z + k, depth),
+        )
+        for k in range(1, depth)
+    ]
+    for send in rounds:
+        send.start()
+    for t in range(16, per_side + 2 * (depth - 1)):
+        line_step(t)
+    for send in rounds:
+        send.wait()
+    total = gain_line[0]
+    for d in range(1, depth):
+        total = total + gain_line[d]
+    sums_ref[...] = total
 
     for m in range(3):
         for send in twins[m] + sends[m]:
@@ -1588,23 +1659,23 @@
             for piece in range(per_part):
                 remote(
                     zin.at[0],
-                    oq_ref.at[slot, piece],
+                    oq_ref.at[(slot, *wide(piece))],
                     home_send.at[0],
                     home_recv.at[slot, piece],
                     source,
                 ).wait_recv()
 
 
-CHUNK = 64
-
-
-def finish(grad_qkv, part_out, part_normed, part_outputs, grad_up, collective_id):
+def finish(
+    grad_qkv, grad_down, part_out, part_normed, part_outputs, x, grad_middle, middle, gain, gains, collective_id
+):
     n, depth = lax.axis_size("seq"), lax.axis_size("batch")
     rows, width = part_out.shape[0] // n, part_out.shape[1]
-    cols = grad_qkv.shape[0] // 3
+    cols = grad_qkv.shape[1]
+    sources, _, feats = grad_down.shape
     if n != 8 or depth != 4:
         me = lax.axis_index("seq")
-        blocks = lax.psum(grad_qkv, "batch").reshape(3, cols, width)
+        blocks = lax.psum(grad_qkv, "batch")
         back = [
             lax.ppermute(
                 give_part(blocks, me, n, j),
@@ -1614,37 +1685,48 @@
             for j in range(3)
         ]
         w_out = lax.psum(scatter_seq(part_out, None).astype(BF16), "batch")
+        normal, scale = norm_parts(x.astype(F32))
+        part, gain_part = norm_back(scatter_seq(part_normed, None), normal, scale, gain)
+        shared = [lax.psum(g, ("batch", "seq")) for g in (gain_part, gains[0][0], gains[1][0])]
+        hidden = lax.all_gather(lax.psum(gains[2][0], "batch"), "seq", axis=0, tiled=True)
+        down = lax.psum(grad_down, "batch")
         return (
             jnp.concatenate(back, axis=0),
+            jnp.swapaxes(down, 0, 1).reshape(rows, sources * feats),
             w_out,
-            scatter_seq(part_normed, None),
-            scatter_seq(part_outputs, None),
-            lax.psum(grad_up, "batch"),
+            grad_middle + part,
+            (middle + scatter_seq(part_outputs, None)).astype(BF16),
+            (*shared, hidden),
         )
-    pieces = grad_up.shape[0] // CHUNK
-    turned = 3 * cols // CHUNK
-    chunks = turned + pieces + rows // CHUNK
-    inside = pl.BlockSpec(memory_space=pltpu.VMEM)
+    chunks = (
+        3 * cols * width + rows * width + sources * rows * feats
+    ) // (CHUNK * feats)
     dma = pltpu.SemaphoreType.DMA
-    line = pltpu.VMEM((chunks, CHUNK, width), BF16)
-    w_qkv, w_out, normed, outputs, w_up = pl.pallas_call(
+    line = pltpu.VMEM((chunks, CHUNK, feats), BF16)
+    w_qkv, w_down, w_out, grad_inputs, outputs, sums = pl.pallas_call(
         functools.partial(finish_kernel, n, depth),
         out_shape=(
-            jax.ShapeDtypeStruct((3, cols // CHUNK, CHUNK, width), BF16),
-            jax.ShapeDtypeStruct((rows // CHUNK, CHUNK, width), BF16),
+            jax.ShapeDtypeStruct((3, cols, width), BF16),
+            jax.ShapeDtypeStruct((rows, sources * feats), BF16),
+            jax.ShapeDtypeStruct((rows, width), BF16),
             jax.ShapeDtypeStruct((rows, width), F32),
-            jax.ShapeDtypeStruct((rows, width), F32),
-            jax.ShapeDtypeStruct((pieces, CHUNK, width), BF16),
-        ),
-        in_specs=[ANY] * 5,
-        out_specs=(ANY, ANY, inside, inside, ANY),
+            jax.ShapeDtypeStruct((rows, width), BF16),
+            jax.ShapeDtypeStruct((16, width), F32),
+        ),
+        in_specs=[ANY] * 5 + [INSIDE] * 7,
+        out_specs=(ANY, ANY, ANY, INSIDE, INSIDE, INSIDE),
         scratch_shapes=[
             pltpu.VMEM((3, 4, rows, width), BF16),
             pltpu.VMEM((3, 4, rows, width), BF16),
             pltpu.VMEM((3, 6, rows // 2, width), BF16),
             line,
             line,
-            dma((14,)),
+            pltpu.VMEM((8, width), F32),
+            pltpu.VMEM((n, 8, width), F32),
+            pltpu.VMEM((16, width), F32),
+            pltpu.VMEM((depth, 16, width), F32),
+            dma((12,)),
+            dma((chunks,)),
             dma((3, 10)),
             dma((3, 10)),
             dma((chunks,)),
@@ -1653,118 +1735,34 @@
             dma((chunks,)),
             dma((chunks,)),
             dma((chunks,)),
-            dma((3, cols // CHUNK)),
+            dma((3, cols * width // (CHUNK * feats))),
+            dma((2, n)),
+            dma((2, n)),
         ],
         compiler_params=pltpu.CompilerParams(
             collective_id=collective_id,
             has_side_effects=True,
-            vmem_limit_bytes=58 * 1024 * 1024,
+            vmem_limit_bytes=60 * 1024 * 1024,
         ),
         name="finish",
     )(
-        grad_qkv.reshape(turned, CHUNK, width),
+        grad_qkv,
+        grad_down,
         *[p.reshape(n, rows, width) for p in (part_out, part_normed, part_outputs)],
-        grad_up.reshape(pieces, CHUNK, width),
+        x,
+        grad_middle,
+        middle,
+        gain[None],
+        *gains,
     )
     return (
         w_qkv.reshape(3 * cols, width),
-        w_out.reshape(rows, width),
-        normed,
+        w_down,
+        w_out,
+        grad_inputs,
         outputs,
-        w_up.reshape(-1, width),
+        (sums[0], sums[1], sums[2], sums[8:, :feats].reshape(-1)),
     )
-
-
-def gains_kernel(
-    n, depth, a_ref, b_ref, oa_ref, ob_ref, held_a, held_b, pack, held_c, send_sem, recv_sem, last_send, last_recv
-):
-    me = lax.axis_index("seq")
-    z = lax.axis_index("batch")
-    p, q = a_ref.shape[0], b_ref.shape[0]
-    barrier = pltpu.get_barrier_semaphore()
-    for k in range(1, n):
-        pl.semaphore_signal(
-            barrier, inc=1, device_id={"seq": lax.rem(me + k, n)}, device_id_type=MESH
-        )
-    for k in range(1, depth):
-        pl.semaphore_signal(
-            barrier,
-            inc=1,
-            device_id={"batch": lax.rem(z + k, depth)},
-            device_id_type=MESH,
-        )
-    pl.semaphore_wait(barrier, n + depth - 2)
-    held_a[me] = a_ref[...]
-    held_b[me] = b_ref[...]
-    copies = []
-    for k in range(1, n):
-        partner = lax.rem(me + k, n)
-        copies.append(
-            remote(a_ref, held_a.at[me], send_sem.at[0, k], recv_sem.at[0, k], partner)
-        )
-        copies.append(
-            remote(b_ref, held_b.at[me], send_sem.at[1, k], recv_sem.at[1, k], partner)
-        )
-    for copy in copies:
-        copy.start()
-    for copy in copies:
-        copy.wait()
-    total = held_a[0]
-    for d in range(1, n):
-        total = total + held_a[d]
-    pack[0:p] = total
-    for d in range(n):
-        pack[p + d * q : p + (d + 1) * q] = held_b[d]
-    held_c[z] = pack[...]
-    copies = [
-        pltpu.make_async_remote_copy(
-            src_ref=pack,
-            dst_ref=held_c.at[z],
-            send_sem=last_send.at[k],
-            recv_sem=last_recv.at[k],
-            device_id={"batch": lax.rem(z + k, depth)},
-            device_id_type=MESH,
-        )
-        for k in range(1, depth)
-    ]
-    for copy in copies:
-        copy.start()
-    for copy in copies:
-        copy.wait()
-    total = held_c[0]
-    for d in range(1, depth):
-        total = total + held_c[d]
-    oa_ref[...] = total[0:p]
-    ob_ref[...] = total[p:]
-
-
-def sum_gains(shared, mine, collective_id):
-    n, depth = lax.axis_size("seq"), lax.axis_size("batch")
-    p, q = shared.shape[0], mine.shape[0]
-    inside = pl.BlockSpec(memory_space=pltpu.VMEM)
-    return pl.pallas_call(
-        functools.partial(gains_kernel, n, depth),
-        out_shape=(
-            jax.ShapeDtypeStruct((p, 128), F32),
-            jax.ShapeDtypeStruct((n * q, 128), F32),
-        ),
-        in_specs=[inside, inside],
-        out_specs=(inside, inside),
-        scratch_shapes=[
-            pltpu.VMEM((n, p, 128), F32),
-            pltpu.VMEM((n, q, 128), F32),
-            pltpu.VMEM((p + n * q, 128), F32),
-            pltpu.VMEM((depth, p + n * q, 128), F32),
-            pltpu.SemaphoreType.DMA((2, n)),
-            pltpu.SemaphoreType.DMA((2, n)),
-            pltpu.SemaphoreType.DMA((depth,)),
-            pltpu.SemaphoreType.DMA((depth,)),
-        ],
-        compiler_params=pltpu.CompilerParams(
-            collective_id=collective_id, has_side_effects=True
-        ),
-        name="sum_gains",
-    )(shared, mine)
 
 
 def body(
@@ -1791,8 +1789,7 @@
     segment = segment_ids[0]
 
     w_out_full = lax.all_gather(w_out, "seq", axis=0, tiled=True)
-    normal_attn, scale_attn = norm_parts(x)
-    normed = (normal_attn * gain_attn).astype(BF16)
+    normed = (norm_parts(x)[0] * gain_attn).astype(BF16)
     before = [jnp.sum((segment < d).astype(jnp.int32)) for d in range(1, DOCS)]
     start = jnp.zeros_like(segment)
     for d in range(1, DOCS):
@@ -1801,13 +1798,13 @@
     first = start[::TILE] // TILE
     start_row = start[None, :]
 
-    normed_full, (wq, wk, wv), w_down_near, tables = start_exchange(
+    normed_full, w_heads, w_down_near, tables = start_exchange(
         normed, w_qkv, w_down, positions.astype(F32), 1
     )
-    cot_late, _ = lax.optimization_barrier((cot, wq))
+    cot_late, _ = lax.optimization_barrier((cot, w_heads))
     cot_full = lax.all_gather(cot_late, "seq", axis=0, tiled=True)
 
-    q, k, v, kt, vt = project_qkv(normed_full, wq, wk, wv, tables)
+    q, k, v, kt, vt = project_qkv(normed_full, w_heads, tables)
     attended_heads, lse = attend(first, start_row, q, k, vt)
     attended = heads_to_tokens(attended_heads, 2)
     mix_in, middle, ffn_in = mix_pass(attended, x_low, w_out_full, gain_mix, gain_ffn)
@@ -1820,58 +1817,42 @@
     stats = join_stats(stat, feats, 8)
     hidden, grad_upper, grad_gain_here = hidden_pass(act, slope, grad_hidden, stats, gain_here)
 
-    grad_w_down = tn(cot_full, hidden).astype(BF16)
-    grad_upper, grad_w_down = lax.optimization_barrier((grad_upper, grad_w_down))
     grad_w_up = tn(grad_upper, ffn_full).astype(BF16)
     grad_upper, grad_w_up = lax.optimization_barrier((grad_upper, grad_w_up))
-    down_part = lax.psum_scatter(
-        grad_w_down.reshape(n, local, feats), "batch", scatter_dimension=1, tiled=True
-    )
-    late = feats // 2
-    grad_up_early = lax.psum(grad_w_up[late:], "batch")
+    grad_w_up = lax.psum(grad_w_up, "batch")
+    grad_w_down = tn(cot_full, hidden).astype(BF16).reshape(n, local, feats)
+    grad_upper, grad_w_down = lax.optimization_barrier((grad_upper, grad_w_down))
     grad_ffn_in = scatter_seq(nn(grad_upper, w_up).astype(BF16), 4)
     grad_middle, grad_branch, grad_att, grad_gain_ffn, grad_gain_mix = branch_pass(
         grad_ffn_in, middle, cot, attended, w_out_full, gain_mix, gain_ffn
     )
     grad_heads = tokens_to_heads(grad_att, 5)
-    down_part, grad_heads = lax.optimization_barrier((down_part, grad_heads))
-    down_part = lax.all_to_all(down_part, "seq", split_axis=0, concat_axis=0, tiled=True)
-    down_part = jnp.swapaxes(down_part, 0, 1).reshape(local // depth, n * feats)
-    grad_w_down = lax.all_gather(down_part, "batch", axis=0, tiled=True)
-
-    dq, dk, dv = attend_back(
+    grad_w_down, grad_heads = lax.optimization_barrier((grad_w_down, grad_heads))
+    grad_w_down = lax.all_to_all(grad_w_down, "seq", split_axis=0, concat_axis=0, tiled=True)
+    grads = attend_back(
         first, start_row, q, k, kt, v, attended_heads, lse, grad_heads, tables
     )
-    grads = jnp.concatenate([dq, dk, dv], axis=1)
-    weights = jnp.concatenate([wq, wk, wv], axis=0)
-    grad_w_qkv, grad_w_out, grad_normed, down_sum, grad_up_late = finish(
-        tn(grads, normed_full).astype(BF16),
+    grad_w_qkv, grad_w_down, grad_w_out, grad_inputs, outputs, gains = finish(
+        tn(grads, normed_full).astype(BF16).reshape(3, -1, width),
+        grad_w_down,
         tn(grad_branch, mix_in).astype(BF16),
-        nn(grads, weights).astype(BF16),
+        nn(grads, w_heads).astype(BF16),
         nt(hidden, w_down_cols).astype(BF16),
-        grad_w_up[:late],
+        x_low,
+        grad_middle,
+        middle,
+        gain_attn,
+        (grad_gain_mix, grad_gain_ffn, grad_gain_here),
         6,
     )
-    grad_part, grad_gain_attn = norm_back(grad_normed, normal_attn, scale_attn, gain_attn)
-    grad_inputs = grad_middle + grad_part
-    outputs = (middle + down_sum).astype(BF16)
-    shared, hidden_gains = sum_gains(
-        jnp.concatenate([grad_gain_attn, grad_gain_mix[0], grad_gain_ffn[0]]).reshape(-1, 128),
-        grad_gain_here.reshape(-1, 128),
-        9,
-    )
-    shared = shared.reshape(-1)
     return (
         outputs[None],
         grad_inputs[None],
         grad_w_qkv.astype(F32),
         grad_w_out.astype(F32),
-        jnp.concatenate([grad_up_late.astype(F32), grad_up_early.astype(F32)], axis=0),
+        grad_w_up.astype(F32),
         grad_w_down.astype(F32),
-        shared[:width],
-        shared[width : 2 * width],
-        shared[2 * width :],
-        hidden_gains.reshape(-1),
+        *gains,
     )
 
 

time: 799 us -> 820 us (1.026)
  the two profiles are of different devices: /device:TPU:0 before, /device:TPU:26 now
where the time goes in v3:
time: 820 us; the launch traced here: 808 us
  Pallas kernels  645 us (79%)
  matrix products  73.3 us (9%)
  local copies, waits for them, and re-layouts  37.9 us (5%)
  other arithmetic  30.4 us (4%)
  between operations  14.4 us (2%)
    pallas_call x1, Pallas kernels, finish(): pl.pallas_call(functools.partial(finish_kernel, n, depth), out_shape=(jax...  265 us
    pallas_call x1, Pallas kernels, start_exchange(): pl.pallas_call(functools.partial(start_kernel, n, depth), out_shape=(jax....  110 us
    pallas_call x1, Pallas kernels, gather_seq(): pl.pallas_call(functools.partial(gather_kernel, n, depth), out_shape=(jax...  54.4 us
    pallas_call x1, Pallas kernels, scatter_seq(): pl.pallas_call(scatter_kernel, out_shape=jax.ShapeDtypeStruct((rows, widt...  40.6 us
    dot_general x4, matrix products, tn(): lax.dot_general(a, b, (((0,), (0,)), ((), ())), preferred_element_type=F32)  39.2 us
    pallas_call x1, Pallas kernels, attend_back(): pl.pallas_call(functools.partial(attend_back_kernel, heads), out_shape=ja...  36.5 us
    unnamed x98, local copies, waits for them, and re-layouts  35.5 us
    pallas_call x1, Pallas kernels, upper_pass(): pl.pallas_call(upper_kernel, grid=(length // rows,), out_shape=(jax.Shape...  28.4 us
  transfers between devices with their start and end apart: 4, of which 0 were waited for; matrix products, arithmetic and copies ran while one was open for 9% of the time, Pallas kernels for 74%

profile of v3, /device:TPU:26, one launch (start us, length us, event | category | flops | bytes accessed | tf_op | source)
XLA Modules:
  0.0 807.8 jit_solution(7188655673983787965)
XLA Ops:
  8.0 1.4 fusion.5
  9.4 1.4 convert_reduce_fusion
  10.8 1.6 fusion.2
  12.5 2.7 compare_select_fusion.2.start_ref
  15.7 2.6 fusion.4.x_ref
  18.3 110.2 %start_exchange.1 = (bf16[8,256,2048]{2,1,0:T(8,128)(2,1)}, bf16[3,256,2048]{2,1,0:T(8,128)(2,1)}, bf16[8,4,64,1024]{3,2,1,0:T(8,128)(2,1)}, f32[2048,128]{1,0:T...) custom-call(bf16[256,2048]{1,0:T(8,128)(2,1)} %fusion.4.x_ref, ...), custom_call_target="tpu_custom_call" | custom-call | tf_op jit(solution)/shard_map/start_exchange/pallas_call | solution.py:469
  128.7 1.9 copy-done.25
  130.6 1.2 copy-done.27
  131.8 1.2 copy-done.28
  133.0 1.2 copy-done.29
  134.3 1.2 copy-done.30
  135.5 11.8 %project_qkv.1 = (bf16[2048,256]{1,0:T(8,128)(2,1)S(1)}, bf16[2048,256]{1,0:T(8,128)(2,1)S(1)}, bf16[2048,256]{1,0:T(8,128)(2,1)S(1)}, bf16[256,2048]{1,0:T(8,128)(2,1)S(1)}, bf16[256,2048]{1,0:T(8,128)(2,1)S(1)}) custom-call(bf16[2048,2048]{1,0:T(8,128)(2,1)} %bitcast.77, bf16[768,2048]{1,0:T(8,128)(2,1)S(1)} %bitcast.62, f32[2048,128]{1,0:T(8,128)S(1)} %copy-done.27, ...), custom_call_target="tpu_custom_call" | custom-call | flops 6442450944 | bytes 16777216 | tf_op jit(solution)/shard_map/project_qkv/pallas_call | solution.py:780
  147.4 25.9 %attend.1 = (bf16[2048,256]{1,0:T(8,128)(2,1)S(1)}, f32[8,4,256]{2,1,0:T(4,128)S(1)}) custom-call(s32[8]{0:T(128)S(1)} %and_select_fusion.first_ref, s32[1,2048]{1,0:T(1,128)S(1)} %compare_select_fusion.2.start_ref, bf16[2048,256]{1,0:T(8,128)(2,1)S(1)} %get-tuple-element.60.q_ref, bf16[2048,256]{1,0:T(8,128)(2,1)S(1)} %get-tuple-element.61.k_ref, ...), custom_call_target="tpu_custom_call" | custom-call | flops 2147483648 | bytes 4194304 | tf_op jit(solution)/shard_map/attend/pallas_call | solution.py:860
  174.3 16.4 %heads_to_tokens.1.att_ref = bf16[256,2048]{1,0:T(8,128)(2,1)} custom-call(bf16[2048,256]{1,0:T(8,128)(2,1)} %copy-done.12), custom_call_target="tpu_custom_call" | custom-call | tf_op jit(solution)/shard_map/heads_to_tokens/pallas_call | solution.py:680
  191.5 3.4 copy-done
  194.9 1.2 copy-done.2
  196.1 7.4 mix_pass.1
  205.5 54.4 %gather_seq.1 = (bf16[8,256,2048]{2,1,0:T(8,128)(2,1)}, bf16[8,4,64,1024]{3,2,1,0:T(8,128)(2,1)}) custom-call(bf16[256,2048]{1,0:T(8,128)(2,1)} %copy-done.11, bf16[8,4,64,1024]{3,2,1,0:T(8,128)(2,1)} %get-tuple-element.68.near_ref), custom_call_target="tpu_custom_call" | custom-call | tf_op jit(solution)/shard_map/gather_seq/pallas_call | solution.py:293
  259.9 28.4 %upper_pass.1 = (f32[2048,1024]{1,0:T(8,128)}, bf16[2048,1024]{1,0:T(8,128)(2,1)S(1)}, f32[2048,1024]{1,0:T(8,128)}, f32[8,2048]{1,0:T(8,128)S(1)}) custom-call(bf16[2048,2048]{1,0:T(8,128)(2,1)} %bitcast.81, bf16[1024,2048]{1,0:T(8,128)(2,1)} %wu_ref.1, bf16[2048,2048]{1,0:T(8,128)(2,1)} %all-gather.5.cloned.1.call-done.c_ref, bf16[2048,1024]{1,0:T(8,128)(2,1)} %bitcast.83, ...), custom_call_target="tpu_custom_call" | custom-call | flops 17179869184 | bytes 50331648 | tf_op jit(solution)/shard_map/upper_pass/pallas_call | solution.py:1041
  288.3 2.0 copy-done.6
  291.0 10.3 %join_stats.1.stat_ref = f32[8,2048]{1,0:T(8,128)} custom-call(f32[8,2048]{1,0:T(8,128)} %copy-done.16), custom_call_target="tpu_custom_call" | custom-call | tf_op jit(solution)/shard_map/join_stats/pallas_call | solution.py:1152
  301.3 2.2 copy-done.7
  304.3 10.6 %hidden_pass.1 = (bf16[2048,1024]{1,0:T(8,128)(2,1)S(1)}, bf16[2048,1024]{1,0:T(8,128)(2,1)S(1)}, f32[1,1024]{1,0:T(1,128)S(1)}) custom-call(f32[2048,1024]{1,0:T(8,128)} %get-tuple-element.72.act_ref, bf16[2048,1024]{1,0:T(8,128)(2,1)S(1)} %copy-done.7, f32[2048,1024]{1,0:T(8,128)} %get-tuple-element.74.grad_ref, f32[8,2048]{1,0:T(8,128)S(1)} %copy-done.15, ...), custom_call_target="tpu_custom_call" | custom-call | flops 25165824 | bytes 29360128 | tf_op jit(solution)/shard_map/hidden_pass/pallas_call | solution.py:1096
  315.5 2.0 copy-done.22
  317.5 2.0 copy-done.24
  319.5 11.0 %convolution_convert_fusion.4 = bf16[1024,2048]{1,0:T(8,128)(2,1)} fusion(bf16[2048,1024]{1,0:T(8,128)(2,1)S(1)} %get-tuple-element.80, bf16[2048,2048]{1,0:T(8,128)(2,1)S(1)} %bitcast.82), kind=kOutput, calls=%fused_computation.4 | convolution fusion | flops 8592031744 | bytes 16777216 | tf_op jit(solution)/shard_map/dot_general | solution.py:36
  330.6 14.2 %convolution_convert_fusion.5 = bf16[2048,1024]{1,0:T(8,128)(2,1)} fusion(bf16[2048,2048]{1,0:T(8,128)(2,1)} %all-gather.5.cloned.1.call-done.c_ref, bf16[2048,1024]{1,0:T(8,128)(2,1)} %copy-done.22), kind=kOutput, calls=%fused_computation.5 | convolution fusion | flops 8592031744 | bytes 16777216 | tf_op jit(solution)/shard_map/dot_general | solution.py:36
  344.8 11.9 %convolution_convert_fusion.3 = bf16[2048,2048]{1,0:T(8,128)(2,1)S(1)} fusion(bf16[2048,1024]{1,0:T(8,128)(2,1)} %copy-done.24, bf16[1024,2048]{1,0:T(8,128)(2,1)} %wu_ref.1), kind=kOutput, calls=%fused_computation.3 | convolution fusion | flops 8594128896 | bytes 16777216 | tf_op jit(solution)/shard_map/dot_general | solution.py:28
  356.7 40.6 %scatter_seq.1.g_ref = f32[256,2048]{1,0:T(8,128)S(1)} custom-call(bf16[8,256,2048]{2,1,0:T(8,128)(2,1)S(1)} %bitcast.51), custom_call_target="tpu_custom_call" | custom-call | tf_op jit(solution)/shard_map/scatter_seq/pallas_call | solution.py:604
  397.3 13.6 %branch_pass.1 = (f32[256,2048]{1,0:T(8,128)S(1)}, bf16[256,2048]{1,0:T(8,128)(2,1)S(1)}, bf16[256,2048]{1,0:T(8,128)(2,1)S(1)}, f32[1,2048]{1,0:T(1,128)S(1)}, f32[1,2048]{1,0:T(1,128)S(1)}) custom-call(f32[256,2048]{1,0:T(8,128)S(1)} %scatter_seq.1.g_ref, f32[256,2048]{1,0:T(8,128)S(1)} %get-tuple-element.81.mid_ref, bf16[256,2048]{1,0:T(8,128)(2,1)S(1)} %bitcast.53, ...), custom_call_target="tpu_custom_call" | custom-call | flops 2147483648 | bytes 18874368 | tf_op jit(solution)/shard_map/branch_pass/pallas_call | solution.py:1273
  411.0 1.3 copy-done.8
  414.4 13.8 %tokens_to_heads.1.do_ref = bf16[2048,256]{1,0:T(8,128)(2,1)} custom-call(bf16[256,2048]{1,0:T(8,128)(2,1)} %copy-done.14), custom_call_target="tpu_custom_call" | custom-call | tf_op jit(solution)/shard_map/tokens_to_heads/pallas_call | solution.py:717
  428.2 6.0 all-to-all-start
  434.3 1.2 copy-done.34
  435.5 1.2 copy-done.36
  436.7 1.2 copy-done.38
  438.0 36.5 %attend_back.1 = bf16[2048,768]{1,0:T(8,128)(2,1)} custom-call(s32[8]{0:T(128)S(1)} %and_select_fusion.first_ref, s32[1,2048]{1,0:T(1,128)S(1)} %compare_select_fusion.2.start_ref, bf16[2048,256]{1,0:T(8,128)(2,1)S(1)} %copy-done.32, bf16[2048,256]{1,0:T(8,128)(2,1)S(1)} %copy-done.34, bf16[256,2048]{1,0:T(8,128)(2,1)S(1)} %copy-done.38, ...), custom_call_target="tpu_custom_call" | custom-call | flops 5368709120 | bytes 8388608 | tf_op jit(solution)/shard_map/attend_back/pallas_call | solution.py:975
  474.5 11.0 %convolution_convert_fusion.1 = bf16[2048,2048]{1,0:T(8,128)(2,1)} fusion(bf16[2048,768]{1,0:T(8,128)(2,1)} %attend_back.1, bf16[768,2048]{1,0:T(8,128)(2,1)S(1)} %bitcast.63), kind=kOutput, calls=%fused_computation.1 | convolution fusion | flops 6446645248 | bytes 14680064 | tf_op jit(solution)/shard_map/dot_general | solution.py:28
  485.5 8.2 %convolution_convert_fusion.6 = bf16[768,2048]{1,0:T(8,128)(2,1)} fusion(bf16[2048,768]{1,0:T(8,128)(2,1)S(1)} %copy-done.44, bf16[2048,2048]{1,0:T(8,128)(2,1)S(1)} %bitcast.80), kind=kOutput, calls=%fused_computation.6 | convolution fusion | flops 6444023808 | bytes 14680064 | tf_op jit(solution)/shard_map/dot_general | solution.py:36
  493.7 5.8 convolution_convert_fusion.2
  499.5 11.2 %convolution_convert_fusion = bf16[2048,2048]{1,0:T(8,128)(2,1)} fusion(bf16[2048,1024]{1,0:T(8,128)(2,1)S(1)} %copy-done.23, bf16[2048,1024]{1,0:T(8,128)(2,1)S(1)} %bitcast.84), kind=kOutput, calls=%fused_computation | convolution fusion | flops 8594128896 | bytes 16777216 | tf_op jit(solution)/shard_map/dot_general | solution.py:32
  510.7 265.0 %finish.1 = (bf16[3,256,2048]{2,1,0:T(8,128)(2,1)}, bf16[256,8192]{1,0:T(8,128)(2,1)}, bf16[256,2048]{1,0:T(8,128)(2,1)}, f32[256,2048]{1,0:T(8,128)}, bf16[256,2048]{1,0:T(8,128)(2,1)}, /*index=5*/f32[16,2048]{1,0:T(8,128)}) custom-call(bf16[3,256,2048]{2,1,0:T(8,128)(2,1)} %bitcast.68, bf16[8,256,1024]{2,1,0:T(8,128)(2,1)} %all-to-all-done.gd_ref, ...), custom_call_target="tpu_custom_call" | custom-call | tf_op jit(solution)/shard_map/finish/pallas_call | solution.py:1706
  777.1 2.8 convert_element_type.73
  779.9 6.7 convert_element_type.75
  786.6 1.6 fusion.8
  788.2 3.8 bitcast_convert_fusion
  792.0 6.8 convert_element_type.74
  799.7 1.3 copy.28
  (99 shorter events, 11.9 us)
Async XLA Ops:
  7.2 184.3 %all-gather.3.cloned.1.call-start = ((), (), s32[]{:S(2)}) async-start(), calls=%async_computation.1 | async-start | bytes 9437184 | tf_op jit(solution)/shard_map/all_gather | solution.py:1791
  7.9 252.0 %all-gather.5.cloned.1.call-start = ((), (), s32[]{:S(2)}) async-start(), calls=%async_computation.2 | async-start | bytes 9437184 | tf_op jit(solution)/shard_map/all_gather | solution.py:1805
  128.5 663.4 %all-reduce.2.cloned.1.call-start = ((), (), s32[]{:S(2)}) async-start(), calls=%async_computation.3 | async-start | bytes 8388608 | tf_op jit(solution)/shard_map/psum | solution.py:1822
  128.7 1.9 copy-start.25
  130.6 1.2 copy-start.27
  131.8 1.2 copy-start.28
  133.0 1.2 copy-start.29
  134.3 1.3 copy-start.30
  147.4 26.0 %copy-start.31 = (bf16[2048,256]{1,0:T(8,128)(2,1)}, bf16[2048,256]{1,0:T(8,128)(2,1)S(1)}, u32[]{:S(2)}) copy-start(bf16[2048,256]{1,0:T(8,128)(2,1)S(1)} %get-tuple-element.60.q_ref) | copy-start | bytes 3145732
  147.4 25.9 %copy-start.33 = (bf16[2048,256]{1,0:T(8,128)(2,1)}, bf16[2048,256]{1,0:T(8,128)(2,1)S(1)}, u32[]{:S(2)}) copy-start(bf16[2048,256]{1,0:T(8,128)(2,1)S(1)} %get-tuple-element.61.k_ref) | copy-start | bytes 3145732
  147.4 25.9 %copy-start.35 = (bf16[2048,256]{1,0:T(8,128)(2,1)}, bf16[2048,256]{1,0:T(8,128)(2,1)S(1)}, u32[]{:S(2)}) copy-start(bf16[2048,256]{1,0:T(8,128)(2,1)S(1)} %get-tuple-element.63.v_ref) | copy-start | bytes 3145732
  147.4 25.9 %copy-start.37 = (bf16[256,2048]{1,0:T(8,128)(2,1)}, bf16[256,2048]{1,0:T(8,128)(2,1)S(1)}, u32[]{:S(2)}) copy-start(bf16[256,2048]{1,0:T(8,128)(2,1)S(1)} %get-tuple-element.62.kt_ref) | copy-start | bytes 3145732
  147.4 44.1 %copy-start.1 = (bf16[1,256,2048]{2,1,0:T(8,128)(2,1)S(1)}, bf16[1,256,2048]{2,1,0:T(8,128)(2,1)}, u32[]{:S(2)}) copy-start(bf16[1,256,2048]{2,1,0:T(8,128)(2,1)} %param.11) | copy-start | bytes 3145732
  147.4 44.1 %copy-start.17 = (f32[2048]{0:T(1024)S(1)}, f32[2048]{0:T(1024)}, u32[]{:S(2)}) copy-start(f32[2048]{0:T(1024)} %param.18) | copy-start | bytes 24580
  147.4 44.0 %copy-start.18 = (f32[2048]{0:T(1024)S(1)}, f32[2048]{0:T(1024)}, u32[]{:S(2)}) copy-start(f32[2048]{0:T(1024)} %param.19) | copy-start | bytes 24580
  173.4 1.0 copy-start.12
  191.5 3.4 copy-start
  194.9 1.2 copy-start.2
  203.5 1.0 copy-start.9
  204.5 1.0 copy-start.11
  205.5 191.9 %copy-start.4 = (f32[256,2048]{1,0:T(8,128)}, f32[256,2048]{1,0:T(8,128)S(1)}, u32[]{:S(2)}) copy-start(f32[256,2048]{1,0:T(8,128)S(1)} %get-tuple-element.81.mid_ref) | copy-start | bytes 6291460
  288.3 2.0 copy-start.6
  290.3 0.6 copy-start.16
  301.2 2.2 copy-start.7
  303.4 0.8 copy-start.15
  304.3 15.3 %copy-start.42 = (bf16[8,256,2048]{2,1,0:T(8,128)(2,1)S(1)}, bf16[8,256,2048]{2,1,0:T(8,128)(2,1)}, u32[]{:S(2)}) copy-start(bf16[8,256,2048]{2,1,0:T(8,128)(2,1)} %get-tuple-element.69) | copy-start | bytes 25165828
  315.5 2.0 copy-start.22
  317.5 2.0 copy-start.24
  356.7 40.6 %copy-start.3 = (bf16[256,2048]{1,0:T(8,128)(2,1)S(1)}, bf16[256,2048]{1,0:T(8,128)(2,1)}, u32[]{:S(2)}) copy-start(bf16[256,2048]{1,0:T(8,128)(2,1)} %heads_to_tokens.1.att_ref) | copy-start | bytes 3145732
  356.7 40.6 %copy-start.5 = (bf16[1,256,2048]{2,1,0:T(8,128)(2,1)S(1)}, bf16[1,256,2048]{2,1,0:T(8,128)(2,1)}, u32[]{:S(2)}) copy-start(bf16[1,256,2048]{2,1,0:T(8,128)(2,1)} %param.21) | copy-start | bytes 3145732
  411.0 1.3 copy-start.8
  412.3 1.0 copy-start.14
  428.2 6.0 copy-start.13
  428.2 6.0 copy-start.32
  428.2 82.4 %all-to-all-start = ((bf16[8,256,1024]{2,1,0:T(8,128)(2,1)}), bf16[8,256,1024]{2,1,0:T(8,128)(2,1)}, u32[]{:S(2)}, u32[]{:S(2)}) async-start(bf16[8,256,1024]{2,1,0:T(8,128)(2,1)} %bitcast.67), calls=%async_computation | async-start | bytes 8388608 | tf_op jit(solution)/shard_map/all_to_all | solution.py:1831
  434.3 1.2 copy-start.34
  435.5 1.2 copy-start.36
  436.7 1.2 copy-start.38
  438.0 36.5 %copy-start.26 = (bf16[3,256,2048]{2,1,0:T(8,128)(2,1)S(1)}, bf16[3,256,2048]{2,1,0:T(8,128)(2,1)}, u32[]{:S(2)}) copy-start(bf16[3,256,2048]{2,1,0:T(8,128)(2,1)} %get-tuple-element.55) | copy-start | bytes 9437188
  438.0 47.5 %slice-start = ((s8[8388608]{0:T(1024)(128)(4,1)}), s8[4194304]{0:T(1024)(128)(4,1)S(1)}, s32[]{:S(2)}) async-start(s8[8388608]{0:T(1024)(128)(4,1)} %bitcast.78), calls=%async_computation.4 | async-start | bytes 8388608
  474.5 11.0 %slice-start.1 = ((s8[8388608]{0:T(1024)(128)(4,1)}), s8[4194304]{0:T(1024)(128)(4,1)S(1)}, s32[]{:S(2)}) async-start(s8[8388608]{0:T(1024)(128)(4,1)} %bitcast.78), calls=%async_computation.5 | async-start | bytes 8388608
  474.5 11.0 %copy-start.44 = (bf16[2048,768]{1,0:T(8,128)(2,1)S(1)}, bf16[2048,768]{1,0:T(8,128)(2,1)}, u32[]{:S(2)}) copy-start(bf16[2048,768]{1,0:T(8,128)(2,1)} %attend_back.1) | copy-start | bytes 9437188
  485.5 8.2 %copy-start.10 = (bf16[256,2048]{1,0:T(8,128)(2,1)S(1)}, bf16[256,2048]{1,0:T(8,128)(2,1)}, u32[]{:S(2)}) copy-start(bf16[256,2048]{1,0:T(8,128)(2,1)} %copy-done.9) | copy-start | bytes 3145732
  493.7 5.8 copy-start.23
  493.7 5.8 copy-start.43
  779.9 8.3 %copy-start.39 = (bf16[3,256,2048]{2,1,0:T(8,128)(2,1)S(1)}, bf16[3,256,2048]{2,1,0:T(8,128)(2,1)}, u32[]{:S(2)}) copy-start(bf16[3,256,2048]{2,1,0:T(8,128)(2,1)} %get-tuple-element.93) | copy-start | bytes 9437188
  792.0 6.8 copy-start.41
  792.0 7.8 copy-start.40
  (3 other events, 1.8 us)
Sparse Core Ops, SparseCore 0:
  9.9 92.9 all-gather.2
  128.6 58.1 all-gather.4
  344.9 153.5 all-reduce.1

commit v4 on v3

--- a/solution.py
+++ b/solution.py
@@ -16,6 +16,7 @@
 EPSILON = 1e-05
 MASKED = -1e30
 TILE = 256
+VMEM_LIMIT = 60 * 1024 * 1024
 
 MESH = pl.DeviceIdType.MESH
 F32 = jnp.float32
@@ -115,7 +116,7 @@
     ]
 
 
-def gather_run(sends, between=None):
+def gather_run(sends, between=None, later=None):
     sends[0].wait_recv()
     sends[5].start()
     sends[7].start()
@@ -132,6 +133,8 @@
     sends[11].start()
     sends[6].wait_recv()
     sends[12].start()
+    if later is not None:
+        later()
     for k in (4, 7, 8, 9, 10, 11, 12):
         sends[k].wait_recv()
     for send in sends:
@@ -307,7 +310,7 @@
             pltpu.SemaphoreType.DMA((2, depth)),
         ],
         compiler_params=pltpu.CompilerParams(
-            collective_id=collective_id, has_side_effects=True
+            collective_id=collective_id, has_side_effects=True, vmem_limit_bytes=VMEM_LIMIT
         ),
         name="gather_seq",
     )(block, near)
@@ -332,7 +335,8 @@
 def start_kernel(
     n, depth, x_ref, w_ref, wd_ref, pos_ref,
     o_ref, wt_ref, wc_ref, cq_ref, sq_ref, ck_ref, sk_ref,
-    keep_w, keep_c, local_sem, send_sem, recv_sem, hop_send, hop_recv, col_send, col_recv, line_send, line_recv,
+    keep_w, keep_c, local_sem, send_sem, recv_sem, hop_send, hop_recv, col_send, col_recv,
+    line_send, line_recv, w_send, w_recv,
 ):
     z = lax.axis_index("batch")
     rows_z = wc_ref.shape[2]
@@ -351,6 +355,37 @@
     meet_all(n, depth)
     load_column.wait()
     own_column.start()
+    w_rows = pl.ds(
+        pl.multiple_of(z * wt_ref.shape[2], wt_ref.shape[2]), wt_ref.shape[2]
+    )
+
+    def hop(j, part, target):
+        return remote(
+            w_ref.at[j, w_rows], wt_ref.at[part, z], hop_send.at[j], hop_recv.at[part], target
+        )
+
+    def load(j):
+        return pltpu.make_async_copy(w_ref.at[j, w_rows], keep_w, local_sem.at[6])
+
+    def here(j, part):
+        return pltpu.make_async_copy(keep_w, wt_ref.at[part, z], local_sem.at[1 + j])
+
+    for j in range(3):
+        block = 3 * me + j
+        target = lax.rem(block, n)
+        for part in range(3):
+            inside = block // n == part
+
+            @pl.when(inside & (target != me))
+            def _():
+                hop(j, part, target).start()
+
+            @pl.when(inside & (target == me))
+            def _():
+                load(j).start()
+                load(j).wait()
+                here(j, part).start()
+
     turns = [
         remote(
             column(lax.rem(me + k, n)),
@@ -375,32 +410,30 @@
         line_recv,
     )
 
-    def hop(j, part, target):
-        return remote(
-            w_ref.at[j], wt_ref.at[part], hop_send.at[j], hop_recv.at[part], target
-        )
-
-    def load(j):
-        return pltpu.make_async_copy(w_ref.at[j], keep_w, local_sem.at[6])
-
-    def here(j, part):
-        return pltpu.make_async_copy(keep_w, wt_ref.at[part], local_sem.at[1 + j])
-
+    line_w = Line(
+        depth,
+        lambda owner, k: wt_ref.at[:, owner],
+        lambda owner: wt_ref.at[:, owner],
+        w_send,
+        w_recv,
+    )
     for j in range(3):
         block = 3 * me + j
         target = lax.rem(block, n)
         for part in range(3):
-            inside = block // n == part
-
-            @pl.when(inside & (target != me))
+
+            @pl.when((block // n == part) & (target == me))
             def _():
-                hop(j, part, target).start()
-
-            @pl.when(inside & (target == me))
-            def _():
-                load(j).start()
-                load(j).wait()
-                here(j, part).start()
+                here(j, part).wait()
+
+    for part in range(3):
+        source = (part * n + me) // 3
+
+        @pl.when(source != me)
+        def _():
+            hop(0, part, source).wait_recv()
+
+    line_w.start(0)
 
     @pl.loop(0, pos_ref.shape[0])
     def _(r):
@@ -413,33 +446,33 @@
     own_column.wait()
     for turn in turns:
         turn.wait_recv()
-    line.start(0)
-    gather_run(sends)
+
+    def between():
+        line_w.land(0)
+        line_w.start(1)
+        line.start(0)
+
+    def later():
+        for k in range(2, depth - 1):
+            line_w.land(k - 1)
+            line_w.start(k)
+
+    gather_run(sends, between, later)
+    line_w.land(depth - 2)
     line.land(0)
+    for k in range(depth - 1):
+        line_w.sent(k)
     line.sent(0)
     for turn in turns:
         turn.wait_send()
     for j in range(3):
         block = 3 * me + j
         target = lax.rem(block, n)
-
         for part in range(3):
-            inside = block // n == part
-
-            @pl.when(inside & (target != me))
+
+            @pl.when((block // n == part) & (target != me))
             def _():
                 hop(j, part, target).wait_send()
-
-            @pl.when(inside & (target == me))
-            def _():
-                here(j, part).wait()
-
-    for part in range(3):
-        source = (part * n + me) // 3
-
-        @pl.when(source != me)
-        def _():
-            hop(0, part, source).wait_recv()
 
     own.wait()
 
@@ -470,14 +503,14 @@
         functools.partial(start_kernel, n, depth),
         out_shape=(
             jax.ShapeDtypeStruct((n, rows, width), block.dtype),
-            jax.ShapeDtypeStruct((3, piece, width), w.dtype),
+            jax.ShapeDtypeStruct((3, depth, piece // depth, width), w.dtype),
             jax.ShapeDtypeStruct((n, depth, rows_z, cols), w_down.dtype),
             *([table] * 4),
         ),
         in_specs=[INSIDE, ANY, ANY, INSIDE],
         out_specs=(ANY, ANY, ANY, *([INSIDE] * 4)),
         scratch_shapes=[
-            pltpu.VMEM((piece, width), BF16),
+            pltpu.VMEM((piece // depth, width), BF16),
             pltpu.VMEM((rows_z, cols), BF16),
             pltpu.SemaphoreType.DMA((7,)),
             pltpu.SemaphoreType.DMA((13,)),
@@ -488,9 +521,11 @@
             pltpu.SemaphoreType.DMA((n,)),
             pltpu.SemaphoreType.DMA((2, depth)),
             pltpu.SemaphoreType.DMA((2, depth)),
+            pltpu.SemaphoreType.DMA((2, depth)),
+            pltpu.SemaphoreType.DMA((2, depth)),
         ],
         compiler_params=pltpu.CompilerParams(
-            collective_id=collective_id, has_side_effects=True
+            collective_id=collective_id, has_side_effects=True, vmem_limit_bytes=VMEM_LIMIT
         ),
         name="start_exchange",
     )(block, w, w_down, positions.reshape(-1, 128))
@@ -617,7 +652,7 @@
         compiler_params=pltpu.CompilerParams(
             collective_id=collective_id,
             has_side_effects=True,
-            vmem_limit_bytes=32 * 1024 * 1024,
+            vmem_limit_bytes=VMEM_LIMIT,
         ),
         name="scatter_seq",
     )(partial.reshape(n, rows, width))
@@ -689,7 +724,7 @@
             pltpu.SemaphoreType.DMA((n,)),
         ],
         compiler_params=pltpu.CompilerParams(
-            collective_id=collective_id, has_side_effects=True
+            collective_id=collective_id, has_side_effects=True, vmem_limit_bytes=VMEM_LIMIT
         ),
         name="heads_to_tokens",
     )(heads)
@@ -726,7 +761,7 @@
             pltpu.SemaphoreType.DMA((n,)),
         ],
         compiler_params=pltpu.CompilerParams(
-            collective_id=collective_id, has_side_effects=True
+            collective_id=collective_id, has_side_effects=True, vmem_limit_bytes=VMEM_LIMIT
         ),
         name="tokens_to_heads",
     )(tokens)
@@ -785,7 +820,7 @@
         + [weight]
         + [table] * 4,
         out_specs=(row_out, row_out, row_out, col_out, col_out),
-        compiler_params=pltpu.CompilerParams(vmem_limit_bytes=40 * 1024 * 1024),
+        compiler_params=pltpu.CompilerParams(vmem_limit_bytes=VMEM_LIMIT),
         cost_estimate=pl.CostEstimate(
             flops=6 * length * width * cols,
             bytes_accessed=2 * length * width + 6 * width * cols + 10 * length * cols,
@@ -882,7 +917,7 @@
                 pltpu.VMEM((cols, TILE), F32),
             ],
         ),
-        compiler_params=pltpu.CompilerParams(vmem_limit_bytes=32 * 1024 * 1024),
+        compiler_params=pltpu.CompilerParams(vmem_limit_bytes=VMEM_LIMIT),
         cost_estimate=pl.CostEstimate(
             flops=4 * length * 1024 * cols,
             bytes_accessed=8 * length * cols,
@@ -996,7 +1031,7 @@
                 pltpu.VMEM((length, cols), F32),
             ],
         ),
-        compiler_params=pltpu.CompilerParams(vmem_limit_bytes=48 * 1024 * 1024),
+        compiler_params=pltpu.CompilerParams(vmem_limit_bytes=VMEM_LIMIT),
         cost_estimate=pl.CostEstimate(
             flops=10 * length * 1024 * cols,
             bytes_accessed=16 * length * cols,
@@ -1055,7 +1090,7 @@
             pl.BlockSpec((1, feats), lambda i: (0, 0)),
         ],
         out_specs=(out, out, out, pl.BlockSpec((8, rows), lambda i: (0, i))),
-        compiler_params=pltpu.CompilerParams(vmem_limit_bytes=48 * 1024 * 1024),
+        compiler_params=pltpu.CompilerParams(vmem_limit_bytes=VMEM_LIMIT),
         cost_estimate=pl.CostEstimate(
             flops=4 * length * width * feats,
             bytes_accessed=8 * length * width + 8 * length * feats,
@@ -1103,7 +1138,7 @@
         ),
         in_specs=[out, out, out, pl.BlockSpec((8, TILE), lambda i: (0, i)), one],
         out_specs=(out, out, one),
-        compiler_params=pltpu.CompilerParams(vmem_limit_bytes=40 * 1024 * 1024),
+        compiler_params=pltpu.CompilerParams(vmem_limit_bytes=VMEM_LIMIT),
         cost_estimate=pl.CostEstimate(
             flops=12 * length * feats,
             bytes_accessed=14 * length * feats,
@@ -1160,7 +1195,7 @@
             pltpu.SemaphoreType.DMA((n,)),
         ],
         compiler_params=pltpu.CompilerParams(
-            collective_id=collective_id, has_side_effects=True
+            collective_id=collective_id, has_side_effects=True, vmem_limit_bytes=VMEM_LIMIT
         ),
         name="join_stats",
     )(stat)
@@ -1213,7 +1248,7 @@
             gain,
         ],
         out_specs=(whole, whole, whole),
-        compiler_params=pltpu.CompilerParams(vmem_limit_bytes=32 * 1024 * 1024),
+        compiler_params=pltpu.CompilerParams(vmem_limit_bytes=VMEM_LIMIT),
         cost_estimate=pl.CostEstimate(
             flops=2 * rows * width * width,
             bytes_accessed=2 * width * width + 12 * rows * width,
@@ -1285,7 +1320,7 @@
         ],
         out_specs=(whole, whole, whole, gain, gain),
         scratch_shapes=[pltpu.VMEM((rows, width), F32)],
-        compiler_params=pltpu.CompilerParams(vmem_limit_bytes=40 * 1024 * 1024),
+        compiler_params=pltpu.CompilerParams(vmem_limit_bytes=VMEM_LIMIT),
         cost_estimate=pl.CostEstimate(
             flops=2 * rows * width * width,
             bytes_accessed=2 * width * width + 20 * rows * width,
@@ -1301,8 +1336,8 @@
 def finish_kernel(
     n, depth, gq_ref, gd_ref, pw_ref, pn_ref, po_ref, x_ref, grad_ref, mid_ref, ga_ref, gm_ref, gf_ref, gh_ref,
     oq_ref, od_ref, ow_ref, gi_ref, out_ref, sums_ref,
-    own, twin_in, held, zown, zin, gain_here, gain_row, gain_pack, gain_line,
-    local_sem, load_sem, send_sem, recv_sem, keep_sem,
+    own, twin_in, held, zown, zin, stage, gain_here, gain_row, gain_pack, gain_line,
+    local_sem, load_sem, stage_sem, send_sem, recv_sem, keep_sem,
     up_send, up_recv, down_send, down_recv, home_send, home_recv, gain_send, gain_recv,
 ):
     me, twin, near_x, near_y, across = places()
@@ -1315,8 +1350,8 @@
     across_width = width // cols
     per_part = (gq_ref.shape[1] // chunk) * across_width
     turned = gq_ref.shape[0] * per_part
-    outer = turned + (rows // chunk) * across_width
     per_source = gd_ref.shape[1] // chunk
+    outer = turned + gd_ref.shape[0] * per_source
     chunks = zown.shape[0]
     per_side = chunks // 2
 
@@ -1330,9 +1365,9 @@
     for g in range(turned):
         source = gq_ref.at[(g // per_part, *wide(g % per_part))]
         line_loads.append(pltpu.make_async_copy(source, zown.at[g], load_sem.at[g]))
-    for g in range(outer, chunks):
+    for g in range(turned, outer):
         source = gd_ref.at[
-            (g - outer) // per_source, cut((g - outer) % per_source, chunk)
+            (g - turned) // per_source, cut((g - turned) % per_source, chunk)
         ]
         line_loads.append(pltpu.make_async_copy(source, zown.at[g], load_sem.at[g]))
     for load in line_loads:
@@ -1437,7 +1472,7 @@
         value = value.astype(BF16)
         for side in range(across_width):
             zown[
-                turned + (place // chunk) * across_width + side,
+                outer + (place // chunk) * across_width + side,
                 pl.ds(pl.multiple_of(lax.rem(place, chunk), STEP), STEP),
             ] = value[:, side * cols : (side + 1) * cols]
 
@@ -1471,34 +1506,51 @@
             zin.at[g], oq_ref.at[(slot, *wide(lax.rem(g, per_part)))], keep_sem.at[g]
         )
 
-    def deliver_out(g):
-        return pltpu.make_async_copy(
-            zin.at[g], ow_ref.at[wide(g - turned)], keep_sem.at[g]
-        )
-
-    def deliver_down(g):
-        at = g - outer
-        place = cut(lax.rem(at, per_source), chunk), cut(at // per_source, cols)
-        return pltpu.make_async_copy(zin.at[g], od_ref.at[place], keep_sem.at[g])
-
-    def deliver(g, wait):
+    def widen(g):
+        @pl.loop(0, chunk // STEP)
+        def _(r):
+            at = cut(r, STEP)
+            stage[at] = zin[g, at].astype(F32)
+
+    def deliver(g):
         target, _ = home(g // per_part)
 
         @pl.when((g < turned) & (target != me))
         def _():
-            deliver_far(g).wait_send() if wait else deliver_far(g).start()
+            deliver_far(g).start()
 
         @pl.when((g < turned) & (target == me))
         def _():
-            deliver_near(g).wait() if wait else deliver_near(g).start()
+            deliver_near(g).start()
 
         @pl.when((g >= turned) & (g < outer))
         def _():
-            deliver_out(g).wait() if wait else deliver_out(g).start()
+            widen(g)
+            at = g - turned
+            place = cut(lax.rem(at, per_source), chunk), cut(at // per_source, cols)
+            store = pltpu.make_async_copy(stage, od_ref.at[place], stage_sem)
+            store.start()
+            store.wait()
 
         @pl.when(g >= outer)
         def _():
-            deliver_down(g).wait() if wait else deliver_down(g).start()
+            widen(g)
+            store = pltpu.make_async_copy(
+                stage, ow_ref.at[wide(g - outer)], stage_sem
+            )
+            store.start()
+            store.wait()
+
+    def delivered(g):
+        target, _ = home(g // per_part)
+
+        @pl.when(target != me)
+        def _():
+            deliver_far(g).wait_send()
+
+        @pl.when(target == me)
+        def _():
+            deliver_near(g).wait()
 
     def go_up(g, ahead):
         return line_remote(zown.at[g], zin.at[g], up_send.at[g], up_recv.at[g], ahead)
@@ -1521,17 +1573,25 @@
                 BF16
             )
 
+    lead = 4
+
+    def line_enter(c):
+        for side in (0, 1):
+            rank, ahead, _ = ranks(side)
+
+            @pl.when(rank == 0)
+            def _():
+                go_up(2 * c + side, ahead).start()
+
     def line_step(t):
+        if t + lead < per_side:
+            line_enter(t + lead)
         for side in (0, 1):
             rank, ahead, behind = ranks(side)
             c = t - rank
             g = 2 * c + side
             there = (c >= 0) & (c < per_side)
 
-            @pl.when(there & (rank == 0))
-            def _():
-                go_up(g, ahead).start()
-
             @pl.when(there & (rank > 0) & (rank < depth - 1))
             def _():
                 go_up(g, behind).wait_recv()
@@ -1543,7 +1603,7 @@
                 go_up(g, behind).wait_recv()
                 add_line(g, zin)
                 go_down(g, behind).start()
-                deliver(g, False)
+                deliver(g)
 
             c_back = t - 2 * (depth - 1) + rank
             g_back = 2 * c_back + side
@@ -1559,27 +1619,29 @@
 
             @pl.when(there)
             def _():
-                deliver(g_back, False)
+                deliver(g_back)
 
     gain_here[...] = jnp.zeros_like(gain_here)
-    first(0)
     for load in line_loads:
         load.wait()
+    for c in range(lead):
+        line_enter(c)
+    first(0)
     line_step(0)
     line_step(1)
     first(1)
     line_step(2)
+    line_step(3)
     second(0)
-    line_step(3)
+    line_step(4)
+    first(2)
+    line_step(5)
+    line_step(6)
     last(0, store_line)
-    for t in (4, 5, 6):
-        line_step(t)
-    first(2)
-    for t in (7, 8):
-        line_step(t)
+    line_step(7)
     second(1)
-    for t in (9, 10):
-        line_step(t)
+    line_step(8)
+    line_step(9)
     last(1, store_inputs)
 
     gain_here[1:2] = gm_ref[...]
@@ -1598,13 +1660,13 @@
     ]
     for send in rounds:
         send.start()
-    for t in (11, 12):
+    line_step(10)
+    second(2)
+    line_step(11)
+    line_step(12)
+    last(2, store_outputs)
+    for t in (13, 14, 15):
         line_step(t)
-    second(2)
-    for t in (13, 14):
-        line_step(t)
-    last(2, store_outputs)
-    line_step(15)
     for send in rounds:
         send.wait()
     total = gain_row[0]
@@ -1649,7 +1711,8 @@
         def _():
             go_down(g, behind).wait_send()
 
-        deliver(g, True)
+    for g in range(turned):
+        delivered(g)
     for slot in range(3):
         block = 3 * me + slot
         source = lax.rem(block, n)
@@ -1692,8 +1755,8 @@
         down = lax.psum(grad_down, "batch")
         return (
             jnp.concatenate(back, axis=0),
-            jnp.swapaxes(down, 0, 1).reshape(rows, sources * feats),
-            w_out,
+            jnp.swapaxes(down, 0, 1).reshape(rows, sources * feats).astype(F32),
+            w_out.astype(F32),
             grad_middle + part,
             (middle + scatter_seq(part_outputs, None)).astype(BF16),
             (*shared, hidden),
@@ -1707,8 +1770,8 @@
         functools.partial(finish_kernel, n, depth),
         out_shape=(
             jax.ShapeDtypeStruct((3, cols, width), BF16),
-            jax.ShapeDtypeStruct((rows, sources * feats), BF16),
-            jax.ShapeDtypeStruct((rows, width), BF16),
+            jax.ShapeDtypeStruct((rows, sources * feats), F32),
+            jax.ShapeDtypeStruct((rows, width), F32),
             jax.ShapeDtypeStruct((rows, width), F32),
             jax.ShapeDtypeStruct((rows, width), BF16),
             jax.ShapeDtypeStruct((16, width), F32),
@@ -1721,12 +1784,14 @@
             pltpu.VMEM((3, 6, rows // 2, width), BF16),
             line,
             line,
+            pltpu.VMEM((CHUNK, feats), F32),
             pltpu.VMEM((8, width), F32),
             pltpu.VMEM((n, 8, width), F32),
             pltpu.VMEM((16, width), F32),
             pltpu.VMEM((depth, 16, width), F32),
             dma((12,)),
             dma((chunks,)),
+            dma,
             dma((3, 10)),
             dma((3, 10)),
             dma((chunks,)),
@@ -1742,7 +1807,7 @@
         compiler_params=pltpu.CompilerParams(
             collective_id=collective_id,
             has_side_effects=True,
-            vmem_limit_bytes=60 * 1024 * 1024,
+            vmem_limit_bytes=VMEM_LIMIT,
         ),
         name="finish",
     )(
@@ -1849,9 +1914,9 @@
         outputs[None],
         grad_inputs[None],
         grad_w_qkv.astype(F32),
-        grad_w_out.astype(F32),
+        grad_w_out,
         grad_w_up.astype(F32),
-        grad_w_down.astype(F32),
+        grad_w_down,
         *gains,
     )
 

time: 820 us -> 822 us (level)
  the two profiles are of different devices: /device:TPU:26 before, /device:TPU:0 now
where the time goes in v4:
time: 822 us; the launch traced here: 817 us
  Pallas kernels  680 us (83%)
  matrix products  80.7 us (10%)
  other arithmetic  23.2 us (3%)
  between operations  14.1 us (2%)
  local copies, waits for them, and re-layouts  13.7 us (2%)
    pallas_call x1, Pallas kernels, finish(): pl.pallas_call(functools.partial(finish_kernel, n, depth), out_shape=(jax...  256 us
    pallas_call x1, Pallas kernels, start_exchange(): pl.pallas_call(functools.partial(start_kernel, n, depth), out_shape=(jax....  126 us
    pallas_call x1, Pallas kernels, gather_seq(): pl.pallas_call(functools.partial(gather_kernel, n, depth), out_shape=(jax...  55.8 us
    dot_general x4, matrix products, tn(): lax.dot_general(a, b, (((0,), (0,)), ((), ())), preferred_element_type=F32)  44.8 us
    pallas_call x1, Pallas kernels, scatter_seq(): pl.pallas_call(scatter_kernel, out_shape=jax.ShapeDtypeStruct((rows, widt...  42.3 us
    pallas_call x1, Pallas kernels, attend_back(): pl.pallas_call(functools.partial(attend_back_kernel, heads), out_shape=ja...  33 us
    pallas_call x1, Pallas kernels, heads_to_tokens(): pl.pallas_call(functools.partial(heads_to_tokens_kernel, n), out_shape=ja...  30.6 us
    pallas_call x1, Pallas kernels, upper_pass(): pl.pallas_call(upper_kernel, grid=(length // rows,), out_shape=(jax.Shape...  28.5 us
  transfers between devices with their start and end apart: 4, of which 0 were waited for; matrix products, arithmetic and copies ran while one was open for 9% of the time, Pallas kernels for 77%

profile of v4, /device:TPU:0, one launch (start us, length us, event | category | flops | bytes accessed | tf_op | source)
XLA Modules:
  0.0 817.5 jit_solution(14840379425763318663)
XLA Ops:
  7.2 0.0 all-gather.3.cloned.1.call-start
  7.2 0.7 all-gather.3.cloned.1.call-update
  7.9 0.0 all-gather.5.cloned.1.call-start
  8.0 1.4 fusion.5
  9.4 1.4 convert_reduce_fusion
  10.8 1.6 fusion.2
  12.5 2.7 compare_select_fusion.2.start_ref
  15.1 0.6 subtract_convert_fusion.pos_ref
  15.7 2.6 fusion.4.x_ref
  18.3 126.3 %start_exchange.1 = (bf16[8,256,2048]{2,1,0:T(8,128)(2,1)}, bf16[3,4,64,2048]{3,2,1,0:T(8,128)(2,1)}, bf16[8,4,64,1024]{3,2,1,0:T(8,128)(2,1)}, f32[2048,128]{1,...) custom-call(bf16[256,2048]{1,0:T(8,128)(2,1)} %fusion.4.x_ref, ...), custom_call_target="tpu_custom_call" | custom-call | tf_op jit(solution)/shard_map/start_exchange/pallas_call | solution.py:502
  144.7 0.0 all-gather.5.cloned.1.call-update
  144.7 0.3 all-reduce.2.cloned.1.call-start
  145.0 0.1 slice.15
  145.1 0.6 and_select_fusion.first_ref
  145.7 14.2 %project_qkv.1 = (bf16[2048,256]{1,0:T(8,128)(2,1)}, bf16[2048,256]{1,0:T(8,128)(2,1)}, bf16[2048,256]{1,0:T(8,128)(2,1)}, bf16[256,2048]{1,0:T(8,128)(2,1)}, bf16[256,2048]{1,0:T(8,128)(2,1)}) custom-call(bf16[2048,2048]{1,0:T(8,128)(2,1)} %bitcast.75, bf16[768,2048]{1,0:T(8,128)(2,1)} %bitcast.81, f32[2048,128]{1,0:T(8,128)} %get-tuple-element.56.cq_ref, ...), custom_call_target="tpu_custom_call" | custom-call | flops 6442450944 | bytes 16777216 | tf_op jit(solution)/shard_map/project_qkv/pallas_call | solution.py:815
  159.8 24.1 %attend.1 = (bf16[2048,256]{1,0:T(8,128)(2,1)}, f32[8,4,256]{2,1,0:T(4,128)}) custom-call(s32[8]{0:T(128)} %and_select_fusion.first_ref, s32[1,2048]{1,0:T(1,128)} %copy-done.6, bf16[2048,256]{1,0:T(8,128)(2,1)} %get-tuple-element.60.q_ref, bf16[2048,256]{1,0:T(8,128)(2,1)} %get-tuple-element.61.k_ref, bf16[256,2048]{1,0:T(8,128)(2,1)} %get-tuple-element.64.vt_ref), custom_call_target="tpu_custom_call" | custom-call | flops 2147483648 | bytes 4194304 | tf_op jit(solution)/shard_map/attend/pallas_call | solution.py:895
  184.0 30.6 %heads_to_tokens.1.att_ref = bf16[256,2048]{1,0:T(8,128)(2,1)} custom-call(bf16[2048,256]{1,0:T(8,128)(2,1)} %get-tuple-element.65.x_ref.o_ref), custom_call_target="tpu_custom_call" | custom-call | tf_op jit(solution)/shard_map/heads_to_tokens/pallas_call | solution.py:715
  214.6 1.3 dynamic_slice.3
  215.8 13.8 %mix_pass.1 = (bf16[256,2048]{1,0:T(8,128)(2,1)}, f32[256,2048]{1,0:T(8,128)}, bf16[256,2048]{1,0:T(8,128)(2,1)}) custom-call(bf16[256,2048]{1,0:T(8,128)(2,1)} %heads_to_tokens.1.att_ref, bf16[256,2048]{1,0:T(8,128)(2,1)} %bitcast.50, bf16[2048,2048]{1,0:T(8,128)(2,1)} %all-gather.3.cloned.1.call-done.w_ref, f32[1,2048]{1,0:T(1,128)} %bitcast.62, ...), custom_call_target="tpu_custom_call" | custom-call | flops 2147483648 | bytes 14680064 | tf_op jit(solution)/shard_map/mix_pass/pallas_call | solution.py:1239
  229.6 55.8 %gather_seq.1 = (bf16[8,256,2048]{2,1,0:T(8,128)(2,1)}, bf16[8,4,64,1024]{3,2,1,0:T(8,128)(2,1)}) custom-call(bf16[256,2048]{1,0:T(8,128)(2,1)} %get-tuple-element.67.x_ref, bf16[8,4,64,1024]{3,2,1,0:T(8,128)(2,1)} %get-tuple-element.68.near_ref), custom_call_target="tpu_custom_call" | custom-call | tf_op jit(solution)/shard_map/gather_seq/pallas_call | solution.py:296
  285.5 0.0 all-gather.5.cloned.1.call-done.c_ref
  285.5 28.5 %upper_pass.1 = (f32[2048,1024]{1,0:T(8,128)}, bf16[2048,1024]{1,0:T(8,128)(2,1)}, f32[2048,1024]{1,0:T(8,128)}, f32[8,2048]{1,0:T(8,128)}) custom-call(bf16[2048,2048]{1,0:T(8,128)(2,1)} %bitcast.77, bf16[1024,2048]{1,0:T(8,128)(2,1)} %wu_ref.1, bf16[2048,2048]{1,0:T(8,128)(2,1)} %all-gather.5.cloned.1.call-done.c_ref, bf16[2048,1024]{1,0:T(8,128)(2,1)} %bitcast.79, ...), custom_call_target="tpu_custom_call" | custom-call | flops 17179869184 | bytes 50331648 | tf_op jit(solution)/shard_map/upper_pass/pallas_call | solution.py:1076
  314.0 9.8 %join_stats.1.stat_ref = f32[8,2048]{1,0:T(8,128)} custom-call(f32[8,2048]{1,0:T(8,128)} %get-tuple-element.75.x_ref), custom_call_target="tpu_custom_call" | custom-call | tf_op jit(solution)/shard_map/join_stats/pallas_call | solution.py:1187
  323.8 14.2 %hidden_pass.1 = (bf16[2048,1024]{1,0:T(8,128)(2,1)}, bf16[2048,1024]{1,0:T(8,128)(2,1)}, f32[1,1024]{1,0:T(1,128)}) custom-call(f32[2048,1024]{1,0:T(8,128)} %get-tuple-element.72.act_ref, bf16[2048,1024]{1,0:T(8,128)(2,1)} %get-tuple-element.73.slope_ref, f32[2048,1024]{1,0:T(8,128)} %get-tuple-element.74.grad_ref, f32[8,2048]{1,0:T(8,128)} %join_stats.1.stat_ref, ...), custom_call_target="tpu_custom_call" | custom-call | flops 25165824 | bytes 29360128 | tf_op jit(solution)/shard_map/hidden_pass/pallas_call | solution.py:1131
  338.0 14.1 %convolution_convert_fusion.4 = bf16[1024,2048]{1,0:T(8,128)(2,1)} fusion(bf16[2048,1024]{1,0:T(8,128)(2,1)} %get-tuple-element.80, bf16[2048,2048]{1,0:T(8,128)(2,1)} %bitcast.78), kind=kOutput, calls=%fused_computation.4 | convolution fusion | flops 8592031744 | bytes 16777216 | tf_op jit(solution)/shard_map/dot_general | solution.py:37
  352.1 14.2 %convolution_convert_fusion.5 = bf16[2048,1024]{1,0:T(8,128)(2,1)} fusion(bf16[2048,2048]{1,0:T(8,128)(2,1)} %all-gather.5.cloned.1.call-done.c_ref, bf16[2048,1024]{1,0:T(8,128)(2,1)} %get-tuple-element.78), kind=kOutput, calls=%fused_computation.5 | convolution fusion | flops 8592031744 | bytes 16777216 | tf_op jit(solution)/shard_map/dot_general | solution.py:37
  366.3 0.0 all-reduce.2.cloned.1.call-update
  366.3 13.9 %convolution_convert_fusion.3 = bf16[2048,2048]{1,0:T(8,128)(2,1)} fusion(bf16[2048,1024]{1,0:T(8,128)(2,1)} %get-tuple-element.80, bf16[1024,2048]{1,0:T(8,128)(2,1)} %wu_ref.1), kind=kOutput, calls=%fused_computation.3 | convolution fusion | flops 8594128896 | bytes 16777216 | tf_op jit(solution)/shard_map/dot_general | solution.py:29
  380.2 42.3 %scatter_seq.1.g_ref = f32[256,2048]{1,0:T(8,128)} custom-call(bf16[8,256,2048]{2,1,0:T(8,128)(2,1)} %bitcast.54), custom_call_target="tpu_custom_call" | custom-call | tf_op jit(solution)/shard_map/scatter_seq/pallas_call | solution.py:639
  422.5 17.7 %branch_pass.1 = (f32[256,2048]{1,0:T(8,128)}, bf16[256,2048]{1,0:T(8,128)(2,1)}, bf16[256,2048]{1,0:T(8,128)(2,1)}, f32[1,2048]{1,0:T(1,128)}, f32[1,2048]{1,0:T(1,128)}) custom-call(f32[256,2048]{1,0:T(8,128)} %scatter_seq.1.g_ref, f32[256,2048]{1,0:T(8,128)} %get-tuple-element.81.mid_ref, bf16[256,2048]{1,0:T(8,128)(2,1)} %bitcast.56, ...), custom_call_target="tpu_custom_call" | custom-call | flops 2147483648 | bytes 18874368 | tf_op jit(solution)/shard_map/branch_pass/pallas_call | solution.py:1308
  440.2 13.7 %tokens_to_heads.1.do_ref = bf16[2048,256]{1,0:T(8,128)(2,1)} custom-call(bf16[256,2048]{1,0:T(8,128)(2,1)} %get-tuple-element.82.x_ref), custom_call_target="tpu_custom_call" | custom-call | tf_op jit(solution)/shard_map/tokens_to_heads/pallas_call | solution.py:752
  453.9 5.0 all-to-all-start
  458.9 33.0 %attend_back.1 = bf16[2048,768]{1,0:T(8,128)(2,1)} custom-call(s32[8]{0:T(128)} %and_select_fusion.first_ref, s32[1,2048]{1,0:T(1,128)} %copy-done.6, bf16[2048,256]{1,0:T(8,128)(2,1)} %get-tuple-element.60.q_ref, bf16[2048,256]{1,0:T(8,128)(2,1)} %get-tuple-element.61.k_ref, bf16[256,2048]{1,0:T(8,128)(2,1)} %get-tuple-element.62.kt_ref, ...), custom_call_target="tpu_custom_call" | custom-call | flops 5368709120 | bytes 8388608 | tf_op jit(solution)/shard_map/attend_back/pallas_call | solution.py:1010
  492.0 11.0 %convolution_convert_fusion.1 = bf16[2048,2048]{1,0:T(8,128)(2,1)} fusion(bf16[2048,768]{1,0:T(8,128)(2,1)} %attend_back.1, bf16[768,2048]{1,0:T(8,128)(2,1)S(1)} %bitcast.82), kind=kOutput, calls=%fused_computation.1 | convolution fusion | flops 6446645248 | bytes 14680064 | tf_op jit(solution)/shard_map/dot_general | solution.py:29
  502.9 10.7 %convolution_convert_fusion.6 = bf16[768,2048]{1,0:T(8,128)(2,1)} fusion(bf16[2048,768]{1,0:T(8,128)(2,1)S(1)} %copy-done.10, bf16[2048,2048]{1,0:T(8,128)(2,1)} %bitcast.76), kind=kOutput, calls=%fused_computation.6 | convolution fusion | flops 6444023808 | bytes 14680064 | tf_op jit(solution)/shard_map/dot_general | solution.py:37
  513.6 5.8 convolution_convert_fusion.2
  519.4 11.0 %convolution_convert_fusion = bf16[2048,2048]{1,0:T(8,128)(2,1)} fusion(bf16[2048,1024]{1,0:T(8,128)(2,1)S(1)} %copy-done.8, bf16[2048,1024]{1,0:T(8,128)(2,1)S(1)} %bitcast.80), kind=kOutput, calls=%fused_computation | convolution fusion | flops 8594128896 | bytes 16777216 | tf_op jit(solution)/shard_map/dot_general | solution.py:33
  530.4 255.8 %finish.1 = (bf16[3,256,2048]{2,1,0:T(8,128)(2,1)}, f32[256,8192]{1,0:T(8,128)}, f32[256,2048]{1,0:T(8,128)}, f32[256,2048]{1,0:T(8,128)}, bf16[256,2048]{1,0:T(8,128)(2,1)}, /*index=5*/f32[16,2048]{1,0:T(8,128)}) custom-call(bf16[3,256,2048]{2,1,0:T(8,128)(2,1)} %bitcast.58, bf16[8,256,1024]{2,1,0:T(8,128)(2,1)} %all-to-all-done.gd_ref, ...), custom_call_target="tpu_custom_call" | custom-call | tf_op jit(solution)/shard_map/finish/pallas_call | solution.py:1769
  786.2 0.8 slice_bitcast_fusion
  787.0 0.6 copy.23
  787.6 1.6 fusion.8
  789.2 5.4 bitcast_convert_fusion
  794.6 6.8 convert_element_type.67
  801.4 1.0 copy.29
  802.4 1.3 copy.30
  803.7 1.3 copy.31
  805.1 2.3 copy-done
  807.3 3.4 copy.32
  (26 shorter events, 0.1 us)
Async XLA Ops:
  7.2 208.7 %all-gather.3.cloned.1.call-start = ((), (), s32[]{:S(2)}) async-start(), calls=%async_computation.1 | async-start | bytes 9437184 | tf_op jit(solution)/shard_map/all_gather | solution.py:1856
  7.9 277.6 %all-gather.5.cloned.1.call-start = ((), (), s32[]{:S(2)}) async-start(), calls=%async_computation.2 | async-start | bytes 9437184 | tf_op jit(solution)/shard_map/all_gather | solution.py:1870
  15.1 129.8 %copy-start.6 = (s32[1,2048]{1,0:T(1,128)}, s32[1,2048]{1,0:T(1,128)S(1)}, u32[]{:S(2)}) copy-start(s32[1,2048]{1,0:T(1,128)S(1)} %compare_select_fusion.2.start_ref) | copy-start | bytes 24580
  144.7 649.9 %all-reduce.2.cloned.1.call-start = ((), (), s32[]{:S(2)}) async-start(), calls=%async_computation.3 | async-start | bytes 8388608 | tf_op jit(solution)/shard_map/psum | solution.py:1887
  453.9 76.6 %all-to-all-start = ((bf16[8,256,1024]{2,1,0:T(8,128)(2,1)}), bf16[8,256,1024]{2,1,0:T(8,128)(2,1)}, u32[]{:S(2)}, u32[]{:S(2)}) async-start(bf16[8,256,1024]{2,1,0:T(8,128)(2,1)} %bitcast.57), calls=%async_computation | async-start | bytes 8388608 | tf_op jit(solution)/shard_map/all_to_all | solution.py:1896
  458.9 33.0 %copy-start.9 = (bf16[3,4,64,2048]{3,2,1,0:T(8,128)(2,1)S(1)}, bf16[3,4,64,2048]{3,2,1,0:T(8,128)(2,1)}, u32[]{:S(2)}) copy-start(bf16[3,4,64,2048]{3,2,1,0:T(8,128)(2,1)} %get-tuple-element.55) | copy-start | bytes 9437188
  491.9 11.0 %copy-start.10 = (bf16[2048,768]{1,0:T(8,128)(2,1)S(1)}, bf16[2048,768]{1,0:T(8,128)(2,1)}, u32[]{:S(2)}) copy-start(bf16[2048,768]{1,0:T(8,128)(2,1)} %attend_back.1) | copy-start | bytes 9437188
  502.9 10.7 %copy-start.3 = (bf16[256,2048]{1,0:T(8,128)(2,1)S(1)}, bf16[256,2048]{1,0:T(8,128)(2,1)}, u32[]{:S(2)}) copy-start(bf16[256,2048]{1,0:T(8,128)(2,1)} %get-tuple-element.85) | copy-start | bytes 3145732
  502.9 10.7 %copy-start.4 = (bf16[256,2048]{1,0:T(8,128)(2,1)S(1)}, bf16[256,2048]{1,0:T(8,128)(2,1)}, u32[]{:S(2)}) copy-start(bf16[256,2048]{1,0:T(8,128)(2,1)} %get-tuple-element.86) | copy-start | bytes 3145732
  513.6 5.8 copy-start.7
  513.6 5.8 copy-start.8
  794.6 6.8 copy-start.5
  794.6 7.8 copy-start.2
  801.4 2.3 copy-start.1
  801.4 5.9 copy-start
Sparse Core Ops, SparseCore 0:
  9.9 93.7 all-gather.2
  144.8 73.6 all-gather.4
  366.4 154.1 all-reduce.1

commit v5 on v4

--- a/solution.py
+++ b/solution.py
@@ -116,25 +116,30 @@
     ]
 
 
-def gather_run(sends, between=None, later=None):
+def gather_run(sends, *between):
+    between = (*between, *([None] * 3))[:3]
+
+    def pause(i):
+        if between[i] is not None:
+            between[i]()
+
     sends[0].wait_recv()
     sends[5].start()
     sends[7].start()
     sends[1].wait_recv()
     sends[6].start()
     sends[8].start()
+    pause(0)
     sends[2].wait_recv()
     sends[9].start()
     sends[3].wait_recv()
     sends[10].start()
-    if between is not None:
-        between()
+    pause(1)
     sends[5].wait_recv()
     sends[11].start()
     sends[6].wait_recv()
     sends[12].start()
-    if later is not None:
-        later()
+    pause(2)
     for k in (4, 7, 8, 9, 10, 11, 12):
         sends[k].wait_recv()
     for send in sends:
@@ -275,7 +280,7 @@
             line.land(k - 1)
             line.start(k)
 
-    gather_run(sends, between)
+    gather_run(sends, None, between)
     line.land(depth - 2)
     for k in range(1, depth - 1):
         line.sent(k)
@@ -447,17 +452,17 @@
     for turn in turns:
         turn.wait_recv()
 
-    def between():
+    def hop_one():
         line_w.land(0)
         line_w.start(1)
-        line.start(0)
-
-    def later():
+
+    def hop_two():
         for k in range(2, depth - 1):
             line_w.land(k - 1)
             line_w.start(k)
-
-    gather_run(sends, between, later)
+        line.start(0)
+
+    gather_run(sends, hop_one, hop_two)
     line_w.land(depth - 2)
     line.land(0)
     for k in range(depth - 1):
@@ -1330,7 +1335,7 @@
     )(grad_ffn_in, middle, cot, attended, w_out, gain_mix[None], gain_ffn[None])
 
 
-CHUNK = 128
+CHUNK = 64
 
 
 def finish_kernel(
@@ -1573,7 +1578,9 @@
                 BF16
             )
 
-    lead = 4
+    lead = 2
+    far = 2 * (depth - 1)
+    steps = per_side + 2 * far
 
     def line_enter(c):
         for side in (0, 1):
@@ -1584,11 +1591,29 @@
                 go_up(2 * c + side, ahead).start()
 
     def line_step(t):
-        if t + lead < per_side:
+        @pl.when(t + lead < per_side)
+        def _():
             line_enter(t + lead)
+
+        back = []
         for side in (0, 1):
             rank, ahead, behind = ranks(side)
-            c = t - rank
+            c_back = t - 2 * far + 2 * rank
+            g_back = 2 * c_back + side
+            there = (c_back >= 0) & (c_back < per_side) & (rank < depth - 1)
+            back.append((there, g_back))
+
+            @pl.when(there)
+            def _():
+                go_down(g_back, ahead).wait_recv()
+
+            @pl.when(there & (rank > 0))
+            def _():
+                go_down(g_back, behind).start()
+
+        for side in (0, 1):
+            rank, ahead, behind = ranks(side)
+            c = t - 2 * rank
             g = 2 * c + side
             there = (c >= 0) & (c < per_side)
 
@@ -1605,21 +1630,16 @@
                 go_down(g, behind).start()
                 deliver(g)
 
-            c_back = t - 2 * (depth - 1) + rank
-            g_back = 2 * c_back + side
-            there = (c_back >= 0) & (c_back < per_side) & (rank < depth - 1)
-
-            @pl.when(there)
-            def _():
-                go_down(g_back, ahead).wait_recv()
-
-            @pl.when(there & (rank > 0))
-            def _():
-                go_down(g_back, behind).start()
+        for there, g_back in back:
 
             @pl.when(there)
             def _():
                 deliver(g_back)
+
+    def line_steps(first_step, last_step):
+        @pl.loop(first_step, last_step)
+        def _(t):
+            line_step(t)
 
     gain_here[...] = jnp.zeros_like(gain_here)
     for load in line_loads:
@@ -1627,21 +1647,17 @@
     for c in range(lead):
         line_enter(c)
     first(0)
-    line_step(0)
-    line_step(1)
+    line_steps(0, 8)
+    second(0)
+    line_steps(8, 9)
     first(1)
-    line_step(2)
-    line_step(3)
-    second(0)
-    line_step(4)
+    line_steps(9, 18)
+    last(0, store_line)
+    line_steps(18, 20)
+    second(1)
+    line_steps(20, 21)
     first(2)
-    line_step(5)
-    line_step(6)
-    last(0, store_line)
-    line_step(7)
-    second(1)
-    line_step(8)
-    line_step(9)
+    line_steps(21, 28)
     last(1, store_inputs)
 
     gain_here[1:2] = gm_ref[...]
@@ -1660,13 +1676,11 @@
     ]
     for send in rounds:
         send.start()
-    line_step(10)
+    line_steps(28, 32)
     second(2)
-    line_step(11)
-    line_step(12)
+    line_steps(32, 40)
     last(2, store_outputs)
-    for t in (13, 14, 15):
-        line_step(t)
+    line_steps(40, 42)
     for send in rounds:
         send.wait()
     total = gain_row[0]
@@ -1688,8 +1702,7 @@
     ]
     for send in rounds:
         send.start()
-    for t in range(16, per_side + 2 * (depth - 1)):
-        line_step(t)
+    line_steps(42, steps)
     for send in rounds:
         send.wait()
     total = gain_line[0]

time: 822 us -> 783 us (0.953)
  Pallas kernels: 680 us -> 638 us
    pallas_call x1, Pallas kernels: 256 us -> 230 us  [finish(): pl.pallas_call(functools.partial(finish_kernel, n, depth), out_shape=(jax...]
    pallas_call x1, Pallas kernels: 126 us -> 109 us  [start_exchange(): pl.pallas_call(functools.partial(start_kernel, n, depth), out_shape=(jax....]
  transfers between devices with their start and end apart: 4 -> 4, of which waited for: 0 -> 0; matrix products, arithmetic and copies ran while one was open for 9% -> 9% of each run, Pallas kernels for 77% -> 76%
where the time goes in v5:
time: 783 us; the launch traced here: 775 us
  Pallas kernels  638 us (81%)
  matrix products  80.7 us (10%)
  other arithmetic  23.2 us (3%)
  between operations  14.1 us (2%)
  local copies, waits for them, and re-layouts  13.7 us (2%)
    pallas_call x1, Pallas kernels, finish(): pl.pallas_call(functools.partial(finish_kernel, n, depth), out_shape=(jax...  230 us
    pallas_call x1, Pallas kernels, start_exchange(): pl.pallas_call(functools.partial(start_kernel, n, depth), out_shape=(jax....  109 us
    pallas_call x1, Pallas kernels, gather_seq(): pl.pallas_call(functools.partial(gather_kernel, n, depth), out_shape=(jax...  56 us
    dot_general x4, matrix products, tn(): lax.dot_general(a, b, (((0,), (0,)), ((), ())), preferred_element_type=F32)  44.7 us
    pallas_call x1, Pallas kernels, scatter_seq(): pl.pallas_call(scatter_kernel, out_shape=jax.ShapeDtypeStruct((rows, widt...  42.5 us
    pallas_call x1, Pallas kernels, attend_back(): pl.pallas_call(functools.partial(attend_back_kernel, heads), out_shape=ja...  33 us
    pallas_call x1, Pallas kernels, heads_to_tokens(): pl.pallas_call(functools.partial(heads_to_tokens_kernel, n), out_shape=ja...  30.6 us
    pallas_call x1, Pallas kernels, upper_pass(): pl.pallas_call(upper_kernel, grid=(length // rows,), out_shape=(jax.Shape...  28.5 us
  transfers between devices with their start and end apart: 4, of which 0 were waited for; matrix products, arithmetic and copies ran while one was open for 9% of the time, Pallas kernels for 76%

profile of v5, /device:TPU:0, one launch (start us, length us, event | category | flops | bytes accessed | tf_op | source)
XLA Modules:
  0.0 775.2 jit_solution(11829576556111555512)
XLA Ops:
  7.2 0.0 all-gather.3.cloned.1.call-start
  7.2 0.7 all-gather.3.cloned.1.call-update
  7.9 0.0 all-gather.5.cloned.1.call-start
  8.0 1.4 fusion.5
  9.4 1.4 convert_reduce_fusion
  10.8 1.6 fusion.2
  12.5 2.7 compare_select_fusion.2.start_ref
  15.1 0.6 subtract_convert_fusion.pos_ref
  15.7 2.6 fusion.4.x_ref
  18.3 109.5 %start_exchange.1 = (bf16[8,256,2048]{2,1,0:T(8,128)(2,1)}, bf16[3,4,64,2048]{3,2,1,0:T(8,128)(2,1)}, bf16[8,4,64,1024]{3,2,1,0:T(8,128)(2,1)}, f32[2048,128]{1,...) custom-call(bf16[256,2048]{1,0:T(8,128)(2,1)} %fusion.4.x_ref, ...), custom_call_target="tpu_custom_call" | custom-call | tf_op jit(solution)/shard_map/start_exchange/pallas_call | solution.py:507
  127.8 0.0 all-gather.5.cloned.1.call-update
  127.8 0.2 all-reduce.2.cloned.1.call-start
  128.1 0.1 slice.15
  128.2 0.6 and_select_fusion.first_ref
  128.8 14.2 %project_qkv.1 = (bf16[2048,256]{1,0:T(8,128)(2,1)}, bf16[2048,256]{1,0:T(8,128)(2,1)}, bf16[2048,256]{1,0:T(8,128)(2,1)}, bf16[256,2048]{1,0:T(8,128)(2,1)}, bf16[256,2048]{1,0:T(8,128)(2,1)}) custom-call(bf16[2048,2048]{1,0:T(8,128)(2,1)} %bitcast.75, bf16[768,2048]{1,0:T(8,128)(2,1)} %bitcast.81, f32[2048,128]{1,0:T(8,128)} %get-tuple-element.56.cq_ref, ...), custom_call_target="tpu_custom_call" | custom-call | flops 6442450944 | bytes 16777216 | tf_op jit(solution)/shard_map/project_qkv/pallas_call | solution.py:820
  142.9 24.1 %attend.1 = (bf16[2048,256]{1,0:T(8,128)(2,1)}, f32[8,4,256]{2,1,0:T(4,128)}) custom-call(s32[8]{0:T(128)} %and_select_fusion.first_ref, s32[1,2048]{1,0:T(1,128)} %copy-done.6, bf16[2048,256]{1,0:T(8,128)(2,1)} %get-tuple-element.60.q_ref, bf16[2048,256]{1,0:T(8,128)(2,1)} %get-tuple-element.61.k_ref, bf16[256,2048]{1,0:T(8,128)(2,1)} %get-tuple-element.64.vt_ref), custom_call_target="tpu_custom_call" | custom-call | flops 2147483648 | bytes 4194304 | tf_op jit(solution)/shard_map/attend/pallas_call | solution.py:900
  167.1 30.6 %heads_to_tokens.1.att_ref = bf16[256,2048]{1,0:T(8,128)(2,1)} custom-call(bf16[2048,256]{1,0:T(8,128)(2,1)} %get-tuple-element.65.x_ref.o_ref), custom_call_target="tpu_custom_call" | custom-call | tf_op jit(solution)/shard_map/heads_to_tokens/pallas_call | solution.py:720
  197.7 1.3 dynamic_slice.3
  199.0 13.8 %mix_pass.1 = (bf16[256,2048]{1,0:T(8,128)(2,1)}, f32[256,2048]{1,0:T(8,128)}, bf16[256,2048]{1,0:T(8,128)(2,1)}) custom-call(bf16[256,2048]{1,0:T(8,128)(2,1)} %heads_to_tokens.1.att_ref, bf16[256,2048]{1,0:T(8,128)(2,1)} %bitcast.50, bf16[2048,2048]{1,0:T(8,128)(2,1)} %all-gather.3.cloned.1.call-done.w_ref, f32[1,2048]{1,0:T(1,128)} %bitcast.62, ...), custom_call_target="tpu_custom_call" | custom-call | flops 2147483648 | bytes 14680064 | tf_op jit(solution)/shard_map/mix_pass/pallas_call | solution.py:1244
  212.8 56.0 %gather_seq.1 = (bf16[8,256,2048]{2,1,0:T(8,128)(2,1)}, bf16[8,4,64,1024]{3,2,1,0:T(8,128)(2,1)}) custom-call(bf16[256,2048]{1,0:T(8,128)(2,1)} %get-tuple-element.67.x_ref, bf16[8,4,64,1024]{3,2,1,0:T(8,128)(2,1)} %get-tuple-element.68.near_ref), custom_call_target="tpu_custom_call" | custom-call | tf_op jit(solution)/shard_map/gather_seq/pallas_call | solution.py:301
  268.8 0.0 all-gather.5.cloned.1.call-done.c_ref
  268.8 28.5 %upper_pass.1 = (f32[2048,1024]{1,0:T(8,128)}, bf16[2048,1024]{1,0:T(8,128)(2,1)}, f32[2048,1024]{1,0:T(8,128)}, f32[8,2048]{1,0:T(8,128)}) custom-call(bf16[2048,2048]{1,0:T(8,128)(2,1)} %bitcast.77, bf16[1024,2048]{1,0:T(8,128)(2,1)} %wu_ref.1, bf16[2048,2048]{1,0:T(8,128)(2,1)} %all-gather.5.cloned.1.call-done.c_ref, bf16[2048,1024]{1,0:T(8,128)(2,1)} %bitcast.79, ...), custom_call_target="tpu_custom_call" | custom-call | flops 17179869184 | bytes 50331648 | tf_op jit(solution)/shard_map/upper_pass/pallas_call | solution.py:1081
  297.3 9.6 %join_stats.1.stat_ref = f32[8,2048]{1,0:T(8,128)} custom-call(f32[8,2048]{1,0:T(8,128)} %get-tuple-element.75.x_ref), custom_call_target="tpu_custom_call" | custom-call | tf_op jit(solution)/shard_map/join_stats/pallas_call | solution.py:1192
  306.9 14.2 %hidden_pass.1 = (bf16[2048,1024]{1,0:T(8,128)(2,1)}, bf16[2048,1024]{1,0:T(8,128)(2,1)}, f32[1,1024]{1,0:T(1,128)}) custom-call(f32[2048,1024]{1,0:T(8,128)} %get-tuple-element.72.act_ref, bf16[2048,1024]{1,0:T(8,128)(2,1)} %get-tuple-element.73.slope_ref, f32[2048,1024]{1,0:T(8,128)} %get-tuple-element.74.grad_ref, f32[8,2048]{1,0:T(8,128)} %join_stats.1.stat_ref, ...), custom_call_target="tpu_custom_call" | custom-call | flops 25165824 | bytes 29360128 | tf_op jit(solution)/shard_map/hidden_pass/pallas_call | solution.py:1136
  321.1 14.1 %convolution_convert_fusion.4 = bf16[1024,2048]{1,0:T(8,128)(2,1)} fusion(bf16[2048,1024]{1,0:T(8,128)(2,1)} %get-tuple-element.80, bf16[2048,2048]{1,0:T(8,128)(2,1)} %bitcast.78), kind=kOutput, calls=%fused_computation.4 | convolution fusion | flops 8592031744 | bytes 16777216 | tf_op jit(solution)/shard_map/dot_general | solution.py:37
  335.2 14.2 %convolution_convert_fusion.5 = bf16[2048,1024]{1,0:T(8,128)(2,1)} fusion(bf16[2048,2048]{1,0:T(8,128)(2,1)} %all-gather.5.cloned.1.call-done.c_ref, bf16[2048,1024]{1,0:T(8,128)(2,1)} %get-tuple-element.78), kind=kOutput, calls=%fused_computation.5 | convolution fusion | flops 8592031744 | bytes 16777216 | tf_op jit(solution)/shard_map/dot_general | solution.py:37
  349.4 0.0 all-reduce.2.cloned.1.call-update
  349.4 13.9 %convolution_convert_fusion.3 = bf16[2048,2048]{1,0:T(8,128)(2,1)} fusion(bf16[2048,1024]{1,0:T(8,128)(2,1)} %get-tuple-element.80, bf16[1024,2048]{1,0:T(8,128)(2,1)} %wu_ref.1), kind=kOutput, calls=%fused_computation.3 | convolution fusion | flops 8594128896 | bytes 16777216 | tf_op jit(solution)/shard_map/dot_general | solution.py:29
  363.3 42.5 %scatter_seq.1.g_ref = f32[256,2048]{1,0:T(8,128)} custom-call(bf16[8,256,2048]{2,1,0:T(8,128)(2,1)} %bitcast.54), custom_call_target="tpu_custom_call" | custom-call | tf_op jit(solution)/shard_map/scatter_seq/pallas_call | solution.py:644
  405.8 17.7 %branch_pass.1 = (f32[256,2048]{1,0:T(8,128)}, bf16[256,2048]{1,0:T(8,128)(2,1)}, bf16[256,2048]{1,0:T(8,128)(2,1)}, f32[1,2048]{1,0:T(1,128)}, f32[1,2048]{1,0:T(1,128)}) custom-call(f32[256,2048]{1,0:T(8,128)} %scatter_seq.1.g_ref, f32[256,2048]{1,0:T(8,128)} %get-tuple-element.81.mid_ref, bf16[256,2048]{1,0:T(8,128)(2,1)} %bitcast.56, ...), custom_call_target="tpu_custom_call" | custom-call | flops 2147483648 | bytes 18874368 | tf_op jit(solution)/shard_map/branch_pass/pallas_call | solution.py:1313
  423.5 13.7 %tokens_to_heads.1.do_ref = bf16[2048,256]{1,0:T(8,128)(2,1)} custom-call(bf16[256,2048]{1,0:T(8,128)(2,1)} %get-tuple-element.82.x_ref), custom_call_target="tpu_custom_call" | custom-call | tf_op jit(solution)/shard_map/tokens_to_heads/pallas_call | solution.py:757
  437.2 5.0 all-to-all-start
  442.2 33.0 %attend_back.1 = bf16[2048,768]{1,0:T(8,128)(2,1)} custom-call(s32[8]{0:T(128)} %and_select_fusion.first_ref, s32[1,2048]{1,0:T(1,128)} %copy-done.6, bf16[2048,256]{1,0:T(8,128)(2,1)} %get-tuple-element.60.q_ref, bf16[2048,256]{1,0:T(8,128)(2,1)} %get-tuple-element.61.k_ref, bf16[256,2048]{1,0:T(8,128)(2,1)} %get-tuple-element.62.kt_ref, ...), custom_call_target="tpu_custom_call" | custom-call | flops 5368709120 | bytes 8388608 | tf_op jit(solution)/shard_map/attend_back/pallas_call | solution.py:1015
  475.2 11.0 %convolution_convert_fusion.1 = bf16[2048,2048]{1,0:T(8,128)(2,1)} fusion(bf16[2048,768]{1,0:T(8,128)(2,1)} %attend_back.1, bf16[768,2048]{1,0:T(8,128)(2,1)S(1)} %bitcast.82), kind=kOutput, calls=%fused_computation.1 | convolution fusion | flops 6446645248 | bytes 14680064 | tf_op jit(solution)/shard_map/dot_general | solution.py:29
  486.2 10.7 %convolution_convert_fusion.6 = bf16[768,2048]{1,0:T(8,128)(2,1)} fusion(bf16[2048,768]{1,0:T(8,128)(2,1)S(1)} %copy-done.10, bf16[2048,2048]{1,0:T(8,128)(2,1)} %bitcast.76), kind=kOutput, calls=%fused_computation.6 | convolution fusion | flops 6444023808 | bytes 14680064 | tf_op jit(solution)/shard_map/dot_general | solution.py:37
  496.9 5.8 convolution_convert_fusion.2
  502.7 11.0 %convolution_convert_fusion = bf16[2048,2048]{1,0:T(8,128)(2,1)} fusion(bf16[2048,1024]{1,0:T(8,128)(2,1)S(1)} %copy-done.8, bf16[2048,1024]{1,0:T(8,128)(2,1)S(1)} %bitcast.80), kind=kOutput, calls=%fused_computation | convolution fusion | flops 8594128896 | bytes 16777216 | tf_op jit(solution)/shard_map/dot_general | solution.py:33
  513.7 230.3 %finish.1 = (bf16[3,256,2048]{2,1,0:T(8,128)(2,1)}, f32[256,8192]{1,0:T(8,128)}, f32[256,2048]{1,0:T(8,128)}, f32[256,2048]{1,0:T(8,128)}, bf16[256,2048]{1,0:T(8,128)(2,1)}, /*index=5*/f32[16,2048]{1,0:T(8,128)}) custom-call(bf16[3,256,2048]{2,1,0:T(8,128)(2,1)} %bitcast.58, bf16[8,256,1024]{2,1,0:T(8,128)(2,1)} %all-to-all-done.gd_ref, ...), custom_call_target="tpu_custom_call" | custom-call | tf_op jit(solution)/shard_map/finish/pallas_call | solution.py:1782
  744.0 0.8 slice_bitcast_fusion
  744.7 0.6 copy.23
  745.4 1.6 fusion.8
  746.9 5.4 bitcast_convert_fusion
  752.4 6.8 convert_element_type.67
  759.2 1.0 copy.29
  760.2 1.3 copy.30
  761.5 1.3 copy.31
  762.8 2.3 copy-done
  765.1 3.4 copy.32
  (26 shorter events, 0.1 us)
Async XLA Ops:
  7.2 191.8 %all-gather.3.cloned.1.call-start = ((), (), s32[]{:S(2)}) async-start(), calls=%async_computation.1 | async-start | bytes 9437184 | tf_op jit(solution)/shard_map/all_gather | solution.py:1869
  7.9 260.9 %all-gather.5.cloned.1.call-start = ((), (), s32[]{:S(2)}) async-start(), calls=%async_computation.2 | async-start | bytes 9437184 | tf_op jit(solution)/shard_map/all_gather | solution.py:1883
  15.1 113.0 %copy-start.6 = (s32[1,2048]{1,0:T(1,128)}, s32[1,2048]{1,0:T(1,128)S(1)}, u32[]{:S(2)}) copy-start(s32[1,2048]{1,0:T(1,128)S(1)} %compare_select_fusion.2.start_ref) | copy-start | bytes 24580
  127.8 624.5 %all-reduce.2.cloned.1.call-start = ((), (), s32[]{:S(2)}) async-start(), calls=%async_computation.3 | async-start | bytes 8388608 | tf_op jit(solution)/shard_map/psum | solution.py:1900
  437.2 76.5 %all-to-all-start = ((bf16[8,256,1024]{2,1,0:T(8,128)(2,1)}), bf16[8,256,1024]{2,1,0:T(8,128)(2,1)}, u32[]{:S(2)}, u32[]{:S(2)}) async-start(bf16[8,256,1024]{2,1,0:T(8,128)(2,1)} %bitcast.57), calls=%async_computation | async-start | bytes 8388608 | tf_op jit(solution)/shard_map/all_to_all | solution.py:1909
  442.2 33.0 %copy-start.9 = (bf16[3,4,64,2048]{3,2,1,0:T(8,128)(2,1)S(1)}, bf16[3,4,64,2048]{3,2,1,0:T(8,128)(2,1)}, u32[]{:S(2)}) copy-start(bf16[3,4,64,2048]{3,2,1,0:T(8,128)(2,1)} %get-tuple-element.55) | copy-start | bytes 9437188
  475.2 11.0 %copy-start.10 = (bf16[2048,768]{1,0:T(8,128)(2,1)S(1)}, bf16[2048,768]{1,0:T(8,128)(2,1)}, u32[]{:S(2)}) copy-start(bf16[2048,768]{1,0:T(8,128)(2,1)} %attend_back.1) | copy-start | bytes 9437188
  486.2 10.7 %copy-start.3 = (bf16[256,2048]{1,0:T(8,128)(2,1)S(1)}, bf16[256,2048]{1,0:T(8,128)(2,1)}, u32[]{:S(2)}) copy-start(bf16[256,2048]{1,0:T(8,128)(2,1)} %get-tuple-element.85) | copy-start | bytes 3145732
  486.2 10.7 %copy-start.4 = (bf16[256,2048]{1,0:T(8,128)(2,1)S(1)}, bf16[256,2048]{1,0:T(8,128)(2,1)}, u32[]{:S(2)}) copy-start(bf16[256,2048]{1,0:T(8,128)(2,1)} %get-tuple-element.86) | copy-start | bytes 3145732
  496.9 5.8 copy-start.7
  496.9 5.8 copy-start.8
  752.4 6.8 copy-start.5
  752.4 7.8 %copy-start.2 = (f32[256,2048]{1,0:T(8,128)S(1)}, f32[256,2048]{1,0:T(8,128)}, u32[]{:S(2)}) copy-start(f32[256,2048]{1,0:T(8,128)} %get-tuple-element.92) | copy-start | bytes 6291460
  759.2 2.3 copy-start.1
  759.2 5.9 copy-start
Sparse Core Ops, SparseCore 0:
  9.9 93.7 all-gather.2
  128.0 73.6 all-gather.4
  349.5 154.1 all-reduce.1

commit v6 on v5

--- a/solution.py
+++ b/solution.py
@@ -229,99 +229,6 @@
                 self.message(side, k).wait_send()
 
 
-def gather_kernel(
-    n, depth, x_ref, near_ref, o_ref, all_ref, keep_ref, local_sem, send_sem, recv_sem, line_send, line_recv
-):
-    me, twin, near_x, near_y, _ = places()
-    z = lax.axis_index("batch")
-    own = pltpu.make_async_copy(x_ref, o_ref.at[me], local_sem.at[0])
-    own.start()
-
-    def load(shift):
-        return pltpu.make_async_copy(
-            near_ref.at[:, z + shift], keep_ref.at[1 + shift], local_sem.at[2 + shift]
-        )
-
-    def keep(shift):
-        return pltpu.make_async_copy(
-            keep_ref.at[1 + shift], all_ref.at[:, z + shift], local_sem.at[5 + shift]
-        )
-
-    def kept(shift):
-        return (z + shift >= 0) & (z + shift < depth)
-
-    for shift in (-1, 0, 1):
-
-        @pl.when(kept(shift))
-        def _():
-            load(shift).start()
-
-    meet_all(n, depth)
-    sends = gather_copies(x_ref, o_ref, send_sem, recv_sem)
-    for k in range(5):
-        sends[k].start()
-    line = Line(
-        depth,
-        lambda owner, k: (near_ref if k == 1 else all_ref).at[:, owner],
-        lambda owner: all_ref.at[:, owner],
-        line_send,
-        line_recv,
-    )
-    line.start(1)
-    for shift in (-1, 0, 1):
-
-        @pl.when(kept(shift))
-        def _():
-            load(shift).wait()
-            keep(shift).start()
-
-    def between():
-        for k in range(2, depth - 1):
-            line.land(k - 1)
-            line.start(k)
-
-    gather_run(sends, None, between)
-    line.land(depth - 2)
-    for k in range(1, depth - 1):
-        line.sent(k)
-    for shift in (-1, 0, 1):
-
-        @pl.when(kept(shift))
-        def _():
-            keep(shift).wait()
-
-    own.wait()
-
-
-def gather_seq(block, near, collective_id):
-    n, depth = lax.axis_size("seq"), lax.axis_size("batch")
-    rows, width = block.shape
-    if n != 8:
-        return lax.all_gather(block, "seq", axis=0, tiled=True), near
-    gathered, every = pl.pallas_call(
-        functools.partial(gather_kernel, n, depth),
-        out_shape=(
-            jax.ShapeDtypeStruct((n, rows, width), block.dtype),
-            jax.ShapeDtypeStruct(near.shape, near.dtype),
-        ),
-        in_specs=[INSIDE, ANY],
-        out_specs=(ANY, ANY),
-        scratch_shapes=[
-            pltpu.VMEM((3, n, *near.shape[2:]), near.dtype),
-            pltpu.SemaphoreType.DMA((7,)),
-            pltpu.SemaphoreType.DMA((13,)),
-            pltpu.SemaphoreType.DMA((13,)),
-            pltpu.SemaphoreType.DMA((2, depth)),
-            pltpu.SemaphoreType.DMA((2, depth)),
-        ],
-        compiler_params=pltpu.CompilerParams(
-            collective_id=collective_id, has_side_effects=True, vmem_limit_bytes=VMEM_LIMIT
-        ),
-        name="gather_seq",
-    )(block, near)
-    return gathered.reshape(n * rows, width), every.reshape(-1, near.shape[-1])
-
-
 def lane_tables(place):
     half = HEAD_DIM // 2
     lane = lax.broadcasted_iota(jnp.int32, (1, 128), 1)
@@ -463,11 +370,14 @@
         line.start(0)
 
     gather_run(sends, hop_one, hop_two)
+    line.land(0)
+    line.start(1)
     line_w.land(depth - 2)
-    line.land(0)
     for k in range(depth - 1):
         line_w.sent(k)
+    line.land(1)
     line.sent(0)
+    line.sent(1)
     for turn in turns:
         turn.wait_send()
     for j in range(3):
@@ -663,20 +573,65 @@
     )(partial.reshape(n, rows, width))
 
 
-def heads_to_tokens_kernel(n, x_ref, o_ref, keep, local_sem, send_sem, recv_sem):
+def heads_to_tokens_kernel(
+    n, depth, x_ref, near_ref, o_ref, extra_ref, keep, local_sem, send_sem, recv_sem, line_send, line_recv
+):
     me = lax.axis_index("seq")
+    z = lax.axis_index("batch")
     rows = o_ref.shape[0]
     cols = x_ref.shape[1]
-    exchange(
-        n,
-        me,
-        lambda k: x_ref.at[pl.ds(pl.multiple_of(k * rows, rows), rows)],
-        o_ref.at[:, pl.ds(pl.multiple_of(me * cols, cols), cols)],
-        keep,
-        local_sem,
-        send_sem,
-        recv_sem,
+    load = pltpu.make_async_copy(
+        x_ref.at[pl.ds(pl.multiple_of(me * rows, rows), rows)], keep, local_sem.at[0]
     )
+    target = o_ref.at[:, pl.ds(pl.multiple_of(me * cols, cols), cols)]
+    own = pltpu.make_async_copy(keep, target, local_sem.at[1])
+    load.start()
+    meet_all(n, depth)
+    copies = [
+        remote(
+            x_ref.at[pl.ds(pl.multiple_of(lax.rem(me + k, n) * rows, rows), rows)],
+            target,
+            send_sem.at[k],
+            recv_sem.at[k],
+            lax.rem(me + k, n),
+        )
+        for k in range(1, n)
+    ]
+    for copy in copies:
+        copy.start()
+
+    def last_hop(side):
+        owner, end = (depth - 1, 0) if side == 0 else (0, depth - 1)
+        return line_remote(
+            near_ref.at[:, owner],
+            extra_ref,
+            line_send.at[side],
+            line_recv.at[side],
+            end,
+        )
+
+    for side, sender in ((0, 1), (1, depth - 2)):
+
+        @pl.when(z == sender)
+        def _():
+            last_hop(side).start()
+
+    load.wait()
+    own.start()
+    for copy in copies:
+        copy.wait()
+    own.wait()
+    for side, sender, end in ((0, 1, 0), (1, depth - 2, depth - 1)):
+
+        @pl.when(z == sender)
+        def _():
+            last_hop(side).wait_send()
+
+        @pl.when(z == end)
+        def _():
+            line_remote(
+                extra_ref, extra_ref, line_send.at[side], line_recv.at[side], sender
+            ).wait_recv()
 
 
 def exchange(n, me, source, target, keep, local_sem, send_sem, recv_sem):
@@ -713,26 +668,34 @@
     own.wait()
 
 
-def heads_to_tokens(heads, collective_id):
-    n = lax.axis_size("seq")
+def heads_to_tokens(heads, near, collective_id):
+    n, depth = lax.axis_size("seq"), lax.axis_size("batch")
     total, cols = heads.shape
     rows = total // n
+    if n != 8 or depth != 4:
+        tokens = lax.all_to_all(heads, "seq", split_axis=0, concat_axis=1, tiled=True)
+        return tokens, None
     return pl.pallas_call(
-        functools.partial(heads_to_tokens_kernel, n),
-        out_shape=jax.ShapeDtypeStruct((rows, n * cols), heads.dtype),
-        in_specs=[ANY],
-        out_specs=ANY,
+        functools.partial(heads_to_tokens_kernel, n, depth),
+        out_shape=(
+            jax.ShapeDtypeStruct((rows, n * cols), heads.dtype),
+            jax.ShapeDtypeStruct((n, *near.shape[2:]), near.dtype),
+        ),
+        in_specs=[ANY, ANY],
+        out_specs=(ANY, ANY),
         scratch_shapes=[
             pltpu.VMEM((rows, cols), heads.dtype),
             pltpu.SemaphoreType.DMA((2,)),
             pltpu.SemaphoreType.DMA((n,)),
             pltpu.SemaphoreType.DMA((n,)),
+            pltpu.SemaphoreType.DMA((2,)),
+            pltpu.SemaphoreType.DMA((2,)),
         ],
         compiler_params=pltpu.CompilerParams(
             collective_id=collective_id, has_side_effects=True, vmem_limit_bytes=VMEM_LIMIT
         ),
         name="heads_to_tokens",
-    )(heads)
+    )(heads, near)
 
 
 def tokens_to_heads_kernel(n, x_ref, o_ref, keep, local_sem, send_sem, recv_sem):
@@ -1153,18 +1116,247 @@
     )(act, slope, grad, stats, gain)
 
 
-def stat_kernel(n, feats, x_ref, o_ref, held, send_sem, recv_sem):
-    me = lax.axis_index("seq")
-    held[me] = x_ref[...]
+def ffn_kernel(
+    n, depth, x_ref, wu_ref, cot_ref, near_ref, extra_ref, gain_ref,
+    full_ref, wd_out_ref, hid_ref, gu_ref, gg_ref,
+    rows_in, wd, cot_in, act, slope, grad, stat, held, results,
+    local_sem, cot_sem, out_sem, full_sem, send_sem, recv_sem, stat_send, stat_recv,
+):
+    me, twin, near_x, near_y, across = places()
+    z = lax.axis_index("batch")
+    rows = x_ref.shape[0]
+    feats = wu_ref.shape[0]
+    quarter = extra_ref.shape[1]
+
+    def cut(i, size=rows):
+        return pl.ds(pl.multiple_of(i * size, size), size)
+
+    own = pltpu.make_async_copy(x_ref, rows_in.at[me], local_sem.at[0])
+    own.start()
+    load_wd = pltpu.make_async_copy(near_ref, wd, local_sem.at[1])
+    load_wd.start()
+
+    def load_cot(i, slot):
+        return pltpu.make_async_copy(
+            cot_ref.at[cut(i)], cot_in.at[slot], cot_sem.at[slot]
+        )
+
+    load_cot(0, 0).start()
     meet([lax.rem(me + k, n) for k in range(1, n)])
-    copies = [
-        remote(x_ref, held.at[me], send_sem.at[k], recv_sem.at[k], lax.rem(me + k, n))
+    sends = gather_copies(x_ref, rows_in, send_sem, recv_sem)
+    for k in range(5):
+        sends[k].start()
+
+    load_wd.wait()
+    for end, owner in ((0, depth - 1), (depth - 1, 0)):
+
+        @pl.when(z == end)
+        def _():
+            fills = [
+                pltpu.make_async_copy(
+                    extra_ref.at[d],
+                    wd.at[pl.ds((d * depth + owner) * quarter, quarter)],
+                    full_sem.at[d],
+                )
+                for d in range(n)
+            ]
+            for fill in fills:
+                fill.start()
+            for fill in fills:
+                fill.wait()
+
+    keep_wd = pltpu.make_async_copy(wd, wd_out_ref, local_sem.at[2])
+    keep_wd.start()
+
+    def incoming(first, last):
+        @pl.loop(first, last)
+        def _(i):
+            slot = lax.rem(i, 2)
+
+            @pl.when(i + 1 < n)
+            def _():
+                load_cot(i + 1, 1 - slot).start()
+
+            load_cot(i, slot).wait()
+            grad[cut(i)] = nn(cot_in[slot], wd[...])
+
+    incoming(0, n - 2)
+    sends[0].wait_recv()
+    sends[5].start()
+    sends[7].start()
+    sends[1].wait_recv()
+    sends[6].start()
+    sends[8].start()
+    incoming(n - 2, n)
+    own.wait()
+
+    def keep(b):
+        return pltpu.make_async_copy(rows_in.at[b], full_ref.at[b], full_sem.at[b])
+
+    @pl.loop(0, n)
+    def _(i):
+        @pl.when(i == 1)
+        def _():
+            sends[4].wait_recv()
+
+        @pl.when(i == 2)
+        def _():
+            sends[2].wait_recv()
+            sends[9].start()
+            sends[3].wait_recv()
+            sends[10].start()
+
+        @pl.when(i == 4)
+        def _():
+            sends[7].wait_recv()
+            sends[9].wait_recv()
+
+        @pl.when(i == 5)
+        def _():
+            sends[8].wait_recv()
+            sends[10].wait_recv()
+            sends[5].wait_recv()
+            sends[11].start()
+            sends[6].wait_recv()
+            sends[12].start()
+
+        @pl.when(i == 7)
+        def _():
+            sends[11].wait_recv()
+            sends[12].wait_recv()
+
+        other = jnp.where((i == 1) | (i == 4) | (i == 5) | (i == 7), twin, 0)
+        place = jnp.where(i < 2, me, jnp.where(i >= 6, across, jnp.where(lax.rem(i, 2) == 0, near_x, near_y)))
+        b = place + other
+        keep(b).start()
+        at = cut(b)
+        upper = nt(rows_in[b], wu_ref[...])
+        below = 0.5 * (1.0 + lax.erf(upper * (0.5**0.5)))
+        value = upper * below
+        act[at] = value
+        slope[at] = (
+            below + upper * (jnp.exp(-0.5 * upper * upper) * ((2.0 * math.pi) ** -0.5))
+        ).astype(BF16)
+        part = grad[at] * gain_ref[...]
+        average = jnp.mean(value, axis=-1, keepdims=True)
+        centered = value - average
+        spread = jnp.sum(centered * centered, axis=-1, keepdims=True)
+        part_sum = jnp.sum(part, axis=-1, keepdims=True)
+        cross = jnp.sum(part * centered, axis=-1, keepdims=True)
+        lane = lax.broadcasted_iota(jnp.int32, (rows, 128), 1)
+        columns = jnp.where(
+            lane == 0,
+            average,
+            jnp.where(lane == 1, spread, jnp.where(lane == 2, part_sum, cross)),
+        )
+        stat[:, at] = columns.T[:8]
+
+    held[me] = stat[...]
+    rounds = [
+        remote(
+            stat, held.at[me], stat_send.at[k], stat_recv.at[k], lax.rem(me + k, n)
+        )
         for k in range(1, n)
     ]
-    for copy in copies:
-        copy.start()
-    for copy in copies:
-        copy.wait()
+    for send in rounds:
+        send.start()
+    for send in rounds:
+        send.wait()
+    join_rows(n, feats, held, stat)
+
+    def store(i, slot):
+        return [
+            pltpu.make_async_copy(
+                results.at[slot, j], ref.at[cut(i)], out_sem.at[slot, j]
+            )
+            for j, ref in enumerate((hid_ref, gu_ref))
+        ]
+
+    gg_ref[...] = jnp.zeros_like(gg_ref)
+
+    @pl.loop(0, n)
+    def _(i):
+        slot = lax.rem(i, 2)
+
+        @pl.when(i >= 2)
+        def _():
+            for copy in store(i - 2, slot):
+                copy.wait()
+
+        at = cut(i)
+        stats = stat[:, at].T
+        gain = gain_ref[...]
+        scale = stats[:, 1:2]
+        normal = (act[at] - stats[:, 0:1]) * scale
+        coming = grad[at]
+        results[slot, 0] = (normal * gain).astype(BF16)
+        back = scale * (coming * gain - stats[:, 2:3] - normal * stats[:, 3:4])
+        results[slot, 1] = (slope[at].astype(F32) * back).astype(BF16)
+        gg_ref[...] = gg_ref[...] + jnp.sum(coming * normal, axis=0, keepdims=True)
+        for copy in store(i, slot):
+            copy.start()
+
+    for i in (n - 2, n - 1):
+        for copy in store(i, i % 2):
+            copy.wait()
+    for b in range(n):
+        keep(b).wait()
+    keep_wd.wait()
+    for send in sends:
+        send.wait_send()
+
+
+def ffn_pass(ffn_in, w_up, cot, near, extra, gain, collective_id):
+    n, depth = lax.axis_size("seq"), lax.axis_size("batch")
+    rows, width = ffn_in.shape
+    feats = w_up.shape[0]
+    if n != 8 or depth != 4:
+        full = lax.all_gather(ffn_in, "seq", axis=0, tiled=True)
+        act, slope, grad, stat = upper_pass(full, w_up, cot, near, gain)
+        stats = join_stats(stat, feats, collective_id)
+        return (full, near, *hidden_pass(act, slope, grad, stats, gain))
+    length = n * rows
+    dma = pltpu.SemaphoreType.DMA
+    low = jax.ShapeDtypeStruct((length, feats), BF16)
+    full, w_down, hidden, grad_upper, gain_grad = pl.pallas_call(
+        functools.partial(ffn_kernel, n, depth),
+        out_shape=(
+            jax.ShapeDtypeStruct((n, rows, width), BF16),
+            jax.ShapeDtypeStruct((width, feats), BF16),
+            low,
+            low,
+            jax.ShapeDtypeStruct((1, feats), F32),
+        ),
+        in_specs=[INSIDE, INSIDE, ANY, ANY, ANY, INSIDE],
+        out_specs=(ANY, ANY, ANY, ANY, INSIDE),
+        scratch_shapes=[
+            pltpu.VMEM((n, rows, width), BF16),
+            pltpu.VMEM((width, feats), BF16),
+            pltpu.VMEM((2, rows, width), BF16),
+            pltpu.VMEM((length, feats), F32),
+            pltpu.VMEM((length, feats), BF16),
+            pltpu.VMEM((length, feats), F32),
+            pltpu.VMEM((8, length), F32),
+            pltpu.VMEM((n, 8, length), F32),
+            pltpu.VMEM((2, 2, rows, feats), BF16),
+            dma((3,)),
+            dma((2,)),
+            dma((2, 2)),
+            dma((n,)),
+            dma((13,)),
+            dma((13,)),
+            dma((n,)),
+            dma((n,)),
+        ],
+        compiler_params=pltpu.CompilerParams(
+            collective_id=collective_id, has_side_effects=True, vmem_limit_bytes=VMEM_LIMIT
+        ),
+        name="ffn_pass",
+    )(ffn_in, w_up, cot, near.reshape(width, feats), extra, gain)
+    return full.reshape(length, width), w_down, hidden, grad_upper, gain_grad
+
+
+def join_rows(n, feats, held, o_ref):
     average = held[0, 0:1]
     for d in range(1, n):
         average = average + held[d, 0:1]
@@ -1184,6 +1376,21 @@
     o_ref[2:3] = part * whole
     o_ref[3:4] = cross * scale * whole
     o_ref[4:8] = jnp.zeros((4, average.shape[1]), F32)
+
+
+def stat_kernel(n, feats, x_ref, o_ref, held, send_sem, recv_sem):
+    me = lax.axis_index("seq")
+    held[me] = x_ref[...]
+    meet([lax.rem(me + k, n) for k in range(1, n)])
+    copies = [
+        remote(x_ref, held.at[me], send_sem.at[k], recv_sem.at[k], lax.rem(me + k, n))
+        for k in range(1, n)
+    ]
+    for copy in copies:
+        copy.start()
+    for copy in copies:
+        copy.wait()
+    join_rows(n, feats, held, o_ref)
 
 
 def join_stats(stat, feats, collective_id):
@@ -1884,16 +2091,12 @@
 
     q, k, v, kt, vt = project_qkv(normed_full, w_heads, tables)
     attended_heads, lse = attend(first, start_row, q, k, vt)
-    attended = heads_to_tokens(attended_heads, 2)
+    attended, w_down_extra = heads_to_tokens(attended_heads, w_down_near, 2)
     mix_in, middle, ffn_in = mix_pass(attended, x_low, w_out_full, gain_mix, gain_ffn)
-    ffn_full, w_down_cols = gather_seq(ffn_in, w_down_near, 3)
-
     gain_here = lax.dynamic_slice_in_dim(gain_hidden, me * feats, feats, 0)[None, :]
-    act, slope, grad_hidden, stat = upper_pass(
-        ffn_full, w_up, cot_full, w_down_cols, gain_here
+    ffn_full, w_down_cols, hidden, grad_upper, grad_gain_here = ffn_pass(
+        ffn_in, w_up, cot_full, w_down_near, w_down_extra, gain_here, 3
     )
-    stats = join_stats(stat, feats, 8)
-    hidden, grad_upper, grad_gain_here = hidden_pass(act, slope, grad_hidden, stats, gain_here)
 
     grad_w_up = tn(grad_upper, ffn_full).astype(BF16)
     grad_upper, grad_w_up = lax.optimization_barrier((grad_upper, grad_w_up))

time: 783 us -> 767 us (0.980)
  Pallas kernels: 638 us -> 628 us
    pallas_call x5 -> x2, Pallas kernels: 139 us -> 92.5 us  [the longest x1 62.4 us: ffn_pass(): pl.pallas_call(functools.partial(ffn_kernel, n, depth), out_shape=(jax.Sh...]
    pallas_call x1, Pallas kernels: 109 us -> 132 us  [start_exchange(): pl.pallas_call(functools.partial(start_kernel, n, depth), out_shape=(jax....]
  transfers between devices with their start and end apart: 4 -> 4, of which waited for: 0 -> 0; matrix products, arithmetic and copies ran while one was open for 9% -> 10% of each run, Pallas kernels for 76% -> 74%
where the time goes in v6:
time: 767 us; the launch traced here: 765 us
  Pallas kernels  628 us (82%)
  matrix products  80.6 us (11%)
  other arithmetic  23.1 us (3%)
  between operations  14.1 us (2%)
  local copies, waits for them, and re-layouts  13.7 us (2%)
    pallas_call x1, Pallas kernels, finish(): pl.pallas_call(functools.partial(finish_kernel, n, depth), out_shape=(jax...  230 us
    pallas_call x1, Pallas kernels, start_exchange(): pl.pallas_call(functools.partial(start_kernel, n, depth), out_shape=(jax....  132 us
    pallas_call x1, Pallas kernels, ffn_pass(): pl.pallas_call(functools.partial(ffn_kernel, n, depth), out_shape=(jax.Sh...  62.4 us
    dot_general x4, matrix products, tn(): lax.dot_general(a, b, (((0,), (0,)), ((), ())), preferred_element_type=F32)  44.7 us
    pallas_call x1, Pallas kernels, scatter_seq(): pl.pallas_call(scatter_kernel, out_shape=jax.ShapeDtypeStruct((rows, widt...  42.7 us
    pallas_call x1, Pallas kernels, attend_back(): pl.pallas_call(functools.partial(attend_back_kernel, heads), out_shape=ja...  40.5 us
    pallas_call x1, Pallas kernels, attend(): pl.pallas_call(functools.partial(attend_kernel, heads), out_shape=(jax.Sh...  30.9 us
    pallas_call x1, Pallas kernels, heads_to_tokens(): pl.pallas_call(functools.partial(heads_to_tokens_kernel, n, depth), out_s...  30 us
  transfers between devices with their start and end apart: 4, of which 0 were waited for; matrix products, arithmetic and copies ran while one was open for 10% of the time, Pallas kernels for 74%

profile of v6, /device:TPU:0, one launch (start us, length us, event | category | flops | bytes accessed | tf_op | source)
XLA Modules:
  0.0 765.4 jit_solution(17779799454424601197)
XLA Ops:
  7.2 0.0 all-gather.3.cloned.1.call-start
  7.2 0.7 all-gather.3.cloned.1.call-update
  7.9 0.0 all-gather.5.cloned.1.call-start
  8.0 1.4 fusion.5
  9.4 1.4 convert_reduce_fusion
  10.8 1.6 fusion.2
  12.5 2.7 compare_select_fusion.2.start_ref
  15.1 0.0 copy-start.6
  15.1 0.6 subtract_convert_fusion.pos_ref
  15.7 2.6 fusion.4.x_ref
  18.3 131.9 %start_exchange.1 = (bf16[8,256,2048]{2,1,0:T(8,128)(2,1)}, bf16[3,4,64,2048]{3,2,1,0:T(8,128)(2,1)}, bf16[8,4,64,1024]{3,2,1,0:T(8,128)(2,1)}, f32[2048,128]{1,...) custom-call(bf16[256,2048]{1,0:T(8,128)(2,1)} %fusion.4.x_ref, ...), custom_call_target="tpu_custom_call" | custom-call | tf_op jit(solution)/shard_map/start_exchange/pallas_call | solution.py:417
  150.3 0.0 all-gather.5.cloned.1.call-update
  150.3 0.0 all-reduce.2.cloned.1.call-start
  150.4 0.0 copy-done.6
  150.4 0.1 slice.15
  150.5 1.3 dynamic_slice.3
  151.7 0.5 and_select_fusion.first_ref
  152.2 14.3 %project_qkv.1 = (bf16[2048,256]{1,0:T(8,128)(2,1)}, bf16[2048,256]{1,0:T(8,128)(2,1)}, bf16[2048,256]{1,0:T(8,128)(2,1)}, bf16[256,2048]{1,0:T(8,128)(2,1)}, bf16[256,2048]{1,0:T(8,128)(2,1)}) custom-call(bf16[2048,2048]{1,0:T(8,128)(2,1)} %bitcast.75, bf16[768,2048]{1,0:T(8,128)(2,1)} %bitcast.78, f32[2048,128]{1,0:T(8,128)} %get-tuple-element.54.cq_ref, ...), custom_call_target="tpu_custom_call" | custom-call | flops 6442450944 | bytes 16777216 | tf_op jit(solution)/shard_map/project_qkv/pallas_call | solution.py:783
  166.6 30.9 %attend.1 = (bf16[2048,256]{1,0:T(8,128)(2,1)}, f32[8,4,256]{2,1,0:T(4,128)}) custom-call(s32[8]{0:T(128)} %and_select_fusion.first_ref, s32[1,2048]{1,0:T(1,128)} %copy-done.6, bf16[2048,256]{1,0:T(8,128)(2,1)} %get-tuple-element.58.q_ref, bf16[2048,256]{1,0:T(8,128)(2,1)} %get-tuple-element.59.k_ref, bf16[256,2048]{1,0:T(8,128)(2,1)} %get-tuple-element.62.vt_ref), custom_call_target="tpu_custom_call" | custom-call | flops 2147483648 | bytes 4194304 | tf_op jit(solution)/shard_map/attend/pallas_call | solution.py:863
  197.4 30.0 %heads_to_tokens.1 = (bf16[256,2048]{1,0:T(8,128)(2,1)}, bf16[8,64,1024]{2,1,0:T(8,128)(2,1)}) custom-call(bf16[2048,256]{1,0:T(8,128)(2,1)} %get-tuple-element.63.x_ref.o_ref, bf16[8,4,64,1024]{3,2,1,0:T(8,128)(2,1)} %get-tuple-element.65.near_ref), custom_call_target="tpu_custom_call" | custom-call | tf_op jit(solution)/shard_map/heads_to_tokens/pallas_call | solution.py:678
  227.5 0.0 all-gather.3.cloned.1.call-done.w_ref
  227.5 13.8 %mix_pass.1 = (bf16[256,2048]{1,0:T(8,128)(2,1)}, f32[256,2048]{1,0:T(8,128)}, bf16[256,2048]{1,0:T(8,128)(2,1)}) custom-call(bf16[256,2048]{1,0:T(8,128)(2,1)} %get-tuple-element.66.att_ref, bf16[256,2048]{1,0:T(8,128)(2,1)} %bitcast.50, bf16[2048,2048]{1,0:T(8,128)(2,1)} %all-gather.3.cloned.1.call-done.w_ref, f32[1,2048]{1,0:T(1,128)} %bitcast.63, ...), custom_call_target="tpu_custom_call" | custom-call | flops 2147483648 | bytes 14680064 | tf_op jit(solution)/shard_map/mix_pass/pallas_call | solution.py:1451
  241.3 62.4 %ffn_pass.1 = (bf16[8,256,2048]{2,1,0:T(8,128)(2,1)}, bf16[2048,1024]{1,0:T(8,128)(2,1)}, bf16[2048,1024]{1,0:T(8,128)(2,1)}, bf16[2048,1024]{1,0:T(8,128)(2,1)}, f32[1,1024]{1,0:T(1,128)}) custom-call(bf16[256,2048]{1,0:T(8,128)(2,1)} %get-tuple-element.67.x_ref, bf16[1024,2048]{1,0:T(8,128)(2,1)} %wu_ref.1, ...), custom_call_target="tpu_custom_call" | custom-call | tf_op jit(solution)/shard_map/ffn_pass/pallas_call | solution.py:1321
  303.8 14.1 %convolution_convert_fusion.4 = bf16[1024,2048]{1,0:T(8,128)(2,1)} fusion(bf16[2048,1024]{1,0:T(8,128)(2,1)} %get-tuple-element.75, bf16[2048,2048]{1,0:T(8,128)(2,1)} %bitcast.77), kind=kOutput, calls=%fused_computation.4 | convolution fusion | flops 8592031744 | bytes 16777216 | tf_op jit(solution)/shard_map/dot_general | solution.py:37
  317.8 14.2 %convolution_convert_fusion.5 = bf16[2048,1024]{1,0:T(8,128)(2,1)} fusion(bf16[2048,2048]{1,0:T(8,128)(2,1)} %all-gather.5.cloned.1.call-done.cot_ref, bf16[2048,1024]{1,0:T(8,128)(2,1)} %get-tuple-element.73), kind=kOutput, calls=%fused_computation.5 | convolution fusion | flops 8592031744 | bytes 16777216 | tf_op jit(solution)/shard_map/dot_general | solution.py:37
  332.0 0.0 all-reduce.2.cloned.1.call-update
  332.0 13.9 %convolution_convert_fusion.3 = bf16[2048,2048]{1,0:T(8,128)(2,1)} fusion(bf16[2048,1024]{1,0:T(8,128)(2,1)} %get-tuple-element.75, bf16[1024,2048]{1,0:T(8,128)(2,1)} %wu_ref.1), kind=kOutput, calls=%fused_computation.3 | convolution fusion | flops 8594128896 | bytes 16777216 | tf_op jit(solution)/shard_map/dot_general | solution.py:29
  346.0 42.7 %scatter_seq.1.g_ref = f32[256,2048]{1,0:T(8,128)} custom-call(bf16[8,256,2048]{2,1,0:T(8,128)(2,1)} %bitcast.55), custom_call_target="tpu_custom_call" | custom-call | tf_op jit(solution)/shard_map/scatter_seq/pallas_call | solution.py:554
  388.6 17.6 %branch_pass.1 = (f32[256,2048]{1,0:T(8,128)}, bf16[256,2048]{1,0:T(8,128)(2,1)}, bf16[256,2048]{1,0:T(8,128)(2,1)}, f32[1,2048]{1,0:T(1,128)}, f32[1,2048]{1,0:T(1,128)}) custom-call(f32[256,2048]{1,0:T(8,128)} %scatter_seq.1.g_ref, f32[256,2048]{1,0:T(8,128)} %get-tuple-element.76.mid_ref, bf16[256,2048]{1,0:T(8,128)(2,1)} %bitcast.57, ...), custom_call_target="tpu_custom_call" | custom-call | flops 2147483648 | bytes 18874368 | tf_op jit(solution)/shard_map/branch_pass/pallas_call | solution.py:1520
  406.3 13.7 %tokens_to_heads.1.do_ref = bf16[2048,256]{1,0:T(8,128)(2,1)} custom-call(bf16[256,2048]{1,0:T(8,128)(2,1)} %get-tuple-element.77.x_ref), custom_call_target="tpu_custom_call" | custom-call | tf_op jit(solution)/shard_map/tokens_to_heads/pallas_call | solution.py:720
  420.0 5.0 all-to-all-start
  425.0 40.5 %attend_back.1 = bf16[2048,768]{1,0:T(8,128)(2,1)} custom-call(s32[8]{0:T(128)} %and_select_fusion.first_ref, s32[1,2048]{1,0:T(1,128)} %copy-done.6, bf16[2048,256]{1,0:T(8,128)(2,1)} %get-tuple-element.58.q_ref, bf16[2048,256]{1,0:T(8,128)(2,1)} %get-tuple-element.59.k_ref, bf16[256,2048]{1,0:T(8,128)(2,1)} %get-tuple-element.60.kt_ref, ...), custom_call_target="tpu_custom_call" | custom-call | flops 5368709120 | bytes 8388608 | tf_op jit(solution)/shard_map/attend_back/pallas_call | solution.py:978
  465.5 11.0 %convolution_convert_fusion.1 = bf16[2048,2048]{1,0:T(8,128)(2,1)} fusion(bf16[2048,768]{1,0:T(8,128)(2,1)} %attend_back.1, bf16[768,2048]{1,0:T(8,128)(2,1)S(1)} %bitcast.79), kind=kOutput, calls=%fused_computation.1 | convolution fusion | flops 6446645248 | bytes 14680064 | tf_op jit(solution)/shard_map/dot_general | solution.py:29
  476.5 10.7 %convolution_convert_fusion.6 = bf16[768,2048]{1,0:T(8,128)(2,1)} fusion(bf16[2048,768]{1,0:T(8,128)(2,1)S(1)} %copy-done.10, bf16[2048,2048]{1,0:T(8,128)(2,1)} %bitcast.76), kind=kOutput, calls=%fused_computation.6 | convolution fusion | flops 6444023808 | bytes 14680064 | tf_op jit(solution)/shard_map/dot_general | solution.py:37
  487.1 5.8 convolution_convert_fusion.2
  492.9 11.0 %convolution_convert_fusion = bf16[2048,2048]{1,0:T(8,128)(2,1)} fusion(bf16[2048,1024]{1,0:T(8,128)(2,1)S(1)} %copy-done.8, bf16[2048,1024]{1,0:T(8,128)(2,1)S(1)} %copy-done.7), kind=kOutput, calls=%fused_computation | convolution fusion | flops 8594128896 | bytes 16777216 | tf_op jit(solution)/shard_map/dot_general | solution.py:33
  503.9 0.0 all-to-all-done.gd_ref
  503.9 230.2 %finish.1 = (bf16[3,256,2048]{2,1,0:T(8,128)(2,1)}, f32[256,8192]{1,0:T(8,128)}, f32[256,2048]{1,0:T(8,128)}, f32[256,2048]{1,0:T(8,128)}, bf16[256,2048]{1,0:T(8,128)(2,1)}, /*index=5*/f32[16,2048]{1,0:T(8,128)}) custom-call(bf16[3,256,2048]{2,1,0:T(8,128)(2,1)} %bitcast.59, bf16[8,256,1024]{2,1,0:T(8,128)(2,1)} %all-to-all-done.gd_ref, ...), custom_call_target="tpu_custom_call" | custom-call | tf_op jit(solution)/shard_map/finish/pallas_call | solution.py:1989
  734.1 0.8 slice_bitcast_fusion
  734.9 0.6 copy.23
  735.5 1.6 fusion.8
  737.1 5.4 bitcast_convert_fusion
  742.5 6.8 convert_element_type.67
  749.4 1.0 copy.29
  750.3 1.3 copy.30
  751.7 1.3 copy.31
  753.0 2.3 copy-done
  755.3 3.4 copy.32
  (23 shorter events, 0.1 us)
Async XLA Ops:
  7.2 220.3 %all-gather.3.cloned.1.call-start = ((), (), s32[]{:S(2)}) async-start(), calls=%async_computation.1 | async-start | bytes 9437184 | tf_op jit(solution)/shard_map/all_gather | solution.py:2076
  7.9 233.4 %all-gather.5.cloned.1.call-start = ((), (), s32[]{:S(2)}) async-start(), calls=%async_computation.2 | async-start | bytes 9437184 | tf_op jit(solution)/shard_map/all_gather | solution.py:2090
  15.1 135.2 %copy-start.6 = (s32[1,2048]{1,0:T(1,128)}, s32[1,2048]{1,0:T(1,128)S(1)}, u32[]{:S(2)}) copy-start(s32[1,2048]{1,0:T(1,128)S(1)} %compare_select_fusion.2.start_ref) | copy-start | bytes 24580
  150.3 592.2 %all-reduce.2.cloned.1.call-start = ((), (), s32[]{:S(2)}) async-start(), calls=%async_computation.3 | async-start | bytes 8388608 | tf_op jit(solution)/shard_map/psum | solution.py:2103
  420.0 84.0 %all-to-all-start = ((bf16[8,256,1024]{2,1,0:T(8,128)(2,1)}), bf16[8,256,1024]{2,1,0:T(8,128)(2,1)}, u32[]{:S(2)}, u32[]{:S(2)}) async-start(bf16[8,256,1024]{2,1,0:T(8,128)(2,1)} %bitcast.58), calls=%async_computation | async-start | bytes 8388608 | tf_op jit(solution)/shard_map/all_to_all | solution.py:2112
  425.0 40.5 %copy-start.9 = (bf16[3,4,64,2048]{3,2,1,0:T(8,128)(2,1)S(1)}, bf16[3,4,64,2048]{3,2,1,0:T(8,128)(2,1)}, u32[]{:S(2)}) copy-start(bf16[3,4,64,2048]{3,2,1,0:T(8,128)(2,1)} %get-tuple-element.53) | copy-start | bytes 9437188
  465.5 11.0 %copy-start.10 = (bf16[2048,768]{1,0:T(8,128)(2,1)S(1)}, bf16[2048,768]{1,0:T(8,128)(2,1)}, u32[]{:S(2)}) copy-start(bf16[2048,768]{1,0:T(8,128)(2,1)} %attend_back.1) | copy-start | bytes 9437188
  476.5 10.7 %copy-start.3 = (bf16[256,2048]{1,0:T(8,128)(2,1)S(1)}, bf16[256,2048]{1,0:T(8,128)(2,1)}, u32[]{:S(2)}) copy-start(bf16[256,2048]{1,0:T(8,128)(2,1)} %get-tuple-element.80) | copy-start | bytes 3145732
  476.5 10.7 %copy-start.4 = (bf16[256,2048]{1,0:T(8,128)(2,1)S(1)}, bf16[256,2048]{1,0:T(8,128)(2,1)}, u32[]{:S(2)}) copy-start(bf16[256,2048]{1,0:T(8,128)(2,1)} %get-tuple-element.81) | copy-start | bytes 3145732
  487.1 5.8 copy-start.7
  487.1 5.8 copy-start.8
  742.5 6.8 copy-start.5
  742.5 7.8 %copy-start.2 = (f32[256,2048]{1,0:T(8,128)S(1)}, f32[256,2048]{1,0:T(8,128)}, u32[]{:S(2)}) copy-start(f32[256,2048]{1,0:T(8,128)} %get-tuple-element.88) | copy-start | bytes 6291460
  749.4 2.3 copy-start.1
  749.4 5.9 copy-start
Sparse Core Ops, SparseCore 0:
  9.9 93.7 all-gather.2
  150.4 69.2 all-gather.4
  332.1 157.2 all-reduce.1

commit v7 on v6

--- a/solution.py
+++ b/solution.py
@@ -248,7 +248,7 @@
     n, depth, x_ref, w_ref, wd_ref, pos_ref,
     o_ref, wt_ref, wc_ref, cq_ref, sq_ref, ck_ref, sk_ref,
     keep_w, keep_c, local_sem, send_sem, recv_sem, hop_send, hop_recv, col_send, col_recv,
-    line_send, line_recv, w_send, w_recv,
+    line_send, line_recv,
 ):
     z = lax.axis_index("batch")
     rows_z = wc_ref.shape[2]
@@ -267,36 +267,16 @@
     meet_all(n, depth)
     load_column.wait()
     own_column.start()
-    w_rows = pl.ds(
-        pl.multiple_of(z * wt_ref.shape[2], wt_ref.shape[2]), wt_ref.shape[2]
-    )
-
     def hop(j, part, target):
         return remote(
-            w_ref.at[j, w_rows], wt_ref.at[part, z], hop_send.at[j], hop_recv.at[part], target
+            w_ref.at[j], wt_ref.at[part], hop_send.at[j], hop_recv.at[part], target
         )
 
     def load(j):
-        return pltpu.make_async_copy(w_ref.at[j, w_rows], keep_w, local_sem.at[6])
+        return pltpu.make_async_copy(w_ref.at[j], keep_w, local_sem.at[6])
 
     def here(j, part):
-        return pltpu.make_async_copy(keep_w, wt_ref.at[part, z], local_sem.at[1 + j])
-
-    for j in range(3):
-        block = 3 * me + j
-        target = lax.rem(block, n)
-        for part in range(3):
-            inside = block // n == part
-
-            @pl.when(inside & (target != me))
-            def _():
-                hop(j, part, target).start()
-
-            @pl.when(inside & (target == me))
-            def _():
-                load(j).start()
-                load(j).wait()
-                here(j, part).start()
+        return pltpu.make_async_copy(keep_w, wt_ref.at[part], local_sem.at[1 + j])
 
     turns = [
         remote(
@@ -310,6 +290,20 @@
     ]
     for turn in turns:
         turn.start()
+    for j in range(3):
+        block = 3 * me + j
+        target = lax.rem(block, n)
+        for part in range(3):
+            inside = block // n == part
+
+            @pl.when(inside & (target != me))
+            def _():
+                hop(j, part, target).start()
+
+            @pl.when(inside & (target == me))
+            def _():
+                load(j).start()
+
     sends = gather_copies(x_ref, o_ref, send_sem, recv_sem)
     for k in range(5):
         sends[k].start()
@@ -322,13 +316,10 @@
         line_recv,
     )
 
-    line_w = Line(
-        depth,
-        lambda owner, k: wt_ref.at[:, owner],
-        lambda owner: wt_ref.at[:, owner],
-        w_send,
-        w_recv,
-    )
+    own_column.wait()
+    for turn in turns:
+        turn.wait_recv()
+    line.start(0)
     for j in range(3):
         block = 3 * me + j
         target = lax.rem(block, n)
@@ -336,16 +327,8 @@
 
             @pl.when((block // n == part) & (target == me))
             def _():
-                here(j, part).wait()
-
-    for part in range(3):
-        source = (part * n + me) // 3
-
-        @pl.when(source != me)
-        def _():
-            hop(0, part, source).wait_recv()
-
-    line_w.start(0)
+                load(j).wait()
+                here(j, part).start()
 
     @pl.loop(0, pos_ref.shape[0])
     def _(r):
@@ -355,39 +338,39 @@
         for ref, table in zip((cq_ref, sq_ref, ck_ref, sk_ref), tables, strict=True):
             ref[at] = table
 
-    own_column.wait()
-    for turn in turns:
-        turn.wait_recv()
-
-    def hop_one():
-        line_w.land(0)
-        line_w.start(1)
-
-    def hop_two():
-        for k in range(2, depth - 1):
-            line_w.land(k - 1)
-            line_w.start(k)
-        line.start(0)
-
-    gather_run(sends, hop_one, hop_two)
-    line.land(0)
-    line.start(1)
-    line_w.land(depth - 2)
+    def hand_on(k):
+        def step():
+            line.land(k - 1)
+            line.start(k)
+
+        return step
+
+    gather_run(sends, *[hand_on(k) for k in range(1, depth - 1)])
+    line.land(depth - 2)
     for k in range(depth - 1):
-        line_w.sent(k)
-    line.land(1)
-    line.sent(0)
-    line.sent(1)
+        line.sent(k)
     for turn in turns:
         turn.wait_send()
     for j in range(3):
         block = 3 * me + j
         target = lax.rem(block, n)
         for part in range(3):
-
-            @pl.when((block // n == part) & (target != me))
+            inside = block // n == part
+
+            @pl.when(inside & (target != me))
             def _():
                 hop(j, part, target).wait_send()
+
+            @pl.when(inside & (target == me))
+            def _():
+                here(j, part).wait()
+
+    for part in range(3):
+        source = (part * n + me) // 3
+
+        @pl.when(source != me)
+        def _():
+            hop(0, part, source).wait_recv()
 
     own.wait()
 
@@ -418,14 +401,14 @@
         functools.partial(start_kernel, n, depth),
         out_shape=(
             jax.ShapeDtypeStruct((n, rows, width), block.dtype),
-            jax.ShapeDtypeStruct((3, depth, piece // depth, width), w.dtype),
+            jax.ShapeDtypeStruct((3, piece, width), w.dtype),
             jax.ShapeDtypeStruct((n, depth, rows_z, cols), w_down.dtype),
             *([table] * 4),
         ),
         in_specs=[INSIDE, ANY, ANY, INSIDE],
         out_specs=(ANY, ANY, ANY, *([INSIDE] * 4)),
         scratch_shapes=[
-            pltpu.VMEM((piece // depth, width), BF16),
+            pltpu.VMEM((piece, width), BF16),
             pltpu.VMEM((rows_z, cols), BF16),
             pltpu.SemaphoreType.DMA((7,)),
             pltpu.SemaphoreType.DMA((13,)),
@@ -436,8 +419,6 @@
             pltpu.SemaphoreType.DMA((n,)),
             pltpu.SemaphoreType.DMA((2, depth)),
             pltpu.SemaphoreType.DMA((2, depth)),
-            pltpu.SemaphoreType.DMA((2, depth)),
-            pltpu.SemaphoreType.DMA((2, depth)),
         ],
         compiler_params=pltpu.CompilerParams(
             collective_id=collective_id, has_side_effects=True, vmem_limit_bytes=VMEM_LIMIT
@@ -447,7 +428,7 @@
     return (
         gathered.reshape(n * rows, width),
         turned.reshape(3 * piece, width),
-        columns,
+        columns.reshape(-1, cols),
         tables,
     )
 
@@ -573,65 +554,20 @@
     )(partial.reshape(n, rows, width))
 
 
-def heads_to_tokens_kernel(
-    n, depth, x_ref, near_ref, o_ref, extra_ref, keep, local_sem, send_sem, recv_sem, line_send, line_recv
-):
+def heads_to_tokens_kernel(n, x_ref, o_ref, keep, local_sem, send_sem, recv_sem):
     me = lax.axis_index("seq")
-    z = lax.axis_index("batch")
     rows = o_ref.shape[0]
     cols = x_ref.shape[1]
-    load = pltpu.make_async_copy(
-        x_ref.at[pl.ds(pl.multiple_of(me * rows, rows), rows)], keep, local_sem.at[0]
+    exchange(
+        n,
+        me,
+        lambda k: x_ref.at[pl.ds(pl.multiple_of(k * rows, rows), rows)],
+        o_ref.at[:, pl.ds(pl.multiple_of(me * cols, cols), cols)],
+        keep,
+        local_sem,
+        send_sem,
+        recv_sem,
     )
-    target = o_ref.at[:, pl.ds(pl.multiple_of(me * cols, cols), cols)]
-    own = pltpu.make_async_copy(keep, target, local_sem.at[1])
-    load.start()
-    meet_all(n, depth)
-    copies = [
-        remote(
-            x_ref.at[pl.ds(pl.multiple_of(lax.rem(me + k, n) * rows, rows), rows)],
-            target,
-            send_sem.at[k],
-            recv_sem.at[k],
-            lax.rem(me + k, n),
-        )
-        for k in range(1, n)
-    ]
-    for copy in copies:
-        copy.start()
-
-    def last_hop(side):
-        owner, end = (depth - 1, 0) if side == 0 else (0, depth - 1)
-        return line_remote(
-            near_ref.at[:, owner],
-            extra_ref,
-            line_send.at[side],
-            line_recv.at[side],
-            end,
-        )
-
-    for side, sender in ((0, 1), (1, depth - 2)):
-
-        @pl.when(z == sender)
-        def _():
-            last_hop(side).start()
-
-    load.wait()
-    own.start()
-    for copy in copies:
-        copy.wait()
-    own.wait()
-    for side, sender, end in ((0, 1, 0), (1, depth - 2, depth - 1)):
-
-        @pl.when(z == sender)
-        def _():
-            last_hop(side).wait_send()
-
-        @pl.when(z == end)
-        def _():
-            line_remote(
-                extra_ref, extra_ref, line_send.at[side], line_recv.at[side], sender
-            ).wait_recv()
 
 
 def exchange(n, me, source, target, keep, local_sem, send_sem, recv_sem):
@@ -668,34 +604,26 @@
     own.wait()
 
 
-def heads_to_tokens(heads, near, collective_id):
-    n, depth = lax.axis_size("seq"), lax.axis_size("batch")
+def heads_to_tokens(heads, collective_id):
+    n = lax.axis_size("seq")
     total, cols = heads.shape
     rows = total // n
-    if n != 8 or depth != 4:
-        tokens = lax.all_to_all(heads, "seq", split_axis=0, concat_axis=1, tiled=True)
-        return tokens, None
     return pl.pallas_call(
-        functools.partial(heads_to_tokens_kernel, n, depth),
-        out_shape=(
-            jax.ShapeDtypeStruct((rows, n * cols), heads.dtype),
-            jax.ShapeDtypeStruct((n, *near.shape[2:]), near.dtype),
-        ),
-        in_specs=[ANY, ANY],
-        out_specs=(ANY, ANY),
+        functools.partial(heads_to_tokens_kernel, n),
+        out_shape=jax.ShapeDtypeStruct((rows, n * cols), heads.dtype),
+        in_specs=[ANY],
+        out_specs=ANY,
         scratch_shapes=[
             pltpu.VMEM((rows, cols), heads.dtype),
             pltpu.SemaphoreType.DMA((2,)),
             pltpu.SemaphoreType.DMA((n,)),
             pltpu.SemaphoreType.DMA((n,)),
-            pltpu.SemaphoreType.DMA((2,)),
-            pltpu.SemaphoreType.DMA((2,)),
         ],
         compiler_params=pltpu.CompilerParams(
             collective_id=collective_id, has_side_effects=True, vmem_limit_bytes=VMEM_LIMIT
         ),
         name="heads_to_tokens",
-    )(heads, near)
+    )(heads)
 
 
 def tokens_to_heads_kernel(n, x_ref, o_ref, keep, local_sem, send_sem, recv_sem):
@@ -1117,23 +1045,21 @@
 
 
 def ffn_kernel(
-    n, depth, x_ref, wu_ref, cot_ref, near_ref, extra_ref, gain_ref,
-    full_ref, wd_out_ref, hid_ref, gu_ref, gg_ref,
+    n, x_ref, wu_ref, cot_ref, wd_ref, gain_ref,
+    full_ref, hid_ref, gu_ref, gg_ref,
     rows_in, wd, cot_in, act, slope, grad, stat, held, results,
     local_sem, cot_sem, out_sem, full_sem, send_sem, recv_sem, stat_send, stat_recv,
 ):
     me, twin, near_x, near_y, across = places()
-    z = lax.axis_index("batch")
     rows = x_ref.shape[0]
     feats = wu_ref.shape[0]
-    quarter = extra_ref.shape[1]
 
     def cut(i, size=rows):
         return pl.ds(pl.multiple_of(i * size, size), size)
 
     own = pltpu.make_async_copy(x_ref, rows_in.at[me], local_sem.at[0])
     own.start()
-    load_wd = pltpu.make_async_copy(near_ref, wd, local_sem.at[1])
+    load_wd = pltpu.make_async_copy(wd_ref, wd, local_sem.at[1])
     load_wd.start()
 
     def load_cot(i, slot):
@@ -1148,26 +1074,6 @@
         sends[k].start()
 
     load_wd.wait()
-    for end, owner in ((0, depth - 1), (depth - 1, 0)):
-
-        @pl.when(z == end)
-        def _():
-            fills = [
-                pltpu.make_async_copy(
-                    extra_ref.at[d],
-                    wd.at[pl.ds((d * depth + owner) * quarter, quarter)],
-                    full_sem.at[d],
-                )
-                for d in range(n)
-            ]
-            for fill in fills:
-                fill.start()
-            for fill in fills:
-                fill.wait()
-
-    keep_wd = pltpu.make_async_copy(wd, wd_out_ref, local_sem.at[2])
-    keep_wd.start()
-
     def incoming(first, last):
         @pl.loop(first, last)
         def _(i):
@@ -1301,34 +1207,32 @@
             copy.wait()
     for b in range(n):
         keep(b).wait()
-    keep_wd.wait()
     for send in sends:
         send.wait_send()
 
 
-def ffn_pass(ffn_in, w_up, cot, near, extra, gain, collective_id):
-    n, depth = lax.axis_size("seq"), lax.axis_size("batch")
+def ffn_pass(ffn_in, w_up, cot, w_down, gain, collective_id):
+    n = lax.axis_size("seq")
     rows, width = ffn_in.shape
     feats = w_up.shape[0]
-    if n != 8 or depth != 4:
+    if n != 8:
         full = lax.all_gather(ffn_in, "seq", axis=0, tiled=True)
-        act, slope, grad, stat = upper_pass(full, w_up, cot, near, gain)
+        act, slope, grad, stat = upper_pass(full, w_up, cot, w_down, gain)
         stats = join_stats(stat, feats, collective_id)
-        return (full, near, *hidden_pass(act, slope, grad, stats, gain))
+        return (full, *hidden_pass(act, slope, grad, stats, gain))
     length = n * rows
     dma = pltpu.SemaphoreType.DMA
     low = jax.ShapeDtypeStruct((length, feats), BF16)
-    full, w_down, hidden, grad_upper, gain_grad = pl.pallas_call(
-        functools.partial(ffn_kernel, n, depth),
+    full, hidden, grad_upper, gain_grad = pl.pallas_call(
+        functools.partial(ffn_kernel, n),
         out_shape=(
             jax.ShapeDtypeStruct((n, rows, width), BF16),
-            jax.ShapeDtypeStruct((width, feats), BF16),
             low,
             low,
             jax.ShapeDtypeStruct((1, feats), F32),
         ),
-        in_specs=[INSIDE, INSIDE, ANY, ANY, ANY, INSIDE],
-        out_specs=(ANY, ANY, ANY, ANY, INSIDE),
+        in_specs=[INSIDE, INSIDE, ANY, ANY, INSIDE],
+        out_specs=(ANY, ANY, ANY, INSIDE),
         scratch_shapes=[
             pltpu.VMEM((n, rows, width), BF16),
             pltpu.VMEM((width, feats), BF16),
@@ -1339,7 +1243,7 @@
             pltpu.VMEM((8, length), F32),
             pltpu.VMEM((n, 8, length), F32),
             pltpu.VMEM((2, 2, rows, feats), BF16),
-            dma((3,)),
+            dma((2,)),
             dma((2,)),
             dma((2, 2)),
             dma((n,)),
@@ -1352,8 +1256,8 @@
             collective_id=collective_id, has_side_effects=True, vmem_limit_bytes=VMEM_LIMIT
         ),
         name="ffn_pass",
-    )(ffn_in, w_up, cot, near.reshape(width, feats), extra, gain)
-    return full.reshape(length, width), w_down, hidden, grad_upper, gain_grad
+    )(ffn_in, w_up, cot, w_down, gain)
+    return full.reshape(length, width), hidden, grad_upper, gain_grad
 
 
 def join_rows(n, feats, held, o_ref):
@@ -1411,6 +1315,33 @@
         ),
         name="join_stats",
     )(stat)
+
+
+def weight_kernel(a_ref, b_ref, o_ref):
+    o_ref[...] = tn(a_ref[...], b_ref[...]).astype(BF16)
+
+
+def weight_grad(a, b):
+    length, outs = a.shape
+    cols = b.shape[1]
+    block = 2 * TILE
+    return pl.pallas_call(
+        weight_kernel,
+        grid=(outs // block,),
+        out_shape=jax.ShapeDtypeStruct((outs, cols), BF16),
+        in_specs=[
+            pl.BlockSpec((length, block), lambda i: (0, i)),
+            pl.BlockSpec((length, cols), lambda i: (0, 0)),
+        ],
+        out_specs=pl.BlockSpec((block, cols), lambda i: (i, 0)),
+        compiler_params=pltpu.CompilerParams(vmem_limit_bytes=VMEM_LIMIT),
+        cost_estimate=pl.CostEstimate(
+            flops=2 * length * outs * cols,
+            bytes_accessed=2 * (length * outs + length * cols + outs * cols),
+            transcendentals=0,
+        ),
+        name="weight_grad",
+    )(a, b)
 
 
 STEP = 32
@@ -2083,25 +2014,24 @@
     first = start[::TILE] // TILE
     start_row = start[None, :]
 
-    normed_full, w_heads, w_down_near, tables = start_exchange(
+    normed_full, w_heads, w_down_cols, tables = start_exchange(
         normed, w_qkv, w_down, positions.astype(F32), 1
     )
-    cot_late, _ = lax.optimization_barrier((cot, w_heads))
-    cot_full = lax.all_gather(cot_late, "seq", axis=0, tiled=True)
+    cot_full = lax.all_gather(lax.optimization_barrier(cot), "seq", axis=0, tiled=True)
 
     q, k, v, kt, vt = project_qkv(normed_full, w_heads, tables)
     attended_heads, lse = attend(first, start_row, q, k, vt)
-    attended, w_down_extra = heads_to_tokens(attended_heads, w_down_near, 2)
+    attended = heads_to_tokens(attended_heads, 2)
     mix_in, middle, ffn_in = mix_pass(attended, x_low, w_out_full, gain_mix, gain_ffn)
     gain_here = lax.dynamic_slice_in_dim(gain_hidden, me * feats, feats, 0)[None, :]
-    ffn_full, w_down_cols, hidden, grad_upper, grad_gain_here = ffn_pass(
-        ffn_in, w_up, cot_full, w_down_near, w_down_extra, gain_here, 3
+    ffn_full, hidden, grad_upper, grad_gain_here = ffn_pass(
+        ffn_in, w_up, cot_full, w_down_cols, gain_here, 3
     )
 
     grad_w_up = tn(grad_upper, ffn_full).astype(BF16)
     grad_upper, grad_w_up = lax.optimization_barrier((grad_upper, grad_w_up))
     grad_w_up = lax.psum(grad_w_up, "batch")
-    grad_w_down = tn(cot_full, hidden).astype(BF16).reshape(n, local, feats)
+    grad_w_down = weight_grad(cot_full, hidden).reshape(n, local, feats)
     grad_upper, grad_w_down = lax.optimization_barrier((grad_upper, grad_w_down))
     grad_ffn_in = scatter_seq(nn(grad_upper, w_up).astype(BF16), 4)
     grad_middle, grad_branch, grad_att, grad_gain_ffn, grad_gain_mix = branch_pass(

time: 767 us -> 754 us (0.983)
  matrix products: 80.6 us -> 66.7 us
    dot_general x4 -> x3, matrix products: 44.7 us -> 30.7 us  [tn(): lax.dot_general(a, b, (((0,), (0,)), ((), ())), preferred_element_type=F32)]
    pallas_call x2 -> x3, Pallas kernels: 92.5 us -> 97.5 us  [the longest x1 61.8 us: ffn_pass(): pl.pallas_call(functools.partial(ffn_kernel, n), out_shape=(jax.ShapeDtyp...]
where the time goes in v7:
time: 754 us; the launch traced here: 747 us
  Pallas kernels  624 us (83%)
  matrix products  66.7 us (9%)
  other arithmetic  22 us (3%)
  between operations  14.3 us (2%)
  local copies, waits for them, and re-layouts  13.7 us (2%)
    pallas_call x1, Pallas kernels, finish(): pl.pallas_call(functools.partial(finish_kernel, n, depth), out_shape=(jax...  228 us
    pallas_call x1, Pallas kernels, start_exchange(): pl.pallas_call(functools.partial(start_kernel, n, depth), out_shape=(jax....  126 us
    pallas_call x1, Pallas kernels, ffn_pass(): pl.pallas_call(functools.partial(ffn_kernel, n), out_shape=(jax.ShapeDtyp...  61.8 us
    pallas_call x1, Pallas kernels, scatter_seq(): pl.pallas_call(scatter_kernel, out_shape=jax.ShapeDtypeStruct((rows, widt...  42.2 us
    pallas_call x1, Pallas kernels, attend_back(): pl.pallas_call(functools.partial(attend_back_kernel, heads), out_shape=ja...  40.5 us
    dot_general x3, matrix products, tn(): lax.dot_general(a, b, (((0,), (0,)), ((), ())), preferred_element_type=F32)  30.7 us
    pallas_call x1, Pallas kernels, attend(): pl.pallas_call(functools.partial(attend_kernel, heads), out_shape=(jax.Sh...  30.7 us
    dot_general x2, matrix products, nn(): lax.dot_general(a, b, (((1,), (0,)), ((), ())), preferred_element_type=F32)  24.9 us
  transfers between devices with their start and end apart: 4, of which 0 were waited for; matrix products, arithmetic and copies ran while one was open for 10% of the time, Pallas kernels for 74%

profile of v7, /device:TPU:0, one launch (start us, length us, event | category | flops | bytes accessed | tf_op | source)
XLA Modules:
  0.0 747.4 jit_solution(9304895065891705804)
XLA Ops:
  7.2 0.0 copy-start
  7.2 0.0 copy-start.8
  7.2 0.0 all-gather.3.cloned.1.call-start
  7.2 0.7 all-gather.3.cloned.1.call-update
  7.9 0.0 all-gather.5.cloned.1.call-start
  8.0 0.7 all-gather.5.cloned.1.call-update
  8.7 0.0 all-reduce.2.cloned.1.call-start
  8.7 1.4 fusion.5
  10.1 2.7 compare_select_fusion.2.start_ref
  12.8 0.0 copy-start.9
  12.8 0.1 slice.15
  12.9 1.4 convert_reduce_fusion
  14.3 1.6 fusion.2
  16.0 0.6 subtract_convert_fusion.pos_ref
  16.6 1.4 fusion.4.x_ref
  18.0 125.7 %start_exchange.1 = (bf16[8,256,2048]{2,1,0:T(8,128)(2,1)}, bf16[3,256,2048]{2,1,0:T(8,128)(2,1)}, bf16[8,4,64,1024]{3,2,1,0:T(8,128)(2,1)}, f32[2048,128]{1,0:T...) custom-call(bf16[256,2048]{1,0:T(8,128)(2,1)} %fusion.4.x_ref, ...), custom_call_target="tpu_custom_call" | custom-call | tf_op jit(solution)/shard_map/start_exchange/pallas_call | solution.py:400
  143.7 0.6 and_select_fusion.first_ref
  144.3 14.3 %project_qkv.1 = (bf16[2048,256]{1,0:T(8,128)(2,1)}, bf16[2048,256]{1,0:T(8,128)(2,1)}, bf16[2048,256]{1,0:T(8,128)(2,1)}, bf16[256,2048]{1,0:T(8,128)(2,1)}, bf16[256,2048]{1,0:T(8,128)(2,1)}) custom-call(bf16[2048,2048]{1,0:T(8,128)(2,1)} %bitcast.74, bf16[768,2048]{1,0:T(8,128)(2,1)} %bitcast.77, f32[2048,128]{1,0:T(8,128)} %get-tuple-element.50.cq_ref, ...), custom_call_target="tpu_custom_call" | custom-call | flops 6442450944 | bytes 16777216 | tf_op jit(solution)/shard_map/project_qkv/pallas_call | solution.py:711
  158.6 30.7 %attend.1 = (bf16[2048,256]{1,0:T(8,128)(2,1)}, f32[8,4,256]{2,1,0:T(4,128)}) custom-call(s32[8]{0:T(128)} %and_select_fusion.first_ref, s32[1,2048]{1,0:T(1,128)} %copy-done.9, bf16[2048,256]{1,0:T(8,128)(2,1)} %get-tuple-element.54.q_ref, bf16[2048,256]{1,0:T(8,128)(2,1)} %get-tuple-element.55.k_ref, bf16[256,2048]{1,0:T(8,128)(2,1)} %get-tuple-element.58.vt_ref), custom_call_target="tpu_custom_call" | custom-call | flops 2147483648 | bytes 4194304 | tf_op jit(solution)/shard_map/attend/pallas_call | solution.py:791
  189.3 22.5 %heads_to_tokens.1.att_ref = bf16[256,2048]{1,0:T(8,128)(2,1)} custom-call(bf16[2048,256]{1,0:T(8,128)(2,1)} %get-tuple-element.59.x_ref.o_ref), custom_call_target="tpu_custom_call" | custom-call | tf_op jit(solution)/shard_map/heads_to_tokens/pallas_call | solution.py:611
  211.7 1.3 dynamic_slice.3
  213.0 13.8 %mix_pass.1 = (bf16[256,2048]{1,0:T(8,128)(2,1)}, f32[256,2048]{1,0:T(8,128)}, bf16[256,2048]{1,0:T(8,128)(2,1)}) custom-call(bf16[256,2048]{1,0:T(8,128)(2,1)} %heads_to_tokens.1.att_ref, bf16[256,2048]{1,0:T(8,128)(2,1)} %bitcast.48, bf16[2048,2048]{1,0:T(8,128)(2,1)} %all-gather.3.cloned.1.call-done.w_ref, f32[1,2048]{1,0:T(1,128)} %bitcast.62, ...), custom_call_target="tpu_custom_call" | custom-call | flops 2147483648 | bytes 14680064 | tf_op jit(solution)/shard_map/mix_pass/pallas_call | solution.py:1382
  226.8 61.8 %ffn_pass.1 = (bf16[8,256,2048]{2,1,0:T(8,128)(2,1)}, bf16[2048,1024]{1,0:T(8,128)(2,1)}, bf16[2048,1024]{1,0:T(8,128)(2,1)}, f32[1,1024]{1,0:T(1,128)}) custom-call(bf16[256,2048]{1,0:T(8,128)(2,1)} %get-tuple-element.61.x_ref, bf16[1024,2048]{1,0:T(8,128)(2,1)} %wu_ref.1, bf16[2048,2048]{1,0:T(8,128)(2,1)} %all-gather.5.cloned.1.call-done.cot_ref.a_ref, ...), custom_call_target="tpu_custom_call" | custom-call | tf_op jit(solution)/shard_map/ffn_pass/pallas_call | solution.py:1226
  288.6 14.3 %convolution_convert_fusion.4 = bf16[1024,2048]{1,0:T(8,128)(2,1)} fusion(bf16[2048,1024]{1,0:T(8,128)(2,1)} %get-tuple-element.68, bf16[2048,2048]{1,0:T(8,128)(2,1)} %bitcast.76), kind=kOutput, calls=%fused_computation.4 | convolution fusion | flops 8592031744 | bytes 16777216 | tf_op jit(solution)/shard_map/dot_general | solution.py:37
  302.9 13.3 %weight_grad.1 = bf16[2048,1024]{1,0:T(8,128)(2,1)} custom-call(bf16[2048,2048]{1,0:T(8,128)(2,1)} %all-gather.5.cloned.1.call-done.cot_ref.a_ref, bf16[2048,1024]{1,0:T(8,128)(2,1)} %get-tuple-element.66.b_ref), custom_call_target="tpu_custom_call" | custom-call | flops 8589934592 | bytes 16777216 | tf_op jit(solution)/shard_map/weight_grad/pallas_call | solution.py:1328
  316.2 0.0 all-reduce.2.cloned.1.call-update
  316.2 13.9 %convolution_convert_fusion.3 = bf16[2048,2048]{1,0:T(8,128)(2,1)} fusion(bf16[2048,1024]{1,0:T(8,128)(2,1)} %get-tuple-element.68, bf16[1024,2048]{1,0:T(8,128)(2,1)} %wu_ref.1), kind=kOutput, calls=%fused_computation.3 | convolution fusion | flops 8594128896 | bytes 16777216 | tf_op jit(solution)/shard_map/dot_general | solution.py:29
  330.1 42.2 %scatter_seq.1.g_ref = f32[256,2048]{1,0:T(8,128)} custom-call(bf16[8,256,2048]{2,1,0:T(8,128)(2,1)} %bitcast.52), custom_call_target="tpu_custom_call" | custom-call | tf_op jit(solution)/shard_map/scatter_seq/pallas_call | solution.py:535
  372.3 17.7 %branch_pass.1 = (f32[256,2048]{1,0:T(8,128)}, bf16[256,2048]{1,0:T(8,128)(2,1)}, bf16[256,2048]{1,0:T(8,128)(2,1)}, f32[1,2048]{1,0:T(1,128)}, f32[1,2048]{1,0:T(1,128)}) custom-call(f32[256,2048]{1,0:T(8,128)} %scatter_seq.1.g_ref, f32[256,2048]{1,0:T(8,128)} %get-tuple-element.69.mid_ref, bf16[256,2048]{1,0:T(8,128)(2,1)} %bitcast.56, ...), custom_call_target="tpu_custom_call" | custom-call | flops 2147483648 | bytes 18874368 | tf_op jit(solution)/shard_map/branch_pass/pallas_call | solution.py:1451
  390.1 13.6 %tokens_to_heads.1.do_ref = bf16[2048,256]{1,0:T(8,128)(2,1)} custom-call(bf16[256,2048]{1,0:T(8,128)(2,1)} %get-tuple-element.70.x_ref), custom_call_target="tpu_custom_call" | custom-call | tf_op jit(solution)/shard_map/tokens_to_heads/pallas_call | solution.py:648
  403.7 4.8 all-to-all-start
  408.5 40.5 %attend_back.1 = bf16[2048,768]{1,0:T(8,128)(2,1)} custom-call(s32[8]{0:T(128)} %and_select_fusion.first_ref, s32[1,2048]{1,0:T(1,128)} %copy-done.9, bf16[2048,256]{1,0:T(8,128)(2,1)} %get-tuple-element.54.q_ref, bf16[2048,256]{1,0:T(8,128)(2,1)} %get-tuple-element.55.k_ref, bf16[256,2048]{1,0:T(8,128)(2,1)} %get-tuple-element.56.kt_ref, ...), custom_call_target="tpu_custom_call" | custom-call | flops 5368709120 | bytes 8388608 | tf_op jit(solution)/shard_map/attend_back/pallas_call | solution.py:906
  449.0 11.0 %convolution_convert_fusion.1 = bf16[2048,2048]{1,0:T(8,128)(2,1)} fusion(bf16[2048,768]{1,0:T(8,128)(2,1)} %attend_back.1, bf16[768,2048]{1,0:T(8,128)(2,1)S(1)} %bitcast.78), kind=kOutput, calls=%fused_computation.1 | convolution fusion | flops 6446645248 | bytes 14680064 | tf_op jit(solution)/shard_map/dot_general | solution.py:29
  459.9 10.7 %convolution_convert_fusion.5 = bf16[768,2048]{1,0:T(8,128)(2,1)} fusion(bf16[2048,768]{1,0:T(8,128)(2,1)S(1)} %copy-done.12, bf16[2048,2048]{1,0:T(8,128)(2,1)} %bitcast.75), kind=kOutput, calls=%fused_computation.5 | convolution fusion | flops 6444023808 | bytes 14680064 | tf_op jit(solution)/shard_map/dot_general | solution.py:37
  470.6 5.8 convolution_convert_fusion.2
  476.4 11.1 %convolution_convert_fusion = bf16[2048,2048]{1,0:T(8,128)(2,1)} fusion(bf16[2048,1024]{1,0:T(8,128)(2,1)S(1)} %copy-done.10, bf16[2048,1024]{1,0:T(8,128)(2,1)S(1)} %bitcast.54), kind=kOutput, calls=%fused_computation | convolution fusion | flops 8594128896 | bytes 16777216 | tf_op jit(solution)/shard_map/dot_general | solution.py:33
  487.5 0.0 all-to-all-done.gd_ref
  487.5 228.4 %finish.1 = (bf16[3,256,2048]{2,1,0:T(8,128)(2,1)}, f32[256,8192]{1,0:T(8,128)}, f32[256,2048]{1,0:T(8,128)}, f32[256,2048]{1,0:T(8,128)}, bf16[256,2048]{1,0:T(8,128)(2,1)}, /*index=5*/f32[16,2048]{1,0:T(8,128)}) custom-call(bf16[3,256,2048]{2,1,0:T(8,128)(2,1)} %bitcast.58, bf16[8,256,1024]{2,1,0:T(8,128)(2,1)} %all-to-all-done.gd_ref, ...), custom_call_target="tpu_custom_call" | custom-call | tf_op jit(solution)/shard_map/finish/pallas_call | solution.py:1920
  715.9 0.8 slice_bitcast_fusion
  716.7 0.6 copy.23
  717.3 1.6 fusion.8
  718.9 5.4 bitcast_convert_fusion
  724.3 6.8 convert_element_type.63
  731.1 1.0 copy.29
  732.1 1.3 copy.30
  733.4 1.3 copy.31
  734.7 2.3 copy-done.1
  737.0 3.4 copy.32
  (27 shorter events, 0.1 us)
Async XLA Ops:
  7.2 9.4 %copy-start = (bf16[1,256,2048]{2,1,0:T(8,128)(2,1)S(1)}, bf16[1,256,2048]{2,1,0:T(8,128)(2,1)}, u32[]{:S(2)}) copy-start(bf16[1,256,2048]{2,1,0:T(8,128)(2,1)} %param.11) | copy-start | bytes 3145732
  7.2 9.4 %copy-start.8 = (f32[2048]{0:T(1024)S(1)}, f32[2048]{0:T(1024)}, u32[]{:S(2)}) copy-start(f32[2048]{0:T(1024)} %param.17) | copy-start | bytes 24580
  7.2 205.8 %all-gather.3.cloned.1.call-start = ((), (), s32[]{:S(2)}) async-start(), calls=%async_computation.1 | async-start | bytes 9437184 | tf_op jit(solution)/shard_map/all_gather | solution.py:2007
  7.9 218.9 %all-gather.5.cloned.1.call-start = ((), (), s32[]{:S(2)}) async-start(), calls=%async_computation.2 | async-start | bytes 9437184 | tf_op jit(solution)/shard_map/all_gather | solution.py:2020
  8.7 715.6 %all-reduce.2.cloned.1.call-start = ((), (), s32[]{:S(2)}) async-start(), calls=%async_computation.3 | async-start | bytes 8388608 | tf_op jit(solution)/shard_map/psum | solution.py:2033
  12.8 130.9 %copy-start.9 = (s32[1,2048]{1,0:T(1,128)}, s32[1,2048]{1,0:T(1,128)S(1)}, u32[]{:S(2)}) copy-start(s32[1,2048]{1,0:T(1,128)S(1)} %compare_select_fusion.2.start_ref) | copy-start | bytes 24580
  403.7 83.8 %all-to-all-start = ((bf16[8,256,1024]{2,1,0:T(8,128)(2,1)}), bf16[8,256,1024]{2,1,0:T(8,128)(2,1)}, u32[]{:S(2)}, u32[]{:S(2)}) async-start(bf16[8,256,1024]{2,1,0:T(8,128)(2,1)} %bitcast.57), calls=%async_computation | async-start | bytes 8388608 | tf_op jit(solution)/shard_map/all_to_all | solution.py:2042
  408.5 40.5 %copy-start.11 = (bf16[3,256,2048]{2,1,0:T(8,128)(2,1)S(1)}, bf16[3,256,2048]{2,1,0:T(8,128)(2,1)}, u32[]{:S(2)}) copy-start(bf16[3,256,2048]{2,1,0:T(8,128)(2,1)} %get-tuple-element.49) | copy-start | bytes 9437188
  449.0 11.0 %copy-start.12 = (bf16[2048,768]{1,0:T(8,128)(2,1)S(1)}, bf16[2048,768]{1,0:T(8,128)(2,1)}, u32[]{:S(2)}) copy-start(bf16[2048,768]{1,0:T(8,128)(2,1)} %attend_back.1) | copy-start | bytes 9437188
  459.9 10.7 %copy-start.5 = (bf16[256,2048]{1,0:T(8,128)(2,1)S(1)}, bf16[256,2048]{1,0:T(8,128)(2,1)}, u32[]{:S(2)}) copy-start(bf16[256,2048]{1,0:T(8,128)(2,1)} %get-tuple-element.73) | copy-start | bytes 3145732
  459.9 10.7 %copy-start.6 = (bf16[256,2048]{1,0:T(8,128)(2,1)S(1)}, bf16[256,2048]{1,0:T(8,128)(2,1)}, u32[]{:S(2)}) copy-start(bf16[256,2048]{1,0:T(8,128)(2,1)} %get-tuple-element.74) | copy-start | bytes 3145732
  470.6 5.8 copy-start.2
  470.6 5.8 copy-start.10
  724.3 6.8 copy-start.7
  724.3 7.8 %copy-start.4 = (f32[256,2048]{1,0:T(8,128)S(1)}, f32[256,2048]{1,0:T(8,128)}, u32[]{:S(2)}) copy-start(f32[256,2048]{1,0:T(8,128)} %get-tuple-element.80) | copy-start | bytes 6291460
  731.1 2.3 copy-start.3
  731.1 5.9 copy-start.1
Sparse Core Ops, SparseCore 0:
  9.9 95.5 all-gather.2
  107.4 60.2 all-gather.4
  316.3 152.6 all-reduce.1

commit v8 on v7

--- a/solution.py
+++ b/solution.py
@@ -433,125 +433,8 @@
     )
 
 
-def scatter_kernel(
-    p_ref, o_ref, own, twin_in, held, local_sem, send_sem, recv_sem
-):
-    me, twin, near_x, near_y, across = places()
-    rows = p_ref.shape[1]
-    half = rows // 2
-    low, high = pl.ds(0, half), pl.ds(half, half)
-    mine = (across, near_x, near_y, me)
-
-    loads = [
-        pltpu.make_async_copy(p_ref.at[block], own.at[i], local_sem.at[i])
-        for i, block in enumerate(mine)
-    ]
-    for load in loads:
-        load.start()
-    meet((me + twin, near_x, near_y))
-
-    def copy(k, src, dst, partner):
-        return remote(src, dst, send_sem.at[k], recv_sem.at[k], partner)
-
-    twins = [
-        copy(i, p_ref.at[block + twin], twin_in.at[i], me + twin)
-        for i, block in enumerate(mine)
-    ]
-    for send in twins:
-        send.start()
-    sends = [
-        copy(4, own.at[0, low], held.at[0], near_x),
-        copy(5, own.at[0, high], held.at[1], near_y),
-        copy(6, own.at[1, low], held.at[2], near_x),
-        copy(7, own.at[2, high], held.at[3], near_y),
-        copy(8, own.at[1, high], held.at[4], near_x),
-        copy(9, own.at[2, low], held.at[5], near_y),
-    ]
-    step = 32
-
-    def add_twin(i):
-        loads[i].wait()
-        twins[i].wait_recv()
-
-        @pl.loop(0, rows // step)
-        def _(r):
-            at = pl.ds(pl.multiple_of(r * step, step), step)
-            own[i, at] = (
-                own[i, at].astype(F32) + twin_in[i, at].astype(F32)
-            ).astype(own.dtype)
-
-    def add_held(i, base, slot):
-        @pl.loop(0, half // step)
-        def _(r):
-            at = pl.ds(pl.multiple_of(r * step, step), step)
-            to = pl.ds(pl.multiple_of(base + r * step, step), step)
-            own[i, to] = (
-                own[i, to].astype(F32) + held[slot, at].astype(F32)
-            ).astype(own.dtype)
-
-    add_twin(0)
-    sends[0].start()
-    sends[1].start()
-    add_twin(1)
-    sends[2].start()
-    add_twin(2)
-    sends[3].start()
-    sends[1].wait_recv()
-    add_held(1, half, 1)
-    sends[4].start()
-    sends[0].wait_recv()
-    add_held(2, 0, 0)
-    sends[5].start()
-    loads[3].wait()
-    twins[3].wait_recv()
-    for k in (2, 3, 4, 5):
-        sends[k].wait_recv()
-
-    def final(base, first, second):
-        @pl.loop(0, half // step)
-        def _(r):
-            at = pl.ds(pl.multiple_of(r * step, step), step)
-            to = pl.ds(pl.multiple_of(base + r * step, step), step)
-            o_ref[to] = (
-                own[3, to].astype(F32)
-                + twin_in[3, to].astype(F32)
-                + held[first, at].astype(F32)
-                + held[second, at].astype(F32)
-            )
-
-    final(0, 2, 5)
-    final(half, 3, 4)
-    for send in twins + sends:
-        send.wait_send()
-
-
-def scatter_seq(partial, collective_id):
-    n = lax.axis_size("seq")
-    rows, width = partial.shape[0] // n, partial.shape[1]
-    if n != 8:
-        return lax.psum_scatter(
-            partial, "seq", scatter_dimension=0, tiled=True
-        ).astype(F32)
-    return pl.pallas_call(
-        scatter_kernel,
-        out_shape=jax.ShapeDtypeStruct((rows, width), F32),
-        in_specs=[ANY],
-        out_specs=pl.BlockSpec(memory_space=pltpu.VMEM),
-        scratch_shapes=[
-            pltpu.VMEM((4, rows, width), BF16),
-            pltpu.VMEM((4, rows, width), BF16),
-            pltpu.VMEM((6, rows // 2, width), BF16),
-            pltpu.SemaphoreType.DMA((4,)),
-            pltpu.SemaphoreType.DMA((10,)),
-            pltpu.SemaphoreType.DMA((10,)),
-        ],
-        compiler_params=pltpu.CompilerParams(
-            collective_id=collective_id,
-            has_side_effects=True,
-            vmem_limit_bytes=VMEM_LIMIT,
-        ),
-        name="scatter_seq",
-    )(partial.reshape(n, rows, width))
+def scatter_seq(partial):
+    return lax.psum_scatter(partial, "seq", scatter_dimension=0, tiled=True).astype(F32)
 
 
 def heads_to_tokens_kernel(n, x_ref, o_ref, keep, local_sem, send_sem, recv_sem):
@@ -1401,31 +1284,20 @@
     )(attended, x, w_out, gain_mix[None], gain_ffn[None])
 
 
-def branch_kernel(
-    g_ref, mid_ref, cot_ref, att_ref, w_ref, gm_ref, gf_ref,
-    gmid_ref, gbr_ref, gatt_ref, ggf_ref, ggm_ref, total,
-):
+def branch_kernel(gbr_ref, att_ref, w_ref, gm_ref, gatt_ref, ggm_ref, total):
     j = pl.program_id(0)
     rows = att_ref.shape[0]
     cols = w_ref.shape[0]
+    here = pl.ds(pl.multiple_of(j * cols, cols), cols)
+    term = nn(gbr_ref[:, here], w_ref[...])
 
     @pl.when(j == 0)
     def _():
-        ggf_ref[...] = jnp.zeros_like(ggf_ref)
-        total[...] = jnp.zeros_like(total)
-
-        @pl.loop(0, rows // STEP)
-        def _(r):
-            at = pl.ds(pl.multiple_of(r * STEP, STEP), STEP)
-            normal, scale = norm_parts(mid_ref[at])
-            part, gain_part = norm_back(g_ref[at], normal, scale, gf_ref[...])
-            ggf_ref[...] += gain_part[None]
-            grad = cot_ref[at].astype(F32) + part
-            gmid_ref[at] = grad
-            gbr_ref[at] = grad.astype(BF16)
-
-    here = pl.ds(pl.multiple_of(j * cols, cols), cols)
-    total[...] += nn(gbr_ref[:, here], w_ref[...])
+        total[...] = term
+
+    @pl.when(j > 0)
+    def _():
+        total[...] = total[...] + term
 
     @pl.when(j == pl.num_programs(0) - 1)
     def _():
@@ -1440,37 +1312,188 @@
             gatt_ref[at] = part.astype(BF16)
 
 
-def branch_pass(grad_ffn_in, middle, cot, attended, w_out, gain_mix, gain_ffn):
-    rows, width = cot.shape
+def branch_pass(grad_branch, attended, w_out, gain_mix):
+    rows, width = grad_branch.shape
     cols = TILE
     n = width // cols
     whole = pl.BlockSpec((rows, width), lambda j: (0, 0))
     gain = pl.BlockSpec((1, width), lambda j: (0, 0))
-    low = jax.ShapeDtypeStruct((rows, width), BF16)
-    sums = jax.ShapeDtypeStruct((1, width), F32)
     return pl.pallas_call(
         branch_kernel,
         grid=(n,),
-        out_shape=(jax.ShapeDtypeStruct((rows, width), F32), low, low, sums, sums),
-        in_specs=[
-            whole,
-            whole,
-            whole,
-            whole,
-            pl.BlockSpec((cols, width), lambda j: (j, 0)),
-            gain,
-            gain,
-        ],
-        out_specs=(whole, whole, whole, gain, gain),
+        out_shape=(
+            jax.ShapeDtypeStruct((rows, width), BF16),
+            jax.ShapeDtypeStruct((1, width), F32),
+        ),
+        in_specs=[whole, whole, pl.BlockSpec((cols, width), lambda j: (j, 0)), gain],
+        out_specs=(whole, gain),
         scratch_shapes=[pltpu.VMEM((rows, width), F32)],
         compiler_params=pltpu.CompilerParams(vmem_limit_bytes=VMEM_LIMIT),
         cost_estimate=pl.CostEstimate(
             flops=2 * rows * width * width,
-            bytes_accessed=2 * width * width + 20 * rows * width,
+            bytes_accessed=2 * width * width + 8 * rows * width,
             transcendentals=0,
         ),
         name="branch_pass",
-    )(grad_ffn_in, middle, cot, attended, w_out, gain_mix[None], gain_ffn[None])
+    )(grad_branch, attended, w_out, gain_mix[None])
+
+
+def ffn_back_kernel(
+    n, gu_ref, wu_ref, hid_ref, wd_ref, mid_ref, cot_ref, gf_ref,
+    po_ref, gmid_ref, gbr_ref, ggf_ref,
+    gu, hid, own, far, twin_in, held, made,
+    local_sem, hid_sem, made_sem, send_sem, recv_sem,
+):
+    me, twin, near_x, near_y, across = places()
+    rows, width = mid_ref.shape
+    half = rows // 2
+    low, high = pl.ds(0, half), pl.ds(half, half)
+    mine = (across, near_x, near_y, me)
+
+    def cut(i, size=rows):
+        return pl.ds(pl.multiple_of(i * size, size), size)
+
+    def load_hid(i, slot):
+        return pltpu.make_async_copy(hid_ref.at[cut(i)], hid.at[slot], hid_sem.at[slot])
+
+    load_gu = pltpu.make_async_copy(gu_ref, gu, local_sem)
+    load_gu.start()
+    load_hid(0, 0).start()
+    meet((me + twin, near_x, near_y))
+    load_gu.wait()
+
+    def copy(k, src, dst, partner):
+        return remote(src, dst, send_sem.at[k], recv_sem.at[k], partner)
+
+    twins = [copy(i, far.at[i], twin_in.at[i], me + twin) for i in range(4)]
+    sends = [
+        copy(4, own.at[0, low], held.at[0], near_x),
+        copy(5, own.at[0, high], held.at[1], near_y),
+        copy(6, own.at[1, low], held.at[2], near_x),
+        copy(7, own.at[2, high], held.at[3], near_y),
+        copy(8, own.at[1, high], held.at[4], near_x),
+        copy(9, own.at[2, low], held.at[5], near_y),
+    ]
+
+    def add(i, base, count, source):
+        @pl.loop(0, count // STEP)
+        def _(r):
+            at = cut(r, STEP)
+            to = pl.ds(pl.multiple_of(base + r * STEP, STEP), STEP)
+            own[i, to] = (own[i, to].astype(F32) + source[at].astype(F32)).astype(BF16)
+
+    for i, block in enumerate(mine):
+        far[i] = nn(gu[cut(block + twin)], wu_ref[...]).astype(BF16)
+        twins[i].start()
+        own[i] = nn(gu[cut(block)], wu_ref[...]).astype(BF16)
+        if i < 3:
+            twins[i].wait_recv()
+            add(i, 0, rows, twin_in.at[i])
+        if i == 0:
+            sends[0].start()
+            sends[1].start()
+        elif i < 3:
+            sends[i + 1].start()
+
+    def store(i, slot):
+        return pltpu.make_async_copy(made.at[slot], po_ref.at[cut(i)], made_sem.at[slot])
+
+    def outputs(first, last):
+        @pl.loop(first, last)
+        def _(i):
+            slot = lax.rem(i, 2)
+
+            @pl.when(i + 1 < n)
+            def _():
+                load_hid(i + 1, 1 - slot).start()
+
+            load_hid(i, slot).wait()
+
+            @pl.when(i >= 2)
+            def _():
+                store(i - 2, slot).wait()
+
+            made[slot] = nt(hid[slot], wd_ref[...]).astype(BF16)
+            store(i, slot).start()
+
+    outputs(0, n // 2)
+    sends[1].wait_recv()
+    add(1, half, half, held.at[1])
+    sends[4].start()
+    sends[0].wait_recv()
+    add(2, 0, half, held.at[0])
+    sends[5].start()
+    outputs(n // 2, n)
+    twins[3].wait_recv()
+    for k in (2, 3, 4, 5):
+        sends[k].wait_recv()
+    ggf_ref[...] = jnp.zeros_like(ggf_ref)
+    for base, one, two in ((0, 2, 5), (half, 3, 4)):
+
+        @pl.loop(0, half // STEP)
+        def _(r):
+            at = cut(r, STEP)
+            to = pl.ds(pl.multiple_of(base + r * STEP, STEP), STEP)
+            value = (
+                own[3, to].astype(F32)
+                + twin_in[3, to].astype(F32)
+                + held[one, at].astype(F32)
+                + held[two, at].astype(F32)
+            )
+            normal, scale = norm_parts(mid_ref[to])
+            part, gain_part = norm_back(value, normal, scale, gf_ref[...])
+            ggf_ref[...] = ggf_ref[...] + gain_part[None]
+            grad = cot_ref[to].astype(F32) + part
+            gmid_ref[to] = grad
+            gbr_ref[to] = grad.astype(BF16)
+
+    for i in (n - 2, n - 1):
+        store(i, i % 2).wait()
+    for send in twins + sends:
+        send.wait_send()
+
+
+def ffn_back(grad_upper, w_up, hidden, w_down, middle, cot, gain, collective_id):
+    n = lax.axis_size("seq")
+    rows, width = middle.shape
+    feats = w_up.shape[0]
+    if n != 8:
+        normal, scale = norm_parts(middle)
+        value = scatter_seq(nn(grad_upper, w_up).astype(BF16))
+        part, gain_part = norm_back(value, normal, scale, gain)
+        grad = cot.astype(F32) + part
+        return nt(hidden, w_down).astype(BF16), grad, grad.astype(BF16), gain_part[None]
+    dma = pltpu.SemaphoreType.DMA
+    block = pltpu.VMEM((4, rows, width), BF16)
+    return pl.pallas_call(
+        functools.partial(ffn_back_kernel, n),
+        out_shape=(
+            jax.ShapeDtypeStruct((n * rows, width), BF16),
+            jax.ShapeDtypeStruct((rows, width), F32),
+            jax.ShapeDtypeStruct((rows, width), BF16),
+            jax.ShapeDtypeStruct((1, width), F32),
+        ),
+        in_specs=[ANY, INSIDE, ANY, INSIDE, INSIDE, INSIDE, INSIDE],
+        out_specs=(ANY, INSIDE, INSIDE, INSIDE),
+        scratch_shapes=[
+            pltpu.VMEM((n * rows, feats), BF16),
+            pltpu.VMEM((2, rows, feats), BF16),
+            block,
+            block,
+            block,
+            pltpu.VMEM((6, rows // 2, width), BF16),
+            pltpu.VMEM((2, rows, width), BF16),
+            dma,
+            dma((2,)),
+            dma((2,)),
+            dma((10,)),
+            dma((10,)),
+        ],
+        compiler_params=pltpu.CompilerParams(
+            collective_id=collective_id, has_side_effects=True, vmem_limit_bytes=VMEM_LIMIT
+        ),
+        name="ffn_back",
+    )(grad_upper, w_up, hidden, w_down, middle, cot, gain[None])
 
 
 CHUNK = 64
@@ -1898,9 +1921,9 @@
             )
             for j in range(3)
         ]
-        w_out = lax.psum(scatter_seq(part_out, None).astype(BF16), "batch")
+        w_out = lax.psum(scatter_seq(part_out).astype(BF16), "batch")
         normal, scale = norm_parts(x.astype(F32))
-        part, gain_part = norm_back(scatter_seq(part_normed, None), normal, scale, gain)
+        part, gain_part = norm_back(scatter_seq(part_normed), normal, scale, gain)
         shared = [lax.psum(g, ("batch", "seq")) for g in (gain_part, gains[0][0], gains[1][0])]
         hidden = lax.all_gather(lax.psum(gains[2][0], "batch"), "seq", axis=0, tiled=True)
         down = lax.psum(grad_down, "batch")
@@ -1909,7 +1932,7 @@
             jnp.swapaxes(down, 0, 1).reshape(rows, sources * feats).astype(F32),
             w_out.astype(F32),
             grad_middle + part,
-            (middle + scatter_seq(part_outputs, None)).astype(BF16),
+            (middle + scatter_seq(part_outputs)).astype(BF16),
             (*shared, hidden),
         )
     chunks = (
@@ -2033,10 +2056,10 @@
     grad_w_up = lax.psum(grad_w_up, "batch")
     grad_w_down = weight_grad(cot_full, hidden).reshape(n, local, feats)
     grad_upper, grad_w_down = lax.optimization_barrier((grad_upper, grad_w_down))
-    grad_ffn_in = scatter_seq(nn(grad_upper, w_up).astype(BF16), 4)
-    grad_middle, grad_branch, grad_att, grad_gain_ffn, grad_gain_mix = branch_pass(
-        grad_ffn_in, middle, cot, attended, w_out_full, gain_mix, gain_ffn
+    part_outputs, grad_middle, grad_branch, grad_gain_ffn = ffn_back(
+        grad_upper, w_up, hidden, w_down_cols, middle, cot, gain_ffn, 4
     )
+    grad_att, grad_gain_mix = branch_pass(grad_branch, attended, w_out_full, gain_mix)
     grad_heads = tokens_to_heads(grad_att, 5)
     grad_w_down, grad_heads = lax.optimization_barrier((grad_w_down, grad_heads))
     grad_w_down = lax.all_to_all(grad_w_down, "seq", split_axis=0, concat_axis=0, tiled=True)
@@ -2048,7 +2071,7 @@
         grad_w_down,
         tn(grad_branch, mix_in).astype(BF16),
         nn(grads, w_heads).astype(BF16),
-        nt(hidden, w_down_cols).astype(BF16),
+        part_outputs,
         x_low,
         grad_middle,
         middle,

time: 754 us -> 733 us (0.972)
  matrix products: 66.7 us -> 41.5 us
    dot_general x2 -> x1, matrix products: 24.9 us -> 8.97 us  [nn(): lax.dot_general(a, b, (((1,), (0,)), ((), ())), preferred_element_type=F32)]
    dot_general x1 -> x0, matrix products: 11.1 us -> none  [nt(): lax.dot_general(a, b, (((1,), (1,)), ((), ())), preferred_element_type=F32)]
    pallas_call x1, Pallas kernels: 42.2 us -> 52.3 us  [ffn_back(): pl.pallas_call(functools.partial(ffn_back_kernel, n), out_shape=(jax.Shap...]
  transfers between devices with their start and end apart: 4 -> 4, of which waited for: 0 -> 0; matrix products, arithmetic and copies ran while one was open for 10% -> 6% of each run, Pallas kernels for 74% -> 76%
where the time goes in v8:
time: 733 us; the launch traced here: 720 us
  Pallas kernels  622 us (85%)
  matrix products  41.5 us (6%)
  other arithmetic  21.9 us (3%)
  between operations  14.1 us (2%)
  local copies, waits for them, and re-layouts  13.7 us (2%)
    pallas_call x1, Pallas kernels, finish(): pl.pallas_call(functools.partial(finish_kernel, n, depth), out_shape=(jax...  230 us
    pallas_call x1, Pallas kernels, start_exchange(): pl.pallas_call(functools.partial(start_kernel, n, depth), out_shape=(jax....  126 us
    pallas_call x1, Pallas kernels, ffn_pass(): pl.pallas_call(functools.partial(ffn_kernel, n), out_shape=(jax.ShapeDtyp...  61.8 us
    pallas_call x1, Pallas kernels, ffn_back(): pl.pallas_call(functools.partial(ffn_back_kernel, n), out_shape=(jax.Shap...  52.3 us
    pallas_call x1, Pallas kernels, attend_back(): pl.pallas_call(functools.partial(attend_back_kernel, heads), out_shape=ja...  35.4 us
    dot_general x3, matrix products, tn(): lax.dot_general(a, b, (((0,), (0,)), ((), ())), preferred_element_type=F32)  32.5 us
    pallas_call x1, Pallas kernels, attend(): pl.pallas_call(functools.partial(attend_kernel, heads), out_shape=(jax.Sh...  26.2 us
    pallas_call x1, Pallas kernels, heads_to_tokens(): pl.pallas_call(functools.partial(heads_to_tokens_kernel, n), out_shape=ja...  22.5 us
  transfers between devices with their start and end apart: 4, of which 0 were waited for; matrix products, arithmetic and copies ran while one was open for 6% of the time, Pallas kernels for 76%

profile of v8, /device:TPU:0, one launch (start us, length us, event | category | flops | bytes accessed | tf_op | source)
XLA Modules:
  0.0 719.6 jit_solution(4482631875964840873)
XLA Ops:
  7.2 0.0 copy-start
  7.2 0.0 copy-start.7
  7.2 0.0 all-gather.3.cloned.1.call-start
  7.2 0.7 all-gather.3.cloned.1.call-update
  7.9 0.0 all-gather.5.cloned.1.call-start
  8.0 0.7 all-gather.5.cloned.1.call-update
  8.7 0.0 all-reduce.2.cloned.1.call-start
  8.7 1.4 fusion.5
  10.1 2.7 compare_select_fusion.2.start_ref
  12.8 0.0 copy-start.8
  12.8 0.1 slice.15
  12.9 1.4 convert_reduce_fusion
  14.3 1.6 fusion.2
  16.0 0.6 subtract_convert_fusion.pos_ref
  16.6 0.0 copy-done
  16.6 1.4 fusion.4.x_ref
  18.0 125.7 %start_exchange.1 = (bf16[8,256,2048]{2,1,0:T(8,128)(2,1)}, bf16[3,256,2048]{2,1,0:T(8,128)(2,1)}, bf16[8,4,64,1024]{3,2,1,0:T(8,128)(2,1)}, f32[2048,128]{1,0:T...) custom-call(bf16[256,2048]{1,0:T(8,128)(2,1)} %fusion.4.x_ref, ...), custom_call_target="tpu_custom_call" | custom-call | tf_op jit(solution)/shard_map/start_exchange/pallas_call | solution.py:400
  143.7 0.5 and_select_fusion.first_ref
  144.2 14.3 %project_qkv.1 = (bf16[2048,256]{1,0:T(8,128)(2,1)}, bf16[2048,256]{1,0:T(8,128)(2,1)}, bf16[2048,256]{1,0:T(8,128)(2,1)}, bf16[256,2048]{1,0:T(8,128)(2,1)}, bf16[256,2048]{1,0:T(8,128)(2,1)}) custom-call(bf16[2048,2048]{1,0:T(8,128)(2,1)} %bitcast.68, bf16[768,2048]{1,0:T(8,128)(2,1)} %bitcast.71, f32[2048,128]{1,0:T(8,128)} %get-tuple-element.51.cq_ref, ...), custom_call_target="tpu_custom_call" | custom-call | flops 6442450944 | bytes 16777216 | tf_op jit(solution)/shard_map/project_qkv/pallas_call | solution.py:594
  158.5 26.2 %attend.1 = (bf16[2048,256]{1,0:T(8,128)(2,1)}, f32[8,4,256]{2,1,0:T(4,128)}) custom-call(s32[8]{0:T(128)} %and_select_fusion.first_ref, s32[1,2048]{1,0:T(1,128)} %copy-done.8, bf16[2048,256]{1,0:T(8,128)(2,1)} %get-tuple-element.55.q_ref, bf16[2048,256]{1,0:T(8,128)(2,1)} %get-tuple-element.56.k_ref, bf16[256,2048]{1,0:T(8,128)(2,1)} %get-tuple-element.59.vt_ref), custom_call_target="tpu_custom_call" | custom-call | flops 2147483648 | bytes 4194304 | tf_op jit(solution)/shard_map/attend/pallas_call | solution.py:674
  184.8 22.5 %heads_to_tokens.1.att_ref = bf16[256,2048]{1,0:T(8,128)(2,1)} custom-call(bf16[2048,256]{1,0:T(8,128)(2,1)} %get-tuple-element.60.x_ref.o_ref), custom_call_target="tpu_custom_call" | custom-call | tf_op jit(solution)/shard_map/heads_to_tokens/pallas_call | solution.py:494
  207.3 1.3 dynamic_slice.3
  208.6 13.8 %mix_pass.1 = (bf16[256,2048]{1,0:T(8,128)(2,1)}, f32[256,2048]{1,0:T(8,128)}, bf16[256,2048]{1,0:T(8,128)(2,1)}) custom-call(bf16[256,2048]{1,0:T(8,128)(2,1)} %heads_to_tokens.1.att_ref, bf16[256,2048]{1,0:T(8,128)(2,1)} %bitcast.43, bf16[2048,2048]{1,0:T(8,128)(2,1)} %all-gather.3.cloned.1.call-done.w_ref, f32[1,2048]{1,0:T(1,128)} %bitcast.62, ...), custom_call_target="tpu_custom_call" | custom-call | flops 2147483648 | bytes 14680064 | tf_op jit(solution)/shard_map/mix_pass/pallas_call | solution.py:1265
  222.4 61.8 %ffn_pass.1 = (bf16[8,256,2048]{2,1,0:T(8,128)(2,1)}, bf16[2048,1024]{1,0:T(8,128)(2,1)}, bf16[2048,1024]{1,0:T(8,128)(2,1)}, f32[1,1024]{1,0:T(1,128)}) custom-call(bf16[256,2048]{1,0:T(8,128)(2,1)} %get-tuple-element.62.x_ref, bf16[1024,2048]{1,0:T(8,128)(2,1)} %wu_ref.3, bf16[2048,2048]{1,0:T(8,128)(2,1)} %all-gather.5.cloned.1.call-done.cot_ref.a_ref, ...), custom_call_target="tpu_custom_call" | custom-call | tf_op jit(solution)/shard_map/ffn_pass/pallas_call | solution.py:1109
  284.2 14.5 %convolution_convert_fusion.2 = bf16[1024,2048]{1,0:T(8,128)(2,1)} fusion(bf16[2048,1024]{1,0:T(8,128)(2,1)} %get-tuple-element.69.gu_ref, bf16[2048,2048]{1,0:T(8,128)(2,1)} %bitcast.70), kind=kOutput, calls=%fused_computation.2 | convolution fusion | flops 8592031744 | bytes 16777216 | tf_op jit(solution)/shard_map/dot_general | solution.py:37
  298.7 13.3 %weight_grad.1 = bf16[2048,1024]{1,0:T(8,128)(2,1)} custom-call(bf16[2048,2048]{1,0:T(8,128)(2,1)} %all-gather.5.cloned.1.call-done.cot_ref.a_ref, bf16[2048,1024]{1,0:T(8,128)(2,1)} %get-tuple-element.67.b_ref.hid_ref), custom_call_target="tpu_custom_call" | custom-call | flops 8589934592 | bytes 16777216 | tf_op jit(solution)/shard_map/weight_grad/pallas_call | solution.py:1211
  312.0 0.0 all-reduce.2.cloned.1.call-update
  312.0 52.3 %ffn_back.1 = (bf16[2048,2048]{1,0:T(8,128)(2,1)}, f32[256,2048]{1,0:T(8,128)}, bf16[256,2048]{1,0:T(8,128)(2,1)}, f32[1,2048]{1,0:T(1,128)}) custom-call(bf16[2048,1024]{1,0:T(8,128)(2,1)} %get-tuple-element.69.gu_ref, bf16[1024,2048]{1,0:T(8,128)(2,1)} %wu_ref.3, bf16[2048,1024]{1,0:T(8,128)(2,1)} %get-tuple-element.67.b_ref.hid_ref, ...), custom_call_target="tpu_custom_call" | custom-call | tf_op jit(solution)/shard_map/ffn_back/pallas_call | solution.py:1468
  364.3 12.9 %branch_pass.1 = (bf16[256,2048]{1,0:T(8,128)(2,1)}, f32[1,2048]{1,0:T(1,128)}) custom-call(bf16[256,2048]{1,0:T(8,128)(2,1)} %get-tuple-element.71.gbr_ref, bf16[256,2048]{1,0:T(8,128)(2,1)} %heads_to_tokens.1.att_ref, bf16[2048,2048]{1,0:T(8,128)(2,1)} %all-gather.3.cloned.1.call-done.w_ref, f32[1,2048]{1,0:T(1,128)} %bitcast.63), custom_call_target="tpu_custom_call" | custom-call | flops 2147483648 | bytes 12582912 | tf_op jit(solution)/shard_map/branch_pass/pallas_call | solution.py:1321
  377.2 13.7 %tokens_to_heads.1.do_ref = bf16[2048,256]{1,0:T(8,128)(2,1)} custom-call(bf16[256,2048]{1,0:T(8,128)(2,1)} %get-tuple-element.72.x_ref), custom_call_target="tpu_custom_call" | custom-call | tf_op jit(solution)/shard_map/tokens_to_heads/pallas_call | solution.py:531
  390.9 4.8 all-to-all-start
  395.7 35.4 %attend_back.1 = bf16[2048,768]{1,0:T(8,128)(2,1)} custom-call(s32[8]{0:T(128)} %and_select_fusion.first_ref, s32[1,2048]{1,0:T(1,128)} %copy-done.8, bf16[2048,256]{1,0:T(8,128)(2,1)} %get-tuple-element.55.q_ref, bf16[2048,256]{1,0:T(8,128)(2,1)} %get-tuple-element.56.k_ref, bf16[256,2048]{1,0:T(8,128)(2,1)} %get-tuple-element.57.kt_ref, ...), custom_call_target="tpu_custom_call" | custom-call | flops 5368709120 | bytes 8388608 | tf_op jit(solution)/shard_map/attend_back/pallas_call | solution.py:789
  431.1 12.2 %convolution_convert_fusion.3 = bf16[768,2048]{1,0:T(8,128)(2,1)} fusion(bf16[2048,768]{1,0:T(8,128)(2,1)} %attend_back.1, bf16[2048,2048]{1,0:T(8,128)(2,1)} %bitcast.69), kind=kOutput, calls=%fused_computation.3 | convolution fusion | flops 6444023808 | bytes 14680064 | tf_op jit(solution)/shard_map/dot_general | solution.py:37
  443.3 0.0 copy-start.10
  443.3 5.8 convolution_convert_fusion.1
  449.1 9.0 %convolution_convert_fusion = bf16[2048,2048]{1,0:T(8,128)(2,1)} fusion(bf16[2048,768]{1,0:T(8,128)(2,1)S(1)} %copy-done.10, bf16[768,2048]{1,0:T(8,128)(2,1)S(1)} %bitcast.72), kind=kOutput, calls=%fused_computation | convolution fusion | flops 6446645248 | bytes 14680064 | tf_op jit(solution)/shard_map/dot_general | solution.py:29
  458.0 0.0 all-to-all-done.gd_ref
  458.0 230.3 %finish.1 = (bf16[3,256,2048]{2,1,0:T(8,128)(2,1)}, f32[256,8192]{1,0:T(8,128)}, f32[256,2048]{1,0:T(8,128)}, f32[256,2048]{1,0:T(8,128)}, bf16[256,2048]{1,0:T(8,128)(2,1)}, /*index=5*/f32[16,2048]{1,0:T(8,128)}) custom-call(bf16[3,256,2048]{2,1,0:T(8,128)(2,1)} %bitcast.52, bf16[8,256,1024]{2,1,0:T(8,128)(2,1)} %all-to-all-done.gd_ref, ...), custom_call_target="tpu_custom_call" | custom-call | tf_op jit(solution)/shard_map/finish/pallas_call | solution.py:1943
  688.3 0.8 slice_bitcast_fusion
  689.1 0.6 copy.23
  689.7 1.6 fusion.8
  691.3 5.4 bitcast_convert_fusion
  696.7 6.8 convert_element_type.55
  703.5 1.0 copy.29
  704.5 1.3 copy.30
  705.8 1.3 copy.31
  707.2 2.3 copy-done.1
  709.5 3.4 copy.32
  (21 shorter events, 0.0 us)
Async XLA Ops:
  7.2 9.4 %copy-start = (bf16[1,256,2048]{2,1,0:T(8,128)(2,1)S(1)}, bf16[1,256,2048]{2,1,0:T(8,128)(2,1)}, u32[]{:S(2)}) copy-start(bf16[1,256,2048]{2,1,0:T(8,128)(2,1)} %param.11) | copy-start | bytes 3145732
  7.2 9.4 %copy-start.7 = (f32[2048]{0:T(1024)S(1)}, f32[2048]{0:T(1024)}, u32[]{:S(2)}) copy-start(f32[2048]{0:T(1024)} %param.17) | copy-start | bytes 24580
  7.2 201.4 %all-gather.3.cloned.1.call-start = ((), (), s32[]{:S(2)}) async-start(), calls=%async_computation.1 | async-start | bytes 9437184 | tf_op jit(solution)/shard_map/all_gather | solution.py:2030
  7.9 214.4 %all-gather.5.cloned.1.call-start = ((), (), s32[]{:S(2)}) async-start(), calls=%async_computation.2 | async-start | bytes 9437184 | tf_op jit(solution)/shard_map/all_gather | solution.py:2043
  8.7 688.0 %all-reduce.2.cloned.1.call-start = ((), (), s32[]{:S(2)}) async-start(), calls=%async_computation.3 | async-start | bytes 8388608 | tf_op jit(solution)/shard_map/psum | solution.py:2056
  12.8 130.9 %copy-start.8 = (s32[1,2048]{1,0:T(1,128)}, s32[1,2048]{1,0:T(1,128)S(1)}, u32[]{:S(2)}) copy-start(s32[1,2048]{1,0:T(1,128)S(1)} %compare_select_fusion.2.start_ref) | copy-start | bytes 24580
  390.9 67.2 %all-to-all-start = ((bf16[8,256,1024]{2,1,0:T(8,128)(2,1)}), bf16[8,256,1024]{2,1,0:T(8,128)(2,1)}, u32[]{:S(2)}, u32[]{:S(2)}) async-start(bf16[8,256,1024]{2,1,0:T(8,128)(2,1)} %bitcast.51), calls=%async_computation | async-start | bytes 8388608 | tf_op jit(solution)/shard_map/all_to_all | solution.py:2065
  431.1 12.2 %copy-start.2 = (bf16[256,2048]{1,0:T(8,128)(2,1)S(1)}, bf16[256,2048]{1,0:T(8,128)(2,1)}, u32[]{:S(2)}) copy-start(bf16[256,2048]{1,0:T(8,128)(2,1)} %get-tuple-element.71.gbr_ref) | copy-start | bytes 3145732
  431.1 12.2 %copy-start.5 = (bf16[256,2048]{1,0:T(8,128)(2,1)S(1)}, bf16[256,2048]{1,0:T(8,128)(2,1)}, u32[]{:S(2)}) copy-start(bf16[256,2048]{1,0:T(8,128)(2,1)} %get-tuple-element.75) | copy-start | bytes 3145732
  443.2 5.8 copy-start.9
  443.3 5.8 copy-start.10
  696.7 6.8 copy-start.6
  696.7 7.8 %copy-start.4 = (f32[256,2048]{1,0:T(8,128)S(1)}, f32[256,2048]{1,0:T(8,128)}, u32[]{:S(2)}) copy-start(f32[256,2048]{1,0:T(8,128)} %get-tuple-element.82) | copy-start | bytes 6291460
  703.5 2.3 copy-start.3
  703.5 5.9 copy-start.1
Sparse Core Ops, SparseCore 0:
  9.9 95.5 all-gather.2
  107.4 60.2 all-gather.4
  312.1 154.1 all-reduce.1

commit v9 on v8

--- a/solution.py
+++ b/solution.py
@@ -16,6 +16,7 @@
 EPSILON = 1e-05
 MASKED = -1e30
 TILE = 256
+STEP = 32
 VMEM_LIMIT = 60 * 1024 * 1024
 
 MESH = pl.DeviceIdType.MESH
@@ -245,17 +246,16 @@
 
 
 def start_kernel(
-    n, depth, x_ref, w_ref, wd_ref, pos_ref,
+    n, depth, x_ref, gain_ref, w_ref, wd_ref, pos_ref,
     o_ref, wt_ref, wc_ref, cq_ref, sq_ref, ck_ref, sk_ref,
-    keep_w, keep_c, local_sem, send_sem, recv_sem, hop_send, hop_recv, col_send, col_recv,
+    normed, keep_w, keep_c, local_sem, send_sem, recv_sem, hop_send, hop_recv, col_send, col_recv,
     line_send, line_recv,
 ):
     z = lax.axis_index("batch")
     rows_z = wc_ref.shape[2]
     cols = wc_ref.shape[3]
     me, twin, near_x, near_y, _ = places()
-    own = pltpu.make_async_copy(x_ref, o_ref.at[me], local_sem.at[0])
-    own.start()
+    own = pltpu.make_async_copy(normed, o_ref.at[me], local_sem.at[0])
     wd_rows = pl.ds(pl.multiple_of(z * rows_z, rows_z), rows_z)
 
     def column(k):
@@ -267,6 +267,7 @@
     meet_all(n, depth)
     load_column.wait()
     own_column.start()
+
     def hop(j, part, target):
         return remote(
             w_ref.at[j], wt_ref.at[part], hop_send.at[j], hop_recv.at[part], target
@@ -304,7 +305,14 @@
             def _():
                 load(j).start()
 
-    sends = gather_copies(x_ref, o_ref, send_sem, recv_sem)
+    @pl.loop(0, x_ref.shape[0] // STEP)
+    def _(r):
+        at = pl.ds(pl.multiple_of(r * STEP, STEP), STEP)
+        normal, _ = norm_parts(x_ref[at].astype(F32))
+        normed[at] = (normal * gain_ref[...]).astype(BF16)
+
+    own.start()
+    sends = gather_copies(normed, o_ref, send_sem, recv_sem)
     for k in range(5):
         sends[k].start()
 
@@ -375,7 +383,7 @@
     own.wait()
 
 
-def start_exchange(block, w_qkv, w_down, positions, collective_id):
+def start_exchange(block, gain, w_qkv, w_down, positions, collective_id):
     n, depth = lax.axis_size("seq"), lax.axis_size("batch")
     rows, width = block.shape
     piece = w_qkv.shape[0] // 3
@@ -388,8 +396,9 @@
         ]
         parts = [pick_part(turned, me, n, part) for part in range(3)]
         place = jnp.broadcast_to(positions[:, None], (positions.shape[0], 128))
+        normed = (norm_parts(block.astype(F32))[0] * gain).astype(BF16)
         return (
-            lax.all_gather(block, "seq", axis=0, tiled=True),
+            lax.all_gather(normed, "seq", axis=0, tiled=True),
             jnp.concatenate(parts, axis=0),
             lax.all_to_all(w_down, "seq", split_axis=1, concat_axis=0, tiled=True),
             lane_tables(place),
@@ -405,9 +414,10 @@
             jax.ShapeDtypeStruct((n, depth, rows_z, cols), w_down.dtype),
             *([table] * 4),
         ),
-        in_specs=[INSIDE, ANY, ANY, INSIDE],
+        in_specs=[INSIDE, INSIDE, ANY, ANY, INSIDE],
         out_specs=(ANY, ANY, ANY, *([INSIDE] * 4)),
         scratch_shapes=[
+            pltpu.VMEM((rows, width), BF16),
             pltpu.VMEM((piece, width), BF16),
             pltpu.VMEM((rows_z, cols), BF16),
             pltpu.SemaphoreType.DMA((7,)),
@@ -424,7 +434,7 @@
             collective_id=collective_id, has_side_effects=True, vmem_limit_bytes=VMEM_LIMIT
         ),
         name="start_exchange",
-    )(block, w, w_down, positions.reshape(-1, 128))
+    )(block, gain[None], w, w_down, positions.reshape(-1, 128))
     return (
         gathered.reshape(n * rows, width),
         turned.reshape(3 * piece, width),
@@ -811,11 +821,6 @@
             ],
         ),
         compiler_params=pltpu.CompilerParams(vmem_limit_bytes=VMEM_LIMIT),
-        cost_estimate=pl.CostEstimate(
-            flops=10 * length * 1024 * cols,
-            bytes_accessed=16 * length * cols,
-            transcendentals=length * 1024 * heads,
-        ),
         name="attend_back",
     )(first, start, q, k, kt, v, o, lse, do, *tables)
 
@@ -1200,36 +1205,6 @@
     )(stat)
 
 
-def weight_kernel(a_ref, b_ref, o_ref):
-    o_ref[...] = tn(a_ref[...], b_ref[...]).astype(BF16)
-
-
-def weight_grad(a, b):
-    length, outs = a.shape
-    cols = b.shape[1]
-    block = 2 * TILE
-    return pl.pallas_call(
-        weight_kernel,
-        grid=(outs // block,),
-        out_shape=jax.ShapeDtypeStruct((outs, cols), BF16),
-        in_specs=[
-            pl.BlockSpec((length, block), lambda i: (0, i)),
-            pl.BlockSpec((length, cols), lambda i: (0, 0)),
-        ],
-        out_specs=pl.BlockSpec((block, cols), lambda i: (i, 0)),
-        compiler_params=pltpu.CompilerParams(vmem_limit_bytes=VMEM_LIMIT),
-        cost_estimate=pl.CostEstimate(
-            flops=2 * length * outs * cols,
-            bytes_accessed=2 * (length * outs + length * cols + outs * cols),
-            transcendentals=0,
-        ),
-        name="weight_grad",
-    )(a, b)
-
-
-STEP = 32
-
-
 def mix_kernel(att_ref, x_ref, w_ref, gm_ref, gf_ref, mix_ref, mid_ref, ffn_ref):
     j = pl.program_id(0)
     rows = att_ref.shape[0]
@@ -1329,20 +1304,15 @@
         out_specs=(whole, gain),
         scratch_shapes=[pltpu.VMEM((rows, width), F32)],
         compiler_params=pltpu.CompilerParams(vmem_limit_bytes=VMEM_LIMIT),
-        cost_estimate=pl.CostEstimate(
-            flops=2 * rows * width * width,
-            bytes_accessed=2 * width * width + 8 * rows * width,
-            transcendentals=0,
-        ),
         name="branch_pass",
     )(grad_branch, attended, w_out, gain_mix[None])
 
 
 def ffn_back_kernel(
-    n, gu_ref, wu_ref, hid_ref, wd_ref, mid_ref, cot_ref, gf_ref,
-    po_ref, gmid_ref, gbr_ref, ggf_ref,
-    gu, hid, own, far, twin_in, held, made,
-    local_sem, hid_sem, made_sem, send_sem, recv_sem,
+    n, gu_ref, wu_ref, hid_ref, wd_ref, all_ref, mid_ref, cot_ref, gf_ref,
+    po_ref, gd_ref, gmid_ref, gbr_ref, ggf_ref,
+    gu, hid, every, own, far, twin_in, held, made, made_grad,
+    local_sem, made_sem, grad_sem, send_sem, recv_sem,
 ):
     me, twin, near_x, near_y, across = places()
     rows, width = mid_ref.shape
@@ -1353,12 +1323,11 @@
     def cut(i, size=rows):
         return pl.ds(pl.multiple_of(i * size, size), size)
 
-    def load_hid(i, slot):
-        return pltpu.make_async_copy(hid_ref.at[cut(i)], hid.at[slot], hid_sem.at[slot])
-
-    load_gu = pltpu.make_async_copy(gu_ref, gu, local_sem)
-    load_gu.start()
-    load_hid(0, 0).start()
+    load_gu = pltpu.make_async_copy(gu_ref, gu, local_sem.at[0])
+    load_hid = pltpu.make_async_copy(hid_ref, hid, local_sem.at[1])
+    load_all = pltpu.make_async_copy(all_ref, every, local_sem.at[2])
+    for load in (load_gu, load_hid, load_all):
+        load.start()
     meet((me + twin, near_x, near_y))
     load_gu.wait()
 
@@ -1403,27 +1372,39 @@
         def _(i):
             slot = lax.rem(i, 2)
 
-            @pl.when(i + 1 < n)
-            def _():
-                load_hid(i + 1, 1 - slot).start()
-
-            load_hid(i, slot).wait()
-
             @pl.when(i >= 2)
             def _():
                 store(i - 2, slot).wait()
 
-            made[slot] = nt(hid[slot], wd_ref[...]).astype(BF16)
+            made[slot] = nt(hid[cut(i)], wd_ref[...]).astype(BF16)
             store(i, slot).start()
 
-    outputs(0, n // 2)
+    def store_grad(i, slot):
+        return pltpu.make_async_copy(
+            made_grad.at[slot], gd_ref.at[i], grad_sem.at[slot]
+        )
+
+    def weight_grads(first, last):
+        for i in range(first, last):
+            slot = i % 2
+            if i >= 2:
+                store_grad(i - 2, slot).wait()
+            made_grad[slot] = tn(
+                every[:, i * rows : (i + 1) * rows], hid[...]
+            ).astype(BF16)
+            store_grad(i, slot).start()
+
+    load_hid.wait()
+    load_all.wait()
+    weight_grads(0, n // 2)
     sends[1].wait_recv()
     add(1, half, half, held.at[1])
     sends[4].start()
     sends[0].wait_recv()
     add(2, 0, half, held.at[0])
     sends[5].start()
-    outputs(n // 2, n)
+    weight_grads(n // 2, n)
+    outputs(0, n)
     twins[3].wait_recv()
     for k in (2, 3, 4, 5):
         sends[k].wait_recv()
@@ -1449,11 +1430,12 @@
 
     for i in (n - 2, n - 1):
         store(i, i % 2).wait()
+        store_grad(i, i % 2).wait()
     for send in twins + sends:
         send.wait_send()
 
 
-def ffn_back(grad_upper, w_up, hidden, w_down, middle, cot, gain, collective_id):
+def ffn_back(grad_upper, w_up, hidden, w_down, cot_full, middle, cot, gain, collective_id):
     n = lax.axis_size("seq")
     rows, width = middle.shape
     feats = w_up.shape[0]
@@ -1462,28 +1444,33 @@
         value = scatter_seq(nn(grad_upper, w_up).astype(BF16))
         part, gain_part = norm_back(value, normal, scale, gain)
         grad = cot.astype(F32) + part
-        return nt(hidden, w_down).astype(BF16), grad, grad.astype(BF16), gain_part[None]
+        down = tn(cot_full, hidden).astype(BF16).reshape(n, rows, feats)
+        outputs = nt(hidden, w_down).astype(BF16)
+        return outputs, down, grad, grad.astype(BF16), gain_part[None]
     dma = pltpu.SemaphoreType.DMA
     block = pltpu.VMEM((4, rows, width), BF16)
     return pl.pallas_call(
         functools.partial(ffn_back_kernel, n),
         out_shape=(
             jax.ShapeDtypeStruct((n * rows, width), BF16),
+            jax.ShapeDtypeStruct((n, rows, feats), BF16),
             jax.ShapeDtypeStruct((rows, width), F32),
             jax.ShapeDtypeStruct((rows, width), BF16),
             jax.ShapeDtypeStruct((1, width), F32),
         ),
-        in_specs=[ANY, INSIDE, ANY, INSIDE, INSIDE, INSIDE, INSIDE],
-        out_specs=(ANY, INSIDE, INSIDE, INSIDE),
+        in_specs=[ANY, INSIDE, ANY, INSIDE, ANY, INSIDE, INSIDE, INSIDE],
+        out_specs=(ANY, ANY, INSIDE, INSIDE, INSIDE),
         scratch_shapes=[
             pltpu.VMEM((n * rows, feats), BF16),
-            pltpu.VMEM((2, rows, feats), BF16),
+            pltpu.VMEM((n * rows, feats), BF16),
+            pltpu.VMEM((n * rows, width), BF16),
             block,
             block,
             block,
             pltpu.VMEM((6, rows // 2, width), BF16),
             pltpu.VMEM((2, rows, width), BF16),
-            dma,
+            pltpu.VMEM((2, rows, feats), BF16),
+            dma((3,)),
             dma((2,)),
             dma((2,)),
             dma((10,)),
@@ -1493,7 +1480,7 @@
             collective_id=collective_id, has_side_effects=True, vmem_limit_bytes=VMEM_LIMIT
         ),
         name="ffn_back",
-    )(grad_upper, w_up, hidden, w_down, middle, cot, gain[None])
+    )(grad_upper, w_up, hidden, w_down, cot_full, middle, cot, gain[None])
 
 
 CHUNK = 64
@@ -2004,6 +1991,26 @@
     )
 
 
+def widen_kernel(*refs):
+    half = len(refs) // 2
+    for source, target in zip(refs[:half], refs[half:], strict=True):
+        target[...] = source[...].astype(F32)
+
+
+def widen(arrays):
+    steps = 8
+    specs = [pl.BlockSpec((x.shape[0] // steps, x.shape[1]), lambda i: (i, 0)) for x in arrays]
+    return pl.pallas_call(
+        widen_kernel,
+        grid=(steps,),
+        out_shape=[jax.ShapeDtypeStruct(x.shape, F32) for x in arrays],
+        in_specs=specs,
+        out_specs=specs,
+        compiler_params=pltpu.CompilerParams(vmem_limit_bytes=VMEM_LIMIT),
+        name="widen",
+    )(*arrays)
+
+
 def body(
     inputs,
     segment_ids,
@@ -2023,12 +2030,10 @@
     length = local * n
     feats = w_up.shape[0]
     x_low = inputs[0]
-    x = x_low.astype(F32)
     cot = cotangent[0]
     segment = segment_ids[0]
 
     w_out_full = lax.all_gather(w_out, "seq", axis=0, tiled=True)
-    normed = (norm_parts(x)[0] * gain_attn).astype(BF16)
     before = [jnp.sum((segment < d).astype(jnp.int32)) for d in range(1, DOCS)]
     start = jnp.zeros_like(segment)
     for d in range(1, DOCS):
@@ -2038,7 +2043,7 @@
     start_row = start[None, :]
 
     normed_full, w_heads, w_down_cols, tables = start_exchange(
-        normed, w_qkv, w_down, positions.astype(F32), 1
+        x_low, gain_attn, w_qkv, w_down, positions.astype(F32), 1
     )
     cot_full = lax.all_gather(lax.optimization_barrier(cot), "seq", axis=0, tiled=True)
 
@@ -2054,10 +2059,8 @@
     grad_w_up = tn(grad_upper, ffn_full).astype(BF16)
     grad_upper, grad_w_up = lax.optimization_barrier((grad_upper, grad_w_up))
     grad_w_up = lax.psum(grad_w_up, "batch")
-    grad_w_down = weight_grad(cot_full, hidden).reshape(n, local, feats)
-    grad_upper, grad_w_down = lax.optimization_barrier((grad_upper, grad_w_down))
-    part_outputs, grad_middle, grad_branch, grad_gain_ffn = ffn_back(
-        grad_upper, w_up, hidden, w_down_cols, middle, cot, gain_ffn, 4
+    part_outputs, grad_w_down, grad_middle, grad_branch, grad_gain_ffn = ffn_back(
+        grad_upper, w_up, hidden, w_down_cols, cot_full, middle, cot, gain_ffn, 4
     )
     grad_att, grad_gain_mix = branch_pass(grad_branch, attended, w_out_full, gain_mix)
     grad_heads = tokens_to_heads(grad_att, 5)
@@ -2066,8 +2069,10 @@
     grads = attend_back(
         first, start_row, q, k, kt, v, attended_heads, lse, grad_heads, tables
     )
+    grad_w_qkv = tn(grads, normed_full).astype(BF16).reshape(3, -1, width)
+    grad_w_qkv, grad_w_up = lax.optimization_barrier((grad_w_qkv, grad_w_up))
     grad_w_qkv, grad_w_down, grad_w_out, grad_inputs, outputs, gains = finish(
-        tn(grads, normed_full).astype(BF16).reshape(3, -1, width),
+        grad_w_qkv,
         grad_w_down,
         tn(grad_branch, mix_in).astype(BF16),
         nn(grads, w_heads).astype(BF16),
@@ -2079,12 +2084,13 @@
         (grad_gain_mix, grad_gain_ffn, grad_gain_here),
         6,
     )
+    grad_w_qkv, grad_w_up = widen([grad_w_qkv, grad_w_up])
     return (
         outputs[None],
         grad_inputs[None],
-        grad_w_qkv.astype(F32),
+        grad_w_qkv,
         grad_w_out,
-        grad_w_up.astype(F32),
+        grad_w_up,
         grad_w_down,
         *gains,
     )

time: 733 us -> 719 us (0.981)
  waiting for transfers between devices: 1.4 us -> 19.8 us
  other arithmetic: 21.9 us -> 5.18 us
  Pallas kernels: 622 us -> 613 us
    psum x1, waiting for transfers between devices: 0.01 us -> 18.4 us  [body(): grad_w_up = lax.psum(grad_w_up, 'batch')]
    convert_element_type x3 -> x0, other arithmetic: 13.6 us -> none  [the longest x1 6.81 us: body(): grad_w_up.astype(F32)]
  transfers between devices with their start and end apart: 4 -> 4, of which waited for: 0 -> 1; matrix products, arithmetic and copies ran while one was open for 6% -> 4% of each run, Pallas kernels for 76% -> 44%
where the time goes in v9:
time: 719 us; the launch traced here: 713 us
  Pallas kernels  613 us (85%)
  matrix products  39.8 us (6%)
  waiting for transfers between devices  19.8 us (3%)
  local copies, waits for them, and re-layouts  15.7 us (2%)
  between operations  14.3 us (2%)
    pallas_call x1, Pallas kernels, finish(): pl.pallas_call(functools.partial(finish_kernel, n, depth), out_shape=(jax...  229 us
    pallas_call x1, Pallas kernels, start_exchange(): pl.pallas_call(functools.partial(start_kernel, n, depth), out_shape=(jax....  128 us
    pallas_call x1, Pallas kernels, ffn_pass(): pl.pallas_call(functools.partial(ffn_kernel, n), out_shape=(jax.ShapeDtyp...  62 us
    pallas_call x1, Pallas kernels, ffn_back(): pl.pallas_call(functools.partial(ffn_back_kernel, n), out_shape=(jax.Shap...  51.6 us
    pallas_call x1, Pallas kernels, attend_back(): pl.pallas_call(functools.partial(attend_back_kernel, heads), out_shape=ja...  32.9 us
    dot_general x3, matrix products, tn(): lax.dot_general(a, b, (((0,), (0,)), ((), ())), preferred_element_type=F32)  30.8 us
    pallas_call x1, Pallas kernels, attend(): pl.pallas_call(functools.partial(attend_kernel, heads), out_shape=(jax.Sh...  24 us
    pallas_call x1, Pallas kernels, heads_to_tokens(): pl.pallas_call(functools.partial(heads_to_tokens_kernel, n), out_shape=ja...  21.7 us
  transfers between devices with their start and end apart: 4, of which 1 were waited for; matrix products, arithmetic and copies ran while one was open for 4% of the time, Pallas kernels for 44%

profile of v9, /device:TPU:0, one launch (start us, length us, event | category | flops | bytes accessed | tf_op | source)
XLA Modules:
  0.0 712.5 jit_solution(8708203108263216709)
XLA Ops:
  7.2 0.0 all-gather.3.cloned.1.call-start
  7.2 0.7 all-gather.3.cloned.1.call-update
  7.9 0.0 all-gather.5.cloned.1.call-start
  8.0 0.7 all-gather.5.cloned.1.call-update
  8.7 0.0 all-reduce.2.cloned.1.call-start
  8.7 1.4 fusion
  10.1 2.7 compare_select_fusion.2.start_ref
  12.8 0.0 copy-start.6
  12.8 0.1 slice.15
  12.9 0.6 subtract_convert_fusion.pos_ref
  13.5 127.7 %start_exchange.1 = (bf16[8,256,2048]{2,1,0:T(8,128)(2,1)}, bf16[3,256,2048]{2,1,0:T(8,128)(2,1)}, bf16[8,4,64,1024]{3,2,1,0:T(8,128)(2,1)}, f32[2048,128]{1,0:T...) custom-call(bf16[256,2048]{1,0:T(8,128)(2,1)} %bitcast.39, f32[1,2048]{1,0:T(1,128)} %bitcast.56, ...), custom_call_target="tpu_custom_call" | custom-call | tf_op jit(solution)/shard_map/start_exchange/pallas_call | solution.py:409
  141.2 0.0 copy-done.6
  141.2 0.5 and_select_fusion.first_ref
  141.8 14.3 %project_qkv.1 = (bf16[2048,256]{1,0:T(8,128)(2,1)}, bf16[2048,256]{1,0:T(8,128)(2,1)}, bf16[2048,256]{1,0:T(8,128)(2,1)}, bf16[256,2048]{1,0:T(8,128)(2,1)}, bf16[256,2048]{1,0:T(8,128)(2,1)}) custom-call(bf16[2048,2048]{1,0:T(8,128)(2,1)} %bitcast.64, bf16[768,2048]{1,0:T(8,128)(2,1)} %bitcast.67, f32[2048,128]{1,0:T(8,128)} %get-tuple-element.54.cq_ref, ...), custom_call_target="tpu_custom_call" | custom-call | flops 6442450944 | bytes 16777216 | tf_op jit(solution)/shard_map/project_qkv/pallas_call | solution.py:604
  156.1 24.0 %attend.1 = (bf16[2048,256]{1,0:T(8,128)(2,1)}, f32[8,4,256]{2,1,0:T(4,128)}) custom-call(s32[8]{0:T(128)} %and_select_fusion.first_ref, s32[1,2048]{1,0:T(1,128)} %copy-done.6, bf16[2048,256]{1,0:T(8,128)(2,1)} %get-tuple-element.58.q_ref, bf16[2048,256]{1,0:T(8,128)(2,1)} %get-tuple-element.59.k_ref, bf16[256,2048]{1,0:T(8,128)(2,1)} %get-tuple-element.62.vt_ref), custom_call_target="tpu_custom_call" | custom-call | flops 2147483648 | bytes 4194304 | tf_op jit(solution)/shard_map/attend/pallas_call | solution.py:684
  180.1 21.7 %heads_to_tokens.1.att_ref = bf16[256,2048]{1,0:T(8,128)(2,1)} custom-call(bf16[2048,256]{1,0:T(8,128)(2,1)} %get-tuple-element.63.x_ref.o_ref), custom_call_target="tpu_custom_call" | custom-call | tf_op jit(solution)/shard_map/heads_to_tokens/pallas_call | solution.py:504
  201.7 1.3 dynamic_slice.3
  203.0 13.8 %mix_pass.1 = (bf16[256,2048]{1,0:T(8,128)(2,1)}, f32[256,2048]{1,0:T(8,128)}, bf16[256,2048]{1,0:T(8,128)(2,1)}) custom-call(bf16[256,2048]{1,0:T(8,128)(2,1)} %heads_to_tokens.1.att_ref, bf16[256,2048]{1,0:T(8,128)(2,1)} %bitcast.40, bf16[2048,2048]{1,0:T(8,128)(2,1)} %all-gather.3.cloned.1.call-done.w_ref, f32[1,2048]{1,0:T(1,128)} %bitcast.54, ...), custom_call_target="tpu_custom_call" | custom-call | flops 2147483648 | bytes 14680064 | tf_op jit(solution)/shard_map/mix_pass/pallas_call | solution.py:1240
  216.8 62.0 %ffn_pass.1 = (bf16[8,256,2048]{2,1,0:T(8,128)(2,1)}, bf16[2048,1024]{1,0:T(8,128)(2,1)}, bf16[2048,1024]{1,0:T(8,128)(2,1)}, f32[1,1024]{1,0:T(1,128)}) custom-call(bf16[256,2048]{1,0:T(8,128)(2,1)} %get-tuple-element.65.x_ref, bf16[1024,2048]{1,0:T(8,128)(2,1)} %wu_ref.3, bf16[2048,2048]{1,0:T(8,128)(2,1)} %all-gather.5.cloned.1.call-done.cot_ref.all_ref, ...), custom_call_target="tpu_custom_call" | custom-call | tf_op jit(solution)/shard_map/ffn_pass/pallas_call | solution.py:1114
  278.8 14.5 %convolution_convert_fusion.2 = bf16[1024,2048]{1,0:T(8,128)(2,1)} fusion(bf16[2048,1024]{1,0:T(8,128)(2,1)} %get-tuple-element.69.gu_ref, bf16[2048,2048]{1,0:T(8,128)(2,1)} %bitcast.66), kind=kOutput, calls=%fused_computation.2 | convolution fusion | flops 8592031744 | bytes 16777216 | tf_op jit(solution)/shard_map/dot_general | solution.py:38
  293.3 0.0 all-reduce.2.cloned.1.call-update
  293.3 51.6 %ffn_back.1 = (bf16[2048,2048]{1,0:T(8,128)(2,1)}, bf16[8,256,1024]{2,1,0:T(8,128)(2,1)}, f32[256,2048]{1,0:T(8,128)}, bf16[256,2048]{1,0:T(8,128)(2,1)}, f32[1,2048]{1,0:T(1,128)}) custom-call(bf16[2048,1024]{1,0:T(8,128)(2,1)} %get-tuple-element.69.gu_ref, bf16[1024,2048]{1,0:T(8,128)(2,1)} %wu_ref.3, bf16[2048,1024]{1,0:T(8,128)(2,1)} %get-tuple-element.70.hid_ref, ...), custom_call_target="tpu_custom_call" | custom-call | tf_op jit(solution)/shard_map/ffn_back/pallas_call | solution.py:1452
  344.9 12.9 %branch_pass.1 = (bf16[256,2048]{1,0:T(8,128)(2,1)}, f32[1,2048]{1,0:T(1,128)}) custom-call(bf16[256,2048]{1,0:T(8,128)(2,1)} %get-tuple-element.73.gbr_ref, bf16[256,2048]{1,0:T(8,128)(2,1)} %heads_to_tokens.1.att_ref, bf16[2048,2048]{1,0:T(8,128)(2,1)} %all-gather.3.cloned.1.call-done.w_ref, f32[1,2048]{1,0:T(1,128)} %bitcast.55), custom_call_target="tpu_custom_call" | custom-call | tf_op jit(solution)/shard_map/branch_pass/pallas_call | solution.py:1296
  357.8 13.8 %tokens_to_heads.1.do_ref = bf16[2048,256]{1,0:T(8,128)(2,1)} custom-call(bf16[256,2048]{1,0:T(8,128)(2,1)} %get-tuple-element.74.x_ref), custom_call_target="tpu_custom_call" | custom-call | tf_op jit(solution)/shard_map/tokens_to_heads/pallas_call | solution.py:541
  371.6 4.8 all-to-all-start
  376.4 0.0 copy-start
  376.4 0.0 copy-start.4
  376.4 32.9 %attend_back.1 = bf16[2048,768]{1,0:T(8,128)(2,1)} custom-call(s32[8]{0:T(128)} %and_select_fusion.first_ref, s32[1,2048]{1,0:T(1,128)} %copy-done.6, bf16[2048,256]{1,0:T(8,128)(2,1)} %get-tuple-element.58.q_ref, bf16[2048,256]{1,0:T(8,128)(2,1)} %get-tuple-element.59.k_ref, bf16[256,2048]{1,0:T(8,128)(2,1)} %get-tuple-element.60.kt_ref, ...), custom_call_target="tpu_custom_call" | custom-call | tf_op jit(solution)/shard_map/attend_back/pallas_call | solution.py:799
  409.3 0.0 copy-done
  409.3 0.0 copy-done.4
  409.3 0.0 copy-start.1
  409.3 5.8 convolution_convert_fusion.1
  415.1 0.0 copy-done.1
  415.1 10.6 %convolution_convert_fusion.3 = bf16[768,2048]{1,0:T(8,128)(2,1)} fusion(bf16[2048,768]{1,0:T(8,128)(2,1)S(1)} %copy-done.1, bf16[2048,2048]{1,0:T(8,128)(2,1)} %bitcast.65), kind=kOutput, calls=%fused_computation.3 | convolution fusion | flops 6444023808 | bytes 14680064 | tf_op jit(solution)/shard_map/dot_general | solution.py:38
  425.7 0.0 copy-done.7
  425.7 9.0 %convolution_convert_fusion = bf16[2048,2048]{1,0:T(8,128)(2,1)} fusion(bf16[2048,768]{1,0:T(8,128)(2,1)S(1)} %copy-done.1, bf16[768,2048]{1,0:T(8,128)(2,1)S(1)} %bitcast.68), kind=kOutput, calls=%fused_computation | convolution fusion | flops 6446645248 | bytes 14680064 | tf_op jit(solution)/shard_map/dot_general | solution.py:30
  434.7 18.4 %all-reduce.2.cloned.1.call-done.refs_1_ = bf16[1024,2048]{1,0:T(8,128)(2,1)} async-done(((bf16[1024,2048]{1,0:T(8,128)(2,1)}), bf16[1024,2048]{1,0:T(8,128)(2,1)}) %all-reduce.2.cloned.1.call-update) | async-done | bytes 4194320 | tf_op jit(solution)/shard_map/psum | solution.py:2061
  453.1 0.0 all-to-all-done.gd_ref
  453.1 228.7 %finish.1 = (bf16[3,256,2048]{2,1,0:T(8,128)(2,1)}, f32[256,8192]{1,0:T(8,128)}, f32[256,2048]{1,0:T(8,128)}, f32[256,2048]{1,0:T(8,128)}, bf16[256,2048]{1,0:T(8,128)(2,1)}, /*index=5*/f32[16,2048]{1,0:T(8,128)}) custom-call(bf16[3,256,2048]{2,1,0:T(8,128)(2,1)} %bitcast.46, bf16[8,256,1024]{2,1,0:T(8,128)(2,1)} %all-to-all-done.gd_ref, ...), custom_call_target="tpu_custom_call" | custom-call | tf_op jit(solution)/shard_map/finish/pallas_call | solution.py:1930
  681.8 0.0 copy-start.5
  681.8 1.6 fusion.3
  683.4 0.8 slice_bitcast_fusion
  684.1 0.6 copy.23
  684.8 9.5 %widen.1 = (f32[768,2048]{1,0:T(8,128)}, f32[1024,2048]{1,0:T(8,128)}) custom-call(bf16[768,2048]{1,0:T(8,128)(2,1)} %bitcast.47, bf16[1024,2048]{1,0:T(8,128)(2,1)} %all-reduce.2.cloned.1.call-done.refs_1_), custom_call_target="tpu_custom_call" | custom-call | tf_op jit(solution)/shard_map/widen/pallas_call | solution.py:2003
  694.3 1.0 copy.29
  695.2 1.3 copy.30
  696.6 1.3 copy.31
  697.9 7.7 %copy.32 = f32[256,8192]{1,0:T(8,128)} copy(f32[256,8192]{1,0:T(8,128)} %get-tuple-element.115) | data formatting | bytes 16777216
  (8 shorter events, 0.0 us)
Async XLA Ops:
  7.2 195.9 %all-gather.3.cloned.1.call-start = ((), (), s32[]{:S(2)}) async-start(), calls=%async_computation.1 | async-start | bytes 9437184 | tf_op jit(solution)/shard_map/all_gather | solution.py:2036
  7.9 208.9 %all-gather.5.cloned.1.call-start = ((), (), s32[]{:S(2)}) async-start(), calls=%async_computation.2 | async-start | bytes 9437184 | tf_op jit(solution)/shard_map/all_gather | solution.py:2048
  8.7 444.4 %all-reduce.2.cloned.1.call-start = ((), (), s32[]{:S(2)}) async-start(), calls=%async_computation.3 | async-start | bytes 8388608 | tf_op jit(solution)/shard_map/psum | solution.py:2061
  12.8 128.5 %copy-start.6 = (s32[1,2048]{1,0:T(1,128)}, s32[1,2048]{1,0:T(1,128)S(1)}, u32[]{:S(2)}) copy-start(s32[1,2048]{1,0:T(1,128)S(1)} %compare_select_fusion.2.start_ref) | copy-start | bytes 24580
  371.6 81.5 %all-to-all-start = ((bf16[8,256,1024]{2,1,0:T(8,128)(2,1)}), bf16[8,256,1024]{2,1,0:T(8,128)(2,1)}, u32[]{:S(2)}, u32[]{:S(2)}) async-start(bf16[8,256,1024]{2,1,0:T(8,128)(2,1)} %get-tuple-element.78), calls=%async_computation | async-start | bytes 8388608 | tf_op jit(solution)/shard_map/all_to_all | solution.py:2068
  376.4 32.9 %copy-start = (bf16[256,2048]{1,0:T(8,128)(2,1)S(1)}, bf16[256,2048]{1,0:T(8,128)(2,1)}, u32[]{:S(2)}) copy-start(bf16[256,2048]{1,0:T(8,128)(2,1)} %get-tuple-element.73.gbr_ref) | copy-start | bytes 3145732
  376.4 32.9 %copy-start.4 = (bf16[256,2048]{1,0:T(8,128)(2,1)S(1)}, bf16[256,2048]{1,0:T(8,128)(2,1)}, u32[]{:S(2)}) copy-start(bf16[256,2048]{1,0:T(8,128)(2,1)} %get-tuple-element.79) | copy-start | bytes 3145732
  409.3 5.8 copy-start.1
  415.1 10.6 %copy-start.7 = (bf16[3,256,2048]{2,1,0:T(8,128)(2,1)S(1)}, bf16[3,256,2048]{2,1,0:T(8,128)(2,1)}, u32[]{:S(2)}) copy-start(bf16[3,256,2048]{2,1,0:T(8,128)(2,1)} %get-tuple-element.53) | copy-start | bytes 9437188
  681.8 12.5 %copy-start.5 = (bf16[256,2048]{1,0:T(8,128)(2,1)S(1)}, bf16[256,2048]{1,0:T(8,128)(2,1)}, u32[]{:S(2)}) copy-start(bf16[256,2048]{1,0:T(8,128)(2,1)} %get-tuple-element.85) | copy-start | bytes 3145732
  684.8 10.5 %copy-start.3 = (f32[256,2048]{1,0:T(8,128)S(1)}, f32[256,2048]{1,0:T(8,128)}, u32[]{:S(2)}) copy-start(f32[256,2048]{1,0:T(8,128)} %get-tuple-element.86) | copy-start | bytes 6291460
  694.3 2.3 copy-start.2
Sparse Core Ops, SparseCore 0:
  9.9 96.2 all-gather.2
  108.1 56.9 all-gather.4
  293.5 159.5 all-reduce.1

commit v10 on v9

--- a/solution.py
+++ b/solution.py
@@ -2045,7 +2045,8 @@
     normed_full, w_heads, w_down_cols, tables = start_exchange(
         x_low, gain_attn, w_qkv, w_down, positions.astype(F32), 1
     )
-    cot_full = lax.all_gather(lax.optimization_barrier(cot), "seq", axis=0, tiled=True)
+    cot_late, _ = lax.optimization_barrier((cot, w_heads))
+    cot_full = lax.all_gather(cot_late, "seq", axis=0, tiled=True)
 
     q, k, v, kt, vt = project_qkv(normed_full, w_heads, tables)
     attended_heads, lse = attend(first, start_row, q, k, vt)

time: 719 us -> 733 us (1.019)
  matrix products: 39.8 us -> 51.1 us
  Pallas kernels: 613 us -> 622 us
    dot_general x3, matrix products: 30.8 us -> 42.1 us  [tn(): lax.dot_general(a, b, (((0,), (0,)), ((), ())), preferred_element_type=F32)]
    pallas_call x1, Pallas kernels: 21.7 us -> 30.5 us  [heads_to_tokens(): pl.pallas_call(functools.partial(heads_to_tokens_kernel, n), out_shape=ja...]
where the time goes in v10:
time: 733 us; the launch traced here: 728 us
  Pallas kernels  622 us (85%)
  matrix products  51.1 us (7%)
  local copies, waits for them, and re-layouts  15.7 us (2%)
  waiting for transfers between devices  14.5 us (2%)
  between operations  14.1 us (2%)
    pallas_call x1, Pallas kernels, finish(): pl.pallas_call(functools.partial(finish_kernel, n, depth), out_shape=(jax...  229 us
    pallas_call x1, Pallas kernels, start_exchange(): pl.pallas_call(functools.partial(start_kernel, n, depth), out_shape=(jax....  127 us
    pallas_call x1, Pallas kernels, ffn_pass(): pl.pallas_call(functools.partial(ffn_kernel, n), out_shape=(jax.ShapeDtyp...  62.5 us
    pallas_call x1, Pallas kernels, ffn_back(): pl.pallas_call(functools.partial(ffn_back_kernel, n), out_shape=(jax.Shap...  51.6 us
    dot_general x3, matrix products, tn(): lax.dot_general(a, b, (((0,), (0,)), ((), ())), preferred_element_type=F32)  42.1 us
    pallas_call x1, Pallas kernels, attend_back(): pl.pallas_call(functools.partial(attend_back_kernel, heads), out_shape=ja...  33.5 us
    pallas_call x1, Pallas kernels, heads_to_tokens(): pl.pallas_call(functools.partial(heads_to_tokens_kernel, n), out_shape=ja...  30.5 us
    pallas_call x1, Pallas kernels, attend(): pl.pallas_call(functools.partial(attend_kernel, heads), out_shape=(jax.Sh...  24.1 us
  transfers between devices with their start and end apart: 4, of which 1 were waited for; matrix products, arithmetic and copies ran while one was open for 4% of the time, Pallas kernels for 44%

profile of v10, /device:TPU:0, one launch (start us, length us, event | category | flops | bytes accessed | tf_op | source)
XLA Modules:
  0.0 727.8 jit_solution(9672788401192857262)
XLA Ops:
  7.2 0.0 all-gather.3.cloned.1.call-start
  7.2 0.7 all-gather.3.cloned.1.call-update
  7.9 0.0 all-gather.5.cloned.1.call-start
  8.0 1.4 fusion
  9.4 2.7 compare_select_fusion.2.start_ref
  12.0 0.0 copy-start.6
  12.0 0.6 subtract_convert_fusion.pos_ref
  12.6 127.3 %start_exchange.1 = (bf16[8,256,2048]{2,1,0:T(8,128)(2,1)}, bf16[3,256,2048]{2,1,0:T(8,128)(2,1)}, bf16[8,4,64,1024]{3,2,1,0:T(8,128)(2,1)}, f32[2048,128]{1,0:T...) custom-call(bf16[256,2048]{1,0:T(8,128)(2,1)} %bitcast.39, f32[1,2048]{1,0:T(1,128)} %bitcast.56, ...), custom_call_target="tpu_custom_call" | custom-call | tf_op jit(solution)/shard_map/start_exchange/pallas_call | solution.py:409
  139.9 0.0 all-gather.5.cloned.1.call-update
  139.9 0.0 all-reduce.2.cloned.1.call-start
  140.0 0.0 copy-done.6
  140.0 0.1 slice.15
  140.1 0.5 and_select_fusion.first_ref
  140.6 14.2 %project_qkv.1 = (bf16[2048,256]{1,0:T(8,128)(2,1)}, bf16[2048,256]{1,0:T(8,128)(2,1)}, bf16[2048,256]{1,0:T(8,128)(2,1)}, bf16[256,2048]{1,0:T(8,128)(2,1)}, bf16[256,2048]{1,0:T(8,128)(2,1)}) custom-call(bf16[2048,2048]{1,0:T(8,128)(2,1)} %bitcast.64, bf16[768,2048]{1,0:T(8,128)(2,1)} %bitcast.67, f32[2048,128]{1,0:T(8,128)} %get-tuple-element.55.cq_ref, ...), custom_call_target="tpu_custom_call" | custom-call | flops 6442450944 | bytes 16777216 | tf_op jit(solution)/shard_map/project_qkv/pallas_call | solution.py:604
  154.8 24.1 %attend.1 = (bf16[2048,256]{1,0:T(8,128)(2,1)}, f32[8,4,256]{2,1,0:T(4,128)}) custom-call(s32[8]{0:T(128)} %and_select_fusion.first_ref, s32[1,2048]{1,0:T(1,128)} %copy-done.6, bf16[2048,256]{1,0:T(8,128)(2,1)} %get-tuple-element.59.q_ref, bf16[2048,256]{1,0:T(8,128)(2,1)} %get-tuple-element.60.k_ref, bf16[256,2048]{1,0:T(8,128)(2,1)} %get-tuple-element.63.vt_ref), custom_call_target="tpu_custom_call" | custom-call | flops 2147483648 | bytes 4194304 | tf_op jit(solution)/shard_map/attend/pallas_call | solution.py:684
  178.9 30.5 %heads_to_tokens.1.att_ref = bf16[256,2048]{1,0:T(8,128)(2,1)} custom-call(bf16[2048,256]{1,0:T(8,128)(2,1)} %get-tuple-element.64.x_ref.o_ref), custom_call_target="tpu_custom_call" | custom-call | tf_op jit(solution)/shard_map/heads_to_tokens/pallas_call | solution.py:504
  209.4 1.3 dynamic_slice.3
  210.7 13.8 %mix_pass.1 = (bf16[256,2048]{1,0:T(8,128)(2,1)}, f32[256,2048]{1,0:T(8,128)}, bf16[256,2048]{1,0:T(8,128)(2,1)}) custom-call(bf16[256,2048]{1,0:T(8,128)(2,1)} %heads_to_tokens.1.att_ref, bf16[256,2048]{1,0:T(8,128)(2,1)} %bitcast.40, bf16[2048,2048]{1,0:T(8,128)(2,1)} %all-gather.3.cloned.1.call-done.w_ref, f32[1,2048]{1,0:T(1,128)} %bitcast.54, ...), custom_call_target="tpu_custom_call" | custom-call | flops 2147483648 | bytes 14680064 | tf_op jit(solution)/shard_map/mix_pass/pallas_call | solution.py:1240
  224.5 62.5 %ffn_pass.1 = (bf16[8,256,2048]{2,1,0:T(8,128)(2,1)}, bf16[2048,1024]{1,0:T(8,128)(2,1)}, bf16[2048,1024]{1,0:T(8,128)(2,1)}, f32[1,1024]{1,0:T(1,128)}) custom-call(bf16[256,2048]{1,0:T(8,128)(2,1)} %get-tuple-element.66.x_ref, bf16[1024,2048]{1,0:T(8,128)(2,1)} %wu_ref.3, bf16[2048,2048]{1,0:T(8,128)(2,1)} %all-gather.5.cloned.1.call-done.cot_ref.all_ref, ...), custom_call_target="tpu_custom_call" | custom-call | tf_op jit(solution)/shard_map/ffn_pass/pallas_call | solution.py:1114
  287.0 25.7 %convolution_convert_fusion.2 = bf16[1024,2048]{1,0:T(8,128)(2,1)} fusion(bf16[2048,1024]{1,0:T(8,128)(2,1)} %get-tuple-element.71.gu_ref, bf16[2048,2048]{1,0:T(8,128)(2,1)} %bitcast.66), kind=kOutput, calls=%fused_computation.2 | convolution fusion | flops 8592031744 | bytes 16777216 | tf_op jit(solution)/shard_map/dot_general | solution.py:38
  312.8 0.0 all-reduce.2.cloned.1.call-update
  312.8 51.6 %ffn_back.1 = (bf16[2048,2048]{1,0:T(8,128)(2,1)}, bf16[8,256,1024]{2,1,0:T(8,128)(2,1)}, f32[256,2048]{1,0:T(8,128)}, bf16[256,2048]{1,0:T(8,128)(2,1)}, f32[1,2048]{1,0:T(1,128)}) custom-call(bf16[2048,1024]{1,0:T(8,128)(2,1)} %get-tuple-element.71.gu_ref, bf16[1024,2048]{1,0:T(8,128)(2,1)} %wu_ref.3, bf16[2048,1024]{1,0:T(8,128)(2,1)} %get-tuple-element.72.hid_ref, ...), custom_call_target="tpu_custom_call" | custom-call | tf_op jit(solution)/shard_map/ffn_back/pallas_call | solution.py:1452
  364.4 12.9 %branch_pass.1 = (bf16[256,2048]{1,0:T(8,128)(2,1)}, f32[1,2048]{1,0:T(1,128)}) custom-call(bf16[256,2048]{1,0:T(8,128)(2,1)} %get-tuple-element.75.gbr_ref, bf16[256,2048]{1,0:T(8,128)(2,1)} %heads_to_tokens.1.att_ref, bf16[2048,2048]{1,0:T(8,128)(2,1)} %all-gather.3.cloned.1.call-done.w_ref, f32[1,2048]{1,0:T(1,128)} %bitcast.55), custom_call_target="tpu_custom_call" | custom-call | tf_op jit(solution)/shard_map/branch_pass/pallas_call | solution.py:1296
  377.3 13.7 %tokens_to_heads.1.do_ref = bf16[2048,256]{1,0:T(8,128)(2,1)} custom-call(bf16[256,2048]{1,0:T(8,128)(2,1)} %get-tuple-element.76.x_ref), custom_call_target="tpu_custom_call" | custom-call | tf_op jit(solution)/shard_map/tokens_to_heads/pallas_call | solution.py:541
  391.0 5.0 all-to-all-start
  396.0 0.0 copy-start
  396.0 0.0 copy-start.4
  396.0 33.5 %attend_back.1 = bf16[2048,768]{1,0:T(8,128)(2,1)} custom-call(s32[8]{0:T(128)} %and_select_fusion.first_ref, s32[1,2048]{1,0:T(1,128)} %copy-done.6, bf16[2048,256]{1,0:T(8,128)(2,1)} %get-tuple-element.59.q_ref, bf16[2048,256]{1,0:T(8,128)(2,1)} %get-tuple-element.60.k_ref, bf16[256,2048]{1,0:T(8,128)(2,1)} %get-tuple-element.61.kt_ref, ...), custom_call_target="tpu_custom_call" | custom-call | tf_op jit(solution)/shard_map/attend_back/pallas_call | solution.py:799
  429.5 0.0 copy-done
  429.5 0.0 copy-done.4
  429.5 0.0 copy-start.1
  429.5 5.8 convolution_convert_fusion.1
  435.3 0.0 copy-done.1
  435.3 10.6 %convolution_convert_fusion.3 = bf16[768,2048]{1,0:T(8,128)(2,1)} fusion(bf16[2048,768]{1,0:T(8,128)(2,1)S(1)} %copy-done.1, bf16[2048,2048]{1,0:T(8,128)(2,1)} %bitcast.65), kind=kOutput, calls=%fused_computation.3 | convolution fusion | flops 6444023808 | bytes 14680064 | tf_op jit(solution)/shard_map/dot_general | solution.py:38
  445.9 0.0 copy-done.7
  445.9 9.0 %convolution_convert_fusion = bf16[2048,2048]{1,0:T(8,128)(2,1)} fusion(bf16[2048,768]{1,0:T(8,128)(2,1)S(1)} %copy-done.1, bf16[768,2048]{1,0:T(8,128)(2,1)S(1)} %bitcast.68), kind=kOutput, calls=%fused_computation | convolution fusion | flops 6446645248 | bytes 14680064 | tf_op jit(solution)/shard_map/dot_general | solution.py:30
  454.9 13.8 %all-reduce.2.cloned.1.call-done.refs_1_ = bf16[1024,2048]{1,0:T(8,128)(2,1)} async-done(((bf16[1024,2048]{1,0:T(8,128)(2,1)}), bf16[1024,2048]{1,0:T(8,128)(2,1)}) %all-reduce.2.cloned.1.call-update) | async-done | bytes 4194320 | tf_op jit(solution)/shard_map/psum | solution.py:2062
  468.6 0.0 all-to-all-done.gd_ref
  468.6 228.7 %finish.1 = (bf16[3,256,2048]{2,1,0:T(8,128)(2,1)}, f32[256,8192]{1,0:T(8,128)}, f32[256,2048]{1,0:T(8,128)}, f32[256,2048]{1,0:T(8,128)}, bf16[256,2048]{1,0:T(8,128)(2,1)}, /*index=5*/f32[16,2048]{1,0:T(8,128)}) custom-call(bf16[3,256,2048]{2,1,0:T(8,128)(2,1)} %bitcast.46, bf16[8,256,1024]{2,1,0:T(8,128)(2,1)} %all-to-all-done.gd_ref, ...), custom_call_target="tpu_custom_call" | custom-call | tf_op jit(solution)/shard_map/finish/pallas_call | solution.py:1930
  697.3 0.0 copy-start.5
  697.3 1.6 fusion.3
  698.9 0.8 slice_bitcast_fusion
  699.7 0.6 copy.23
  700.3 9.5 %widen.1 = (f32[768,2048]{1,0:T(8,128)}, f32[1024,2048]{1,0:T(8,128)}) custom-call(bf16[768,2048]{1,0:T(8,128)(2,1)} %bitcast.47, bf16[1024,2048]{1,0:T(8,128)(2,1)} %all-reduce.2.cloned.1.call-done.refs_1_), custom_call_target="tpu_custom_call" | custom-call | tf_op jit(solution)/shard_map/widen/pallas_call | solution.py:2003
  709.8 1.0 copy.29
  710.8 1.3 copy.30
  712.1 1.3 copy.31
  713.4 7.7 %copy.32 = f32[256,8192]{1,0:T(8,128)} copy(f32[256,8192]{1,0:T(8,128)} %get-tuple-element.117) | data formatting | bytes 16777216
  (8 shorter events, 0.0 us)
Async XLA Ops:
  7.2 203.5 %all-gather.3.cloned.1.call-start = ((), (), s32[]{:S(2)}) async-start(), calls=%async_computation.1 | async-start | bytes 9437184 | tf_op jit(solution)/shard_map/all_gather | solution.py:2036
  7.9 216.6 %all-gather.5.cloned.1.call-start = ((), (), s32[]{:S(2)}) async-start(), calls=%async_computation.2 | async-start | bytes 9437184 | tf_op jit(solution)/shard_map/all_gather | solution.py:2049
  12.0 128.0 %copy-start.6 = (s32[1,2048]{1,0:T(1,128)}, s32[1,2048]{1,0:T(1,128)S(1)}, u32[]{:S(2)}) copy-start(s32[1,2048]{1,0:T(1,128)S(1)} %compare_select_fusion.2.start_ref) | copy-start | bytes 24580
  139.9 328.7 %all-reduce.2.cloned.1.call-start = ((), (), s32[]{:S(2)}) async-start(), calls=%async_computation.3 | async-start | bytes 8388608 | tf_op jit(solution)/shard_map/psum | solution.py:2062
  391.0 77.6 %all-to-all-start = ((bf16[8,256,1024]{2,1,0:T(8,128)(2,1)}), bf16[8,256,1024]{2,1,0:T(8,128)(2,1)}, u32[]{:S(2)}, u32[]{:S(2)}) async-start(bf16[8,256,1024]{2,1,0:T(8,128)(2,1)} %get-tuple-element.80), calls=%async_computation | async-start | bytes 8388608 | tf_op jit(solution)/shard_map/all_to_all | solution.py:2069
  396.0 33.5 %copy-start = (bf16[256,2048]{1,0:T(8,128)(2,1)S(1)}, bf16[256,2048]{1,0:T(8,128)(2,1)}, u32[]{:S(2)}) copy-start(bf16[256,2048]{1,0:T(8,128)(2,1)} %get-tuple-element.75.gbr_ref) | copy-start | bytes 3145732
  396.0 33.5 %copy-start.4 = (bf16[256,2048]{1,0:T(8,128)(2,1)S(1)}, bf16[256,2048]{1,0:T(8,128)(2,1)}, u32[]{:S(2)}) copy-start(bf16[256,2048]{1,0:T(8,128)(2,1)} %get-tuple-element.81) | copy-start | bytes 3145732
  429.5 5.8 copy-start.1
  435.3 10.6 %copy-start.7 = (bf16[3,256,2048]{2,1,0:T(8,128)(2,1)S(1)}, bf16[3,256,2048]{2,1,0:T(8,128)(2,1)}, u32[]{:S(2)}) copy-start(bf16[3,256,2048]{2,1,0:T(8,128)(2,1)} %get-tuple-element.54) | copy-start | bytes 9437188
  697.3 12.5 %copy-start.5 = (bf16[256,2048]{1,0:T(8,128)(2,1)S(1)}, bf16[256,2048]{1,0:T(8,128)(2,1)}, u32[]{:S(2)}) copy-start(bf16[256,2048]{1,0:T(8,128)(2,1)} %get-tuple-element.87) | copy-start | bytes 3145732
  700.3 10.5 %copy-start.3 = (f32[256,2048]{1,0:T(8,128)S(1)}, f32[256,2048]{1,0:T(8,128)}, u32[]{:S(2)}) copy-start(f32[256,2048]{1,0:T(8,128)} %get-tuple-element.88) | copy-start | bytes 6291460
  709.8 2.3 copy-start.2
Sparse Core Ops, SparseCore 0:
  9.9 96.2 all-gather.2
  140.0 73.3 all-gather.4
  312.9 155.6 all-reduce.1

commit v11 on v10

--- a/solution.py
+++ b/solution.py
@@ -291,6 +291,17 @@
     ]
     for turn in turns:
         turn.start()
+
+    @pl.loop(0, x_ref.shape[0] // STEP)
+    def _(r):
+        at = pl.ds(pl.multiple_of(r * STEP, STEP), STEP)
+        normal, _ = norm_parts(x_ref[at].astype(F32))
+        normed[at] = (normal * gain_ref[...]).astype(BF16)
+
+    own.start()
+    sends = gather_copies(normed, o_ref, send_sem, recv_sem)
+    for k in range(5):
+        sends[k].start()
     for j in range(3):
         block = 3 * me + j
         target = lax.rem(block, n)
@@ -304,17 +315,6 @@
             @pl.when(inside & (target == me))
             def _():
                 load(j).start()
-
-    @pl.loop(0, x_ref.shape[0] // STEP)
-    def _(r):
-        at = pl.ds(pl.multiple_of(r * STEP, STEP), STEP)
-        normal, _ = norm_parts(x_ref[at].astype(F32))
-        normed[at] = (normal * gain_ref[...]).astype(BF16)
-
-    own.start()
-    sends = gather_copies(normed, o_ref, send_sem, recv_sem)
-    for k in range(5):
-        sends[k].start()
 
     line = Line(
         depth,
@@ -353,7 +353,8 @@
 
         return step
 
-    gather_run(sends, *[hand_on(k) for k in range(1, depth - 1)])
+    hand_on(1)()
+    gather_run(sends, *[hand_on(k) for k in range(2, depth - 1)])
     line.land(depth - 2)
     for k in range(depth - 1):
         line.sent(k)
@@ -1726,7 +1727,7 @@
                 BF16
             )
 
-    lead = 2
+    lead = 1
     far = 2 * (depth - 1)
     steps = per_side + 2 * far
 
@@ -1790,22 +1791,25 @@
             line_step(t)
 
     gain_here[...] = jnp.zeros_like(gain_here)
-    for load in line_loads:
+    for load in line_loads[:turned]:
         load.wait()
     for c in range(lead):
         line_enter(c)
+    line_steps(0, 3)
     first(0)
-    line_steps(0, 8)
+    for load in line_loads[turned:]:
+        load.wait()
+    line_steps(3, 10)
     second(0)
-    line_steps(8, 9)
+    line_steps(10, 11)
     first(1)
-    line_steps(9, 18)
+    line_steps(11, 20)
     last(0, store_line)
-    line_steps(18, 20)
+    line_steps(20, 22)
     second(1)
-    line_steps(20, 21)
+    line_steps(22, 23)
     first(2)
-    line_steps(21, 28)
+    line_steps(23, 29)
     last(1, store_inputs)
 
     gain_here[1:2] = gm_ref[...]
@@ -1824,11 +1828,11 @@
     ]
     for send in rounds:
         send.start()
-    line_steps(28, 32)
+    line_steps(29, 33)
     second(2)
-    line_steps(32, 40)
+    line_steps(33, 41)
     last(2, store_outputs)
-    line_steps(40, 42)
+    line_steps(41, 42)
     for send in rounds:
         send.wait()
     total = gain_row[0]

time: 733 us -> 706 us (0.963)
  Pallas kernels: 622 us -> 598 us
    pallas_call x1, Pallas kernels: 127 us -> 115 us  [start_exchange(): pl.pallas_call(functools.partial(start_kernel, n, depth), out_shape=(jax....]
    pallas_call x1, Pallas kernels: 30.5 us -> 19.2 us  [heads_to_tokens(): pl.pallas_call(functools.partial(heads_to_tokens_kernel, n), out_shape=ja...]
  transfers between devices with their start and end apart: 4 -> 4, of which waited for: 1 -> 1; matrix products, arithmetic and copies ran while one was open for 4% -> 5% of each run, Pallas kernels for 44% -> 43%
where the time goes in v11:
time: 706 us; the launch traced here: 701 us
  Pallas kernels  598 us (85%)
  matrix products  51.1 us (7%)
  local copies, waits for them, and re-layouts  15.7 us (2%)
  between operations  14.1 us (2%)
  waiting for transfers between devices  12 us (2%)
    pallas_call x1, Pallas kernels, finish(): pl.pallas_call(functools.partial(finish_kernel, n, depth), out_shape=(jax...  223 us
    pallas_call x1, Pallas kernels, start_exchange(): pl.pallas_call(functools.partial(start_kernel, n, depth), out_shape=(jax....  115 us
    pallas_call x1, Pallas kernels, ffn_pass(): pl.pallas_call(functools.partial(ffn_kernel, n), out_shape=(jax.ShapeDtyp...  62.4 us
    pallas_call x1, Pallas kernels, ffn_back(): pl.pallas_call(functools.partial(ffn_back_kernel, n), out_shape=(jax.Shap...  51.6 us
    dot_general x3, matrix products, tn(): lax.dot_general(a, b, (((0,), (0,)), ((), ())), preferred_element_type=F32)  42.1 us
    pallas_call x1, Pallas kernels, attend_back(): pl.pallas_call(functools.partial(attend_back_kernel, heads), out_shape=ja...  36 us
    pallas_call x1, Pallas kernels, attend(): pl.pallas_call(functools.partial(attend_kernel, heads), out_shape=(jax.Sh...  26.2 us
    pallas_call x1, Pallas kernels, heads_to_tokens(): pl.pallas_call(functools.partial(heads_to_tokens_kernel, n), out_shape=ja...  19.2 us
  transfers between devices with their start and end apart: 4, of which 1 were waited for; matrix products, arithmetic and copies ran while one was open for 5% of the time, Pallas kernels for 43%

profile of v11, /device:TPU:0, one launch (start us, length us, event | category | flops | bytes accessed | tf_op | source)
XLA Modules:
  0.0 700.9 jit_solution(5350525815856933823)
XLA Ops:
  7.2 0.0 all-gather.3.cloned.1.call-start
  7.2 0.7 all-gather.3.cloned.1.call-update
  7.9 0.0 all-gather.5.cloned.1.call-start
  8.0 1.4 fusion
  9.4 2.7 compare_select_fusion.2.start_ref
  12.0 0.0 copy-start.6
  12.0 0.6 subtract_convert_fusion.pos_ref
  12.6 115.1 %start_exchange.1 = (bf16[8,256,2048]{2,1,0:T(8,128)(2,1)}, bf16[3,256,2048]{2,1,0:T(8,128)(2,1)}, bf16[8,4,64,1024]{3,2,1,0:T(8,128)(2,1)}, f32[2048,128]{1,0:T...) custom-call(bf16[256,2048]{1,0:T(8,128)(2,1)} %bitcast.39, f32[1,2048]{1,0:T(1,128)} %bitcast.56, ...), custom_call_target="tpu_custom_call" | custom-call | tf_op jit(solution)/shard_map/start_exchange/pallas_call | solution.py:410
  127.7 0.0 all-gather.5.cloned.1.call-update
  127.7 0.0 all-reduce.2.cloned.1.call-start
  127.8 0.0 copy-done.6
  127.8 0.1 slice.15
  127.9 0.5 and_select_fusion.first_ref
  128.4 14.6 %project_qkv.1 = (bf16[2048,256]{1,0:T(8,128)(2,1)}, bf16[2048,256]{1,0:T(8,128)(2,1)}, bf16[2048,256]{1,0:T(8,128)(2,1)}, bf16[256,2048]{1,0:T(8,128)(2,1)}, bf16[256,2048]{1,0:T(8,128)(2,1)}) custom-call(bf16[2048,2048]{1,0:T(8,128)(2,1)} %bitcast.64, bf16[768,2048]{1,0:T(8,128)(2,1)} %bitcast.67, f32[2048,128]{1,0:T(8,128)} %get-tuple-element.55.cq_ref, ...), custom_call_target="tpu_custom_call" | custom-call | flops 6442450944 | bytes 16777216 | tf_op jit(solution)/shard_map/project_qkv/pallas_call | solution.py:605
  143.0 26.2 %attend.1 = (bf16[2048,256]{1,0:T(8,128)(2,1)}, f32[8,4,256]{2,1,0:T(4,128)}) custom-call(s32[8]{0:T(128)} %and_select_fusion.first_ref, s32[1,2048]{1,0:T(1,128)} %copy-done.6, bf16[2048,256]{1,0:T(8,128)(2,1)} %get-tuple-element.59.q_ref, bf16[2048,256]{1,0:T(8,128)(2,1)} %get-tuple-element.60.k_ref, bf16[256,2048]{1,0:T(8,128)(2,1)} %get-tuple-element.63.vt_ref), custom_call_target="tpu_custom_call" | custom-call | flops 2147483648 | bytes 4194304 | tf_op jit(solution)/shard_map/attend/pallas_call | solution.py:685
  169.2 19.2 %heads_to_tokens.1.att_ref = bf16[256,2048]{1,0:T(8,128)(2,1)} custom-call(bf16[2048,256]{1,0:T(8,128)(2,1)} %get-tuple-element.64.x_ref.o_ref), custom_call_target="tpu_custom_call" | custom-call | tf_op jit(solution)/shard_map/heads_to_tokens/pallas_call | solution.py:505
  188.4 1.3 dynamic_slice.3
  189.7 13.8 %mix_pass.1 = (bf16[256,2048]{1,0:T(8,128)(2,1)}, f32[256,2048]{1,0:T(8,128)}, bf16[256,2048]{1,0:T(8,128)(2,1)}) custom-call(bf16[256,2048]{1,0:T(8,128)(2,1)} %heads_to_tokens.1.att_ref, bf16[256,2048]{1,0:T(8,128)(2,1)} %bitcast.40, bf16[2048,2048]{1,0:T(8,128)(2,1)} %all-gather.3.cloned.1.call-done.w_ref, f32[1,2048]{1,0:T(1,128)} %bitcast.54, ...), custom_call_target="tpu_custom_call" | custom-call | flops 2147483648 | bytes 14680064 | tf_op jit(solution)/shard_map/mix_pass/pallas_call | solution.py:1241
  203.5 62.4 %ffn_pass.1 = (bf16[8,256,2048]{2,1,0:T(8,128)(2,1)}, bf16[2048,1024]{1,0:T(8,128)(2,1)}, bf16[2048,1024]{1,0:T(8,128)(2,1)}, f32[1,1024]{1,0:T(1,128)}) custom-call(bf16[256,2048]{1,0:T(8,128)(2,1)} %get-tuple-element.66.x_ref, bf16[1024,2048]{1,0:T(8,128)(2,1)} %wu_ref.3, bf16[2048,2048]{1,0:T(8,128)(2,1)} %all-gather.5.cloned.1.call-done.cot_ref.all_ref, ...), custom_call_target="tpu_custom_call" | custom-call | tf_op jit(solution)/shard_map/ffn_pass/pallas_call | solution.py:1115
  266.0 25.7 %convolution_convert_fusion.2 = bf16[1024,2048]{1,0:T(8,128)(2,1)} fusion(bf16[2048,1024]{1,0:T(8,128)(2,1)} %get-tuple-element.71.gu_ref, bf16[2048,2048]{1,0:T(8,128)(2,1)} %bitcast.66), kind=kOutput, calls=%fused_computation.2 | convolution fusion | flops 8592031744 | bytes 16777216 | tf_op jit(solution)/shard_map/dot_general | solution.py:38
  291.7 0.0 all-reduce.2.cloned.1.call-update
  291.7 51.6 %ffn_back.1 = (bf16[2048,2048]{1,0:T(8,128)(2,1)}, bf16[8,256,1024]{2,1,0:T(8,128)(2,1)}, f32[256,2048]{1,0:T(8,128)}, bf16[256,2048]{1,0:T(8,128)(2,1)}, f32[1,2048]{1,0:T(1,128)}) custom-call(bf16[2048,1024]{1,0:T(8,128)(2,1)} %get-tuple-element.71.gu_ref, bf16[1024,2048]{1,0:T(8,128)(2,1)} %wu_ref.3, bf16[2048,1024]{1,0:T(8,128)(2,1)} %get-tuple-element.72.hid_ref, ...), custom_call_target="tpu_custom_call" | custom-call | tf_op jit(solution)/shard_map/ffn_back/pallas_call | solution.py:1453
  343.3 13.0 %branch_pass.1 = (bf16[256,2048]{1,0:T(8,128)(2,1)}, f32[1,2048]{1,0:T(1,128)}) custom-call(bf16[256,2048]{1,0:T(8,128)(2,1)} %get-tuple-element.75.gbr_ref, bf16[256,2048]{1,0:T(8,128)(2,1)} %heads_to_tokens.1.att_ref, bf16[2048,2048]{1,0:T(8,128)(2,1)} %all-gather.3.cloned.1.call-done.w_ref, f32[1,2048]{1,0:T(1,128)} %bitcast.55), custom_call_target="tpu_custom_call" | custom-call | tf_op jit(solution)/shard_map/branch_pass/pallas_call | solution.py:1297
  356.3 13.7 %tokens_to_heads.1.do_ref = bf16[2048,256]{1,0:T(8,128)(2,1)} custom-call(bf16[256,2048]{1,0:T(8,128)(2,1)} %get-tuple-element.76.x_ref), custom_call_target="tpu_custom_call" | custom-call | tf_op jit(solution)/shard_map/tokens_to_heads/pallas_call | solution.py:542
  370.0 5.0 all-to-all-start
  374.9 0.0 copy-start
  375.0 0.0 copy-start.4
  375.0 36.0 %attend_back.1 = bf16[2048,768]{1,0:T(8,128)(2,1)} custom-call(s32[8]{0:T(128)} %and_select_fusion.first_ref, s32[1,2048]{1,0:T(1,128)} %copy-done.6, bf16[2048,256]{1,0:T(8,128)(2,1)} %get-tuple-element.59.q_ref, bf16[2048,256]{1,0:T(8,128)(2,1)} %get-tuple-element.60.k_ref, bf16[256,2048]{1,0:T(8,128)(2,1)} %get-tuple-element.61.kt_ref, ...), custom_call_target="tpu_custom_call" | custom-call | tf_op jit(solution)/shard_map/attend_back/pallas_call | solution.py:800
  410.9 0.0 copy-done
  411.0 0.0 copy-done.4
  411.0 0.0 copy-start.1
  411.0 5.8 convolution_convert_fusion.1
  416.8 0.0 copy-done.1
  416.8 10.6 %convolution_convert_fusion.3 = bf16[768,2048]{1,0:T(8,128)(2,1)} fusion(bf16[2048,768]{1,0:T(8,128)(2,1)S(1)} %copy-done.1, bf16[2048,2048]{1,0:T(8,128)(2,1)} %bitcast.65), kind=kOutput, calls=%fused_computation.3 | convolution fusion | flops 6444023808 | bytes 14680064 | tf_op jit(solution)/shard_map/dot_general | solution.py:38
  427.3 0.0 copy-done.7
  427.3 9.0 %convolution_convert_fusion = bf16[2048,2048]{1,0:T(8,128)(2,1)} fusion(bf16[2048,768]{1,0:T(8,128)(2,1)S(1)} %copy-done.1, bf16[768,2048]{1,0:T(8,128)(2,1)S(1)} %bitcast.68), kind=kOutput, calls=%fused_computation | convolution fusion | flops 6446645248 | bytes 14680064 | tf_op jit(solution)/shard_map/dot_general | solution.py:30
  436.3 11.3 %all-reduce.2.cloned.1.call-done.refs_1_ = bf16[1024,2048]{1,0:T(8,128)(2,1)} async-done(((bf16[1024,2048]{1,0:T(8,128)(2,1)}), bf16[1024,2048]{1,0:T(8,128)(2,1)}) %all-reduce.2.cloned.1.call-update) | async-done | bytes 4194320 | tf_op jit(solution)/shard_map/psum | solution.py:2066
  447.6 0.0 all-to-all-done.gd_ref
  447.6 222.7 %finish.1 = (bf16[3,256,2048]{2,1,0:T(8,128)(2,1)}, f32[256,8192]{1,0:T(8,128)}, f32[256,2048]{1,0:T(8,128)}, f32[256,2048]{1,0:T(8,128)}, bf16[256,2048]{1,0:T(8,128)(2,1)}, /*index=5*/f32[16,2048]{1,0:T(8,128)}) custom-call(bf16[3,256,2048]{2,1,0:T(8,128)(2,1)} %bitcast.46, bf16[8,256,1024]{2,1,0:T(8,128)(2,1)} %all-to-all-done.gd_ref, ...), custom_call_target="tpu_custom_call" | custom-call | tf_op jit(solution)/shard_map/finish/pallas_call | solution.py:1934
  670.3 0.0 copy-start.5
  670.3 1.6 fusion.3
  671.9 0.8 slice_bitcast_fusion
  672.7 0.6 copy.23
  673.3 9.5 %widen.1 = (f32[768,2048]{1,0:T(8,128)}, f32[1024,2048]{1,0:T(8,128)}) custom-call(bf16[768,2048]{1,0:T(8,128)(2,1)} %bitcast.47, bf16[1024,2048]{1,0:T(8,128)(2,1)} %all-reduce.2.cloned.1.call-done.refs_1_), custom_call_target="tpu_custom_call" | custom-call | tf_op jit(solution)/shard_map/widen/pallas_call | solution.py:2007
  682.8 1.0 copy.29
  683.8 1.3 copy.30
  685.1 1.3 copy.31
  686.5 7.7 %copy.32 = f32[256,8192]{1,0:T(8,128)} copy(f32[256,8192]{1,0:T(8,128)} %get-tuple-element.117) | data formatting | bytes 16777216
  (8 shorter events, 0.0 us)
Async XLA Ops:
  7.2 182.6 %all-gather.3.cloned.1.call-start = ((), (), s32[]{:S(2)}) async-start(), calls=%async_computation.1 | async-start | bytes 9437184 | tf_op jit(solution)/shard_map/all_gather | solution.py:2040
  7.9 195.6 %all-gather.5.cloned.1.call-start = ((), (), s32[]{:S(2)}) async-start(), calls=%async_computation.2 | async-start | bytes 9437184 | tf_op jit(solution)/shard_map/all_gather | solution.py:2053
  12.0 115.8 %copy-start.6 = (s32[1,2048]{1,0:T(1,128)}, s32[1,2048]{1,0:T(1,128)S(1)}, u32[]{:S(2)}) copy-start(s32[1,2048]{1,0:T(1,128)S(1)} %compare_select_fusion.2.start_ref) | copy-start | bytes 24580
  127.7 319.9 %all-reduce.2.cloned.1.call-start = ((), (), s32[]{:S(2)}) async-start(), calls=%async_computation.3 | async-start | bytes 8388608 | tf_op jit(solution)/shard_map/psum | solution.py:2066
  370.0 77.7 %all-to-all-start = ((bf16[8,256,1024]{2,1,0:T(8,128)(2,1)}), bf16[8,256,1024]{2,1,0:T(8,128)(2,1)}, u32[]{:S(2)}, u32[]{:S(2)}) async-start(bf16[8,256,1024]{2,1,0:T(8,128)(2,1)} %get-tuple-element.80), calls=%async_computation | async-start | bytes 8388608 | tf_op jit(solution)/shard_map/all_to_all | solution.py:2073
  374.9 36.0 %copy-start = (bf16[256,2048]{1,0:T(8,128)(2,1)S(1)}, bf16[256,2048]{1,0:T(8,128)(2,1)}, u32[]{:S(2)}) copy-start(bf16[256,2048]{1,0:T(8,128)(2,1)} %get-tuple-element.75.gbr_ref) | copy-start | bytes 3145732
  375.0 36.0 %copy-start.4 = (bf16[256,2048]{1,0:T(8,128)(2,1)S(1)}, bf16[256,2048]{1,0:T(8,128)(2,1)}, u32[]{:S(2)}) copy-start(bf16[256,2048]{1,0:T(8,128)(2,1)} %get-tuple-element.81) | copy-start | bytes 3145732
  411.0 5.8 copy-start.1
  416.8 10.6 %copy-start.7 = (bf16[3,256,2048]{2,1,0:T(8,128)(2,1)S(1)}, bf16[3,256,2048]{2,1,0:T(8,128)(2,1)}, u32[]{:S(2)}) copy-start(bf16[3,256,2048]{2,1,0:T(8,128)(2,1)} %get-tuple-element.54) | copy-start | bytes 9437188
  670.3 12.5 %copy-start.5 = (bf16[256,2048]{1,0:T(8,128)(2,1)S(1)}, bf16[256,2048]{1,0:T(8,128)(2,1)}, u32[]{:S(2)}) copy-start(bf16[256,2048]{1,0:T(8,128)(2,1)} %get-tuple-element.87) | copy-start | bytes 3145732
  673.3 10.5 %copy-start.3 = (f32[256,2048]{1,0:T(8,128)S(1)}, f32[256,2048]{1,0:T(8,128)}, u32[]{:S(2)}) copy-start(f32[256,2048]{1,0:T(8,128)} %get-tuple-element.88) | copy-start | bytes 6291460
  682.8 2.3 copy-start.2
Sparse Core Ops, SparseCore 0:
  9.9 96.2 all-gather.2
  127.8 64.4 all-gather.4
  291.9 155.7 all-reduce.1

commit v12 on v11

--- a/solution.py
+++ b/solution.py
@@ -1233,7 +1233,7 @@
 
 def mix_pass(attended, x, w_out, gain_mix, gain_ffn):
     rows, width = x.shape
-    cols = TILE
+    cols = 2 * TILE
     n = width // cols
     whole = pl.BlockSpec((rows, width), lambda j: (0, 0))
     gain = pl.BlockSpec((1, width), lambda j: (0, 0))
@@ -1290,7 +1290,7 @@
 
 def branch_pass(grad_branch, attended, w_out, gain_mix):
     rows, width = grad_branch.shape
-    cols = TILE
+    cols = 2 * TILE
     n = width // cols
     whole = pl.BlockSpec((rows, width), lambda j: (0, 0))
     gain = pl.BlockSpec((1, width), lambda j: (0, 0))

time: 706 us -> 695 us (0.984)
  matrix products: 51.1 us -> 39.8 us
    dot_general x3, matrix products: 42.1 us -> 30.8 us  [tn(): lax.dot_general(a, b, (((0,), (0,)), ((), ())), preferred_element_type=F32)]
where the time goes in v12:
time: 695 us; the launch traced here: 688 us
  Pallas kernels  591 us (85%)
  matrix products  39.8 us (6%)
  waiting for transfers between devices  17.1 us (2%)
  local copies, waits for them, and re-layouts  15.7 us (2%)
  between operations  14.3 us (2%)
    pallas_call x1, Pallas kernels, finish(): pl.pallas_call(functools.partial(finish_kernel, n, depth), out_shape=(jax...  223 us
    pallas_call x1, Pallas kernels, start_exchange(): pl.pallas_call(functools.partial(start_kernel, n, depth), out_shape=(jax....  115 us
    pallas_call x1, Pallas kernels, ffn_pass(): pl.pallas_call(functools.partial(ffn_kernel, n), out_shape=(jax.ShapeDtyp...  62.4 us
    pallas_call x1, Pallas kernels, ffn_back(): pl.pallas_call(functools.partial(ffn_back_kernel, n), out_shape=(jax.Shap...  51.6 us
    pallas_call x1, Pallas kernels, attend_back(): pl.pallas_call(functools.partial(attend_back_kernel, heads), out_shape=ja...  33.4 us
    dot_general x3, matrix products, tn(): lax.dot_general(a, b, (((0,), (0,)), ((), ())), preferred_element_type=F32)  30.8 us
    pallas_call x1, Pallas kernels, attend(): pl.pallas_call(functools.partial(attend_kernel, heads), out_shape=(jax.Sh...  24 us
    pallas_call x1, Pallas kernels, heads_to_tokens(): pl.pallas_call(functools.partial(heads_to_tokens_kernel, n), out_shape=ja...  21.4 us
  transfers between devices with their start and end apart: 4, of which 1 were waited for; matrix products, arithmetic and copies ran while one was open for 5% of the time, Pallas kernels for 43%

profile of v12, /device:TPU:0, one launch (start us, length us, event | category | flops | bytes accessed | tf_op | source)
XLA Modules:
  0.0 687.8 jit_solution(17665532557645614983)
XLA Ops:
  7.2 0.0 all-gather.3.cloned.1.call-start
  7.2 0.7 all-gather.3.cloned.1.call-update
  7.9 0.0 all-gather.5.cloned.1.call-start
  8.0 1.4 fusion
  9.4 2.7 compare_select_fusion.2.start_ref
  12.0 0.0 copy-start.6
  12.0 0.6 subtract_convert_fusion.pos_ref
  12.6 115.1 %start_exchange.1 = (bf16[8,256,2048]{2,1,0:T(8,128)(2,1)}, bf16[3,256,2048]{2,1,0:T(8,128)(2,1)}, bf16[8,4,64,1024]{3,2,1,0:T(8,128)(2,1)}, f32[2048,128]{1,0:T...) custom-call(bf16[256,2048]{1,0:T(8,128)(2,1)} %bitcast.39, f32[1,2048]{1,0:T(1,128)} %bitcast.56, ...), custom_call_target="tpu_custom_call" | custom-call | tf_op jit(solution)/shard_map/start_exchange/pallas_call | solution.py:410
  127.7 0.0 all-gather.5.cloned.1.call-update
  127.7 0.0 all-reduce.2.cloned.1.call-start
  127.8 0.0 copy-done.6
  127.8 0.1 slice.15
  127.9 0.5 and_select_fusion.first_ref
  128.4 14.6 %project_qkv.1 = (bf16[2048,256]{1,0:T(8,128)(2,1)}, bf16[2048,256]{1,0:T(8,128)(2,1)}, bf16[2048,256]{1,0:T(8,128)(2,1)}, bf16[256,2048]{1,0:T(8,128)(2,1)}, bf16[256,2048]{1,0:T(8,128)(2,1)}) custom-call(bf16[2048,2048]{1,0:T(8,128)(2,1)} %bitcast.64, bf16[768,2048]{1,0:T(8,128)(2,1)} %bitcast.67, f32[2048,128]{1,0:T(8,128)} %get-tuple-element.55.cq_ref, ...), custom_call_target="tpu_custom_call" | custom-call | flops 6442450944 | bytes 16777216 | tf_op jit(solution)/shard_map/project_qkv/pallas_call | solution.py:605
  143.0 24.0 %attend.1 = (bf16[2048,256]{1,0:T(8,128)(2,1)}, f32[8,4,256]{2,1,0:T(4,128)}) custom-call(s32[8]{0:T(128)} %and_select_fusion.first_ref, s32[1,2048]{1,0:T(1,128)} %copy-done.6, bf16[2048,256]{1,0:T(8,128)(2,1)} %get-tuple-element.59.q_ref, bf16[2048,256]{1,0:T(8,128)(2,1)} %get-tuple-element.60.k_ref, bf16[256,2048]{1,0:T(8,128)(2,1)} %get-tuple-element.63.vt_ref), custom_call_target="tpu_custom_call" | custom-call | flops 2147483648 | bytes 4194304 | tf_op jit(solution)/shard_map/attend/pallas_call | solution.py:685
  167.0 21.4 %heads_to_tokens.1.att_ref = bf16[256,2048]{1,0:T(8,128)(2,1)} custom-call(bf16[2048,256]{1,0:T(8,128)(2,1)} %get-tuple-element.64.x_ref.o_ref), custom_call_target="tpu_custom_call" | custom-call | tf_op jit(solution)/shard_map/heads_to_tokens/pallas_call | solution.py:505
  188.4 1.3 dynamic_slice.3
  189.7 11.9 %mix_pass.1 = (bf16[256,2048]{1,0:T(8,128)(2,1)}, f32[256,2048]{1,0:T(8,128)}, bf16[256,2048]{1,0:T(8,128)(2,1)}) custom-call(bf16[256,2048]{1,0:T(8,128)(2,1)} %heads_to_tokens.1.att_ref, bf16[256,2048]{1,0:T(8,128)(2,1)} %bitcast.40, bf16[2048,2048]{1,0:T(8,128)(2,1)} %all-gather.3.cloned.1.call-done.w_ref, f32[1,2048]{1,0:T(1,128)} %bitcast.54, ...), custom_call_target="tpu_custom_call" | custom-call | flops 2147483648 | bytes 14680064 | tf_op jit(solution)/shard_map/mix_pass/pallas_call | solution.py:1241
  201.6 62.4 %ffn_pass.1 = (bf16[8,256,2048]{2,1,0:T(8,128)(2,1)}, bf16[2048,1024]{1,0:T(8,128)(2,1)}, bf16[2048,1024]{1,0:T(8,128)(2,1)}, f32[1,1024]{1,0:T(1,128)}) custom-call(bf16[256,2048]{1,0:T(8,128)(2,1)} %get-tuple-element.66.x_ref, bf16[1024,2048]{1,0:T(8,128)(2,1)} %wu_ref.3, bf16[2048,2048]{1,0:T(8,128)(2,1)} %all-gather.5.cloned.1.call-done.cot_ref.all_ref, ...), custom_call_target="tpu_custom_call" | custom-call | tf_op jit(solution)/shard_map/ffn_pass/pallas_call | solution.py:1115
  264.0 14.5 %convolution_convert_fusion.2 = bf16[1024,2048]{1,0:T(8,128)(2,1)} fusion(bf16[2048,1024]{1,0:T(8,128)(2,1)} %get-tuple-element.71.gu_ref, bf16[2048,2048]{1,0:T(8,128)(2,1)} %bitcast.66), kind=kOutput, calls=%fused_computation.2 | convolution fusion | flops 8592031744 | bytes 16777216 | tf_op jit(solution)/shard_map/dot_general | solution.py:38
  278.5 0.0 all-reduce.2.cloned.1.call-update
  278.5 51.6 %ffn_back.1 = (bf16[2048,2048]{1,0:T(8,128)(2,1)}, bf16[8,256,1024]{2,1,0:T(8,128)(2,1)}, f32[256,2048]{1,0:T(8,128)}, bf16[256,2048]{1,0:T(8,128)(2,1)}, f32[1,2048]{1,0:T(1,128)}) custom-call(bf16[2048,1024]{1,0:T(8,128)(2,1)} %get-tuple-element.71.gu_ref, bf16[1024,2048]{1,0:T(8,128)(2,1)} %wu_ref.3, bf16[2048,1024]{1,0:T(8,128)(2,1)} %get-tuple-element.72.hid_ref, ...), custom_call_target="tpu_custom_call" | custom-call | tf_op jit(solution)/shard_map/ffn_back/pallas_call | solution.py:1453
  330.1 10.6 %branch_pass.1 = (bf16[256,2048]{1,0:T(8,128)(2,1)}, f32[1,2048]{1,0:T(1,128)}) custom-call(bf16[256,2048]{1,0:T(8,128)(2,1)} %get-tuple-element.75.gbr_ref, bf16[256,2048]{1,0:T(8,128)(2,1)} %heads_to_tokens.1.att_ref, bf16[2048,2048]{1,0:T(8,128)(2,1)} %all-gather.3.cloned.1.call-done.w_ref, f32[1,2048]{1,0:T(1,128)} %bitcast.55), custom_call_target="tpu_custom_call" | custom-call | tf_op jit(solution)/shard_map/branch_pass/pallas_call | solution.py:1297
  340.8 13.7 %tokens_to_heads.1.do_ref = bf16[2048,256]{1,0:T(8,128)(2,1)} custom-call(bf16[256,2048]{1,0:T(8,128)(2,1)} %get-tuple-element.76.x_ref), custom_call_target="tpu_custom_call" | custom-call | tf_op jit(solution)/shard_map/tokens_to_heads/pallas_call | solution.py:542
  354.4 4.8 all-to-all-start
  359.3 0.0 copy-start
  359.3 0.0 copy-start.4
  359.3 33.4 %attend_back.1 = bf16[2048,768]{1,0:T(8,128)(2,1)} custom-call(s32[8]{0:T(128)} %and_select_fusion.first_ref, s32[1,2048]{1,0:T(1,128)} %copy-done.6, bf16[2048,256]{1,0:T(8,128)(2,1)} %get-tuple-element.59.q_ref, bf16[2048,256]{1,0:T(8,128)(2,1)} %get-tuple-element.60.k_ref, bf16[256,2048]{1,0:T(8,128)(2,1)} %get-tuple-element.61.kt_ref, ...), custom_call_target="tpu_custom_call" | custom-call | tf_op jit(solution)/shard_map/attend_back/pallas_call | solution.py:800
  392.6 0.0 copy-done
  392.6 0.0 copy-done.4
  392.7 0.0 copy-start.1
  392.7 5.8 convolution_convert_fusion.1
  398.4 0.0 copy-done.1
  398.5 10.6 %convolution_convert_fusion.3 = bf16[768,2048]{1,0:T(8,128)(2,1)} fusion(bf16[2048,768]{1,0:T(8,128)(2,1)S(1)} %copy-done.1, bf16[2048,2048]{1,0:T(8,128)(2,1)} %bitcast.65), kind=kOutput, calls=%fused_computation.3 | convolution fusion | flops 6444023808 | bytes 14680064 | tf_op jit(solution)/shard_map/dot_general | solution.py:38
  409.0 0.0 copy-done.7
  409.0 9.0 %convolution_convert_fusion = bf16[2048,2048]{1,0:T(8,128)(2,1)} fusion(bf16[2048,768]{1,0:T(8,128)(2,1)S(1)} %copy-done.1, bf16[768,2048]{1,0:T(8,128)(2,1)S(1)} %bitcast.68), kind=kOutput, calls=%fused_computation | convolution fusion | flops 6446645248 | bytes 14680064 | tf_op jit(solution)/shard_map/dot_general | solution.py:30
  418.0 16.3 %all-reduce.2.cloned.1.call-done.refs_1_ = bf16[1024,2048]{1,0:T(8,128)(2,1)} async-done(((bf16[1024,2048]{1,0:T(8,128)(2,1)}), bf16[1024,2048]{1,0:T(8,128)(2,1)}) %all-reduce.2.cloned.1.call-update) | async-done | bytes 4194320 | tf_op jit(solution)/shard_map/psum | solution.py:2066
  434.3 0.0 all-to-all-done.gd_ref
  434.3 222.7 %finish.1 = (bf16[3,256,2048]{2,1,0:T(8,128)(2,1)}, f32[256,8192]{1,0:T(8,128)}, f32[256,2048]{1,0:T(8,128)}, f32[256,2048]{1,0:T(8,128)}, bf16[256,2048]{1,0:T(8,128)(2,1)}, /*index=5*/f32[16,2048]{1,0:T(8,128)}) custom-call(bf16[3,256,2048]{2,1,0:T(8,128)(2,1)} %bitcast.46, bf16[8,256,1024]{2,1,0:T(8,128)(2,1)} %all-to-all-done.gd_ref, ...), custom_call_target="tpu_custom_call" | custom-call | tf_op jit(solution)/shard_map/finish/pallas_call | solution.py:1934
  657.0 0.0 copy-start.5
  657.1 1.6 fusion.3
  658.7 0.8 slice_bitcast_fusion
  659.4 0.6 copy.23
  660.0 9.5 %widen.1 = (f32[768,2048]{1,0:T(8,128)}, f32[1024,2048]{1,0:T(8,128)}) custom-call(bf16[768,2048]{1,0:T(8,128)(2,1)} %bitcast.47, bf16[1024,2048]{1,0:T(8,128)(2,1)} %all-reduce.2.cloned.1.call-done.refs_1_), custom_call_target="tpu_custom_call" | custom-call | tf_op jit(solution)/shard_map/widen/pallas_call | solution.py:2007
  669.6 1.0 copy.29
  670.5 1.3 copy.30
  671.8 1.3 copy.31
  673.2 7.7 %copy.32 = f32[256,8192]{1,0:T(8,128)} copy(f32[256,8192]{1,0:T(8,128)} %get-tuple-element.117) | data formatting | bytes 16777216
  (8 shorter events, 0.0 us)
Async XLA Ops:
  7.2 182.5 %all-gather.3.cloned.1.call-start = ((), (), s32[]{:S(2)}) async-start(), calls=%async_computation.1 | async-start | bytes 9437184 | tf_op jit(solution)/shard_map/all_gather | solution.py:2040
  7.9 193.7 %all-gather.5.cloned.1.call-start = ((), (), s32[]{:S(2)}) async-start(), calls=%async_computation.2 | async-start | bytes 9437184 | tf_op jit(solution)/shard_map/all_gather | solution.py:2053
  12.0 115.8 %copy-start.6 = (s32[1,2048]{1,0:T(1,128)}, s32[1,2048]{1,0:T(1,128)S(1)}, u32[]{:S(2)}) copy-start(s32[1,2048]{1,0:T(1,128)S(1)} %compare_select_fusion.2.start_ref) | copy-start | bytes 24580
  127.7 306.6 %all-reduce.2.cloned.1.call-start = ((), (), s32[]{:S(2)}) async-start(), calls=%async_computation.3 | async-start | bytes 8388608 | tf_op jit(solution)/shard_map/psum | solution.py:2066
  354.4 79.9 %all-to-all-start = ((bf16[8,256,1024]{2,1,0:T(8,128)(2,1)}), bf16[8,256,1024]{2,1,0:T(8,128)(2,1)}, u32[]{:S(2)}, u32[]{:S(2)}) async-start(bf16[8,256,1024]{2,1,0:T(8,128)(2,1)} %get-tuple-element.80), calls=%async_computation | async-start | bytes 8388608 | tf_op jit(solution)/shard_map/all_to_all | solution.py:2073
  359.3 33.4 %copy-start = (bf16[256,2048]{1,0:T(8,128)(2,1)S(1)}, bf16[256,2048]{1,0:T(8,128)(2,1)}, u32[]{:S(2)}) copy-start(bf16[256,2048]{1,0:T(8,128)(2,1)} %get-tuple-element.75.gbr_ref) | copy-start | bytes 3145732
  359.3 33.4 %copy-start.4 = (bf16[256,2048]{1,0:T(8,128)(2,1)S(1)}, bf16[256,2048]{1,0:T(8,128)(2,1)}, u32[]{:S(2)}) copy-start(bf16[256,2048]{1,0:T(8,128)(2,1)} %get-tuple-element.81) | copy-start | bytes 3145732
  392.7 5.8 copy-start.1
  398.5 10.6 %copy-start.7 = (bf16[3,256,2048]{2,1,0:T(8,128)(2,1)S(1)}, bf16[3,256,2048]{2,1,0:T(8,128)(2,1)}, u32[]{:S(2)}) copy-start(bf16[3,256,2048]{2,1,0:T(8,128)(2,1)} %get-tuple-element.54) | copy-start | bytes 9437188
  657.0 12.5 %copy-start.5 = (bf16[256,2048]{1,0:T(8,128)(2,1)S(1)}, bf16[256,2048]{1,0:T(8,128)(2,1)}, u32[]{:S(2)}) copy-start(bf16[256,2048]{1,0:T(8,128)(2,1)} %get-tuple-element.87) | copy-start | bytes 3145732
  660.0 10.5 %copy-start.3 = (f32[256,2048]{1,0:T(8,128)S(1)}, f32[256,2048]{1,0:T(8,128)}, u32[]{:S(2)}) copy-start(f32[256,2048]{1,0:T(8,128)} %get-tuple-element.88) | copy-start | bytes 6291460
  669.5 2.3 copy-start.2
Sparse Core Ops, SparseCore 0:
  9.9 96.2 all-gather.2
  127.8 64.4 all-gather.4
  278.6 155.6 all-reduce.1

commit v13 on v12

--- a/solution.py
+++ b/solution.py
@@ -595,18 +595,19 @@
 def project_qkv(x, w, tables):
     length, width = x.shape
     cols = w.shape[0] // 3
-    steps = length // TILE
+    tile = 2 * TILE
+    steps = length // tile
     weight = pl.BlockSpec((3 * cols, width), lambda i: (0, 0))
-    table = pl.BlockSpec((TILE, tables[0].shape[1]), lambda i: (i, 0))
-    row_out = pl.BlockSpec((TILE, cols), lambda i: (i, 0))
-    col_out = pl.BlockSpec((cols, TILE), lambda i: (0, i))
+    table = pl.BlockSpec((tile, tables[0].shape[1]), lambda i: (i, 0))
+    row_out = pl.BlockSpec((tile, cols), lambda i: (i, 0))
+    col_out = pl.BlockSpec((cols, tile), lambda i: (0, i))
     rows = jax.ShapeDtypeStruct((length, cols), BF16)
     columns = jax.ShapeDtypeStruct((cols, length), BF16)
     return pl.pallas_call(
         qkv_kernel,
         grid=(steps,),
         out_shape=(rows, rows, rows, columns, columns),
-        in_specs=[pl.BlockSpec((TILE, width), lambda i: (i, 0))]
+        in_specs=[pl.BlockSpec((tile, width), lambda i: (i, 0))]
         + [weight]
         + [table] * 4,
         out_specs=(row_out, row_out, row_out, col_out, col_out),
@@ -953,7 +954,7 @@
 
     def load_cot(i, slot):
         return pltpu.make_async_copy(
-            cot_ref.at[cut(i)], cot_in.at[slot], cot_sem.at[slot]
+            cot_ref.at[cut(i, 2 * rows)], cot_in.at[slot], cot_sem.at[slot]
         )
 
     load_cot(0, 0).start()
@@ -968,21 +969,21 @@
         def _(i):
             slot = lax.rem(i, 2)
 
-            @pl.when(i + 1 < n)
+            @pl.when(i + 1 < n // 2)
             def _():
                 load_cot(i + 1, 1 - slot).start()
 
             load_cot(i, slot).wait()
-            grad[cut(i)] = nn(cot_in[slot], wd[...])
-
-    incoming(0, n - 2)
+            grad[cut(i, 2 * rows)] = nn(cot_in[slot], wd[...])
+
+    incoming(0, n // 2 - 1)
     sends[0].wait_recv()
     sends[5].start()
     sends[7].start()
     sends[1].wait_recv()
     sends[6].start()
     sends[8].start()
-    incoming(n - 2, n)
+    incoming(n // 2 - 1, n // 2)
     own.wait()
 
     def keep(b):
@@ -1125,7 +1126,7 @@
         scratch_shapes=[
             pltpu.VMEM((n, rows, width), BF16),
             pltpu.VMEM((width, feats), BF16),
-            pltpu.VMEM((2, rows, width), BF16),
+            pltpu.VMEM((2, 2 * rows, width), BF16),
             pltpu.VMEM((length, feats), F32),
             pltpu.VMEM((length, feats), BF16),
             pltpu.VMEM((length, feats), F32),

time: 695 us -> 696 us (level)
  no operation moved by 1% of the time
where the time goes in v13:
time: 696 us; the launch traced here: 688 us
  Pallas kernels  591 us (85%)
  matrix products  39.8 us (6%)
  waiting for transfers between devices  17.5 us (3%)
  local copies, waits for them, and re-layouts  15.7 us (2%)
  between operations  14.3 us (2%)
    pallas_call x1, Pallas kernels, finish(): pl.pallas_call(functools.partial(finish_kernel, n, depth), out_shape=(jax...  223 us
    pallas_call x1, Pallas kernels, start_exchange(): pl.pallas_call(functools.partial(start_kernel, n, depth), out_shape=(jax....  115 us
    pallas_call x1, Pallas kernels, ffn_pass(): pl.pallas_call(functools.partial(ffn_kernel, n), out_shape=(jax.ShapeDtyp...  62.4 us
    pallas_call x1, Pallas kernels, ffn_back(): pl.pallas_call(functools.partial(ffn_back_kernel, n), out_shape=(jax.Shap...  51.6 us
    pallas_call x1, Pallas kernels, attend_back(): pl.pallas_call(functools.partial(attend_back_kernel, heads), out_shape=ja...  33.3 us
    dot_general x3, matrix products, tn(): lax.dot_general(a, b, (((0,), (0,)), ((), ())), preferred_element_type=F32)  30.8 us
    pallas_call x1, Pallas kernels, attend(): pl.pallas_call(functools.partial(attend_kernel, heads), out_shape=(jax.Sh...  24 us
    pallas_call x1, Pallas kernels, heads_to_tokens(): pl.pallas_call(functools.partial(heads_to_tokens_kernel, n), out_shape=ja...  22.8 us
  transfers between devices with their start and end apart: 4, of which 1 were waited for; matrix products, arithmetic and copies ran while one was open for 5% of the time, Pallas kernels for 43%

profile of v13, /device:TPU:0, one launch (start us, length us, event | category | flops | bytes accessed | tf_op | source)
XLA Modules:
  0.0 688.1 jit_solution(16105558974852818644)
XLA Ops:
  7.2 0.0 all-gather.3.cloned.1.call-start
  7.2 0.7 all-gather.3.cloned.1.call-update
  7.9 0.0 all-gather.5.cloned.1.call-start
  8.0 1.4 fusion
  9.4 2.7 compare_select_fusion.2.start_ref
  12.0 0.0 copy-start.6
  12.0 0.6 subtract_convert_fusion.pos_ref
  12.6 115.1 %start_exchange.1 = (bf16[8,256,2048]{2,1,0:T(8,128)(2,1)}, bf16[3,256,2048]{2,1,0:T(8,128)(2,1)}, bf16[8,4,64,1024]{3,2,1,0:T(8,128)(2,1)}, f32[2048,128]{1,0:T...) custom-call(bf16[256,2048]{1,0:T(8,128)(2,1)} %bitcast.39, f32[1,2048]{1,0:T(1,128)} %bitcast.56, ...), custom_call_target="tpu_custom_call" | custom-call | tf_op jit(solution)/shard_map/start_exchange/pallas_call | solution.py:410
  127.7 0.0 all-gather.5.cloned.1.call-update
  127.7 0.0 all-reduce.2.cloned.1.call-start
  127.8 0.0 copy-done.6
  127.8 0.1 slice.15
  127.9 0.5 and_select_fusion.first_ref
  128.4 13.2 %project_qkv.1 = (bf16[2048,256]{1,0:T(8,128)(2,1)}, bf16[2048,256]{1,0:T(8,128)(2,1)}, bf16[2048,256]{1,0:T(8,128)(2,1)}, bf16[256,2048]{1,0:T(8,128)(2,1)}, bf16[256,2048]{1,0:T(8,128)(2,1)}) custom-call(bf16[2048,2048]{1,0:T(8,128)(2,1)} %bitcast.64, bf16[768,2048]{1,0:T(8,128)(2,1)} %bitcast.67, f32[2048,128]{1,0:T(8,128)} %get-tuple-element.55.cq_ref, ...), custom_call_target="tpu_custom_call" | custom-call | flops 6442450944 | bytes 16777216 | tf_op jit(solution)/shard_map/project_qkv/pallas_call | solution.py:606
  141.6 24.0 %attend.1 = (bf16[2048,256]{1,0:T(8,128)(2,1)}, f32[8,4,256]{2,1,0:T(4,128)}) custom-call(s32[8]{0:T(128)} %and_select_fusion.first_ref, s32[1,2048]{1,0:T(1,128)} %copy-done.6, bf16[2048,256]{1,0:T(8,128)(2,1)} %get-tuple-element.59.q_ref, bf16[2048,256]{1,0:T(8,128)(2,1)} %get-tuple-element.60.k_ref, bf16[256,2048]{1,0:T(8,128)(2,1)} %get-tuple-element.63.vt_ref), custom_call_target="tpu_custom_call" | custom-call | flops 2147483648 | bytes 4194304 | tf_op jit(solution)/shard_map/attend/pallas_call | solution.py:686
  165.6 22.8 %heads_to_tokens.1.att_ref = bf16[256,2048]{1,0:T(8,128)(2,1)} custom-call(bf16[2048,256]{1,0:T(8,128)(2,1)} %get-tuple-element.64.x_ref.o_ref), custom_call_target="tpu_custom_call" | custom-call | tf_op jit(solution)/shard_map/heads_to_tokens/pallas_call | solution.py:505
  188.4 1.3 dynamic_slice.3
  189.7 11.9 %mix_pass.1 = (bf16[256,2048]{1,0:T(8,128)(2,1)}, f32[256,2048]{1,0:T(8,128)}, bf16[256,2048]{1,0:T(8,128)(2,1)}) custom-call(bf16[256,2048]{1,0:T(8,128)(2,1)} %heads_to_tokens.1.att_ref, bf16[256,2048]{1,0:T(8,128)(2,1)} %bitcast.40, bf16[2048,2048]{1,0:T(8,128)(2,1)} %all-gather.3.cloned.1.call-done.w_ref, f32[1,2048]{1,0:T(1,128)} %bitcast.54, ...), custom_call_target="tpu_custom_call" | custom-call | flops 2147483648 | bytes 14680064 | tf_op jit(solution)/shard_map/mix_pass/pallas_call | solution.py:1242
  201.6 62.4 %ffn_pass.1 = (bf16[8,256,2048]{2,1,0:T(8,128)(2,1)}, bf16[2048,1024]{1,0:T(8,128)(2,1)}, bf16[2048,1024]{1,0:T(8,128)(2,1)}, f32[1,1024]{1,0:T(1,128)}) custom-call(bf16[256,2048]{1,0:T(8,128)(2,1)} %get-tuple-element.66.x_ref, bf16[1024,2048]{1,0:T(8,128)(2,1)} %wu_ref.3, bf16[2048,2048]{1,0:T(8,128)(2,1)} %all-gather.5.cloned.1.call-done.cot_ref.all_ref, ...), custom_call_target="tpu_custom_call" | custom-call | tf_op jit(solution)/shard_map/ffn_pass/pallas_call | solution.py:1116
  264.0 14.5 %convolution_convert_fusion.2 = bf16[1024,2048]{1,0:T(8,128)(2,1)} fusion(bf16[2048,1024]{1,0:T(8,128)(2,1)} %get-tuple-element.71.gu_ref, bf16[2048,2048]{1,0:T(8,128)(2,1)} %bitcast.66), kind=kOutput, calls=%fused_computation.2 | convolution fusion | flops 8592031744 | bytes 16777216 | tf_op jit(solution)/shard_map/dot_general | solution.py:38
  278.5 0.0 all-reduce.2.cloned.1.call-update
  278.5 51.6 %ffn_back.1 = (bf16[2048,2048]{1,0:T(8,128)(2,1)}, bf16[8,256,1024]{2,1,0:T(8,128)(2,1)}, f32[256,2048]{1,0:T(8,128)}, bf16[256,2048]{1,0:T(8,128)(2,1)}, f32[1,2048]{1,0:T(1,128)}) custom-call(bf16[2048,1024]{1,0:T(8,128)(2,1)} %get-tuple-element.71.gu_ref, bf16[1024,2048]{1,0:T(8,128)(2,1)} %wu_ref.3, bf16[2048,1024]{1,0:T(8,128)(2,1)} %get-tuple-element.72.hid_ref, ...), custom_call_target="tpu_custom_call" | custom-call | tf_op jit(solution)/shard_map/ffn_back/pallas_call | solution.py:1454
  330.1 10.7 %branch_pass.1 = (bf16[256,2048]{1,0:T(8,128)(2,1)}, f32[1,2048]{1,0:T(1,128)}) custom-call(bf16[256,2048]{1,0:T(8,128)(2,1)} %get-tuple-element.75.gbr_ref, bf16[256,2048]{1,0:T(8,128)(2,1)} %heads_to_tokens.1.att_ref, bf16[2048,2048]{1,0:T(8,128)(2,1)} %all-gather.3.cloned.1.call-done.w_ref, f32[1,2048]{1,0:T(1,128)} %bitcast.55), custom_call_target="tpu_custom_call" | custom-call | tf_op jit(solution)/shard_map/branch_pass/pallas_call | solution.py:1298
  340.7 13.6 %tokens_to_heads.1.do_ref = bf16[2048,256]{1,0:T(8,128)(2,1)} custom-call(bf16[256,2048]{1,0:T(8,128)(2,1)} %get-tuple-element.76.x_ref), custom_call_target="tpu_custom_call" | custom-call | tf_op jit(solution)/shard_map/tokens_to_heads/pallas_call | solution.py:542
  354.4 4.8 all-to-all-start
  359.2 0.0 copy-start
  359.2 0.0 copy-start.4
  359.2 33.3 %attend_back.1 = bf16[2048,768]{1,0:T(8,128)(2,1)} custom-call(s32[8]{0:T(128)} %and_select_fusion.first_ref, s32[1,2048]{1,0:T(1,128)} %copy-done.6, bf16[2048,256]{1,0:T(8,128)(2,1)} %get-tuple-element.59.q_ref, bf16[2048,256]{1,0:T(8,128)(2,1)} %get-tuple-element.60.k_ref, bf16[256,2048]{1,0:T(8,128)(2,1)} %get-tuple-element.61.kt_ref, ...), custom_call_target="tpu_custom_call" | custom-call | tf_op jit(solution)/shard_map/attend_back/pallas_call | solution.py:801
  392.5 0.0 copy-done
  392.5 0.0 copy-done.4
  392.5 0.0 copy-start.1
  392.5 5.8 convolution_convert_fusion.1
  398.3 0.0 copy-done.1
  398.3 10.6 %convolution_convert_fusion.3 = bf16[768,2048]{1,0:T(8,128)(2,1)} fusion(bf16[2048,768]{1,0:T(8,128)(2,1)S(1)} %copy-done.1, bf16[2048,2048]{1,0:T(8,128)(2,1)} %bitcast.65), kind=kOutput, calls=%fused_computation.3 | convolution fusion | flops 6444023808 | bytes 14680064 | tf_op jit(solution)/shard_map/dot_general | solution.py:38
  408.9 9.0 %convolution_convert_fusion = bf16[2048,2048]{1,0:T(8,128)(2,1)} fusion(bf16[2048,768]{1,0:T(8,128)(2,1)S(1)} %copy-done.1, bf16[768,2048]{1,0:T(8,128)(2,1)S(1)} %bitcast.68), kind=kOutput, calls=%fused_computation | convolution fusion | flops 6446645248 | bytes 14680064 | tf_op jit(solution)/shard_map/dot_general | solution.py:30
  417.9 16.8 %all-reduce.2.cloned.1.call-done.refs_1_ = bf16[1024,2048]{1,0:T(8,128)(2,1)} async-done(((bf16[1024,2048]{1,0:T(8,128)(2,1)}), bf16[1024,2048]{1,0:T(8,128)(2,1)}) %all-reduce.2.cloned.1.call-update) | async-done | bytes 4194320 | tf_op jit(solution)/shard_map/psum | solution.py:2067
  434.7 0.0 all-to-all-done.gd_ref
  434.7 222.7 %finish.1 = (bf16[3,256,2048]{2,1,0:T(8,128)(2,1)}, f32[256,8192]{1,0:T(8,128)}, f32[256,2048]{1,0:T(8,128)}, f32[256,2048]{1,0:T(8,128)}, bf16[256,2048]{1,0:T(8,128)(2,1)}, /*index=5*/f32[16,2048]{1,0:T(8,128)}) custom-call(bf16[3,256,2048]{2,1,0:T(8,128)(2,1)} %bitcast.46, bf16[8,256,1024]{2,1,0:T(8,128)(2,1)} %all-to-all-done.gd_ref, ...), custom_call_target="tpu_custom_call" | custom-call | tf_op jit(solution)/shard_map/finish/pallas_call | solution.py:1935
  657.4 1.6 fusion.3
  659.0 0.8 slice_bitcast_fusion
  659.7 0.6 copy.23
  660.4 9.5 %widen.1 = (f32[768,2048]{1,0:T(8,128)}, f32[1024,2048]{1,0:T(8,128)}) custom-call(bf16[768,2048]{1,0:T(8,128)(2,1)} %bitcast.47, bf16[1024,2048]{1,0:T(8,128)(2,1)} %all-reduce.2.cloned.1.call-done.refs_1_), custom_call_target="tpu_custom_call" | custom-call | tf_op jit(solution)/shard_map/widen/pallas_call | solution.py:2008
  669.9 0.0 copy-done.5
  669.9 1.0 copy.29
  670.8 0.0 copy-done.3
  670.8 1.3 copy.30
  672.2 1.3 copy.31
  673.5 7.7 %copy.32 = f32[256,8192]{1,0:T(8,128)} copy(f32[256,8192]{1,0:T(8,128)} %get-tuple-element.117) | data formatting | bytes 16777216
  (8 shorter events, 0.0 us)
Async XLA Ops:
  7.2 182.5 %all-gather.3.cloned.1.call-start = ((), (), s32[]{:S(2)}) async-start(), calls=%async_computation.1 | async-start | bytes 9437184 | tf_op jit(solution)/shard_map/all_gather | solution.py:2041
  7.9 193.7 %all-gather.5.cloned.1.call-start = ((), (), s32[]{:S(2)}) async-start(), calls=%async_computation.2 | async-start | bytes 9437184 | tf_op jit(solution)/shard_map/all_gather | solution.py:2054
  12.0 115.8 %copy-start.6 = (s32[1,2048]{1,0:T(1,128)}, s32[1,2048]{1,0:T(1,128)S(1)}, u32[]{:S(2)}) copy-start(s32[1,2048]{1,0:T(1,128)S(1)} %compare_select_fusion.2.start_ref) | copy-start | bytes 24580
  127.7 306.9 %all-reduce.2.cloned.1.call-start = ((), (), s32[]{:S(2)}) async-start(), calls=%async_computation.3 | async-start | bytes 8388608 | tf_op jit(solution)/shard_map/psum | solution.py:2067
  354.4 80.3 %all-to-all-start = ((bf16[8,256,1024]{2,1,0:T(8,128)(2,1)}), bf16[8,256,1024]{2,1,0:T(8,128)(2,1)}, u32[]{:S(2)}, u32[]{:S(2)}) async-start(bf16[8,256,1024]{2,1,0:T(8,128)(2,1)} %get-tuple-element.80), calls=%async_computation | async-start | bytes 8388608 | tf_op jit(solution)/shard_map/all_to_all | solution.py:2074
  359.2 33.3 %copy-start = (bf16[256,2048]{1,0:T(8,128)(2,1)S(1)}, bf16[256,2048]{1,0:T(8,128)(2,1)}, u32[]{:S(2)}) copy-start(bf16[256,2048]{1,0:T(8,128)(2,1)} %get-tuple-element.75.gbr_ref) | copy-start | bytes 3145732
  359.2 33.3 %copy-start.4 = (bf16[256,2048]{1,0:T(8,128)(2,1)S(1)}, bf16[256,2048]{1,0:T(8,128)(2,1)}, u32[]{:S(2)}) copy-start(bf16[256,2048]{1,0:T(8,128)(2,1)} %get-tuple-element.81) | copy-start | bytes 3145732
  392.5 5.8 copy-start.1
  398.3 10.6 %copy-start.7 = (bf16[3,256,2048]{2,1,0:T(8,128)(2,1)S(1)}, bf16[3,256,2048]{2,1,0:T(8,128)(2,1)}, u32[]{:S(2)}) copy-start(bf16[3,256,2048]{2,1,0:T(8,128)(2,1)} %get-tuple-element.54) | copy-start | bytes 9437188
  657.3 12.5 %copy-start.5 = (bf16[256,2048]{1,0:T(8,128)(2,1)S(1)}, bf16[256,2048]{1,0:T(8,128)(2,1)}, u32[]{:S(2)}) copy-start(bf16[256,2048]{1,0:T(8,128)(2,1)} %get-tuple-element.87) | copy-start | bytes 3145732
  660.4 10.5 %copy-start.3 = (f32[256,2048]{1,0:T(8,128)S(1)}, f32[256,2048]{1,0:T(8,128)}, u32[]{:S(2)}) copy-start(f32[256,2048]{1,0:T(8,128)} %get-tuple-element.88) | copy-start | bytes 6291460
  669.9 2.3 copy-start.2
Sparse Core Ops, SparseCore 0:
  9.9 96.2 all-gather.2
  127.8 64.4 all-gather.4
  278.6 155.9 all-reduce.1
